TPU v7x, 32 devices: a whole 2x2x4 slice. The times are simulated.
32 devices in a mesh: grp: 4 (over y, x), seq: 8 (over z, core).
Axes of the slice: x: 2, y: 2, z: 4, core: 2. Of those that a mesh axis runs over, the one named last changes fastest.
Arguments:
- tokens: bfloat16 [4096, 1536], P(('grp', 'seq')), may hold values from -6 to 6
- cotangent: bfloat16 [4096, 1536], P(('grp', 'seq')), may hold values from -12 to 12
- shard_segment: int32 [4, 8], replicated, may hold values from 0 to 2, as said below
- gain_attn: bfloat16 [1536], replicated, may hold values from 0.099609375 to 1.8984375
- qkv_weight: bfloat16 [2048, 1536], P(('grp', 'seq')), may hold values from -0.21875 to 0.21875
- qkv_bias: bfloat16 [2048], P(('grp', 'seq')), may hold values from -3 to 3
- out_weight: bfloat16 [1536, 1536], P(('grp', 'seq')), may hold values from -0.625 to 0.625
- gain_mlp: bfloat16 [1536], replicated, may hold values from 0.099609375 to 1.8984375
- mlp_weight: bfloat16 [8960, 3, 1536], P(('grp', 'seq')), may hold values from -0.15625 to 0.15625
Outputs:
- output: bfloat16 [4096, 1536], P(('grp', 'seq'))
- grad_tokens: float32 [4096, 1536], P(('grp', 'seq'))
- grad_gain_attn: float32 [1536], P(('grp', 'seq'))
- grad_qkv_weight: float32 [2048, 1536], P(('grp', 'seq'))
- grad_qkv_bias: float32 [2048], P(('grp', 'seq'))
- grad_out_weight: float32 [1536, 1536], P(('grp', 'seq'))
- grad_gain_mlp: float32 [1536], P(('grp', 'seq'))
- grad_mlp_weight: float32 [8960, 3, 1536], P(('grp', 'seq'))
Inputs may be any that keep to these rules, and one draw needn't show every extreme that they name: For every group g, shard_segment[g, s] = 0 for s < 4; the later shards form runs of 2 or 4 shards with one number, one continuation each, numbered 1, 2, ... in order; every run starts at an even shard, a run of 4 at 4 plus a multiple of 4; some group has only runs of 2, and some group has a run of 4.
All inputs are finite; a program needn't handle non-finite values.
Results may differ from a plain program's by a relative error of at most 0.02.
Values may be sent and summed in bfloat16 or wider, within the bound.
A program may use at most 576 MiB of HBM per device.

v0:
```python
import math

import jax
import jax.numpy as jnp
from jax import lax
from jax.sharding import PartitionSpec as P

H = 12
KVH = 2
HD = 128
FF = 8960


EPS = 1e-06
THETA = 10000.0


def rms_scale(values, gain_vec):
    return values * lax.rsqrt(jnp.mean(values * values, axis=-1, keepdims=True) + EPS) * gain_vec


def rotary_tables(positions, head_dim):
    half_dim = head_dim // 2
    freqs = THETA ** (-(jnp.arange(half_dim, dtype=jnp.float32) * 2.0) / head_dim)
    angles = positions.astype(jnp.float32)[:, None] * freqs[None, :]
    cosine_table = jnp.concatenate([jnp.cos(angles), jnp.cos(angles)], axis=-1)
    sine_table = jnp.concatenate([jnp.sin(angles), jnp.sin(angles)], axis=-1)
    return (cosine_table, sine_table)


def rotate(values, cosine_table, sine_table):
    half_dim = values.shape[-1] // 2
    turned = jnp.concatenate([-values[..., half_dim:], values[..., :half_dim]], axis=-1)
    return values * cosine_table[:, None, :] + turned * sine_table[:, None, :]


def unrotate(grad_rows, cosine_table, sine_table):
    half_dim = grad_rows.shape[-1] // 2
    scaled = grad_rows * sine_table[:, None, :]
    turned = jnp.concatenate([scaled[..., half_dim:], -scaled[..., :half_dim]], axis=-1)
    return grad_rows * cosine_table[:, None, :] + turned


def shard_starts(segments, tok_dev, prompt_len):
    shard_total = segments.shape[0]
    shard_order = jnp.arange(shard_total, dtype=jnp.int32)
    same_seg = segments[:, None] == segments[None, :]
    first_shard = jnp.min(jnp.where(same_seg, shard_order[None, :], shard_total), axis=1)
    cont_start = prompt_len + (shard_order - first_shard) * tok_dev
    return jnp.where(segments == 0, shard_order * tok_dev, cont_start)


def swish_product(gate_vals, upper_vals):
    return jax.nn.silu(gate_vals) * upper_vals


def per_device(
    tokens,
    cotangent,
    shard_segment,
    gain_attn,
    qkv_weight,
    qkv_bias,
    out_weight,
    gain_mlp,
    mlp_weight,
):
    tok_rows = tokens.shape[0]
    seq_count = lax.axis_size("seq")
    group_tok = tok_rows * seq_count
    heads_per = H // KVH
    kv_width = KVH * HD
    att_width = H * HD
    query_rows = heads_per * tok_rows
    score_scale = 1.0 / math.sqrt(HD)
    contract_last = (((1,), (1,)), ((), ()))
    contract_first = (((0,), (0,)), ((), ()))
    seq_place = lax.axis_index("seq")
    grp_place = lax.axis_index("grp")
    segments = lax.dynamic_index_in_dim(shard_segment, grp_place, 0, keepdims=False)
    starts = shard_starts(segments, tok_rows, group_tok // 2)
    shard_order = jnp.arange(seq_count, dtype=jnp.int32)
    own_seg = jnp.sum(jnp.where(shard_order == seq_place, segments, 0))
    own_start = jnp.sum(jnp.where(shard_order == seq_place, starts, 0))
    positions = own_start + jnp.arange(tok_rows, dtype=jnp.int32)
    cosine_table, sine_table = rotary_tables(positions, HD)
    query_pos = jnp.tile(positions, heads_per)
    tokens_wide = tokens.astype(jnp.float32)
    gain_one = gain_attn.astype(jnp.float32)
    gain_two = gain_mlp.astype(jnp.float32)
    normed_one = rms_scale(tokens_wide, gain_one).astype(jnp.bfloat16)
    weight_rows = lax.all_gather(qkv_weight, ("grp", "seq"), axis=0, tiled=True)
    bias_rows = lax.all_gather(qkv_bias, ("grp", "seq"), axis=0, tiled=True)
    projected = lax.dot_general(
        normed_one, weight_rows, contract_last, preferred_element_type=jnp.float32
    )
    projected = projected + bias_rows.astype(jnp.float32)[None, :]
    query_rot = rotate(
        projected[:, :att_width].reshape(tok_rows, H, HD), cosine_table, sine_table
    ).astype(jnp.bfloat16)
    key_rot = rotate(
        projected[:, att_width : att_width + kv_width].reshape(tok_rows, KVH, HD),
        cosine_table,
        sine_table,
    ).astype(jnp.bfloat16)
    value_low = projected[:, att_width + kv_width :].astype(jnp.bfloat16)
    keys_all, values_all = (
        lax.all_gather(key_rot.reshape(tok_rows, kv_width), "seq", axis=0, tiled=True),
        lax.all_gather(value_low, "seq", axis=0, tiled=True),
    )
    queries = (
        query_rot.reshape(tok_rows, KVH, heads_per, HD)
        .transpose(1, 2, 0, 3)
        .reshape(KVH, query_rows, HD)
    )
    key_block = min(512, group_tok)
    block_count = group_tok // key_block
    block_order = jnp.arange(block_count, dtype=jnp.int32)

    def block_mask(block_index):
        key_index = block_index * key_block + jnp.arange(key_block, dtype=jnp.int32)
        key_shard = key_index // tok_rows
        onehot = key_shard[:, None] == shard_order[None, :]
        key_seg = jnp.sum(jnp.where(onehot, segments[None, :], 0), axis=1)
        key_pos = jnp.sum(jnp.where(onehot, starts[None, :], 0), axis=1) + key_index % tok_rows
        visible = (key_seg == 0) | (key_seg == own_seg)
        return visible[None, :] & (key_pos[None, :] <= query_pos[:, None])

    def block_keys(block_index):
        key_part = lax.dynamic_slice_in_dim(
            keys_all, block_index * key_block, key_block, 0
        ).reshape(key_block, KVH, HD)
        value_part = lax.dynamic_slice_in_dim(
            values_all, block_index * key_block, key_block, 0
        ).reshape(key_block, KVH, HD)
        return (key_part, value_part)

    def block_scores(key_part):
        return (
            jnp.einsum("krd,jkd->krj", queries, key_part, preferred_element_type=jnp.float32)
            * score_scale
        )

    def stat_step(stats_now, block_index):
        allowed = block_mask(block_index)

        def stat_visit(current):
            top_old, total_old = current
            key_part, value_part = block_keys(block_index)
            scores = jnp.where(allowed[None], block_scores(key_part), -1e30)
            top_new = jnp.maximum(top_old, jnp.max(scores, axis=-1))
            weights = jnp.where(allowed[None], jnp.exp(scores - top_new[..., None]), 0.0)
            return (top_new, total_old * jnp.exp(top_old - top_new) + jnp.sum(weights, axis=-1))

        return (lax.cond(jnp.any(allowed), stat_visit, lambda current: current, stats_now), None)

    start_stats = (
        jnp.full((KVH, query_rows), -1e30, jnp.float32),
        jnp.zeros((KVH, query_rows), jnp.float32),
    )
    (top_all, total_all), unused = lax.scan(stat_step, start_stats, block_order)
    log_total = top_all + jnp.log(total_all)

    def mix_step(mixed_sum, block_index):
        allowed = block_mask(block_index)

        def mix_visit(current):
            key_part, value_part = block_keys(block_index)
            prob_low = jnp.where(
                allowed[None], jnp.exp(block_scores(key_part) - log_total[..., None]), 0.0
            ).astype(jnp.bfloat16)
            return current + jnp.einsum(
                "krj,jkd->krd", prob_low, value_part, preferred_element_type=jnp.float32
            )

        return (lax.cond(jnp.any(allowed), mix_visit, lambda current: current, mixed_sum), None)

    mixed_sum, unused = lax.scan(
        mix_step, jnp.zeros((KVH, query_rows, HD), jnp.float32), block_order
    )
    attn_wide = (
        mixed_sum.reshape(KVH, heads_per, tok_rows, HD)
        .transpose(2, 0, 1, 3)
        .reshape(tok_rows, att_width)
    )
    attn_low = attn_wide.astype(jnp.bfloat16)
    column_part = attn_low
    attn_proj = jnp.dot(
        column_part,
        lax.all_gather(out_weight, ("grp", "seq"), axis=0, tiled=True),
        preferred_element_type=jnp.float32,
    )
    state = tokens_wide + attn_proj
    normed_two = rms_scale(state, gain_two).astype(jnp.bfloat16)

    def gate_up(weight_rows):
        gate_vals = lax.dot_general(
            normed_two, weight_rows[:, 0, :], contract_last, preferred_element_type=jnp.float32
        )
        upper_vals = lax.dot_general(
            normed_two, weight_rows[:, 1, :], contract_last, preferred_element_type=jnp.float32
        )
        return (gate_vals, upper_vals)

    units_zero = jnp.zeros((3, FF, tok_rows), jnp.bfloat16)
    weight_rows = lax.all_gather(mlp_weight, ("grp", "seq"), axis=0, tiled=True)
    gate_vals, upper_vals = gate_up(weight_rows)
    unit_low = swish_product(gate_vals, upper_vals).astype(jnp.bfloat16)
    unit_low, out_part = (
        unit_low,
        jnp.dot(unit_low, weight_rows[:, 2, :], preferred_element_type=jnp.float32),
    )
    offset = jnp.int32(0)
    lead = offset * 0
    units_half = lax.dynamic_update_slice(units_zero, unit_low.T[None], (lead + 2, offset, lead))
    weight_rows = lax.all_gather(mlp_weight, ("grp", "seq"), axis=0, tiled=True)
    gate_vals, upper_vals = gate_up(weight_rows)
    unit_grad = lax.dot_general(
        cotangent, weight_rows[:, 2, :], contract_last, preferred_element_type=jnp.float32
    )
    unused_value, pull_back = jax.vjp(swish_product, gate_vals, upper_vals)
    gate_grad, upper_grad = pull_back(unit_grad)
    pair_low = jnp.stack([gate_grad.T, upper_grad.T], axis=0).astype(jnp.bfloat16)
    input_grad = jnp.einsum(
        "jft,fjd->td", pair_low, weight_rows[:, :2, :], preferred_element_type=jnp.float32
    )
    pair_low, grad_part = (pair_low, input_grad)
    offset = jnp.int32(0)
    lead = offset * 0
    units_stack = lax.dynamic_update_slice(units_half, pair_low, (lead, offset, lead))
    units_owned = lax.all_to_all(
        units_stack, ("grp", "seq"), split_axis=1, concat_axis=2, tiled=True
    )
    normed_piece = lax.all_gather(normed_two, ("grp", "seq"), axis=0, tiled=True)
    cot_piece = lax.all_gather(cotangent, ("grp", "seq"), axis=0, tiled=True)
    gate_terms = jnp.einsum(
        "jfn,nd->fjd", units_owned[:2], normed_piece, preferred_element_type=jnp.float32
    )
    down_terms = jnp.dot(units_owned[2], cot_piece, preferred_element_type=jnp.float32)
    mlp_grad = jnp.concatenate([gate_terms, down_terms[:, None, :]], axis=1)
    output = (state + out_part).astype(jnp.bfloat16)
    unused_state, norm_two_back = jax.vjp(rms_scale, state, gain_two)
    state_norm_grad, gain_two_grad = norm_two_back(grad_part)
    state_grad = state_norm_grad + cotangent.astype(jnp.float32)
    state_low = state_grad.astype(jnp.bfloat16)
    attn_grad = lax.dot_general(
        state_low,
        lax.all_gather(out_weight, ("grp", "seq"), axis=0, tiled=True),
        contract_last,
        preferred_element_type=jnp.float32,
    )
    attn_grad_low = attn_grad.astype(jnp.bfloat16)
    column_part = attn_low
    out_grad = lax.psum_scatter(
        lax.dot_general(column_part, state_low, contract_first, preferred_element_type=jnp.float32),
        ("grp", "seq"),
        scatter_dimension=0,
        tiled=True,
    )
    grad_heads = (
        attn_grad_low.reshape(tok_rows, KVH, heads_per, HD)
        .transpose(1, 2, 0, 3)
        .reshape(KVH, query_rows, HD)
    )
    delta_rows = jnp.sum(
        (attn_grad_low.astype(jnp.float32) * attn_wide).reshape(tok_rows, H, HD), axis=-1
    )
    delta_rows = (
        delta_rows.reshape(tok_rows, KVH, heads_per).transpose(1, 2, 0).reshape(KVH, query_rows)
    )

    def back_step(query_grad, block_index):
        allowed = block_mask(block_index)

        def back_visit(current):
            key_part, value_part = block_keys(block_index)
            prob_vals = jnp.where(
                allowed[None], jnp.exp(block_scores(key_part) - log_total[..., None]), 0.0
            )
            prob_grad = jnp.einsum(
                "krd,jkd->krj", grad_heads, value_part, preferred_element_type=jnp.float32
            )
            score_grad = (prob_vals * (prob_grad - delta_rows[..., None])).astype(jnp.bfloat16)
            new_grad = (
                current
                + jnp.einsum(
                    "krj,jkd->krd", score_grad, key_part, preferred_element_type=jnp.float32
                )
                * score_scale
            )
            key_grad = (
                jnp.einsum("krj,krd->jkd", score_grad, queries, preferred_element_type=jnp.float32)
                * score_scale
            )
            value_grad = jnp.einsum(
                "krj,krd->jkd",
                prob_vals.astype(jnp.bfloat16),
                grad_heads,
                preferred_element_type=jnp.float32,
            )
            return (
                new_grad,
                (key_grad.reshape(key_block, kv_width), value_grad.reshape(key_block, kv_width)),
            )

        def skip_block(current):
            blank_rows = jnp.zeros((key_block, kv_width), jnp.float32)
            return (current, (blank_rows, blank_rows))

        return lax.cond(jnp.any(allowed), back_visit, skip_block, query_grad)

    query_grad, (key_grads, value_grads) = lax.scan(
        back_step, jnp.zeros((KVH, query_rows, HD), jnp.float32), block_order
    )
    key_own, value_own = (
        lax.psum_scatter(
            key_grads.reshape(group_tok, kv_width).astype(jnp.bfloat16),
            "seq",
            scatter_dimension=0,
            tiled=True,
        ).astype(jnp.float32),
        lax.psum_scatter(
            value_grads.reshape(group_tok, kv_width).astype(jnp.bfloat16),
            "seq",
            scatter_dimension=0,
            tiled=True,
        ).astype(jnp.float32),
    )
    query_back = unrotate(
        query_grad.reshape(KVH, heads_per, tok_rows, HD)
        .transpose(2, 0, 1, 3)
        .reshape(tok_rows, H, HD),
        cosine_table,
        sine_table,
    )
    key_back = unrotate(key_own.reshape(tok_rows, KVH, HD), cosine_table, sine_table)
    qkv_grad_low = jnp.concatenate(
        [query_back.reshape(tok_rows, att_width), key_back.reshape(tok_rows, kv_width), value_own],
        axis=1,
    ).astype(jnp.bfloat16)
    bias_grad = jnp.sum(qkv_grad_low.astype(jnp.float32), axis=0)
    column_part = qkv_grad_low
    normed_one_grad = jnp.dot(
        column_part,
        lax.all_gather(qkv_weight, ("grp", "seq"), axis=0, tiled=True),
        preferred_element_type=jnp.float32,
    )
    column_part = qkv_grad_low
    qkv_grad = lax.psum_scatter(
        lax.dot_general(
            column_part, normed_one, contract_first, preferred_element_type=jnp.float32
        ),
        ("grp", "seq"),
        scatter_dimension=0,
        tiled=True,
    )
    unused_tokens, norm_one_back = jax.vjp(rms_scale, tokens_wide, gain_one)
    token_norm_grad, gain_one_grad = norm_one_back(normed_one_grad)
    token_grad = token_norm_grad + state_grad
    bias_part, gain_one_part, gain_two_part = (
        lax.psum_scatter(bias_grad, ("grp", "seq"), scatter_dimension=0, tiled=True),
        lax.psum_scatter(gain_one_grad, ("grp", "seq"), scatter_dimension=0, tiled=True),
        lax.psum_scatter(gain_two_grad, ("grp", "seq"), scatter_dimension=0, tiled=True),
    )
    return (
        output,
        token_grad,
        gain_one_part,
        qkv_grad,
        bias_part,
        out_grad,
        gain_two_part,
        mlp_grad,
    )


def solution(mesh):
    return jax.shard_map(
        per_device,
        mesh=mesh,
        in_specs=(
            P(("grp", "seq"), None),
            P(("grp", "seq"), None),
            P(),
            P(),
            P(("grp", "seq"), None),
            P(("grp", "seq")),
            P(("grp", "seq"), None),
            P(),
            P(("grp", "seq"), None, None),
        ),
        out_specs=(
            P(("grp", "seq"), None),
            P(("grp", "seq"), None),
            P(("grp", "seq")),
            P(("grp", "seq"), None),
            P(("grp", "seq")),
            P(("grp", "seq"), None),
            P(("grp", "seq")),
            P(("grp", "seq"), None, None),
        ),
        check_vma=False,
    )
```

profile of v0, /device:TPU:9, one launch (start us, length us, event | category | flops | bytes accessed | tf_op | source)
XLA Modules:
  0.0 1371.6 jit_solution(7723141530785707198)
XLA Ops:
  10.3 40.8 %all-reduce = bf16[2048]{0:T(1024)(128)(2,1)S(1)} all-reduce(bf16[2048]{0:T(1024)(128)(2,1)S(1)} %dynamic-update-slice), channel_id=1, replica_groups=mesh['grp'=4,'seq'=8] {'grp','seq'}, use_global_device_ids=true, to_apply=%add | all-reduce | flops 2048 | bytes 8192
  58.2 24.2 %all-gather.6.cloned.1.call-done = bf16[2048,1536]{1,0:T(8,128)(2,1)} async-done(((bf16[64,1536]{1,0:T(8,128)(2,1)}), bf16[2048,1536]{1,0:T(8,128)(2,1)}) %all-gather.6.cloned.1.call-update) | async-done | bytes 6291472 | tf_op jit(solution)/shard_map/all_gather | solution.py:92
  82.4 5.1 convolution_add_fusion.1
  88.2 13.8 %all_gather.29 = bf16[1024,256]{1,0:T(8,128)(2,1)S(1)} all-gather(bf16[128,256]{1,0:T(8,128)(2,1)S(1)} %fusion.109), channel_id=1, replica_groups=mesh['grp'=4,'seq'=8] {'seq'}, dimensions={0}, use_global_device_ids=true | all-gather | bytes 589824 | tf_op jit(solution)/shard_map/all_gather | solution.py:108
  103.0 16.0 %all_gather.30 = bf16[1024,256]{1,0:T(8,128)(2,1)S(1)} all-gather(bf16[128,256]{1,0:T(8,128)(2,1)S(1)} %slice.116), channel_id=1, replica_groups=mesh['grp'=4,'seq'=8] {'seq'}, dimensions={0}, use_global_device_ids=true | all-gather | bytes 589824 | tf_op jit(solution)/shard_map/all_gather | solution.py:109
  119.5 11.2 while.51
  132.3 13.0 while.52
  136.7 4.2 conditional.10
  137.4 3.5 fusion.15
  152.7 426.0 %all-gather.10.cloned.1.call-done = bf16[8960,3,1536]{2,0,1:T(8,128)(2,1)} async-done(((bf16[280,3,1536]{2,0,1:T(8,128)(2,1)}), bf16[8960,3,1536]{2,0,1:T(8,128)(2,1)}) %all-gather.10.cloned.1.call-update) | async-done | bytes 82575376 | tf_op jit(solution)/shard_map/all_gather | solution.py:206
  578.7 15.3 %fusion.55 = f32[128,8960]{1,0:T(8,128)} fusion(bf16[128,1536]{1,0:T(8,128)(2,1)S(1)} %multiply_convert_fusion.3, bf16[8960,3,1536]{2,0,1:T(8,128)(2,1)} %all-gather.10.cloned.1.call-done), kind=kOutput, calls=%fused_computation.99 | convolution fusion | flops 3523215360 | bytes 32505856 | tf_op jit(solution)/shard_map/dot_general | solution.py:200
  594.0 15.4 %fusion.56 = f32[128,8960]{1,0:T(8,128)} fusion(bf16[128,1536]{1,0:T(8,128)(2,1)S(1)} %multiply_convert_fusion.3, bf16[8960,3,1536]{2,0,1:T(8,128)(2,1)} %all-gather.10.cloned.1.call-done), kind=kOutput, calls=%fused_computation.101 | convolution fusion | flops 3523215360 | bytes 32505856 | tf_op jit(solution)/shard_map/dot_general | solution.py:197
  609.4 18.1 %fusion.86 = (bf16[1,8960,128]{1,2,0:T(8,128)(2,1)}, bf16[1,8960,128]{1,2,0:T(8,128)(2,1)}, bf16[1,8960,128]{1,2,0:T(8,128)(2,1)}) fusion(f32[128,8960]{1,0:T(8,128)} %fusion.55, f32[128,8960]{1,0:T(8,128)} %fusion.56, bf16[128,1536]{1,0:T(8,128)(2,1)S(1)} %copy-done.12, bf16[8960,3,1536]{2,0,1:T(8,128)(2,1)} %all-gather.10.cloned.1.call-done), kind=kOutput, calls=%fused_computation.138 | convolution fusion | flops 3541565440 | bytes 43974656 | tf_op jit(solution)/shard_map/dot_general | solution.py:218
  627.5 22.9 %multiply_reduce_fusion = (f32[1536]{0:T(1024)}, f32[128]{0:T(128)S(1)}, f32[128,1536]{1,0:T(8,128)}) fusion(f32[128,1536]{1,0:T(8,128)S(1)} %copy-done.8, f32[128]{0:T(128)S(1)} %fusion.116, f32[1536]{0:T(1024)S(1)} %convert_element_type.114, bf16[8960,3,1536]{2,0,1:T(8,128)(2,1)} %all-gather.10.cloned.1.call-done, ...), kind=kOutput, calls=%fused_computation.165 | convolution fusion | flops 7049902592 | bytes 61223936 | tf_op jit(solution)/shard_map/jft,fjd->td/dot_general | solution.py:224
  651.8 5.2 convert_multiply_fusion.4
  662.1 22.4 %while.53 = (s32[]{:T(128)}, f32[2,768,128]{2,1,0:T(8,128)S(1)}, bf16[2,512,256]{1,2,0:T(8,128)(2,1)}, bf16[2,512,256]{2,1,0:T(8,128)(2,1)}, s32[2]{0:T(128)}, /...) while((s32[]{:T(128)}, f32[2,768,128]{2,1,0:T(8,128)S(1)}, ...), condition=%wide.region_29.30_spmd.clone, body=%wide.region_23.29_spmd.clone.sunk | while | flops 1016368128 | bytes 27187196 | solution.py:312
  668.4 7.0 conditional.11
  688.5 6.1 fusion.103
  695.1 6.3 pad_maximum_fusion
  701.4 14.5 %copy.221 = bf16[3,8960,128]{2,0,1:T(4,128)(2,1)} copy(bf16[3,8960,128]{1,2,0:T(8,128)(2,1)} %pad_maximum_fusion) | data formatting | bytes 13762560 | tf_op jit(solution)/shard_map/dynamic_update_slice | solution.py:230
  715.9 11.8 all-to-all-start
  731.0 40.5 %reduce-scatter.13.cloned.1.call-done = bf16[128,256]{1,0:T(8,128)(2,1)} async-done(((bf16[1024,256]{1,0:T(8,128)(2,1)}), bf16[128,256]{1,0:T(8,128)(2,1)}) %reduce-scatter.13.cloned.1.call-update) | async-done | bytes 65552
  772.5 6.5 fusion.110
  780.1 15.4 %fusion.84 = bf16[128,1536]{1,0:T(8,128)(2,1)} fusion(f32[128,1536]{1,0:T(8,128)S(1)} %copy-done.10, bf16[8960,3,1536]{2,0,1:T(8,128)(2,1)} %all-gather.10.cloned.1.call-done, f32[128,8960]{1,0:T(8,128)} %fusion.55, f32[128,8960]{1,0:T(8,128)} %fusion.56), kind=kOutput, calls=%fused_computation.136 | convolution fusion | flops 3530489856 | bytes 37879808 | tf_op jit(solution)/shard_map/dot_general | solution.py:211
  795.7 4.0 fusion.94
  799.7 235.1 %all-reduce.4 = (f32[1536]{0:T(1024)S(1)}, f32[2048]{0:T(1024)S(1)}, f32[1536]{0:T(1024)S(1)}) all-reduce(f32[1536]{0:T(1024)S(1)} %get-tuple-element.902, f32[2048]{0:T(1024)S(1)} %convert_reduce_fusion, f32[1536]{0:T(1024)S(1)} %copy-done.27), channel_id=4, replica_groups=mesh['grp'=4,'seq'=8] {'grp','seq'}, use_global_device_ids=true, to_apply=%region_34.35.clone | all-reduce | flops 5120 | bytes 40960
  1037.8 5.4 copy.222
  1047.9 8.2 convolution_bitcast_fusion
  1056.1 8.1 all-gather.12.cloned.1.call-done
  1064.2 11.2 fusion.73
  1078.1 124.6 %reduce-scatter.11.cloned.1.call-done = f32[48,1536]{1,0:T(8,128)} async-done(((f32[1536,1536]{1,0:T(8,128)}), f32[48,1536]{1,0:T(8,128)}) %reduce-scatter.11.cloned.1.call-update) | async-done | bytes 294928 | tf_op jit(solution)/shard_map/reduce_scatter | solution.py:254
  1202.7 162.2 %reduce-scatter.9.cloned.1.call-done = f32[64,1536]{1,0:T(8,128)} async-done(((f32[2048,1536]{1,0:T(8,128)}), f32[64,1536]{1,0:T(8,128)}) %reduce-scatter.9.cloned.1.call-update) | async-done | bytes 393232 | tf_op jit(solution)/shard_map/reduce_scatter | solution.py:349
  (229 shorter events, 82.6 us)
Async XLA Ops:
  7.2 75.2 %all-gather.6.cloned.1.call-start = ((), (), s32[]{:S(2)}) async-start(), calls=%async_computation.5 | async-start | bytes 6488064 | tf_op jit(solution)/shard_map/all_gather | solution.py:92
  7.9 140.5 %all-gather.8.cloned.1.call-start = ((), (), s32[]{:S(2)}) async-start(), calls=%async_computation.6 | async-start | bytes 4866048 | tf_op jit(solution)/shard_map/all_gather | solution.py:190
  8.6 570.1 %all-gather.10.cloned.1.call-start = ((), (), s32[]{:S(2)}) async-start(), calls=%async_computation.7 | async-start | bytes 85155840 | tf_op jit(solution)/shard_map/all_gather | solution.py:206
  9.4 719.2 %reduce-scatter.7.cloned.1.call-start = ((), (), s32[]{:S(2)}) async-start(), calls=%async_computation.8 | async-start | bytes 589824 | tf_op jit(solution)/shard_map/reduce_scatter | solution.py:316
  51.8 35.8 %copy-start.23 = (f32[1536]{0:T(1024)}, f32[1536]{0:T(1024)S(1)}, u32[]{:S(2)}) copy-start(f32[1536]{0:T(1024)S(1)} %convert_element_type.107) | copy-start | bytes 18436
  54.9 47.8 %copy-start.18 = (f32[128,128]{0,1:T(8,128)}, f32[128,128]{0,1:T(8,128)S(1)}, u32[]{:S(2)}) copy-start(f32[128,128]{0,1:T(8,128)S(1)} %pad_maximum_fusion.6) | copy-start | bytes 196612
  55.0 33.0 %copy-start.20 = (f32[128,128]{1,0:T(8,128)}, f32[128,128]{1,0:T(8,128)S(1)}, u32[]{:S(2)}) copy-start(f32[128,128]{1,0:T(8,128)S(1)} %copy.197) | copy-start | bytes 196612
  55.0 47.7 %copy-start.16 = (f32[128,128]{0,1:T(8,128)}, f32[128,128]{0,1:T(8,128)S(1)}, u32[]{:S(2)}) copy-start(f32[128,128]{0,1:T(8,128)S(1)} %pad_maximum_fusion.5) | copy-start | bytes 196612
  58.2 29.4 %copy-start.28 = (f32[128]{0:T(128)}, f32[128]{0:T(128)S(1)}, u32[]{:S(2)}) copy-start(f32[128]{0:T(128)S(1)} %fusion.97) | copy-start | bytes 1540
  58.2 29.4 %copy-start.25 = (f32[128]{0:T(128)}, f32[128]{0:T(128)S(1)}, u32[]{:S(2)}) copy-start(f32[128]{0:T(128)S(1)} %fusion.115) | copy-start | bytes 1540
  88.2 13.9 %copy-start.14 = (f32[128,2,128]{2,1,0:T(2,128)}, f32[128,2,128]{2,1,0:T(2,128)S(1)}, u32[]{:S(2)}) copy-start(f32[128,2,128]{2,1,0:T(2,128)S(1)} %mul.335) | copy-start | bytes 393220
  132.3 16.2 %copy-start = (bf16[128,1536]{1,0:T(8,128)(2,1)S(1)}, bf16[128,1536]{1,0:T(8,128)(2,1)}, u32[]{:S(2)}) copy-start(bf16[128,1536]{1,0:T(8,128)(2,1)} %param.21) | copy-start | bytes 1179652
  152.7 441.3 %copy-start.13 = (bf16[128,1536]{1,0:T(8,128)(2,1)}, bf16[128,1536]{1,0:T(8,128)(2,1)S(1)}, u32[]{:S(2)}) copy-start(bf16[128,1536]{1,0:T(8,128)(2,1)S(1)} %multiply_convert_fusion.3) | copy-start | bytes 1179652
  594.0 15.4 %copy-start.12 = (bf16[128,1536]{1,0:T(8,128)(2,1)S(1)}, bf16[128,1536]{1,0:T(8,128)(2,1)}, u32[]{:S(2)}) copy-start(bf16[128,1536]{1,0:T(8,128)(2,1)} %param.22) | copy-start | bytes 1179652
  609.4 18.1 %copy-start.8 = (f32[128,1536]{1,0:T(8,128)S(1)}, f32[128,1536]{1,0:T(8,128)}, u32[]{:S(2)}) copy-start(f32[128,1536]{1,0:T(8,128)} %copy-done.7) | copy-start | bytes 2359300
  627.5 22.9 %copy-start.9 = (f32[128,1536]{1,0:T(8,128)S(1)}, f32[128,1536]{1,0:T(8,128)}, u32[]{:S(2)}) copy-start(f32[128,1536]{1,0:T(8,128)} %copy-done.7) | copy-start | bytes 2359300
  627.5 24.3 %copy-start.11 = (f32[128,1536]{1,0:T(8,128)S(1)}, f32[128,1536]{1,0:T(8,128)}, u32[]{:S(2)}) copy-start(f32[128,1536]{1,0:T(8,128)} %copy.209) | copy-start | bytes 2359300
  651.8 8.3 copy-start.2
  670.1 3.5 copy-start.6
  686.5 85.0 %reduce-scatter.13.cloned.1.call-start = ((), (), s32[]{:S(2)}) async-start(), calls=%async_computation.13 | async-start | bytes 589824
  687.1 360.8 %all-gather.14.cloned.1.call-start = ((), (), s32[]{:S(2)}) async-start(), calls=%async_computation.12 | async-start | bytes 12976128 | tf_op jit(solution)/shard_map/all_gather | solution.py:235
  687.7 376.5 %all-gather.12.cloned.1.call-start = ((), (), s32[]{:S(2)}) async-start(), calls=%async_computation.11 | async-start | bytes 12976128 | tf_op jit(solution)/shard_map/all_gather | solution.py:234
  688.4 514.2 %reduce-scatter.11.cloned.1.call-start = ((), (), s32[]{:S(2)}) async-start(), calls=%async_computation.10 | async-start | bytes 9732096 | tf_op jit(solution)/shard_map/reduce_scatter | solution.py:254
  715.9 11.9 copy-start.19
  715.9 321.9 %all-to-all-start = ((bf16[3,8960,128]{2,0,1:T(4,128)(2,1)}), bf16[3,8960,128]{2,0,1:T(4,128)(2,1)}, u32[]{:S(2)}, u32[]{:S(2)}) async-start(bf16[3,8960,128]{2,0,1:T(4,128)(2,1)} %copy.221), calls=%async_computation.3 | async-start | bytes 18350080 | tf_op jit(solution)/shard_map/all_to_all | solution.py:231
  727.7 44.8 %copy-start.1 = (bf16[128,1536]{1,0:T(8,128)(2,1)S(1)}, bf16[128,1536]{1,0:T(8,128)(2,1)}, u32[]{:S(2)}) copy-start(bf16[128,1536]{1,0:T(8,128)(2,1)} %param.21) | copy-start | bytes 1179652
  727.7 44.8 %copy-start.24 = (f32[1536]{0:T(1024)S(1)}, f32[1536]{0:T(1024)}, u32[]{:S(2)}) copy-start(f32[1536]{0:T(1024)} %copy-done.23) | copy-start | bytes 18436
  727.7 44.8 %copy-start.26 = (f32[128]{0:T(128)S(1)}, f32[128]{0:T(128)}, u32[]{:S(2)}) copy-start(f32[128]{0:T(128)} %copy-done.25) | copy-start | bytes 1540
  727.7 637.1 %reduce-scatter.9.cloned.1.call-start = ((), (), s32[]{:S(2)}) async-start(), calls=%async_computation.9 | async-start | bytes 12976128 | tf_op jit(solution)/shard_map/reduce_scatter | solution.py:349
  795.5 4.3 copy-start.27
  795.5 241.2 %copy-start.29 = (f32[128]{0:T(128)S(1)}, f32[128]{0:T(128)}, u32[]{:S(2)}) copy-start(f32[128]{0:T(128)} %copy-done.28) | copy-start | bytes 1540
  795.5 241.2 %copy-start.3 = (f32[128,1536]{1,0:T(8,128)S(1)}, f32[128,1536]{1,0:T(8,128)}, u32[]{:S(2)}) copy-start(f32[128,1536]{1,0:T(8,128)} %copy-done.2) | copy-start | bytes 2359300
  (8 other events, 12.4 us)
Sparse Core Ops, SparseCore 0:
  11.0 71.3 all-gather.5
  85.4 62.9 all-gather.7
  151.6 427.0 all-gather.9
  686.6 30.6 reduce-scatter.6
  719.6 51.9 reduce-scatter.12
  774.4 176.6 all-gather.13
  954.1 110.0 all-gather.11
  1070.7 131.9 reduce-scatter.10
  1210.3 154.4 reduce-scatter.8
where the time goes:
time: 1380 us; the launch traced here: 1370 us
  waiting for transfers between devices  790 us (57%)
  blocking collectives  306 us (22%)
  matrix products  147 us (11%)
  local copies, waits for them, and re-layouts  56.9 us (4%)
  other arithmetic  34.6 us (3%)
  between operations  14.8 us (1%)
    all_gather x1, waiting for transfers between devices, per_device(): weight_rows = lax.all_gather(mlp_weight, ('grp', 'seq'), axis=0, tiled=True)  426 us
    unnamed x2, blocking collectives  276 us
    reduce_scatter x1, waiting for transfers between devices, per_device(): lax.psum_scatter(lax.dot_general(column_part, normed_one, contract_first,...  162 us
    reduce_scatter x1, waiting for transfers between devices, per_device(): lax.psum_scatter(lax.dot_general(column_part, state_low, contract_first,...  125 us
    unnamed x10, waiting for transfers between devices  44.4 us
  transfers between devices with their start and end apart: 10, of which 7 were waited for; matrix products, arithmetic and copies ran while one was open for 9% of the time, Pallas kernels for 0%

commit v1 on v0

--- a/solution.py
+++ b/solution.py
@@ -52,6 +52,27 @@
 
 def swish_product(gate_vals, upper_vals):
     return jax.nn.silu(gate_vals) * upper_vals
+
+
+AXES = ("grp", "seq")
+CONTRACT_LAST = (((1,), (1,)), ((), ()))
+CONTRACT_FIRST = (((0,), (0,)), ((), ()))
+
+
+def columns_to_owners(rows, row_unit):
+    grp_count, seq_count = lax.axis_size("grp"), lax.axis_size("seq")
+    tok_rows = rows.shape[0]
+    split = rows.reshape(tok_rows, grp_count, seq_count, row_unit).transpose(2, 0, 1, 3)
+    split = split.reshape(seq_count * tok_rows, grp_count * row_unit)
+    return lax.all_to_all(split, "seq", split_axis=0, concat_axis=0, tiled=True)
+
+
+def owners_to_columns(rows, row_unit):
+    grp_count, seq_count = lax.axis_size("grp"), lax.axis_size("seq")
+    tok_rows = rows.shape[0] // seq_count
+    moved = lax.all_to_all(rows, "seq", split_axis=0, concat_axis=0, tiled=True)
+    moved = moved.reshape(seq_count, tok_rows, grp_count, row_unit).transpose(1, 2, 0, 3)
+    return moved.reshape(tok_rows, grp_count * seq_count * row_unit)
 
 
 def per_device(
@@ -67,14 +88,15 @@
 ):
     tok_rows = tokens.shape[0]
     seq_count = lax.axis_size("seq")
+    grp_count = lax.axis_size("grp")
     group_tok = tok_rows * seq_count
     heads_per = H // KVH
     kv_width = KVH * HD
     att_width = H * HD
     query_rows = heads_per * tok_rows
     score_scale = 1.0 / math.sqrt(HD)
-    contract_last = (((1,), (1,)), ((), ()))
-    contract_first = (((0,), (0,)), ((), ()))
+    contract_last = CONTRACT_LAST
+    contract_first = CONTRACT_FIRST
     seq_place = lax.axis_index("seq")
     grp_place = lax.axis_index("grp")
     segments = lax.dynamic_index_in_dim(shard_segment, grp_place, 0, keepdims=False)
@@ -89,12 +111,17 @@
     gain_one = gain_attn.astype(jnp.float32)
     gain_two = gain_mlp.astype(jnp.float32)
     normed_one = rms_scale(tokens_wide, gain_one).astype(jnp.bfloat16)
-    weight_rows = lax.all_gather(qkv_weight, ("grp", "seq"), axis=0, tiled=True)
-    bias_rows = lax.all_gather(qkv_bias, ("grp", "seq"), axis=0, tiled=True)
+    normed_one_all = lax.all_gather(normed_one, "seq", axis=0, tiled=True)
+    qkv_rows = lax.all_gather(qkv_weight, "grp", axis=0, tiled=True)
+    bias_rows = lax.all_gather(qkv_bias, "grp", axis=0, tiled=True)
+    mlp_rows = lax.all_gather(mlp_weight, "grp", axis=0, tiled=True)
+    cotangent_all = lax.all_gather(cotangent, "seq", axis=0, tiled=True)
+    out_full = lax.all_gather(out_weight, AXES, axis=0, tiled=True)
     projected = lax.dot_general(
-        normed_one, weight_rows, contract_last, preferred_element_type=jnp.float32
-    )
-    projected = projected + bias_rows.astype(jnp.float32)[None, :]
+        normed_one_all, qkv_rows, contract_last, preferred_element_type=jnp.float32
+    )
+    projected = (projected + bias_rows.astype(jnp.float32)[None, :]).astype(jnp.bfloat16)
+    projected = owners_to_columns(projected, qkv_weight.shape[0]).astype(jnp.float32)
     query_rot = rotate(
         projected[:, :att_width].reshape(tok_rows, H, HD), cosine_table, sine_table
     ).astype(jnp.bfloat16)
@@ -184,76 +211,68 @@
         .reshape(tok_rows, att_width)
     )
     attn_low = attn_wide.astype(jnp.bfloat16)
-    column_part = attn_low
-    attn_proj = jnp.dot(
-        column_part,
-        lax.all_gather(out_weight, ("grp", "seq"), axis=0, tiled=True),
-        preferred_element_type=jnp.float32,
-    )
+    attn_proj = jnp.dot(attn_low, out_full, preferred_element_type=jnp.float32)
     state = tokens_wide + attn_proj
     normed_two = rms_scale(state, gain_two).astype(jnp.bfloat16)
-
-    def gate_up(weight_rows):
-        gate_vals = lax.dot_general(
-            normed_two, weight_rows[:, 0, :], contract_last, preferred_element_type=jnp.float32
-        )
-        upper_vals = lax.dot_general(
-            normed_two, weight_rows[:, 1, :], contract_last, preferred_element_type=jnp.float32
-        )
-        return (gate_vals, upper_vals)
-
-    units_zero = jnp.zeros((3, FF, tok_rows), jnp.bfloat16)
-    weight_rows = lax.all_gather(mlp_weight, ("grp", "seq"), axis=0, tiled=True)
-    gate_vals, upper_vals = gate_up(weight_rows)
-    unit_low = swish_product(gate_vals, upper_vals).astype(jnp.bfloat16)
-    unit_low, out_part = (
-        unit_low,
-        jnp.dot(unit_low, weight_rows[:, 2, :], preferred_element_type=jnp.float32),
-    )
-    offset = jnp.int32(0)
-    lead = offset * 0
-    units_half = lax.dynamic_update_slice(units_zero, unit_low.T[None], (lead + 2, offset, lead))
-    weight_rows = lax.all_gather(mlp_weight, ("grp", "seq"), axis=0, tiled=True)
-    gate_vals, upper_vals = gate_up(weight_rows)
+    normed_two_all = lax.all_gather(normed_two, "seq", axis=0, tiled=True)
+    gate_rows, upper_rows, down_rows = mlp_rows[:, 0, :], mlp_rows[:, 1, :], mlp_rows[:, 2, :]
+    gate_vals = lax.dot_general(
+        normed_two_all, gate_rows, contract_last, preferred_element_type=jnp.float32
+    )
+    upper_vals = lax.dot_general(
+        normed_two_all, upper_rows, contract_last, preferred_element_type=jnp.float32
+    )
+    unit_wide, pull_back = jax.vjp(swish_product, gate_vals, upper_vals)
+    unit_low = unit_wide.astype(jnp.bfloat16)
     unit_grad = lax.dot_general(
-        cotangent, weight_rows[:, 2, :], contract_last, preferred_element_type=jnp.float32
-    )
-    unused_value, pull_back = jax.vjp(swish_product, gate_vals, upper_vals)
+        cotangent_all, down_rows, contract_last, preferred_element_type=jnp.float32
+    )
     gate_grad, upper_grad = pull_back(unit_grad)
-    pair_low = jnp.stack([gate_grad.T, upper_grad.T], axis=0).astype(jnp.bfloat16)
-    input_grad = jnp.einsum(
-        "jft,fjd->td", pair_low, weight_rows[:, :2, :], preferred_element_type=jnp.float32
-    )
-    pair_low, grad_part = (pair_low, input_grad)
-    offset = jnp.int32(0)
-    lead = offset * 0
-    units_stack = lax.dynamic_update_slice(units_half, pair_low, (lead, offset, lead))
-    units_owned = lax.all_to_all(
-        units_stack, ("grp", "seq"), split_axis=1, concat_axis=2, tiled=True
-    )
-    normed_piece = lax.all_gather(normed_two, ("grp", "seq"), axis=0, tiled=True)
-    cot_piece = lax.all_gather(cotangent, ("grp", "seq"), axis=0, tiled=True)
-    gate_terms = jnp.einsum(
-        "jfn,nd->fjd", units_owned[:2], normed_piece, preferred_element_type=jnp.float32
-    )
-    down_terms = jnp.dot(units_owned[2], cot_piece, preferred_element_type=jnp.float32)
-    mlp_grad = jnp.concatenate([gate_terms, down_terms[:, None, :]], axis=1)
+    gate_grad = gate_grad.astype(jnp.bfloat16)
+    upper_grad = upper_grad.astype(jnp.bfloat16)
+    input_grad = jnp.dot(gate_grad, gate_rows, preferred_element_type=jnp.float32) + jnp.dot(
+        upper_grad, upper_rows, preferred_element_type=jnp.float32
+    )
+    grad_part = lax.psum_scatter(
+        input_grad.astype(jnp.bfloat16), "seq", scatter_dimension=0, tiled=True
+    ).astype(jnp.float32)
+    out_part = lax.psum_scatter(
+        jnp.dot(unit_low, down_rows, preferred_element_type=jnp.float32).astype(jnp.bfloat16),
+        "seq",
+        scatter_dimension=0,
+        tiled=True,
+    ).astype(jnp.float32)
+    mlp_terms = jnp.stack(
+        [
+            lax.dot_general(
+                gate_grad, normed_two_all, contract_first, preferred_element_type=jnp.float32
+            ),
+            lax.dot_general(
+                upper_grad, normed_two_all, contract_first, preferred_element_type=jnp.float32
+            ),
+            lax.dot_general(
+                unit_low, cotangent_all, contract_first, preferred_element_type=jnp.float32
+            ),
+        ],
+        axis=1,
+    )
+    mlp_grad = lax.psum_scatter(mlp_terms, "grp", scatter_dimension=0, tiled=True)
     output = (state + out_part).astype(jnp.bfloat16)
     unused_state, norm_two_back = jax.vjp(rms_scale, state, gain_two)
     state_norm_grad, gain_two_grad = norm_two_back(grad_part)
     state_grad = state_norm_grad + cotangent.astype(jnp.float32)
     state_low = state_grad.astype(jnp.bfloat16)
     attn_grad = lax.dot_general(
-        state_low,
-        lax.all_gather(out_weight, ("grp", "seq"), axis=0, tiled=True),
-        contract_last,
-        preferred_element_type=jnp.float32,
+        state_low, out_full, contract_last, preferred_element_type=jnp.float32
     )
     attn_grad_low = attn_grad.astype(jnp.bfloat16)
-    column_part = attn_low
+    attn_owned = columns_to_owners(attn_low, out_weight.shape[0])
+    state_low_all = lax.all_gather(state_low, "seq", axis=0, tiled=True)
     out_grad = lax.psum_scatter(
-        lax.dot_general(column_part, state_low, contract_first, preferred_element_type=jnp.float32),
-        ("grp", "seq"),
+        lax.dot_general(
+            attn_owned, state_low_all, contract_first, preferred_element_type=jnp.float32
+        ),
+        "grp",
         scatter_dimension=0,
         tiled=True,
     )
@@ -338,29 +357,29 @@
         [query_back.reshape(tok_rows, att_width), key_back.reshape(tok_rows, kv_width), value_own],
         axis=1,
     ).astype(jnp.bfloat16)
-    bias_grad = jnp.sum(qkv_grad_low.astype(jnp.float32), axis=0)
-    column_part = qkv_grad_low
-    normed_one_grad = jnp.dot(
-        column_part,
-        lax.all_gather(qkv_weight, ("grp", "seq"), axis=0, tiled=True),
-        preferred_element_type=jnp.float32,
-    )
-    column_part = qkv_grad_low
+    qkv_grad_owned = columns_to_owners(qkv_grad_low, qkv_weight.shape[0])
+    bias_terms = jnp.sum(qkv_grad_owned.astype(jnp.float32), axis=0)
+    normed_one_grad = lax.psum_scatter(
+        jnp.dot(qkv_grad_owned, qkv_rows, preferred_element_type=jnp.float32).astype(jnp.bfloat16),
+        "seq",
+        scatter_dimension=0,
+        tiled=True,
+    ).astype(jnp.float32)
     qkv_grad = lax.psum_scatter(
         lax.dot_general(
-            column_part, normed_one, contract_first, preferred_element_type=jnp.float32
+            qkv_grad_owned, normed_one_all, contract_first, preferred_element_type=jnp.float32
         ),
-        ("grp", "seq"),
+        "grp",
         scatter_dimension=0,
         tiled=True,
     )
     unused_tokens, norm_one_back = jax.vjp(rms_scale, tokens_wide, gain_one)
     token_norm_grad, gain_one_grad = norm_one_back(normed_one_grad)
     token_grad = token_norm_grad + state_grad
-    bias_part, gain_one_part, gain_two_part = (
-        lax.psum_scatter(bias_grad, ("grp", "seq"), scatter_dimension=0, tiled=True),
-        lax.psum_scatter(gain_one_grad, ("grp", "seq"), scatter_dimension=0, tiled=True),
-        lax.psum_scatter(gain_two_grad, ("grp", "seq"), scatter_dimension=0, tiled=True),
+    bias_part = lax.psum_scatter(bias_terms, "grp", scatter_dimension=0, tiled=True)
+    gain_one_part, gain_two_part = (
+        lax.psum_scatter(gain_one_grad, AXES, scatter_dimension=0, tiled=True),
+        lax.psum_scatter(gain_two_grad, AXES, scatter_dimension=0, tiled=True),
     )
     return (
         output,

time: 1380 us -> 900 us (0.65)
  waiting for transfers between devices: 790 us -> 535 us
  blocking collectives: 306 us -> 135 us
  matrix products: 147 us -> 103 us
  local copies, waits for them, and re-layouts: 56.9 us -> 30.3 us
    all_gather x5 -> x6, waiting for transfers between devices: 459 us -> 183 us  [the longest x1 105 us: per_device(): mlp_rows = lax.all_gather(mlp_weight, 'grp', axis=0, tiled=True)]
    unnamed x2 -> x3, blocking collectives: 276 us -> 57.9 us
    dot_general x13 -> x15, matrix products: 136 us -> 95.7 us  [the longest x1 10.9 us: per_device(): lax.dot_general(cotangent_all, down_rows, contract_last, preferred_elemen...]
    all_to_all x0 -> x1, blocking collectives: none -> 31.9 us  [columns_to_owners(): return lax.all_to_all(split, 'seq', split_axis=0, concat_axis=0, tiled=True)]
    unnamed x10 -> x16, waiting for transfers between devices: 44.4 us -> 61 us
    dynamic_update_slice x1 -> x0, local copies, waits for them, and re-layouts: 14.5 us -> none  [per_device(): lax.dynamic_update_slice(units_half, pair_low, (lead, offset, lead))]
    reduce_scatter x3 -> x6, waiting for transfers between devices: 287 us -> 280 us  [the longest x1 189 us: per_device(): lax.psum_scatter(mlp_terms, 'grp', scatter_dimension=0, tiled=True)]
  transfers between devices with their start and end apart: 10 -> 16, of which waited for: 7 -> 11; matrix products, arithmetic and copies ran while one was open for 9% -> 13% of each run, Pallas kernels for 0% -> 0%
where the time goes in v1:
time: 900 us; the launch traced here: 890 us
  waiting for transfers between devices  535 us (59%)
  blocking collectives  135 us (15%)
  matrix products  103 us (11%)
  other arithmetic  46.9 us (5%)
  local copies, waits for them, and re-layouts  30.3 us (3%)
  between operations  16.3 us (2%)
  starting transfers between devices  13.5 us (2%)
  loops' own time  10.3 us (1%)
    reduce_scatter x1, waiting for transfers between devices, per_device(): lax.psum_scatter(mlp_terms, 'grp', scatter_dimension=0, tiled=True)  189 us
    all_gather x1, waiting for transfers between devices, per_device(): mlp_rows = lax.all_gather(mlp_weight, 'grp', axis=0, tiled=True)  105 us
    unnamed x16, waiting for transfers between devices  61 us
    unnamed x3, blocking collectives  57.9 us
    all_gather x1, waiting for transfers between devices, per_device(): normed_two_all = lax.all_gather(normed_two, 'seq', axis=0, tiled=True)  41 us
    reduce_scatter x1, waiting for transfers between devices, per_device(): lax.psum_scatter(input_grad.astype(jnp.bfloat16), 'seq', scatter_dimensio...  35.6 us
    reduce_scatter x1, waiting for transfers between devices, per_device(): lax.psum_scatter(lax.dot_general(attn_owned, state_low_all, contract_firs...  32.1 us
    all_to_all x1, blocking collectives, columns_to_owners(): return lax.all_to_all(split, 'seq', split_axis=0, concat_axis=0, tiled=True)  31.9 us
  transfers between devices with their start and end apart: 16, of which 11 were waited for; matrix products, arithmetic and copies ran while one was open for 13% of the time, Pallas kernels for 0%

profile of v1, /device:TPU:9, one launch (start us, length us, event | category | flops | bytes accessed | tf_op | source)
XLA Modules:
  0.0 890.3 jit_solution(11498734679071262989)
XLA Ops:
  14.6 7.9 all-reduce
  25.1 10.4 %all_gather.31 = bf16[256,1536]{1,0:T(8,128)(2,1)S(1)} all-gather(bf16[64,1536]{1,0:T(8,128)(2,1)} %param.25), channel_id=1, replica_groups=mesh['grp'=4,'seq'=8] {'grp'}, dimensions={0}, use_global_device_ids=true | all-gather | bytes 983040 | tf_op jit(solution)/shard_map/all_gather | solution.py:115
  35.6 14.5 %all-gather.7.cloned.1.call-done = bf16[1024,1536]{1,0:T(8,128)(2,1)} async-done(((bf16[128,1536]{1,0:T(8,128)(2,1)}), bf16[1024,1536]{1,0:T(8,128)(2,1)}) %all-gather.7.cloned.1.call-update) | async-done | bytes 3145744 | tf_op jit(solution)/shard_map/all_gather | solution.py:114
  62.6 10.9 %all-to-all-done = bf16[8,128,256]{1,2,0:T(8,128)(2,1)S(1)} async-done(((bf16[8,128,256]{1,2,0:T(8,128)(2,1)}), bf16[8,128,256]{1,2,0:T(8,128)(2,1)S(1)}, u32[]{:S(2)}, u32[]{:S(2)}) %all-to-all-start) | async-done | bytes 524320 | tf_op jit(solution)/shard_map/all_to_all | solution.py:73
  74.3 15.9 %all_gather.33 = bf16[1024,256]{0,1:T(8,128)(2,1)S(1)} all-gather(bf16[128,256]{0,1:T(8,128)(2,1)S(1)} %fusion.83), channel_id=1, replica_groups=mesh['grp'=4,'seq'=8] {'seq'}, dimensions={0}, use_global_device_ids=true | all-gather | bytes 589824 | tf_op jit(solution)/shard_map/all_gather | solution.py:135
  90.2 12.4 %while.51 = (s32[]{:T(128)}, f32[2,768]{1,0:T(2,128)S(1)}, f32[2,768]{1,0:T(2,128)S(1)}, s32[2]{0:T(128)S(1)}, s32[8]{0:T(128)}, /*index=5*/s32[]{:T(128)}, s32[...) while((s32[]{:T(128)}, f32[2,768]{1,0:T(2,128)S(1)}, ...), condition=%wide.region_12.13_spmd.clone, body=%wide.region_4.12_spmd.clone.sunk | while | flops 208836608 | bytes 8755057 | solution.py:188
  102.7 19.1 %all_gather.34 = bf16[1024,256]{0,1:T(8,128)(2,1)} all-gather(bf16[128,256]{0,1:T(8,128)(2,1)S(1)} %slice.63), channel_id=1, replica_groups=mesh['grp'=4,'seq'=8] {'seq'}, dimensions={0}, use_global_device_ids=true | all-gather | bytes 589824 | tf_op jit(solution)/shard_map/all_gather | solution.py:136
  121.8 13.4 %while.52 = (s32[]{:T(128)}, f32[2,768,128]{2,1,0:T(8,128)S(1)}, s32[2]{0:T(128)S(1)}, s32[8]{0:T(128)}, s32[]{:T(128)}, /*index=5*/s32[8]{0:T(128)}, bf16[1024,...) while((s32[]{:T(128)}, f32[2,768,128]{2,1,0:T(8,128)S(1)}, ...), condition=%wide.region_19.20_spmd.clone, body=%wide.region_13.19_spmd.clone.sunk | while | flops 407211008 | bytes 4355937 | solution.py:205
  142.2 41.0 %all-gather.11.cloned.1.call-done = bf16[1024,1536]{1,0:T(8,128)(2,1)} async-done(((bf16[128,1536]{1,0:T(8,128)(2,1)}), bf16[1024,1536]{1,0:T(8,128)(2,1)}) %all-gather.11.cloned.1.call-update) | async-done | bytes 3145744 | tf_op jit(solution)/shard_map/all_gather | solution.py:217
  183.2 104.9 %all-gather.13.cloned.1.call-done = bf16[1120,3,1536]{2,0,1:T(8,128)(2,1)} async-done(((bf16[280,3,1536]{2,0,1:T(8,128)(2,1)}), bf16[1120,3,1536]{2,0,1:T(8,128)(2,1)}) %all-gather.13.cloned.1.call-update) | async-done | bytes 10321936 | tf_op jit(solution)/shard_map/all_gather | solution.py:117
  288.0 9.0 %fusion.58 = f32[1024,1120]{0,1:T(8,128)} fusion(bf16[1024,1536]{1,0:T(8,128)(2,1)} %all-gather.11.cloned.1.call-done, bf16[1120,3,1536]{2,0,1:T(8,128)(2,1)} %all-gather.13.cloned.1.call-done), kind=kOutput, calls=%fused_computation.114 | convolution fusion | flops 3523215360 | bytes 11173888 | tf_op jit(solution)/shard_map/dot_general | solution.py:219
  297.0 7.7 fusion.59
  304.7 22.6 %all-gather.15.cloned.1.call-done = bf16[1024,1536]{1,0:T(8,128)(2,1)} async-done(((bf16[128,1536]{1,0:T(8,128)(2,1)}), bf16[1024,1536]{1,0:T(8,128)(2,1)}) %all-gather.15.cloned.1.call-update) | async-done | bytes 3145744 | tf_op jit(solution)/shard_map/all_gather | solution.py:118
  327.3 10.9 %multiply_convert_fusion = (bf16[1024,1120]{0,1:T(8,128)(2,1)S(1)}, bf16[1024,1120]{0,1:T(8,128)(2,1)S(1)}, bf16[1024,1120]{0,1:T(8,128)(2,1)}) fusion(f32[1024,1120]{0,1:T(8,128)} %fusion.58, f32[1024,1120]{0,1:T(8,128)} %fusion.59, bf16[1024,1536]{1,0:T(8,128)(2,1)} %all-gather.15.cloned.1.call-done, bf16[1120,3,1536]{2,0,1:T(8,128)(2,1)} %all-gather.13.cloned.1.call-done), kind=kOutput, calls=%fused_computation.104 | convolution fusion | flops 3541565440 | bytes 22642688 | tf_op jit(solution)/shard_map/dot_general | solution.py:227
  338.2 8.0 fusion.57
  346.2 8.0 add_convert_fusion
  356.5 35.6 %reduce-scatter.15.cloned.1.call-done = bf16[128,1536]{1,0:T(8,128)(2,1)} async-done(((bf16[1024,1536]{1,0:T(8,128)(2,1)}), bf16[128,1536]{1,0:T(8,128)(2,1)}) %reduce-scatter.15.cloned.1.call-update) | async-done | bytes 393232 | tf_op jit(solution)/shard_map/reduce_scatter | solution.py:236
  403.7 19.8 %while.53 = (s32[]{:T(128)}, f32[2,768,128]{2,1,0:T(8,128)S(1)}, bf16[2,512,256]{2,1,0:T(8,128)(2,1)}, bf16[2,512,256]{2,1,0:T(8,128)(2,1)}, s32[2]{0:T(128)}, /...) while((s32[]{:T(128)}, f32[2,768,128]{2,1,0:T(8,128)S(1)}, ...), condition=%wide.region_31.32_spmd.clone, body=%wide.region_25.31_spmd.clone.sunk | while | flops 1016368128 | bytes 26187796 | solution.py:331
  409.3 6.2 conditional.11
  427.7 27.4 %reduce-scatter.25.cloned.1.call-done = bf16[128,256]{1,0:T(8,128)(2,1)} async-done(((bf16[1024,256]{1,0:T(8,128)(2,1)}), bf16[128,256]{1,0:T(8,128)(2,1)}) %reduce-scatter.25.cloned.1.call-update) | async-done | bytes 65552
  456.1 30.4 %reduce-scatter.27.cloned.1.call-done = bf16[128,256]{1,0:T(8,128)(2,1)} async-done(((bf16[1024,256]{1,0:T(8,128)(2,1)}), bf16[128,256]{1,0:T(8,128)(2,1)}) %reduce-scatter.27.cloned.1.call-update) | async-done | bytes 65552
  487.5 31.9 %all_to_all.33 = bf16[8,128,256]{1,2,0:T(8,128)(2,1)S(1)} all-to-all(bf16[8,128,256]{1,2,0:T(8,128)(2,1)S(1)} %bitcast.223), channel_id=1, replica_groups=mesh['grp'=4,'seq'=8] {'seq'}, dimensions={0} | all-to-all | bytes 1048576 | tf_op jit(solution)/shard_map/all_to_all | solution.py:67
  522.6 8.6 convolution_convert_fusion.1
  536.6 7.6 all-to-all-start.2
  544.1 9.5 %convolution_bitcast_fusion = f32[1120,1,1536]{2,0,1:T(8,128)} fusion(bf16[1024,1120]{0,1:T(8,128)(2,1)} %get-tuple-element.915, bf16[1024,1536]{1,0:T(8,128)(2,1)} %all-gather.15.cloned.1.call-done), kind=kOutput, calls=%fused_computation.96 | convolution fusion | flops 3523215360 | bytes 12320768 | tf_op jit(solution)/shard_map/dot_general | solution.py:253
  563.2 6.4 convolution_bitcast_fusion.2
  569.6 12.4 %pad_maximum_fusion = f32[1120,3,1536]{2,0,1:T(8,128)} fusion(f32[1120,1,1536]{2,0,1:T(8,128)} %convolution_bitcast_fusion, f32[1120,1,1536]{2,0,1:T(8,128)} %convolution_bitcast_fusion.1, f32[1120,1,1536]{2,0,1:T(8,128)S(1)} %convolution_bitcast_fusion.2), kind=kLoop, calls=%fused_computation.95 | loop fusion | flops 10321920 | bytes 41287680 | tf_op jit(solution)/shard_map/stack | solution.py:245
  582.9 7.9 all-reduce.2
  592.8 42.2 %all-reduce.4 = (f32[1536]{0:T(1024)S(1)}, f32[1536]{0:T(1024)S(1)}) all-reduce(f32[1536]{0:T(1024)S(1)} %get-tuple-element.819, f32[1536]{0:T(1024)S(1)} %copy-done.17), channel_id=7, replica_groups=mesh['grp'=4,'seq'=8] {'grp','seq'}, use_global_device_ids=true, to_apply=%region_37.38.clone | all-reduce | flops 3072 | bytes 24576
  638.7 23.2 %reduce-scatter.19.cloned.1.call-done = f32[64,1536]{1,0:T(8,128)} async-done(((f32[256,1536]{1,0:T(8,128)}), f32[64,1536]{1,0:T(8,128)}) %reduce-scatter.19.cloned.1.call-update) | async-done | bytes 393232 | tf_op jit(solution)/shard_map/reduce_scatter | solution.py:368
  661.9 32.1 %reduce-scatter.21.cloned.1.call-done = f32[48,1536]{1,0:T(8,128)} async-done(((f32[192,1536]{1,0:T(8,128)}), f32[48,1536]{1,0:T(8,128)}) %reduce-scatter.21.cloned.1.call-update) | async-done | bytes 294928 | tf_op jit(solution)/shard_map/reduce_scatter | solution.py:271
  694.0 189.3 %reduce-scatter.23.cloned.1.call-done = f32[280,3,1536]{2,0,1:T(8,128)} async-done(((f32[1120,3,1536]{2,0,1:T(8,128)}), f32[280,3,1536]{2,0,1:T(8,128)}) %reduce-scatter.23.cloned.1.call-update) | async-done | bytes 5160976 | tf_op jit(solution)/shard_map/reduce_scatter | solution.py:259
  (260 shorter events, 114.5 us)
Async XLA Ops:
  7.2 42.9 %all-gather.7.cloned.1.call-start = ((), (), s32[]{:S(2)}) async-start(), calls=%async_computation.11 | async-start | bytes 3538944 | tf_op jit(solution)/shard_map/all_gather | solution.py:114
  7.9 16.4 %copy-start.15 = (f32[1536]{0:T(1024)}, f32[1536]{0:T(1024)S(1)}, u32[]{:S(2)}) copy-start(f32[1536]{0:T(1024)S(1)} %convert_element_type.153) | copy-start | bytes 18436
  9.1 15.2 %copy-start.28 = (f32[128]{0:T(128)}, f32[128]{0:T(128)S(1)}, u32[]{:S(2)}) copy-start(f32[128]{0:T(128)S(1)} %fusion.72) | copy-start | bytes 1540
  9.1 15.2 %copy-start.23 = (f32[128]{0:T(128)}, f32[128]{0:T(128)S(1)}, u32[]{:S(2)}) copy-start(f32[128]{0:T(128)S(1)} %fusion.88) | copy-start | bytes 1540
  11.0 125.4 %all-gather.9.cloned.1.call-start = ((), (), s32[]{:S(2)}) async-start(), calls=%async_computation.12 | async-start | bytes 4866048 | tf_op jit(solution)/shard_map/all_gather | solution.py:119
  35.6 17.4 %copy-start.10 = (bf16[256,1536]{1,0:T(8,128)(2,1)}, bf16[256,1536]{1,0:T(8,128)(2,1)S(1)}, u32[]{:S(2)}) copy-start(bf16[256,1536]{1,0:T(8,128)(2,1)S(1)} %all_gather.31) | copy-start | bytes 2359300
  35.6 23.2 %copy-start.25 = (bf16[1536]{0:T(1024)(128)(2,1)S(1)}, bf16[1536]{0:T(1024)(128)(2,1)}, u32[]{:S(2)}) copy-start(bf16[1536]{0:T(1024)(128)(2,1)} %param.28) | copy-start | bytes 9220
  54.0 19.6 %all-to-all-start = ((bf16[8,128,256]{1,2,0:T(8,128)(2,1)}), bf16[8,128,256]{1,2,0:T(8,128)(2,1)S(1)}, u32[]{:S(2)}, u32[]{:S(2)}) async-start(bf16[8,128,256]{1,2,0:T(8,128)(2,1)} %copy.165), calls=%async_computation | async-start | bytes 1048576 | tf_op jit(solution)/shard_map/all_to_all | solution.py:73
  58.8 124.4 %all-gather.11.cloned.1.call-start = ((), (), s32[]{:S(2)}) async-start(), calls=%async_computation.13 | async-start | bytes 3538944 | tf_op jit(solution)/shard_map/all_gather | solution.py:217
  121.8 14.6 %copy-start = (bf16[128,1536]{1,0:T(8,128)(2,1)S(1)}, bf16[128,1536]{1,0:T(8,128)(2,1)}, u32[]{:S(2)}) copy-start(bf16[128,1536]{1,0:T(8,128)(2,1)} %param.21) | copy-start | bytes 1179652
  139.9 254.0 %copy-start.18 = (f32[128]{0:T(128)}, f32[128]{0:T(128)S(1)}, u32[]{:S(2)}) copy-start(f32[128]{0:T(128)S(1)} %fusion.89) | copy-start | bytes 1540
  140.8 147.2 %all-gather.13.cloned.1.call-start = ((), (), s32[]{:S(2)}) async-start(), calls=%async_computation.14 | async-start | bytes 12902400 | tf_op jit(solution)/shard_map/all_gather | solution.py:117
  141.4 185.9 %all-gather.15.cloned.1.call-start = ((), (), s32[]{:S(2)}) async-start(), calls=%async_computation.16 | async-start | bytes 3538944 | tf_op jit(solution)/shard_map/all_gather | solution.py:118
  142.0 250.1 %reduce-scatter.15.cloned.1.call-start = ((), (), s32[]{:S(2)}) async-start(), calls=%async_computation.17 | async-start | bytes 3538944 | tf_op jit(solution)/shard_map/reduce_scatter | solution.py:236
  354.2 39.7 %copy-start.5 = (bf16[128,1536]{1,0:T(8,128)(2,1)S(1)}, bf16[128,1536]{1,0:T(8,128)(2,1)}, u32[]{:S(2)}) copy-start(bf16[128,1536]{1,0:T(8,128)(2,1)} %param.22) | copy-start | bytes 1179652
  354.2 100.8 %reduce-scatter.25.cloned.1.call-start = ((), (), s32[]{:S(2)}) async-start(), calls=%async_computation.23 | async-start | bytes 589824
  356.5 38.7 %copy-start.9 = (f32[128,1536]{1,0:T(8,128)S(1)}, f32[128,1536]{1,0:T(8,128)}, u32[]{:S(2)}) copy-start(f32[128,1536]{1,0:T(8,128)} %copy.171) | copy-start | bytes 2359300
  423.5 63.0 %reduce-scatter.27.cloned.1.call-start = ((), (), s32[]{:S(2)}) async-start(), calls=%async_computation.24 | async-start | bytes 589824
  424.2 135.2 %all-gather.17.cloned.1.call-start = ((), (), s32[]{:S(2)}) async-start(), calls=%async_computation.20 | async-start | bytes 3538944 | tf_op jit(solution)/shard_map/all_gather | solution.py:270
  425.0 166.4 %reduce-scatter.17.cloned.1.call-start = ((), (), s32[]{:S(2)}) async-start(), calls=%async_computation.18 | async-start | bytes 3538944 | tf_op jit(solution)/shard_map/reduce_scatter | solution.py:362
  427.7 92.0 %copy-start.11 = (bf16[256,1536]{1,0:T(8,128)(2,1)S(1)}, bf16[256,1536]{1,0:T(8,128)(2,1)}, u32[]{:S(2)}) copy-start(bf16[256,1536]{1,0:T(8,128)(2,1)} %copy-done.10) | copy-start | bytes 2359300
  522.3 113.8 %reduce-scatter.13.cloned.1.call-start = ((), (), s32[]{:S(2)}) async-start(), calls=%async_computation.15 | async-start | bytes 3538944 | tf_op jit(solution)/shard_map/reduce_scatter | solution.py:239
  531.3 130.6 %reduce-scatter.19.cloned.1.call-start = ((), (), s32[]{:S(2)}) async-start(), calls=%async_computation.19 | async-start | bytes 1966080 | tf_op jit(solution)/shard_map/reduce_scatter | solution.py:368
  536.6 22.8 %all-to-all-start.2 = ((bf16[8,128,192]{1,2,0:T(8,128)(2,1)}), bf16[8,128,192]{1,2,0:T(8,128)(2,1)S(1)}, u32[]{:S(2)}, u32[]{:S(2)}) async-start(bf16[8,128,192]{1,2,0:T(8,128)(2,1)} %bitcast.57), calls=%async_computation.6 | async-start | bytes 786432 | tf_op jit(solution)/shard_map/all_to_all | solution.py:67
  544.1 149.9 %reduce-scatter.21.cloned.1.call-start = ((), (), s32[]{:S(2)}) async-start(), calls=%async_computation.21 | async-start | bytes 1474560 | tf_op jit(solution)/shard_map/reduce_scatter | solution.py:271
  563.2 320.2 %reduce-scatter.23.cloned.1.call-start = ((), (), s32[]{:S(2)}) async-start(), calls=%async_computation.22 | async-start | bytes 25804800 | tf_op jit(solution)/shard_map/reduce_scatter | solution.py:259
  582.0 10.8 %copy-start.17 = (f32[1536]{0:T(1024)S(1)}, f32[1536]{0:T(1024)}, u32[]{:S(2)}) copy-start(f32[1536]{0:T(1024)} %get-tuple-element.817) | copy-start | bytes 18436
  582.0 54.1 %copy-start.29 = (f32[128]{0:T(128)S(1)}, f32[128]{0:T(128)}, u32[]{:S(2)}) copy-start(f32[128]{0:T(128)} %copy-done.28) | copy-start | bytes 1540
  582.0 54.1 %copy-start.6 = (bf16[128,1536]{1,0:T(8,128)(2,1)S(1)}, bf16[128,1536]{1,0:T(8,128)(2,1)}, u32[]{:S(2)}) copy-start(bf16[128,1536]{1,0:T(8,128)(2,1)} %param.22) | copy-start | bytes 1179652
  582.0 54.1 %copy-start.8 = (bf16[128,1536]{1,0:T(8,128)(2,1)S(1)}, bf16[128,1536]{1,0:T(8,128)(2,1)}, u32[]{:S(2)}) copy-start(bf16[128,1536]{1,0:T(8,128)(2,1)} %reduce-scatter.15.cloned.1.call-done) | copy-start | bytes 1179652
  582.0 54.1 %copy-start.19 = (f32[128]{0:T(128)S(1)}, f32[128]{0:T(128)}, u32[]{:S(2)}) copy-start(f32[128]{0:T(128)} %copy-done.18) | copy-start | bytes 1540
  582.1 54.1 %copy-start.27 = (f32[128]{0:T(128)S(1)}, f32[128]{0:T(128)}, u32[]{:S(2)}) copy-start(f32[128]{0:T(128)} %copy-done.26) | copy-start | bytes 1540
  (19 other events, 103.9 us)
Sparse Core Ops, SparseCore 0:
  11.1 38.8 all-gather.6
  53.1 70.0 all-gather.8
  140.9 42.1 all-gather.10
  184.9 103.1 all-gather.12
  289.5 37.7 all-gather.14
  354.4 37.6 reduce-scatter.14
  423.6 31.3 reduce-scatter.24
  457.4 29.0 reduce-scatter.26
  488.7 47.5 all-gather.16
  538.4 46.9 reduce-scatter.16
  587.7 38.6 reduce-scatter.12
  629.8 32.0 reduce-scatter.18
  665.4 28.5 reduce-scatter.20
  697.6 185.6 reduce-scatter.22

commit v2 on v1

--- a/solution.py
+++ b/solution.py
@@ -1,8 +1,11 @@
+import functools
 import math
 
 import jax
 import jax.numpy as jnp
 from jax import lax
+from jax.experimental import pallas as pl
+from jax.experimental.pallas import tpu as pltpu
 from jax.sharding import PartitionSpec as P
 
 H = 12
@@ -59,6 +62,318 @@
 CONTRACT_FIRST = (((0,), (0,)), ((), ()))
 
 
+MESH = pl.DeviceIdType.MESH
+
+
+def remote(src, dst, send_sem, recv_sem, grp, seq):
+    return pltpu.make_async_remote_copy(
+        src_ref=src, dst_ref=dst, send_sem=send_sem, recv_sem=recv_sem,
+        device_id=(grp, seq), device_id_type=MESH,
+    )
+
+
+def nearest_chip(place, order, chips):
+    both = 2 * jnp.minimum(place, chips - 1 - place)
+    offset = (order + 1) // 2
+    near = jnp.where(order % 2 == 1, place - offset, place + offset)
+    rest = jnp.where(place < chips - 1 - place, order, chips - 1 - order)
+    return jnp.where(order <= both, near, rest)
+
+
+def line_barrier(chips):
+    grp, seq = lax.axis_index("grp"), lax.axis_index("seq")
+    chip, core = seq // 2, seq % 2
+    mate = seq + 1 - 2 * core
+    barrier = pltpu.get_barrier_semaphore()
+
+    def greet(other):
+        pl.semaphore_signal(barrier, inc=1, device_id=(grp, other), device_id_type=MESH)
+
+    greet(mate)
+    pl.when(chip > 0)(lambda: greet(seq - 2))
+    pl.when(chip < chips - 1)(lambda: greet(seq + 2))
+    inner = jnp.where((chip > 0) & (chip < chips - 1), 1, 0)
+    pl.semaphore_wait(barrier, 2 + inner)
+
+
+class LineGather:
+    def __init__(self, buf, send_sem, recv_sem, chips):
+        self.buf, self.send_sem, self.recv_sem, self.chips = buf, send_sem, recv_sem, chips
+        self.grp, self.seq = lax.axis_index("grp"), lax.axis_index("seq")
+        self.chip, self.core = self.seq // 2, self.seq % 2
+        self.mate = self.seq + 1 - 2 * self.core
+
+    def copy(self, way, slot):
+        to = (self.seq + 2, self.seq - 2, self.mate)[way]
+        return remote(
+            self.buf.at[slot], self.buf.at[slot], self.send_sem.at[way, slot],
+            self.recv_sem.at[slot], self.grp, to,
+        )
+
+    def wait_recv(self, slot):
+        self.copy(2, slot).wait_recv()
+
+    def start(self):
+        pl.when(self.chip < self.chips - 1)(lambda: self.copy(0, self.seq).start())
+        pl.when(self.chip > 0)(lambda: self.copy(1, self.seq).start())
+        self.copy(2, self.seq).start()
+
+    def forward(self, step):
+        @pl.when(self.chip - step >= 0)
+        def _():
+            slot = self.seq - 2 * step
+            self.wait_recv(slot)
+            pl.when(self.chip < self.chips - 1)(lambda: self.copy(0, slot).start())
+            self.copy(2, slot).start()
+
+        @pl.when(self.chip + step < self.chips)
+        def _():
+            slot = self.seq + 2 * step
+            self.wait_recv(slot)
+            pl.when(self.chip > 0)(lambda: self.copy(1, slot).start())
+            self.copy(2, slot).start()
+
+    def wait_mate(self, chip):
+        self.wait_recv(2 * chip + 1 - self.core)
+
+    def drain(self):
+        for other in range(self.chips):
+            slot = 2 * other + self.core
+            self.copy(2, slot).wait_send()
+            pl.when((other <= self.chip) & (self.chip < self.chips - 1))(
+                lambda slot=slot: self.copy(0, slot).wait_send()
+            )
+            pl.when((other >= self.chip) & (self.chip > 0))(
+                lambda slot=slot: self.copy(1, slot).wait_send()
+            )
+
+
+class LineScatter:
+    def __init__(self, part, mate_in, left_in, right_in, send_sem, recv_sem, chips):
+        self.part, self.mate_in, self.left_in, self.right_in = part, mate_in, left_in, right_in
+        self.send_sem, self.recv_sem, self.chips = send_sem, recv_sem, chips
+        self.grp, self.seq = lax.axis_index("grp"), lax.axis_index("seq")
+        self.chip, self.core = self.seq // 2, self.seq % 2
+        self.mate = self.seq + 1 - 2 * self.core
+
+    def to_mate(self, r, chip):
+        return remote(
+            self.part.at[r, 2 * chip + 1 - self.core], self.mate_in.at[r, chip],
+            self.send_sem.at[0, r, chip], self.recv_sem.at[0, r, chip], self.grp, self.mate,
+        )
+
+    def to_right(self, r, chip):
+        return remote(
+            self.part.at[r, 2 * chip + self.core], self.left_in.at[r, chip],
+            self.send_sem.at[1, r, chip], self.recv_sem.at[1, r, chip], self.grp, self.seq + 2,
+        )
+
+    def to_left(self, r, chip):
+        return remote(
+            self.part.at[r, 2 * chip + self.core], self.right_in.at[r, chip],
+            self.send_sem.at[2, r, chip], self.recv_sem.at[2, r, chip], self.grp, self.seq - 2,
+        )
+
+    def step(self, r, order):
+        last = self.chips - 1
+        far = last - order
+
+        @pl.when(far > self.chip)
+        def _():
+            self.to_mate(r, far).wait_recv()
+            slot = 2 * far + self.core
+            total = self.part[r, slot].astype(jnp.float32) + self.mate_in[r, far].astype(jnp.float32)
+
+            @pl.when(self.chip > 0)
+            def _():
+                self.to_right(r, far).wait_recv()
+                self.part[r, slot] = (total + self.left_in[r, far].astype(jnp.float32)).astype(jnp.bfloat16)
+
+            @pl.when(self.chip == 0)
+            def _():
+                self.part[r, slot] = total.astype(jnp.bfloat16)
+
+            self.to_right(r, far).start()
+
+        @pl.when(order < self.chip)
+        def _():
+            self.to_mate(r, order).wait_recv()
+            slot = 2 * order + self.core
+            total = self.part[r, slot].astype(jnp.float32) + self.mate_in[r, order].astype(jnp.float32)
+
+            @pl.when(self.chip < last)
+            def _():
+                self.to_left(r, order).wait_recv()
+                self.part[r, slot] = (total + self.right_in[r, order].astype(jnp.float32)).astype(jnp.bfloat16)
+
+            @pl.when(self.chip == last)
+            def _():
+                self.part[r, slot] = total.astype(jnp.bfloat16)
+
+            self.to_left(r, order).start()
+
+    def finish(self, r, out_ref):
+        self.to_mate(r, self.chip).wait_recv()
+        out_ref[...] = self.part[r, self.seq].astype(jnp.float32) + self.mate_in[r, self.chip].astype(jnp.float32)
+
+        @pl.when(self.chip > 0)
+        def _():
+            self.to_right(r, self.chip).wait_recv()
+            out_ref[...] += self.left_in[r, self.chip].astype(jnp.float32)
+
+        @pl.when(self.chip < self.chips - 1)
+        def _():
+            self.to_left(r, self.chip).wait_recv()
+            out_ref[...] += self.right_in[r, self.chip].astype(jnp.float32)
+
+    def drain(self, r):
+        for other in range(self.chips):
+            self.to_mate(r, other).wait_send()
+            pl.when(other > self.chip)(lambda other=other: self.to_right(r, other).wait_send())
+            pl.when(other < self.chip)(lambda other=other: self.to_left(r, other).wait_send())
+
+
+def mlp_kernel(chips, grps, row_tiles, n2_ref, cot_ref, *refs):
+    w_refs, refs = refs[:grps], refs[grps:]
+    (
+        n2g_ref, outp_ref, grads_ref, tok, w, acts, part, mate_in, left_in, right_in, stage,
+        lsem, gsend, grecv, ssend, srecv, wsem, osem,
+    ) = refs
+    seq = lax.axis_index("seq")
+    chip, core = seq // 2, seq % 2
+    shard, width = n2_ref.shape
+    units = w.shape[1]
+    block = units // grps
+    tile = units // row_tiles
+    own = pltpu.make_async_copy(n2_ref, tok.at[0, seq], lsem.at[0])
+    own.start()
+    cot_copy = pltpu.make_async_copy(cot_ref, tok.at[1], lsem.at[1])
+    cot_copy.start()
+
+    def w_copy(j, b):
+        return pltpu.make_async_copy(w_refs[b].at[j], w.at[j, pl.ds(b * block, block)], wsem.at[j, b])
+
+    for j in range(3):
+        for b in range(grps):
+            w_copy(j, b).start()
+    line_barrier(chips)
+    gather = LineGather(tok.at[0], gsend, grecv, chips)
+    scatter = LineScatter(part, mate_in, left_in, right_in, ssend, srecv, chips)
+    own.wait()
+    gather.start()
+
+    @pl.loop(0, chips)
+    def _(order):
+        @pl.when(order == 0)
+        def _():
+            cot_copy.wait()
+            for j in range(3):
+                for b in range(grps):
+                    w_copy(j, b).wait()
+
+        pl.when(order > 0)(lambda: gather.forward(order))
+        at = nearest_chip(chip, order, chips)
+        gather.wait_mate(at)
+        x = tok[0, pl.ds(2 * at, 2)].reshape(2 * shard, width)
+        y = tok[1, pl.ds(2 * at, 2)].reshape(2 * shard, width)
+        gate = lax.dot_general(x, w[0], CONTRACT_LAST, preferred_element_type=jnp.float32)
+        up = lax.dot_general(x, w[1], CONTRACT_LAST, preferred_element_type=jnp.float32)
+        unit_grad = lax.dot_general(y, w[2], CONTRACT_LAST, preferred_element_type=jnp.float32)
+        sig = 1.0 / (1.0 + jnp.exp(-gate))
+        silu = gate * sig
+        rows = pl.ds(at * (2 * shard), 2 * shard)
+        gate_grad = (unit_grad * up * sig * (1.0 + gate * (1.0 - sig))).astype(jnp.bfloat16)
+        up_grad = (unit_grad * silu).astype(jnp.bfloat16)
+        acts[0, rows] = gate_grad
+        acts[1, rows] = up_grad
+        acts[2, rows] = (silu * up).astype(jnp.bfloat16)
+        back = jnp.dot(gate_grad, w[0], preferred_element_type=jnp.float32) + jnp.dot(
+            up_grad, w[1], preferred_element_type=jnp.float32
+        )
+        part[0, pl.ds(2 * at, 2)] = back.astype(jnp.bfloat16).reshape(2, shard, width)
+        scatter.to_mate(0, at).start()
+
+    def out_copy(t):
+        return pltpu.make_async_copy(
+            stage.at[t % 2],
+            grads_ref.at[t // row_tiles, pl.ds((t % row_tiles) * tile, tile)],
+            osem.at[t % 2],
+        )
+
+    @pl.loop(0, 3 * row_tiles)
+    def _(t):
+        @pl.when(t < 2 * chips)
+        def _():
+            scatter.step(t // chips, t % chips)
+
+        @pl.when(t < chips)
+        def _():
+            h = acts[2, pl.ds(t * (2 * shard), 2 * shard)]
+            part[1, pl.ds(2 * t, 2)] = (
+                jnp.dot(h, w[2], preferred_element_type=jnp.float32)
+                .astype(jnp.bfloat16).reshape(2, shard, width)
+            )
+            scatter.to_mate(1, t).start()
+
+        @pl.when(t >= 2)
+        def _():
+            out_copy(t - 2).wait()
+
+        kind = t // row_tiles
+        lhs = acts[kind, :, pl.ds(pl.multiple_of((t % row_tiles) * tile, 128), tile)]
+        rhs = tok[kind // 2].reshape(2 * chips * shard, width)
+        stage[t % 2] = lax.dot_general(
+            lhs, rhs, CONTRACT_FIRST, preferred_element_type=jnp.float32
+        ).astype(jnp.bfloat16)
+        out_copy(t).start()
+
+    scatter.finish(0, n2g_ref)
+    scatter.finish(1, outp_ref)
+    out_copy(3 * row_tiles - 2).wait()
+    out_copy(3 * row_tiles - 1).wait()
+    gather.drain()
+    scatter.drain(0)
+    scatter.drain(1)
+
+
+def mlp_call(n2, cot_all, w_blocks, row_tiles=3):
+    grps, (_, block, width) = len(w_blocks), w_blocks[0].shape
+    slots, shard, _ = cot_all.shape
+    chips = slots // 2
+    units = grps * block
+    vm, anyspace = pltpu.VMEM, pl.BlockSpec(memory_space=pl.ANY)
+    vspec = pl.BlockSpec(memory_space=pltpu.VMEM)
+    dma = pltpu.SemaphoreType.DMA
+    flops = 2 * 9 * slots * shard * units * width
+    return pl.pallas_call(
+        functools.partial(mlp_kernel, chips, grps, row_tiles),
+        out_shape=(
+            jax.ShapeDtypeStruct((shard, width), jnp.float32),
+            jax.ShapeDtypeStruct((shard, width), jnp.float32),
+            jax.ShapeDtypeStruct((3, units, width), jnp.bfloat16),
+        ),
+        in_specs=[vspec, anyspace] + [anyspace] * grps,
+        out_specs=(vspec, vspec, anyspace),
+        scratch_shapes=[
+            vm((2, slots, shard, width), jnp.bfloat16),
+            vm((3, units, width), jnp.bfloat16),
+            vm((3, slots * shard, units), jnp.bfloat16),
+            vm((2, slots, shard, width), jnp.bfloat16),
+            vm((2, chips, shard, width), jnp.bfloat16),
+            vm((2, chips, shard, width), jnp.bfloat16),
+            vm((2, chips, shard, width), jnp.bfloat16),
+            vm((2, units // row_tiles, width), jnp.bfloat16),
+            dma((2,)), dma((3, slots)), dma((slots,)), dma((3, 2, chips)), dma((3, 2, chips)),
+            dma((3, grps)), dma((2,)),
+        ],
+        compiler_params=pltpu.CompilerParams(
+            collective_id=1, has_side_effects=True, vmem_limit_bytes=62 * 2**20
+        ),
+        cost_estimate=pl.CostEstimate(flops=flops, bytes_accessed=30 * 2**20, transcendentals=0),
+        name="mlp",
+    )(n2, cot_all, *w_blocks)
+
+
 def columns_to_owners(rows, row_unit):
     grp_count, seq_count = lax.axis_size("grp"), lax.axis_size("seq")
     tok_rows = rows.shape[0]
@@ -73,6 +388,77 @@
     moved = lax.all_to_all(rows, "seq", split_axis=0, concat_axis=0, tiled=True)
     moved = moved.reshape(seq_count, tok_rows, grp_count, row_unit).transpose(1, 2, 0, 3)
     return moved.reshape(tok_rows, grp_count * seq_count * row_unit)
+
+
+def plain_mlp(normed_two, cotangent_all, mlp_weight):
+    contract_last, contract_first = CONTRACT_LAST, CONTRACT_FIRST
+    mlp_rows = lax.all_gather(mlp_weight, "grp", axis=0, tiled=True)
+    normed_two_all = lax.all_gather(normed_two, "seq", axis=0, tiled=True)
+    gate_rows, upper_rows, down_rows = mlp_rows[:, 0, :], mlp_rows[:, 1, :], mlp_rows[:, 2, :]
+    gate_vals = lax.dot_general(
+        normed_two_all, gate_rows, contract_last, preferred_element_type=jnp.float32
+    )
+    upper_vals = lax.dot_general(
+        normed_two_all, upper_rows, contract_last, preferred_element_type=jnp.float32
+    )
+    unit_wide, pull_back = jax.vjp(swish_product, gate_vals, upper_vals)
+    unit_low = unit_wide.astype(jnp.bfloat16)
+    unit_grad = lax.dot_general(
+        cotangent_all, down_rows, contract_last, preferred_element_type=jnp.float32
+    )
+    gate_grad, upper_grad = pull_back(unit_grad)
+    gate_grad = gate_grad.astype(jnp.bfloat16)
+    upper_grad = upper_grad.astype(jnp.bfloat16)
+    input_grad = jnp.dot(gate_grad, gate_rows, preferred_element_type=jnp.float32) + jnp.dot(
+        upper_grad, upper_rows, preferred_element_type=jnp.float32
+    )
+    grad_part = lax.psum_scatter(
+        input_grad.astype(jnp.bfloat16), "seq", scatter_dimension=0, tiled=True
+    ).astype(jnp.float32)
+    out_part = lax.psum_scatter(
+        jnp.dot(unit_low, down_rows, preferred_element_type=jnp.float32).astype(jnp.bfloat16),
+        "seq",
+        scatter_dimension=0,
+        tiled=True,
+    ).astype(jnp.float32)
+    mlp_terms = jnp.stack(
+        [
+            lax.dot_general(
+                gate_grad, normed_two_all, contract_first, preferred_element_type=jnp.float32
+            ),
+            lax.dot_general(
+                upper_grad, normed_two_all, contract_first, preferred_element_type=jnp.float32
+            ),
+            lax.dot_general(
+                unit_low, cotangent_all, contract_first, preferred_element_type=jnp.float32
+            ),
+        ],
+        axis=1,
+    )
+    mlp_grad = lax.psum_scatter(mlp_terms, "grp", scatter_dimension=0, tiled=True)
+    return grad_part, out_part, mlp_grad
+
+
+def padded_rows(mlp_weight):
+    rows = mlp_weight.transpose(1, 0, 2)
+    return jnp.pad(rows, ((0, 0), (0, -rows.shape[1] % 32), (0, 0)))
+
+
+def from_peer(values, offset, grp_count):
+    return lax.ppermute(values, "grp", [(g, g ^ offset) for g in range(grp_count)])
+
+
+def exchange_blocks(rows, grp_count):
+    return [rows] + [from_peer(rows, offset, grp_count) for offset in range(1, grp_count)]
+
+
+def sum_blocks(terms, grp_count):
+    block = terms.shape[1] // grp_count
+    total = terms[:, :block].astype(jnp.float32)
+    for offset in range(1, grp_count):
+        piece = terms[:, offset * block : (offset + 1) * block]
+        total = total + from_peer(piece, offset, grp_count).astype(jnp.float32)
+    return total
 
 
 def per_device(
@@ -114,7 +500,8 @@
     normed_one_all = lax.all_gather(normed_one, "seq", axis=0, tiled=True)
     qkv_rows = lax.all_gather(qkv_weight, "grp", axis=0, tiled=True)
     bias_rows = lax.all_gather(qkv_bias, "grp", axis=0, tiled=True)
-    mlp_rows = lax.all_gather(mlp_weight, "grp", axis=0, tiled=True)
+    use_kernels = group_tok <= 1024
+    mlp_blocks = exchange_blocks(padded_rows(mlp_weight), grp_count) if use_kernels else None
     cotangent_all = lax.all_gather(cotangent, "seq", axis=0, tiled=True)
     out_full = lax.all_gather(out_weight, AXES, axis=0, tiled=True)
     projected = lax.dot_general(
@@ -214,49 +601,13 @@
     attn_proj = jnp.dot(attn_low, out_full, preferred_element_type=jnp.float32)
     state = tokens_wide + attn_proj
     normed_two = rms_scale(state, gain_two).astype(jnp.bfloat16)
-    normed_two_all = lax.all_gather(normed_two, "seq", axis=0, tiled=True)
-    gate_rows, upper_rows, down_rows = mlp_rows[:, 0, :], mlp_rows[:, 1, :], mlp_rows[:, 2, :]
-    gate_vals = lax.dot_general(
-        normed_two_all, gate_rows, contract_last, preferred_element_type=jnp.float32
-    )
-    upper_vals = lax.dot_general(
-        normed_two_all, upper_rows, contract_last, preferred_element_type=jnp.float32
-    )
-    unit_wide, pull_back = jax.vjp(swish_product, gate_vals, upper_vals)
-    unit_low = unit_wide.astype(jnp.bfloat16)
-    unit_grad = lax.dot_general(
-        cotangent_all, down_rows, contract_last, preferred_element_type=jnp.float32
-    )
-    gate_grad, upper_grad = pull_back(unit_grad)
-    gate_grad = gate_grad.astype(jnp.bfloat16)
-    upper_grad = upper_grad.astype(jnp.bfloat16)
-    input_grad = jnp.dot(gate_grad, gate_rows, preferred_element_type=jnp.float32) + jnp.dot(
-        upper_grad, upper_rows, preferred_element_type=jnp.float32
-    )
-    grad_part = lax.psum_scatter(
-        input_grad.astype(jnp.bfloat16), "seq", scatter_dimension=0, tiled=True
-    ).astype(jnp.float32)
-    out_part = lax.psum_scatter(
-        jnp.dot(unit_low, down_rows, preferred_element_type=jnp.float32).astype(jnp.bfloat16),
-        "seq",
-        scatter_dimension=0,
-        tiled=True,
-    ).astype(jnp.float32)
-    mlp_terms = jnp.stack(
-        [
-            lax.dot_general(
-                gate_grad, normed_two_all, contract_first, preferred_element_type=jnp.float32
-            ),
-            lax.dot_general(
-                upper_grad, normed_two_all, contract_first, preferred_element_type=jnp.float32
-            ),
-            lax.dot_general(
-                unit_low, cotangent_all, contract_first, preferred_element_type=jnp.float32
-            ),
-        ],
-        axis=1,
-    )
-    mlp_grad = lax.psum_scatter(mlp_terms, "grp", scatter_dimension=0, tiled=True)
+    if use_kernels:
+        grad_part, out_part, mlp_terms = mlp_call(
+            normed_two, cotangent_all.reshape(seq_count, tok_rows, -1), mlp_blocks
+        )
+        mlp_grad = sum_blocks(mlp_terms, grp_count)[:, : mlp_weight.shape[0]].transpose(1, 0, 2)
+    else:
+        grad_part, out_part, mlp_grad = plain_mlp(normed_two, cotangent_all, mlp_weight)
     output = (state + out_part).astype(jnp.bfloat16)
     unused_state, norm_two_back = jax.vjp(rms_scale, state, gain_two)
     state_norm_grad, gain_two_grad = norm_two_back(grad_part)

time: 900 us -> 703 us (0.78)
  waiting for transfers between devices: 535 us -> 70.6 us
  blocking collectives: 135 us -> 363 us
  Pallas kernels: 0 us -> 118 us
  matrix products: 103 us -> 30.1 us
    reduce_scatter x3 -> x0, waiting for transfers between devices: 225 us -> none  [the longest x1 189 us: per_device(): lax.psum_scatter(mlp_terms, 'grp', scatter_dimension=0, tiled=True)]
    unnamed x3, blocking collectives: 57.9 us -> 267 us
    all_gather x2 -> x0, waiting for transfers between devices: 146 us -> none  [the longest x1 105 us: per_device(): mlp_rows = lax.all_gather(mlp_weight, 'grp', axis=0, tiled=True)]
    pallas_call x0 -> x1, Pallas kernels: none -> 118 us  [mlp_call(): pl.pallas_call(functools.partial(mlp_kernel, chips, grps, row_tiles), out...]
    dot_general x9 -> x0, matrix products: 73.8 us -> none  [the longest x1 10.9 us: per_device(): lax.dot_general(cotangent_all, down_rows, contract_last, preferred_elemen...]
    reduce_scatter x1, waiting for transfers between devices: 32.1 us -> 0.01 us  [per_device(): lax.psum_scatter(lax.dot_general(attn_owned, state_low_all, contract_firs...]
    all_to_all x1 -> x2, blocking collectives: 31.9 us -> 55.7 us  [columns_to_owners(): return lax.all_to_all(split, 'seq', split_axis=0, concat_axis=0, tiled=True)]
    reduce_scatter x1, waiting for transfers between devices: 23.2 us -> 0.01 us  [per_device(): lax.psum_scatter(lax.dot_general(qkv_grad_owned, normed_one_all, contract...]
  transfers between devices with their start and end apart: 16 -> 16, of which waited for: 11 -> 3; matrix products, arithmetic and copies ran while one was open for 13% -> 11% of each run, Pallas kernels for 0% -> 0%
where the time goes in v2:
time: 703 us; the launch traced here: 700 us
  blocking collectives  363 us (52%)
  Pallas kernels  118 us (17%)
  waiting for transfers between devices  70.6 us (10%)
  other arithmetic  40 us (6%)
  local copies, waits for them, and re-layouts  36.9 us (5%)
  matrix products  30.1 us (4%)
  between operations  16 us (2%)
  starting transfers between devices  14.6 us (2%)
  loops' own time  10.3 us (1%)
    unnamed x3, blocking collectives  267 us
    pallas_call x1, Pallas kernels, mlp_call(): pl.pallas_call(functools.partial(mlp_kernel, chips, grps, row_tiles), out...  118 us
    unnamed x11, waiting for transfers between devices  62.7 us
    all_to_all x2, blocking collectives, columns_to_owners(): return lax.all_to_all(split, 'seq', split_axis=0, concat_axis=0, tiled=True)  55.7 us
    all_gather x1, blocking collectives, per_device(): lax.all_gather(value_low, 'seq', axis=0, tiled=True)  15.3 us
    all_gather x1, blocking collectives, per_device(): lax.all_gather(key_rot.reshape(tok_rows, kv_width), 'seq', axis=0, tiled=...  14.8 us
  transfers between devices with their start and end apart: 16, of which 3 were waited for; matrix products, arithmetic and copies ran while one was open for 11% of the time, Pallas kernels for 0%

profile of v2, /device:TPU:9, one launch (start us, length us, event | category | flops | bytes accessed | tf_op | source)
XLA Modules:
  0.0 699.7 jit_solution(7667184266056718188)
XLA Ops:
  12.9 3.5 pad.4.refs_0_
  22.3 126.9 %all-reduce.1 = bf16[256]{0:T(256)(128)(2,1)S(1)} all-reduce(bf16[256]{0:T(256)(128)(2,1)S(1)} %dynamic-update-slice), channel_id=1, replica_groups=mesh['grp'=4,'seq'=8] {'grp'}, use_global_device_ids=true, to_apply=%add.1 | all-reduce | flops 256 | bytes 1024
  149.2 10.0 %all_gather.25 = bf16[256,1536]{1,0:T(8,128)(2,1)S(1)} all-gather(bf16[64,1536]{1,0:T(8,128)(2,1)S(1)} %copy-done.19), channel_id=1, replica_groups=mesh['grp'=4,'seq'=8] {'grp'}, dimensions={0}, use_global_device_ids=true | all-gather | bytes 983040 | tf_op jit(solution)/shard_map/all_gather | solution.py:501
  159.2 3.2 fusion.53
  163.4 9.0 %all-to-all-start = ((bf16[8,128,256]{1,2,0:T(8,128)(2,1)}), bf16[8,128,256]{1,2,0:T(8,128)(2,1)S(1)}, u32[]{:S(2)}, u32[]{:S(2)}) async-start(bf16[8,128,256]{1,2,0:T(8,128)(2,1)} %copy.165), calls=%async_computation | async-start | bytes 1048576 | tf_op jit(solution)/shard_map/all_to_all | solution.py:388
  176.4 7.9 %all-to-all-done = bf16[8,128,256]{1,2,0:T(8,128)(2,1)S(1)} async-done(((bf16[8,128,256]{1,2,0:T(8,128)(2,1)}), bf16[8,128,256]{1,2,0:T(8,128)(2,1)S(1)}, u32[]{:S(2)}, u32[]{:S(2)}) %all-to-all-start) | async-done | bytes 524320 | tf_op jit(solution)/shard_map/all_to_all | solution.py:388
  185.0 14.8 %all_gather.27 = bf16[1024,256]{0,1:T(8,128)(2,1)S(1)} all-gather(bf16[128,256]{0,1:T(8,128)(2,1)S(1)} %fusion.71), channel_id=1, replica_groups=mesh['grp'=4,'seq'=8] {'seq'}, dimensions={0}, use_global_device_ids=true | all-gather | bytes 589824 | tf_op jit(solution)/shard_map/all_gather | solution.py:522
  200.1 12.5 %while.51 = (s32[]{:T(128)}, f32[2,768]{1,0:T(2,128)S(1)}, f32[2,768]{1,0:T(2,128)S(1)}, s32[2]{0:T(128)S(1)}, s32[8]{0:T(128)}, /*index=5*/s32[]{:T(128)}, s32[...) while((s32[]{:T(128)}, f32[2,768]{1,0:T(2,128)S(1)}, ...), condition=%wide.region_12.13_spmd.clone, body=%wide.region_4.12_spmd.clone.sunk | while | flops 208836608 | bytes 8755049 | solution.py:575
  205.1 2.4 conditional.9
  212.6 15.3 %all_gather.28 = bf16[1024,256]{0,1:T(8,128)(2,1)S(1)} all-gather(bf16[128,256]{0,1:T(8,128)(2,1)S(1)} %slice.71), channel_id=1, replica_groups=mesh['grp'=4,'seq'=8] {'seq'}, dimensions={0}, use_global_device_ids=true | all-gather | bytes 589824 | tf_op jit(solution)/shard_map/all_gather | solution.py:523
  228.0 14.1 %while.52 = (s32[]{:T(128)}, f32[2,768,128]{2,1,0:T(8,128)S(1)}, s32[2]{0:T(128)S(1)}, s32[8]{0:T(128)}, s32[]{:T(128)}, /*index=5*/s32[8]{0:T(128)}, bf16[1024,...) while((s32[]{:T(128)}, f32[2,768,128]{2,1,0:T(8,128)S(1)}, ...), condition=%wide.region_19.20_spmd.clone, body=%wide.region_13.19_spmd.clone.sunk | while | flops 407211008 | bytes 4355929 | solution.py:592
  233.0 4.1 conditional.10
  234.4 2.6 fusion.15
  243.3 2.3 copy.171
  245.6 3.5 multiply_reduce_fusion.2
  250.1 118.3 %mlp.1 = (f32[128,1536]{1,0:T(8,128)}, f32[128,1536]{1,0:T(8,128)}, bf16[3,1152,1536]{2,1,0:T(8,128)(2,1)}) custom-call(bf16[128,1536]{1,0:T(8,128)(2,1)} %multiply_convert_fusion.n2_ref, bf16[8,128,1536]{2,1,0:T(8,128)(2,1)} %bitcast.212, bf16[3,288,1536]{2,1,0:T(8,128)(2,1)} %pad.4.refs_0_, bf16[3,288,1536]{2,1,0:T(8,128)(2,1)} %collective-permute-done.refs_1_, ...), custom_call_target="tpu_custom_call" | custom-call | flops 32614907904 | bytes 31457280 | tf_op jit(solution)/shard_map/mlp/pallas_call | solution.py:348
  368.4 2.0 multiply_reduce_fusion
  371.9 5.1 convert_multiply_fusion.6
  381.1 17.4 %while.53 = (s32[]{:T(128)}, f32[2,768,128]{2,1,0:T(8,128)S(1)}, bf16[2,512,256]{2,1,0:T(8,128)(2,1)}, bf16[2,512,256]{2,1,0:T(8,128)(2,1)}, s32[2]{0:T(128)S(1)...) while((s32[]{:T(128)}, f32[2,768,128]{2,1,0:T(8,128)S(1)}, ...), condition=%wide.region_29.30_spmd.clone, body=%wide.region_23.29_spmd.clone.sunk | while | flops 1016368128 | bytes 27711980 | solution.py:682
  385.5 6.2 conditional.11
  400.6 30.6 %reduce-scatter.16.cloned.1.call-done = bf16[128,256]{1,0:T(8,128)(2,1)} async-done(((bf16[1024,256]{1,0:T(8,128)(2,1)}), bf16[128,256]{1,0:T(8,128)(2,1)}) %reduce-scatter.16.cloned.1.call-update) | async-done | bytes 65552
  432.2 30.3 %reduce-scatter.18.cloned.1.call-done = bf16[128,256]{1,0:T(8,128)(2,1)} async-done(((bf16[1024,256]{1,0:T(8,128)(2,1)}), bf16[128,256]{1,0:T(8,128)(2,1)}) %reduce-scatter.18.cloned.1.call-update) | async-done | bytes 65552
  463.5 32.0 %all_to_all.33 = bf16[8,128,256]{1,2,0:T(8,128)(2,1)S(1)} all-to-all(bf16[8,128,256]{1,2,0:T(8,128)(2,1)S(1)} %bitcast.197), channel_id=1, replica_groups=mesh['grp'=4,'seq'=8] {'seq'}, dimensions={0} | all-to-all | bytes 1048576 | tf_op jit(solution)/shard_map/all_to_all | solution.py:382
  495.7 2.7 convolution_convert_fusion
  498.5 4.0 fusion.85
  502.7 7.3 %fusion.80 = (bf16[3,288,1536]{2,1,0:T(8,128)(2,1)}, bf16[3,288,1536]{2,1,0:T(8,128)(2,1)}, bf16[3,288,1536]{2,1,0:T(8,128)(2,1)}, bf16[3,288,1536]{2,1,0:T(8,128)(2,1)}) fusion(bf16[3,1152,1536]{2,1,0:T(8,128)(2,1)} %get-tuple-element.609), kind=kLoop, calls=%fused_computation.174 | loop fusion | bytes 21233664 | tf_op jit(solution)/shard_map/slice | solution.py:457
  513.0 23.7 %all_to_all.34 = bf16[8,128,192]{1,2,0:T(8,128)(2,1)S(1)} all-to-all(bf16[8,128,192]{1,2,0:T(8,128)(2,1)S(1)} %bitcast.203), channel_id=1, replica_groups=mesh['grp'=4,'seq'=8] {'seq'}, dimensions={0} | all-to-all | bytes 786432 | tf_op jit(solution)/shard_map/all_to_all | solution.py:382
  536.7 3.7 fusion.66
  541.2 96.3 %all-reduce.3 = f32[256]{0:T(256)S(1)} all-reduce(f32[256]{0:T(256)S(1)} %convert_reduce_fusion), channel_id=7, replica_groups=mesh['grp'=4,'seq'=8] {'grp'}, use_global_device_ids=true, to_apply=%region_38.39.clone | all-reduce | flops 256 | bytes 2048
  638.2 6.2 add_bitcast_fusion
  645.8 43.7 %all-reduce.5 = (f32[1536]{0:T(1024)S(1)}, f32[1536]{0:T(1024)S(1)}) all-reduce(f32[1536]{0:T(1024)S(1)} %get-tuple-element.825, f32[1536]{0:T(1024)S(1)} %copy-done.26), channel_id=5, replica_groups=mesh['grp'=4,'seq'=8] {'grp','seq'}, use_global_device_ids=true, to_apply=%region_35.36.clone | all-reduce | flops 3072 | bytes 24576
  690.8 2.4 fusion.59
  (260 shorter events, 66.0 us)
Async XLA Ops:
  7.2 152.1 %all-gather.5.cloned.1.call-start = ((), (), s32[]{:S(2)}) async-start(), calls=%async_computation.8 | async-start | bytes 3538944 | tf_op jit(solution)/shard_map/all_gather | solution.py:500
  12.1 8.6 %copy-start.36 = (u32[32]{0:T(128)S(1)}, u32[32]{0:T(128)}, u32[]{:S(2)}) copy-start(u32[32]{0:T(128)} %constant.279) | copy-start | bytes 388
  12.1 9.9 %copy-start.39 = (bf16[64]{0:T(256)(128)(2,1)S(1)}, bf16[64]{0:T(256)(128)(2,1)}, u32[]{:S(2)}) copy-start(bf16[64]{0:T(256)(128)(2,1)} %param.26) | copy-start | bytes 388
  12.1 137.1 %copy-start.19 = (bf16[64,1536]{1,0:T(8,128)(2,1)S(1)}, bf16[64,1536]{1,0:T(8,128)(2,1)}, u32[]{:S(2)}) copy-start(bf16[64,1536]{1,0:T(8,128)(2,1)} %param.25) | copy-start | bytes 589828
  12.1 233.5 %all-gather.7.cloned.1.call-start = ((), (), s32[]{:S(2)}) async-start(), calls=%async_computation.9 | async-start | bytes 4866048 | tf_op jit(solution)/shard_map/all_gather | solution.py:506
  12.9 237.2 %all-gather.9.cloned.1.call-start = ((), (), s32[]{:S(2)}) async-start(), calls=%async_computation.10 | async-start | bytes 3538944 | tf_op jit(solution)/shard_map/all_gather | solution.py:505
  16.4 233.6 %collective-permute-start = (bf16[3,288,1536]{2,1,0:T(8,128)(2,1)}, bf16[3,288,1536]{2,1,0:T(8,128)(2,1)}, u32[]{:S(2)}, u32[]{:S(2)}) collective-permute-start(bf16[3,288,1536]{2,1,0:T(8,128)(2,1)} %pad.4.refs_0_), channel_id=1, source_target_pairs={{0,8},{8,0},{16,24},{24,16},{1,9},{9,1},{17,25},{25,17},{2,10},{10... | collective-permute-start | bytes 7962632 | tf_op jit(solution)/shard_map/ppermute | solution.py:448
  17.6 232.4 %collective-permute-start.1 = (bf16[3,288,1536]{2,1,0:T(8,128)(2,1)}, bf16[3,288,1536]{2,1,0:T(8,128)(2,1)}, u32[]{:S(2)}, u32[]{:S(2)}) collective-permute-start(bf16[3,288,1536]{2,1,0:T(8,128)(2,1)} %pad.4.refs_0_), channel_id=1, source_target_pairs={{0,16},{8,24},{16,0},{24,8},{1,17},{9,25},{17,1},{25,9},{2,18},{10... | collective-permute-start | bytes 7962632 | tf_op jit(solution)/shard_map/ppermute | solution.py:448
  18.9 231.2 %collective-permute-start.2 = (bf16[3,288,1536]{2,1,0:T(8,128)(2,1)}, bf16[3,288,1536]{2,1,0:T(8,128)(2,1)}, u32[]{:S(2)}, u32[]{:S(2)}) collective-permute-start(bf16[3,288,1536]{2,1,0:T(8,128)(2,1)} %pad.4.refs_0_), channel_id=1, source_target_pairs={{0,24},{8,16},{16,8},{24,0},{1,25},{9,17},{17,9},{25,1},{2,26},{10... | collective-permute-start | bytes 7962632 | tf_op jit(solution)/shard_map/ppermute | solution.py:448
  20.5 152.6 %copy-start.20 = (s32[8]{0:T(128)}, s32[8]{0:T(128)S(1)}, u32[]{:S(2)}) copy-start(s32[8]{0:T(128)S(1)} %get-tuple-element.1288) | copy-start | bytes 100
  159.2 13.3 %copy-start.33 = (bf16[1536]{0:T(1024)(128)(2,1)S(1)}, bf16[1536]{0:T(1024)(128)(2,1)}, u32[]{:S(2)}) copy-start(bf16[1536]{0:T(1024)(128)(2,1)} %param.28) | copy-start | bytes 9220
  163.4 20.8 %all-to-all-start = ((bf16[8,128,256]{1,2,0:T(8,128)(2,1)}), bf16[8,128,256]{1,2,0:T(8,128)(2,1)S(1)}, u32[]{:S(2)}, u32[]{:S(2)}) async-start(bf16[8,128,256]{1,2,0:T(8,128)(2,1)} %copy.165), calls=%async_computation | async-start | bytes 1048576 | tf_op jit(solution)/shard_map/all_to_all | solution.py:388
  172.5 258.7 %reduce-scatter.16.cloned.1.call-start = ((), (), s32[]{:S(2)}) async-start(), calls=%async_computation.15 | async-start | bytes 589824
  176.4 8.6 %copy-start.13 = (f32[128,128]{0,1:T(8,128)}, f32[128,128]{0,1:T(8,128)S(1)}, u32[]{:S(2)}) copy-start(f32[128,128]{0,1:T(8,128)S(1)} %pad_maximum_fusion.4) | copy-start | bytes 196612
  249.2 121.2 %copy-start.27 = (f32[128]{0:T(128)}, f32[128]{0:T(128)S(1)}, u32[]{:S(2)}) copy-start(f32[128]{0:T(128)S(1)} %fusion.77) | copy-start | bytes 1540
  398.5 64.0 %reduce-scatter.18.cloned.1.call-start = ((), (), s32[]{:S(2)}) async-start(), calls=%async_computation.16 | async-start | bytes 589824
  399.1 137.6 %all-gather.11.cloned.1.call-start = ((), (), s32[]{:S(2)}) async-start(), calls=%async_computation.13 | async-start | bytes 3538944 | tf_op jit(solution)/shard_map/all_gather | solution.py:621
  399.7 244.8 %reduce-scatter.10.cloned.1.call-start = ((), (), s32[]{:S(2)}) async-start(), calls=%async_computation.11 | async-start | bytes 3538944 | tf_op jit(solution)/shard_map/reduce_scatter | solution.py:713
  400.6 95.1 %copy-start.12 = (bf16[256,1536]{1,0:T(8,128)(2,1)S(1)}, bf16[256,1536]{1,0:T(8,128)(2,1)}, u32[]{:S(2)}) copy-start(bf16[256,1536]{1,0:T(8,128)(2,1)} %copy-done.11) | copy-start | bytes 2359300
  498.5 194.6 %reduce-scatter.12.cloned.1.call-start = ((), (), s32[]{:S(2)}) async-start(), calls=%async_computation.12 | async-start | bytes 1966080 | tf_op jit(solution)/shard_map/reduce_scatter | solution.py:719
  502.6 190.5 %reduce-scatter.14.cloned.1.call-start = ((), (), s32[]{:S(2)}) async-start(), calls=%async_computation.14 | async-start | bytes 1474560 | tf_op jit(solution)/shard_map/reduce_scatter | solution.py:622
  502.6 10.0 %copy-start.6 = (f32[2,768,128]{2,1,0:T(8,128)S(1)}, f32[2,768,128]{2,1,0:T(8,128)}, u32[]{:S(2)}) copy-start(f32[2,768,128]{2,1,0:T(8,128)} %copy-done.5) | copy-start | bytes 2359300
  510.0 128.1 %collective-permute-start.3 = (bf16[3,288,1536]{2,1,0:T(8,128)(2,1)}, bf16[3,288,1536]{2,1,0:T(8,128)(2,1)}, u32[]{:S(2)}, u32[]{:S(2)}) collective-permute-start(bf16[3,288,1536]{2,1,0:T(8,128)(2,1)} %get-tuple-element.922), channel_id=1, source_target_pairs={{0,8},{8,0},{16,24},{24,16},{1,9},{9,1},{17,25},{25,17},{2,10},{10... | collective-permute-start | bytes 7962632 | tf_op jit(solution)/shard_map/ppermute | solution.py:448
  511.2 126.9 %collective-permute-start.4 = (bf16[3,288,1536]{2,1,0:T(8,128)(2,1)}, bf16[3,288,1536]{2,1,0:T(8,128)(2,1)}, u32[]{:S(2)}, u32[]{:S(2)}) collective-permute-start(bf16[3,288,1536]{2,1,0:T(8,128)(2,1)} %get-tuple-element.921), channel_id=1, source_target_pairs={{0,16},{8,24},{16,0},{24,8},{1,17},{9,25},{17,1},{25,9},{2,18},{10... | collective-permute-start | bytes 7962632 | tf_op jit(solution)/shard_map/ppermute | solution.py:448
  512.4 125.7 %collective-permute-start.5 = (bf16[3,288,1536]{2,1,0:T(8,128)(2,1)}, bf16[3,288,1536]{2,1,0:T(8,128)(2,1)}, u32[]{:S(2)}, u32[]{:S(2)}) collective-permute-start(bf16[3,288,1536]{2,1,0:T(8,128)(2,1)} %get-tuple-element.920), channel_id=1, source_target_pairs={{0,24},{8,16},{16,8},{24,0},{1,25},{9,17},{17,9},{25,1},{2,26},{10... | collective-permute-start | bytes 7962632 | tf_op jit(solution)/shard_map/ppermute | solution.py:448
  638.1 52.6 %copy-start.38 = (f32[128]{0:T(128)S(1)}, f32[128]{0:T(128)}, u32[]{:S(2)}) copy-start(f32[128]{0:T(128)} %copy-done.37) | copy-start | bytes 1540
  638.1 52.6 %copy-start.7 = (f32[128,1536]{1,0:T(8,128)S(1)}, f32[128,1536]{1,0:T(8,128)}, u32[]{:S(2)}) copy-start(f32[128,1536]{1,0:T(8,128)} %get-tuple-element.605) | copy-start | bytes 2359300
  638.1 52.6 %copy-start.8 = (bf16[128,1536]{1,0:T(8,128)(2,1)S(1)}, bf16[128,1536]{1,0:T(8,128)(2,1)}, u32[]{:S(2)}) copy-start(bf16[128,1536]{1,0:T(8,128)(2,1)} %param.22) | copy-start | bytes 1179652
  638.2 52.6 %copy-start.15 = (f32[128,1536]{1,0:T(8,128)S(1)}, f32[128,1536]{1,0:T(8,128)}, u32[]{:S(2)}) copy-start(f32[128,1536]{1,0:T(8,128)} %get-tuple-element.604) | copy-start | bytes 2359300
  638.2 52.6 %copy-start.18 = (f32[1536]{0:T(1024)S(1)}, f32[1536]{0:T(1024)}, u32[]{:S(2)}) copy-start(f32[1536]{0:T(1024)} %convert_element_type.158) | copy-start | bytes 18436
  638.2 52.6 %copy-start.28 = (f32[128]{0:T(128)S(1)}, f32[128]{0:T(128)}, u32[]{:S(2)}) copy-start(f32[128]{0:T(128)} %copy-done.27) | copy-start | bytes 1540
  638.2 52.6 %copy-start.35 = (f32[128]{0:T(128)S(1)}, f32[128]{0:T(128)}, u32[]{:S(2)}) copy-start(f32[128]{0:T(128)} %copy-done.34) | copy-start | bytes 1540
  (24 other events, 95.1 us)
Sparse Core Ops, SparseCore 0:
  12.3 38.8 all-gather.4
  54.2 76.5 all-gather.6
  132.4 34.8 all-gather.8
  398.6 32.4 reduce-scatter.15
  433.4 29.0 reduce-scatter.17
  464.6 47.7 all-gather.10
  514.6 48.2 reduce-scatter.9
  566.5 85.8 reduce-scatter.11
  655.9 28.5 reduce-scatter.13

commit v3 on v2

--- a/solution.py
+++ b/solution.py
@@ -374,6 +374,371 @@
     )(n2, cot_all, *w_blocks)
 
 
+class Place:
+    def __init__(self, chips):
+        self.chips = chips
+        self.grp, self.seq = lax.axis_index("grp"), lax.axis_index("seq")
+        self.chip, self.core = self.seq // 2, self.seq % 2
+        self.mate = self.seq + 1 - 2 * self.core
+
+    def peer(self, offset):
+        low, high = self.grp % 2, self.grp // 2
+        low = 1 - low if offset % 2 else low
+        high = 1 - high if offset // 2 else high
+        return 2 * high + low
+
+    def barrier(self, grps):
+        barrier = pltpu.get_barrier_semaphore()
+        for chip in range(self.chips):
+            @pl.when(chip != self.chip)
+            def _(chip=chip):
+                pl.semaphore_signal(
+                    barrier, inc=1, device_id=(self.grp, 2 * chip + self.core), device_id_type=MESH
+                )
+        pl.semaphore_signal(barrier, inc=1, device_id=(self.grp, self.mate), device_id_type=MESH)
+        for offset in range(1, grps):
+            pl.semaphore_signal(
+                barrier, inc=1, device_id=(self.peer(offset), self.seq), device_id_type=MESH
+            )
+        pl.semaphore_wait(barrier, self.chips - 1 + 1 + grps - 1)
+
+
+class RailGather:
+    def __init__(self, place, view, send_sem, recv_sem):
+        self.place, self.view, self.send_sem, self.recv_sem = place, view, send_sem, recv_sem
+
+    def copy(self, way, chip, core):
+        p = self.place
+        to = (p.seq + 2, p.seq - 2, p.mate)[way]
+        return remote(
+            self.view(chip, core), self.view(chip, core), self.send_sem.at[way, chip],
+            self.recv_sem.at[chip, core], p.grp, to,
+        )
+
+    def start(self):
+        p = self.place
+        pl.when(p.chip < p.chips - 1)(lambda: self.copy(0, p.chip, p.core).start())
+        pl.when(p.chip > 0)(lambda: self.copy(1, p.chip, p.core).start())
+        self.copy(2, p.chip, p.core).start()
+
+    def forward(self, step):
+        p = self.place
+
+        @pl.when(p.chip - step >= 0)
+        def _():
+            chip = p.chip - step
+            self.copy(2, chip, p.core).wait_recv()
+            pl.when(p.chip < p.chips - 1)(lambda: self.copy(0, chip, p.core).start())
+            self.copy(2, chip, p.core).start()
+
+        @pl.when(p.chip + step < p.chips)
+        def _():
+            chip = p.chip + step
+            self.copy(2, chip, p.core).wait_recv()
+            pl.when(p.chip > 0)(lambda: self.copy(1, chip, p.core).start())
+            self.copy(2, chip, p.core).start()
+
+    def wait_mate(self, chip):
+        self.copy(2, chip, 1 - self.place.core).wait_recv()
+
+    def drain(self):
+        p = self.place
+        for chip in range(p.chips):
+            self.copy(2, chip, p.core).wait_send()
+            pl.when((chip <= p.chip) & (p.chip < p.chips - 1))(
+                lambda chip=chip: self.copy(0, chip, p.core).wait_send()
+            )
+            pl.when((chip >= p.chip) & (p.chip > 0))(
+                lambda chip=chip: self.copy(1, chip, p.core).wait_send()
+            )
+
+
+def front_kernel(chips, scale,
+                 n1_ref, cot_ref, wq_ref, bias_ref, wo_ref, wm_ref, cos_ref, sin_ref, mask_ref,
+                 attn_ref, lse_ref, q_out_ref, kv_out_ref, n1_all_ref, cot_all_ref, wo_all_ref, wq_all_ref,
+                 wm1_ref, wm2_ref, wm3_ref,
+                 nbuf, wq, bias, stage, qbuf, kvbuf,
+                 lsem, n_send, n_recv, c_send, c_recv, o_send, o_recv, ox_send, ox_recv, om_send, om_recv,
+                 wq_send, wq_recv, b_send, b_recv, m_send, m_recv, q_send, q_recv, k_send, k_recv):
+    p = Place(chips)
+    grps = 4
+    half = wq_ref.shape[0]
+    rows = pl.ds(p.core * half, half)
+    mates_rows = pl.ds((1 - p.core) * half, half)
+    wm_refs = (wm_ref, wm1_ref, wm2_ref, wm3_ref)
+    part = wm_ref.shape[1] // 2
+
+    own = [
+        pltpu.make_async_copy(n1_ref, nbuf.at[p.chip, p.core], lsem.at[0]),
+        pltpu.make_async_copy(wq_ref, wq.at[0, rows], lsem.at[1]),
+        pltpu.make_async_copy(bias_ref, bias.at[0, p.core], lsem.at[2]),
+        pltpu.make_async_copy(wo_ref, wo_all_ref.at[p.grp, p.chip, p.core], lsem.at[3]),
+        pltpu.make_async_copy(cot_ref, cot_all_ref.at[p.chip, p.core], lsem.at[4]),
+    ]
+    for copy in own:
+        copy.start()
+    p.barrier(grps)
+
+    n1_line = RailGather(p, lambda chip, core: nbuf.at[chip, core], n_send, n_recv)
+    cot_line = RailGather(p, lambda chip, core: cot_all_ref.at[chip, core], c_send, c_recv)
+    out_line = RailGather(p, lambda chip, core: wo_all_ref.at[p.grp, chip, core], o_send, o_recv)
+
+    def wq_direct(b):
+        return remote(wq_ref, wq.at[b, rows], wq_send.at[0, b], wq_recv.at[b, 0], p.peer(b), p.seq)
+
+    def wq_mate(b):
+        return remote(wq.at[b, rows], wq.at[b, rows], wq_send.at[1, b], wq_recv.at[b, 1], p.grp, p.mate)
+
+    def bias_direct(b):
+        return remote(bias_ref, bias.at[b, p.core], b_send.at[0, b], b_recv.at[b, 0], p.peer(b), p.seq)
+
+    def bias_mate(b):
+        return remote(bias.at[b, p.core], bias.at[b, p.core], b_send.at[1, b], b_recv.at[b, 1], p.grp, p.mate)
+
+    def m_half(ref, i):
+        return ref.at[:, pl.ds(i * part, part)]
+
+    def m_direct(b, i):
+        return remote(m_half(wm_ref, i), m_half(wm_refs[b], i), m_send.at[b, i], m_recv.at[b, i], p.peer(b), p.seq)
+
+    def m_forward(b):
+        return remote(
+            m_half(wm_refs[b], b - 1), m_half(wm3_ref, b - 1), m_send.at[3, b - 1], m_recv.at[3, b - 1],
+            p.peer(3 - b), p.seq,
+        )
+
+    def out_cross(b):
+        view = lambda grp: wo_all_ref.at[grp, :, p.core]
+        return remote(view(p.grp), view(p.grp), ox_send.at[b], ox_recv.at[b], p.peer(b), p.seq)
+
+    def out_mate(b):
+        view = wo_all_ref.at[p.peer(b), :, p.core]
+        return remote(view, view, om_send.at[b], om_recv.at[b], p.grp, p.mate)
+
+    def q_copy(chip):
+        return remote(
+            stage.at[chip, pl.ds(0, 3)], qbuf.at[p.chip], q_send.at[chip], q_recv.at[p.chip],
+            p.grp, 2 * chip + p.core,
+        )
+
+    def q_arrival(chip):
+        return remote(stage.at[chip, pl.ds(0, 3)], qbuf.at[chip], q_send.at[chip], q_recv.at[chip], p.grp, p.mate)
+
+    def k_copy(chip, to_chip):
+        return remote(
+            stage.at[chip, 3], kvbuf.at[p.chip, p.core, chip], k_send.at[0, chip, to_chip],
+            k_recv.at[p.chip, p.core, chip], p.grp, 2 * to_chip + p.core,
+        )
+
+    def k_mate(head, chip, src=None):
+        view = kvbuf.at[head, p.core, chip]
+        return remote(
+            view if src is None else src, view, k_send.at[1, head, chip],
+            k_recv.at[head, p.core, chip], p.grp, p.mate,
+        )
+
+    def k_arrival(head, core, chip):
+        view = kvbuf.at[head, core, chip]
+        return remote(view, view, k_send.at[1, head, chip], k_recv.at[head, core, chip], p.grp, p.mate)
+
+    own[1].wait()
+    own[2].wait()
+    for b in range(1, grps):
+        wq_direct(b).start()
+        bias_direct(b).start()
+    wq_mate(0).start()
+    bias_mate(0).start()
+    own[0].wait()
+    n1_line.start()
+    own[3].wait()
+    out_line.start()
+    for b in range(1, grps):
+        wq_direct(b).wait_recv()
+        wq_mate(b).start()
+        bias_direct(b).wait_recv()
+        bias_mate(b).start()
+    m_direct(1, 0).start()
+    m_direct(2, 1).start()
+    for b in range(grps):
+        wq_mate(b).wait_recv()
+        bias_mate(b).wait_recv()
+
+    @pl.loop(0, chips)
+    def _(order):
+        @pl.when(order > 0)
+        def _():
+            n1_line.forward(order)
+            out_line.forward(order)
+
+        at = nearest_chip(p.chip, order, chips)
+        x = nbuf[at, p.core]
+        weights = wq[...].reshape(grps * 2 * half, x.shape[1])
+        rows_all = lax.dot_general(x, weights, CONTRACT_LAST, preferred_element_type=jnp.float32)
+        cosine, sine = cos_ref[at, p.core], sin_ref[at, p.core]
+        for b in range(grps):
+            u = rows_all[:, 2 * half * b : 2 * half * (b + 1)] + (bias[b, 0, 0:1] + bias[b, 1, 0:1])
+            turned = u * cosine + pltpu.roll(u, half, 1) * sine
+            place = p.peer(b)
+            keep = jnp.where((place == grps - 1) & (p.chip >= chips // 2), 1.0, 0.0)
+            value = (u * keep + turned * (1.0 - keep)).astype(jnp.bfloat16)
+            stage[at, place] = value
+
+            @pl.when(place == grps - 1)
+            def _(value=value):
+                kvbuf[p.chip, p.core, at] = value
+
+            @pl.when((place < grps - 1) & (at == p.chip))
+            def _(value=value, place=place):
+                qbuf[p.chip, place] = value
+
+        pl.when(at != p.chip)(lambda: q_copy(at).start())
+        for to_chip in range(chips):
+            pl.when(to_chip != p.chip)(lambda to_chip=to_chip: k_copy(at, to_chip).start())
+        k_mate(p.chip, at, stage.at[at, 3]).start()
+
+    for b in range(1, grps):
+        out_cross(b).start()
+    own[4].wait()
+    cot_line.start()
+
+    @pl.loop(0, chips)
+    def _(order):
+        for head in range(chips):
+            @pl.when(head != p.chip)
+            def _(head=head):
+                chip = nearest_chip(head, order, chips)
+                k_arrival(head, p.core, chip).wait_recv()
+                k_mate(head, chip).start()
+
+    for chip in range(chips):
+        pl.when(chip != p.chip)(lambda chip=chip: q_arrival(chip).wait_recv())
+        for head in range(chips):
+            k_arrival(head, 1 - p.core, chip).wait_recv()
+    for b in (1, 2):
+        m_direct(b, b - 1).wait_recv()
+        m_forward(b).start()
+    cot_line.forward(1)
+
+    mask = mask_ref[...]
+    shard = mask.shape[0]
+    heads_per = H // KVH
+    for kv in range(KVH):
+        heads = [kv * heads_per + i for i in range(heads_per)]
+        queries = jnp.concatenate([qbuf[h % chips, h // chips] for h in heads], axis=0)
+        keys = kvbuf[kv].reshape(mask.shape[1], 2 * half)
+        values = kvbuf[KVH + kv].reshape(mask.shape[1], 2 * half)
+        scores = lax.dot_general(queries, keys, CONTRACT_LAST, preferred_element_type=jnp.float32) * scale
+        scores = scores.reshape(heads_per, shard, mask.shape[1]) + mask[None]
+        top = jnp.max(scores, axis=-1, keepdims=True)
+        weights = jnp.exp(scores - top)
+        total = jnp.sum(weights, axis=-1, keepdims=True)
+        probs = (weights / total).astype(jnp.bfloat16).reshape(heads_per * shard, mask.shape[1])
+        mixed = jnp.dot(probs, values, preferred_element_type=jnp.float32)
+        log_total = (top + jnp.log(total)).reshape(heads_per * shard, 1)
+        lse_ref[kv] = jnp.broadcast_to(log_total, (heads_per * shard, 2 * half))
+        for i, h in enumerate(heads):
+            attn_ref[:, h * 2 * half : (h + 1) * 2 * half] = mixed[i * shard : (i + 1) * shard]
+        cot_line.forward(kv + 2)
+
+    for b in range(1, grps):
+        out_cross(b).wait_recv()
+        out_mate(b).start()
+    m_direct(1, 1).start()
+    m_direct(2, 0).start()
+    outs = [
+        pltpu.make_async_copy(nbuf, n1_all_ref, lsem.at[5]),
+        pltpu.make_async_copy(wq, wq_all_ref, lsem.at[6]),
+        pltpu.make_async_copy(qbuf, q_out_ref, lsem.at[7]),
+        pltpu.make_async_copy(kvbuf, kv_out_ref, lsem.at[8]),
+    ]
+    for chip in range(chips):
+        n1_line.wait_mate(chip)
+        out_line.wait_mate(chip)
+        cot_line.wait_mate(chip)
+    for copy in outs:
+        copy.start()
+    for b in (1, 2):
+        m_direct(b, 2 - b).wait_recv()
+        m_forward(3 - b).wait_recv()
+    for b in range(1, grps):
+        om = remote(
+            wo_all_ref.at[p.peer(b), :, 1 - p.core], wo_all_ref.at[p.peer(b), :, 1 - p.core],
+            om_send.at[b], om_recv.at[b], p.grp, p.mate,
+        )
+        om.wait_recv()
+    for copy in outs:
+        copy.wait()
+    n1_line.drain()
+    out_line.drain()
+    cot_line.drain()
+    for b in range(grps):
+        wq_mate(b).wait_send()
+        bias_mate(b).wait_send()
+    for b in range(1, grps):
+        wq_direct(b).wait_send()
+        bias_direct(b).wait_send()
+        out_cross(b).wait_send()
+        out_mate(b).wait_send()
+    for b in (1, 2):
+        m_direct(b, 0).wait_send()
+        m_direct(b, 1).wait_send()
+        m_forward(b).wait_send()
+    for chip in range(chips):
+        pl.when(chip != p.chip)(lambda chip=chip: q_copy(chip).wait_send())
+        for other in range(chips):
+            pl.when(other != p.chip)(lambda chip=chip, other=other: k_copy(chip, other).wait_send())
+            k_mate(other, chip).wait_send()
+
+
+def front_call(n1, cot, qkv_weight, bias_rows, out_weight, mlp_rows, cosine, sine, mask):
+    chips = cosine.shape[0]
+    grps = 4
+    shard, width = n1.shape
+    half = qkv_weight.shape[0]
+    vm, dma = pltpu.VMEM, pltpu.SemaphoreType.DMA
+    anyspace = pl.BlockSpec(memory_space=pl.ANY)
+    vspec = pl.BlockSpec(memory_space=pltpu.VMEM)
+    low, wide = jnp.bfloat16, jnp.float32
+    struct = jax.ShapeDtypeStruct
+    return pl.pallas_call(
+        functools.partial(front_kernel, chips, 1.0 / math.sqrt(HD)),
+        out_shape=(
+            struct((shard, H * HD), wide),
+            struct((KVH, H // KVH * shard, HD), wide),
+            struct((chips, 3, shard, HD), low),
+            struct((chips, 2, chips, shard, HD), low),
+            struct((chips, 2, shard, width), low),
+            struct((chips, 2, shard, width), low),
+            struct((grps, chips, 2) + out_weight.shape, low),
+            struct((grps, 2 * half, width), low),
+        ) + (struct(mlp_rows.shape, low),) * 3,
+        in_specs=[anyspace] * 6 + [vspec] * 3,
+        out_specs=(vspec,) * 2 + (anyspace,) * 9,
+        scratch_shapes=[
+            vm((chips, 2, shard, width), low),
+            vm((grps, 2 * half, width), low),
+            vm((grps, 2) + bias_rows.shape, wide),
+            vm((chips, grps, shard, HD), low),
+            vm((chips, 3, shard, HD), low),
+            vm((chips, 2, chips, shard, HD), low),
+            dma((9,)),
+            dma((3, chips)), dma((chips, 2)),
+            dma((3, chips)), dma((chips, 2)),
+            dma((3, chips)), dma((chips, 2)),
+            dma((grps,)), dma((grps,)), dma((grps,)), dma((grps,)),
+            dma((2, grps)), dma((grps, 2)),
+            dma((2, grps)), dma((grps, 2)),
+            dma((grps, 2)), dma((grps, 2)),
+            dma((chips,)), dma((chips,)),
+            dma((2, chips, chips)), dma((chips, 2, chips)),
+        ],
+        compiler_params=pltpu.CompilerParams(
+            collective_id=2, has_side_effects=True, vmem_limit_bytes=56 * 2**20
+        ),
+        name="front",
+    )(n1, cot, qkv_weight, bias_rows, out_weight, mlp_rows, cosine, sine, mask)
+
+
 def columns_to_owners(rows, row_unit):
     grp_count, seq_count = lax.axis_size("grp"), lax.axis_size("seq")
     tok_rows = rows.shape[0]
@@ -497,31 +862,63 @@
     gain_one = gain_attn.astype(jnp.float32)
     gain_two = gain_mlp.astype(jnp.float32)
     normed_one = rms_scale(tokens_wide, gain_one).astype(jnp.bfloat16)
-    normed_one_all = lax.all_gather(normed_one, "seq", axis=0, tiled=True)
-    qkv_rows = lax.all_gather(qkv_weight, "grp", axis=0, tiled=True)
-    bias_rows = lax.all_gather(qkv_bias, "grp", axis=0, tiled=True)
-    use_kernels = group_tok <= 1024
-    mlp_blocks = exchange_blocks(padded_rows(mlp_weight), grp_count) if use_kernels else None
-    cotangent_all = lax.all_gather(cotangent, "seq", axis=0, tiled=True)
-    out_full = lax.all_gather(out_weight, AXES, axis=0, tiled=True)
-    projected = lax.dot_general(
-        normed_one_all, qkv_rows, contract_last, preferred_element_type=jnp.float32
-    )
-    projected = (projected + bias_rows.astype(jnp.float32)[None, :]).astype(jnp.bfloat16)
-    projected = owners_to_columns(projected, qkv_weight.shape[0]).astype(jnp.float32)
-    query_rot = rotate(
-        projected[:, :att_width].reshape(tok_rows, H, HD), cosine_table, sine_table
-    ).astype(jnp.bfloat16)
-    key_rot = rotate(
-        projected[:, att_width : att_width + kv_width].reshape(tok_rows, KVH, HD),
-        cosine_table,
-        sine_table,
-    ).astype(jnp.bfloat16)
-    value_low = projected[:, att_width + kv_width :].astype(jnp.bfloat16)
-    keys_all, values_all = (
-        lax.all_gather(key_rot.reshape(tok_rows, kv_width), "seq", axis=0, tiled=True),
-        lax.all_gather(value_low, "seq", axis=0, tiled=True),
-    )
+    use_kernels = (seq_count, grp_count, H, KVH, HD) == (8, 4, 12, 2, 128)
+    if use_kernels:
+        chips = seq_count // 2
+        lanes = jnp.arange(HD)
+        all_pos = (starts[:, None] + jnp.arange(tok_rows, dtype=jnp.int32)[None, :]).reshape(-1)
+        all_cosine, all_sine = rotary_tables(all_pos, HD)
+        all_sine = jnp.where(lanes < HD // 2, -all_sine, all_sine)
+        by_shard = lambda table: table.reshape(chips, 2, tok_rows, HD)
+        key_pos = all_pos.reshape(chips, 2, tok_rows).swapaxes(0, 1).reshape(-1)
+        key_seg = jnp.repeat(segments.reshape(chips, 2).swapaxes(0, 1).reshape(-1), tok_rows)
+        visible = ((key_seg == 0) | (key_seg == own_seg))[None, :] & (
+            key_pos[None, :] <= positions[:, None]
+        )
+        mask = jnp.where(visible, 0.0, -1e30).astype(jnp.float32)
+        bias_half = qkv_bias.astype(jnp.float32)
+        bias_pair = jnp.concatenate([bias_half, jnp.zeros_like(bias_half)])
+        bias_row = jnp.where(seq_place % 2 == 0, bias_pair, jnp.roll(bias_pair, HD // 2))
+        bias_rows8 = jnp.broadcast_to(bias_row[None, :], (8, HD))
+        own_rows = padded_rows(mlp_weight)
+        (
+            attn_wide, lse, q_heads, kv_heads, n1_all, cot_all, out_all, qkv_all, *peer_rows
+        ) = front_call(
+            normed_one, cotangent, qkv_weight, bias_rows8, out_weight, own_rows,
+            by_shard(all_cosine), by_shard(all_sine), mask,
+        )
+        mlp_blocks = [own_rows, *peer_rows]
+        normed_one_all = n1_all.reshape(group_tok, -1)
+        cotangent_all = cot_all.reshape(group_tok, -1)
+        out_full = out_all.reshape(att_width, -1)
+        qkv_rows = lax.all_gather(qkv_weight, "grp", axis=0, tiled=True)
+        query_rot = q_heads.transpose(2, 1, 0, 3).reshape(tok_rows, H, HD)
+        kv_rows = kv_heads.reshape(2, KVH, 2, chips, tok_rows, HD).transpose(0, 3, 2, 4, 1, 5)
+        keys_all, values_all = kv_rows.reshape(2, group_tok, kv_width)
+    else:
+        normed_one_all = lax.all_gather(normed_one, "seq", axis=0, tiled=True)
+        qkv_rows = lax.all_gather(qkv_weight, "grp", axis=0, tiled=True)
+        bias_rows = lax.all_gather(qkv_bias, "grp", axis=0, tiled=True)
+        cotangent_all = lax.all_gather(cotangent, "seq", axis=0, tiled=True)
+        out_full = lax.all_gather(out_weight, AXES, axis=0, tiled=True)
+        projected = lax.dot_general(
+            normed_one_all, qkv_rows, contract_last, preferred_element_type=jnp.float32
+        )
+        projected = (projected + bias_rows.astype(jnp.float32)[None, :]).astype(jnp.bfloat16)
+        projected = owners_to_columns(projected, qkv_weight.shape[0]).astype(jnp.float32)
+        query_rot = rotate(
+            projected[:, :att_width].reshape(tok_rows, H, HD), cosine_table, sine_table
+        ).astype(jnp.bfloat16)
+        key_rot = rotate(
+            projected[:, att_width : att_width + kv_width].reshape(tok_rows, KVH, HD),
+            cosine_table,
+            sine_table,
+        ).astype(jnp.bfloat16)
+        value_low = projected[:, att_width + kv_width :].astype(jnp.bfloat16)
+        keys_all, values_all = (
+            lax.all_gather(key_rot.reshape(tok_rows, kv_width), "seq", axis=0, tiled=True),
+            lax.all_gather(value_low, "seq", axis=0, tiled=True),
+        )
     queries = (
         query_rot.reshape(tok_rows, KVH, heads_per, HD)
         .transpose(1, 2, 0, 3)
@@ -555,48 +952,51 @@
             * score_scale
         )
 
-    def stat_step(stats_now, block_index):
-        allowed = block_mask(block_index)
-
-        def stat_visit(current):
-            top_old, total_old = current
-            key_part, value_part = block_keys(block_index)
-            scores = jnp.where(allowed[None], block_scores(key_part), -1e30)
-            top_new = jnp.maximum(top_old, jnp.max(scores, axis=-1))
-            weights = jnp.where(allowed[None], jnp.exp(scores - top_new[..., None]), 0.0)
-            return (top_new, total_old * jnp.exp(top_old - top_new) + jnp.sum(weights, axis=-1))
-
-        return (lax.cond(jnp.any(allowed), stat_visit, lambda current: current, stats_now), None)
-
-    start_stats = (
-        jnp.full((KVH, query_rows), -1e30, jnp.float32),
-        jnp.zeros((KVH, query_rows), jnp.float32),
-    )
-    (top_all, total_all), unused = lax.scan(stat_step, start_stats, block_order)
-    log_total = top_all + jnp.log(total_all)
-
-    def mix_step(mixed_sum, block_index):
-        allowed = block_mask(block_index)
-
-        def mix_visit(current):
-            key_part, value_part = block_keys(block_index)
-            prob_low = jnp.where(
-                allowed[None], jnp.exp(block_scores(key_part) - log_total[..., None]), 0.0
-            ).astype(jnp.bfloat16)
-            return current + jnp.einsum(
-                "krj,jkd->krd", prob_low, value_part, preferred_element_type=jnp.float32
-            )
-
-        return (lax.cond(jnp.any(allowed), mix_visit, lambda current: current, mixed_sum), None)
-
-    mixed_sum, unused = lax.scan(
-        mix_step, jnp.zeros((KVH, query_rows, HD), jnp.float32), block_order
-    )
-    attn_wide = (
-        mixed_sum.reshape(KVH, heads_per, tok_rows, HD)
-        .transpose(2, 0, 1, 3)
-        .reshape(tok_rows, att_width)
-    )
+    if use_kernels:
+        log_total = lse[:, :, 0]
+    else:
+        def stat_step(stats_now, block_index):
+            allowed = block_mask(block_index)
+
+            def stat_visit(current):
+                top_old, total_old = current
+                key_part, value_part = block_keys(block_index)
+                scores = jnp.where(allowed[None], block_scores(key_part), -1e30)
+                top_new = jnp.maximum(top_old, jnp.max(scores, axis=-1))
+                weights = jnp.where(allowed[None], jnp.exp(scores - top_new[..., None]), 0.0)
+                return (top_new, total_old * jnp.exp(top_old - top_new) + jnp.sum(weights, axis=-1))
+
+            return (lax.cond(jnp.any(allowed), stat_visit, lambda current: current, stats_now), None)
+
+        start_stats = (
+            jnp.full((KVH, query_rows), -1e30, jnp.float32),
+            jnp.zeros((KVH, query_rows), jnp.float32),
+        )
+        (top_all, total_all), unused = lax.scan(stat_step, start_stats, block_order)
+        log_total = top_all + jnp.log(total_all)
+
+        def mix_step(mixed_sum, block_index):
+            allowed = block_mask(block_index)
+
+            def mix_visit(current):
+                key_part, value_part = block_keys(block_index)
+                prob_low = jnp.where(
+                    allowed[None], jnp.exp(block_scores(key_part) - log_total[..., None]), 0.0
+                ).astype(jnp.bfloat16)
+                return current + jnp.einsum(
+                    "krj,jkd->krd", prob_low, value_part, preferred_element_type=jnp.float32
+                )
+
+            return (lax.cond(jnp.any(allowed), mix_visit, lambda current: current, mixed_sum), None)
+
+        mixed_sum, unused = lax.scan(
+            mix_step, jnp.zeros((KVH, query_rows, HD), jnp.float32), block_order
+        )
+        attn_wide = (
+            mixed_sum.reshape(KVH, heads_per, tok_rows, HD)
+            .transpose(2, 0, 1, 3)
+            .reshape(tok_rows, att_width)
+        )
     attn_low = attn_wide.astype(jnp.bfloat16)
     attn_proj = jnp.dot(attn_low, out_full, preferred_element_type=jnp.float32)
     state = tokens_wide + attn_proj

time: 703 us -> 622 us (0.88)
  blocking collectives: 363 us -> 168 us
  Pallas kernels: 118 us -> 256 us
  matrix products: 30.1 us -> 22.6 us
  other arithmetic: 40 us -> 32.7 us
    unnamed x3 -> x2, blocking collectives: 267 us -> 134 us
    pallas_call x0 -> x1, Pallas kernels: none -> 130 us  [front_call(): pl.pallas_call(functools.partial(front_kernel, chips, 1.0 / math.sqrt(HD)...]
    all_to_all x2 -> x1, blocking collectives: 55.7 us -> 23.4 us  [columns_to_owners(): return lax.all_to_all(split, 'seq', split_axis=0, concat_axis=0, tiled=True)]
    all_gather x2 -> x0, blocking collectives: 30.2 us -> none  [the longest x1 15.3 us: per_device(): lax.all_gather(value_low, 'seq', axis=0, tiled=True)]
    pallas_call x1, Pallas kernels: 118 us -> 126 us  [mlp_call(): pl.pallas_call(functools.partial(mlp_kernel, chips, grps, row_tiles), out...]
    unnamed x11 -> x8, waiting for transfers between devices: 62.7 us -> 61.9 us
  transfers between devices with their start and end apart: 16 -> 10, of which waited for: 3 -> 3; matrix products, arithmetic and copies ran while one was open for 11% -> 6% of each run, Pallas kernels for 0% -> 0%
where the time goes in v3:
time: 622 us; the launch traced here: 619 us
  Pallas kernels  256 us (41%)
  blocking collectives  168 us (27%)
  waiting for transfers between devices  75.4 us (12%)
  other arithmetic  32.7 us (5%)
  local copies, waits for them, and re-layouts  31.8 us (5%)
  matrix products  22.6 us (4%)
  between operations  15.2 us (2%)
  starting transfers between devices  14 us (2%)
    unnamed x2, blocking collectives  134 us
    pallas_call x1, Pallas kernels, front_call(): pl.pallas_call(functools.partial(front_kernel, chips, 1.0 / math.sqrt(HD)...  130 us
    pallas_call x1, Pallas kernels, mlp_call(): pl.pallas_call(functools.partial(mlp_kernel, chips, grps, row_tiles), out...  126 us
    unnamed x8, waiting for transfers between devices  61.9 us
    all_to_all x1, blocking collectives, columns_to_owners(): return lax.all_to_all(split, 'seq', split_axis=0, concat_axis=0, tiled=True)  23.4 us
    all_to_all x1, waiting for transfers between devices, columns_to_owners(): return lax.all_to_all(split, 'seq', split_axis=0, concat_axis=0, tiled=True)  13.5 us
  transfers between devices with their start and end apart: 10, of which 3 were waited for; matrix products, arithmetic and copies ran while one was open for 6% of the time, Pallas kernels for 0%

profile of v3, /device:TPU:9, one launch (start us, length us, event | category | flops | bytes accessed | tf_op | source)
XLA Modules:
  0.0 618.9 jit_solution(7004876231691811531)
XLA Ops:
  7.2 1.3 fusion.34
  14.1 1.9 multiply_sine_fusion
  16.0 1.9 fusion.23.n1_ref
  17.9 3.5 pad.6.wm_ref.refs_0_
  22.4 1.3 negate_select_fusion.3
  24.3 130.2 %front.1 = (f32[128,1536]{1,0:T(8,128)}, f32[2,768,128]{2,1,0:T(8,128)}, bf16[4,3,128,128]{3,2,1,0:T(8,128)(2,1)}, bf16[4,2,4,128,128]{4,3,2,1,0:T(8,128)(2,1)},...) custom-call(bf16[128,1536]{1,0:T(8,128)(2,1)} %fusion.23.n1_ref, ...), custom_call_target="tpu_custom_call" | custom-call | tf_op jit(solution)/shard_map/front/pallas_call | solution.py:703
  155.7 3.4 multiply_reduce_fusion.2
  160.0 125.6 %mlp.1 = (f32[128,1536]{1,0:T(8,128)}, f32[128,1536]{1,0:T(8,128)}, bf16[3,1152,1536]{2,1,0:T(8,128)(2,1)}) custom-call(bf16[128,1536]{1,0:T(8,128)(2,1)} %multiply_convert_fusion.n2_ref, bf16[8,128,1536]{2,1,0:T(8,128)(2,1)} %bitcast.168, bf16[3,288,1536]{2,1,0:T(8,128)(2,1)} %pad.6.wm_ref.refs_0_, bf16[3,288,1536]{2,1,0:T(8,128)(2,1)} %get-tuple-element.265.refs_1_, ...), custom_call_target="tpu_custom_call" | custom-call | flops 32614907904 | bytes 31457280 | tf_op jit(solution)/shard_map/mlp/pallas_call | solution.py:348
  285.6 1.4 multiply_reduce_fusion
  287.0 1.4 fusion.39
  288.4 4.1 convert_multiply_fusion.6
  294.3 1.3 fusion.41
  298.3 1.4 copy.131
  299.7 16.0 %while.20 = (s32[]{:T(128)}, f32[2,768,128]{2,1,0:T(8,128)S(1)}, bf16[2,512,256]{2,1,0:T(8,128)(2,1)}, bf16[2,512,256]{2,1,0:T(8,128)(2,1)}, s32[2]{0:T(128)S(1)...) while((s32[]{:T(128)}, f32[2,768,128]{2,1,0:T(8,128)S(1)}, ...), condition=%wide.region_13.14_spmd.clone, body=%wide.region_7.13_spmd.clone.sunk | while | flops 1016368128 | bytes 26139088 | solution.py:1082
  303.5 6.2 %conditional.3 = (f32[2,768,128]{2,1,0:T(8,128)S(1)}, bf16[1,512,256]{1,2,0:T(8,128)(2,1)S(1)}, bf16[1,512,256]{1,2,0:T(8,128)(2,1)S(1)}) conditional(s32[]{:T(128)} %convert_element_type.194, f32[2,768,128]{2,1,0:T(8,128)S(1)} %get-tuple-element.597, (pred[768,512]{0,1:T(8,128)(4,1)S(1)}, s32[]{:T(128)}, bf16[1024,256]{0,1:T(8,128)(2,1)S(1)}, ...), branch_computations={%region_11.11_spmd, %region_12.12_spmd} | conditional | flops 1015152640 | bytes 23623810 | solution.py:1080
  318.3 30.0 %reduce-scatter.16.cloned.1.call-done = bf16[128,256]{1,0:T(8,128)(2,1)} async-done(((bf16[1024,256]{1,0:T(8,128)(2,1)}), bf16[128,256]{1,0:T(8,128)(2,1)}) %reduce-scatter.16.cloned.1.call-update) | async-done | bytes 65552
  349.3 30.4 %reduce-scatter.18.cloned.1.call-done = bf16[128,256]{1,0:T(8,128)(2,1)} async-done(((bf16[1024,256]{1,0:T(8,128)(2,1)}), bf16[128,256]{1,0:T(8,128)(2,1)}) %reduce-scatter.18.cloned.1.call-update) | async-done | bytes 65552
  381.6 10.9 %all-to-all-start = ((bf16[8,128,256]{1,2,0:T(8,128)(2,1)}), bf16[8,128,256]{1,2,0:T(8,128)(2,1)S(1)}, u32[]{:S(2)}, u32[]{:S(2)}) async-start(bf16[8,128,256]{1,2,0:T(8,128)(2,1)} %bitcast.43), calls=%async_computation | async-start | bytes 1048576 | tf_op jit(solution)/shard_map/all_to_all | solution.py:747
  392.5 10.8 %all_gather.6 = bf16[256,1536]{1,0:T(8,128)(2,1)S(1)} all-gather(bf16[64,1536]{1,0:T(8,128)(2,1)S(1)} %copy-done.6), channel_id=1, replica_groups=mesh['grp'=4,'seq'=8] {'grp'}, dimensions={0}, use_global_device_ids=true | all-gather | bytes 983040 | tf_op jit(solution)/shard_map/all_gather | solution.py:894
  403.3 13.5 %all-to-all-done = bf16[8,128,256]{1,2,0:T(8,128)(2,1)S(1)} async-done(((bf16[8,128,256]{1,2,0:T(8,128)(2,1)}), bf16[8,128,256]{1,2,0:T(8,128)(2,1)S(1)}, u32[]{:S(2)}, u32[]{:S(2)}) %all-to-all-start) | async-done | bytes 524320 | tf_op jit(solution)/shard_map/all_to_all | solution.py:747
  417.1 2.7 convolution_convert_fusion
  419.9 4.1 fusion.45
  424.3 6.9 %fusion.40 = (bf16[3,288,1536]{2,1,0:T(8,128)(2,1)S(1)}, bf16[3,288,1536]{2,1,0:T(8,128)(2,1)}, bf16[3,288,1536]{2,1,0:T(8,128)(2,1)}, bf16[3,288,1536]{2,1,0:T(8,128)(2,1)}) fusion(bf16[3,1152,1536]{2,1,0:T(8,128)(2,1)} %get-tuple-element.277), kind=kLoop, calls=%fused_computation.116 | loop fusion | bytes 21233664 | tf_op jit(solution)/shard_map/slice | solution.py:822
  432.3 1.3 collective-permute-start.1
  433.9 1.9 copy.141
  436.8 23.4 %all_to_all.24 = bf16[8,128,192]{1,2,0:T(8,128)(2,1)} all-to-all(bf16[8,128,192]{1,2,0:T(8,128)(2,1)S(1)} %bitcast.152), channel_id=1, replica_groups=mesh['grp'=4,'seq'=8] {'seq'}, dimensions={0} | all-to-all | bytes 786432 | tf_op jit(solution)/shard_map/all_to_all | solution.py:747
  460.2 3.8 fusion.30
  466.5 92.5 %all-reduce.4 = f32[256]{0:T(256)S(1)} all-reduce(f32[256]{0:T(256)S(1)} %convert_reduce_fusion), channel_id=7, replica_groups=mesh['grp'=4,'seq'=8] {'grp'}, use_global_device_ids=true, to_apply=%region_22.23.clone | all-reduce | flops 256 | bytes 2048
  559.6 5.4 add_bitcast_fusion
  565.0 1.7 fusion.24
  566.6 41.1 %all-reduce.6 = (f32[1536]{0:T(1024)S(1)}, f32[1536]{0:T(1024)S(1)}) all-reduce(f32[1536]{0:T(1024)S(1)} %get-tuple-element.394, f32[1536]{0:T(1024)S(1)} %get-tuple-element.392), channel_id=5, replica_groups=mesh['grp'=4,'seq'=8] {'grp','seq'}, use_global_device_ids=true, to_apply=%region_19.20.clone | all-reduce | flops 3072 | bytes 24576
  608.9 3.1 fusion.26
  (145 shorter events, 37.9 us)
Async XLA Ops:
  7.2 341.1 %reduce-scatter.16.cloned.1.call-start = ((), (), s32[]{:S(2)}) async-start(), calls=%async_computation.11 | async-start | bytes 589824
  24.3 131.4 %copy-start = (bf16[128,1536]{1,0:T(8,128)(2,1)S(1)}, bf16[128,1536]{1,0:T(8,128)(2,1)}, u32[]{:S(2)}) copy-start(bf16[128,1536]{1,0:T(8,128)(2,1)} %param.13) | copy-start | bytes 1179652
  155.7 3.4 copy-start.3
  155.7 3.4 copy-start.10
  160.0 127.0 %copy-start.2 = (bf16[128,1536]{1,0:T(8,128)(2,1)S(1)}, bf16[128,1536]{1,0:T(8,128)(2,1)}, u32[]{:S(2)}) copy-start(bf16[128,1536]{1,0:T(8,128)(2,1)} %cot_ref.1) | copy-start | bytes 1179652
  285.6 2.8 copy-start.5
  288.4 4.2 copy-start.4
  294.3 3.7 copy-start.9
  303.5 2.4 copy-start.7
  307.1 1.6 copy-start.8
  315.7 64.1 %reduce-scatter.18.cloned.1.call-start = ((), (), s32[]{:S(2)}) async-start(), calls=%async_computation.12 | async-start | bytes 589824
  316.5 143.7 %all-gather.2.cloned.1.call-start = ((), (), s32[]{:S(2)}) async-start(), calls=%async_computation.9 | async-start | bytes 3538944 | tf_op jit(solution)/shard_map/all_gather | solution.py:1021
  318.2 74.3 %copy-start.6 = (bf16[64,1536]{1,0:T(8,128)(2,1)S(1)}, bf16[64,1536]{1,0:T(8,128)(2,1)}, u32[]{:S(2)}) copy-start(bf16[64,1536]{1,0:T(8,128)(2,1)} %wq_ref.1) | copy-start | bytes 589828
  381.6 35.2 %all-to-all-start = ((bf16[8,128,256]{1,2,0:T(8,128)(2,1)}), bf16[8,128,256]{1,2,0:T(8,128)(2,1)S(1)}, u32[]{:S(2)}, u32[]{:S(2)}) async-start(bf16[8,128,256]{1,2,0:T(8,128)(2,1)} %bitcast.43), calls=%async_computation | async-start | bytes 1048576 | tf_op jit(solution)/shard_map/all_to_all | solution.py:747
  392.5 172.5 %reduce-scatter.10.cloned.1.call-start = ((), (), s32[]{:S(2)}) async-start(), calls=%async_computation.7 | async-start | bytes 3538944 | tf_op jit(solution)/shard_map/reduce_scatter | solution.py:1113
  416.8 3.0 copy-start.1
  419.8 192.2 %reduce-scatter.12.cloned.1.call-start = ((), (), s32[]{:S(2)}) async-start(), calls=%async_computation.8 | async-start | bytes 1966080 | tf_op jit(solution)/shard_map/reduce_scatter | solution.py:1119
  424.0 188.0 %reduce-scatter.14.cloned.1.call-start = ((), (), s32[]{:S(2)}) async-start(), calls=%async_computation.10 | async-start | bytes 1474560 | tf_op jit(solution)/shard_map/reduce_scatter | solution.py:1022
  431.2 128.4 %collective-permute-start = (bf16[3,288,1536]{2,1,0:T(8,128)(2,1)}, bf16[3,288,1536]{2,1,0:T(8,128)(2,1)}, u32[]{:S(2)}, u32[]{:S(2)}) collective-permute-start(bf16[3,288,1536]{2,1,0:T(8,128)(2,1)} %get-tuple-element.443), channel_id=1, source_target_pairs={{0,8},{8,0},{16,24},{24,16},{1,9},{9,1},{17,25},{25,17},{2,10},{10... | collective-permute-start | bytes 7962632 | tf_op jit(solution)/shard_map/ppermute | solution.py:813
  432.3 127.3 %collective-permute-start.1 = (bf16[3,288,1536]{2,1,0:T(8,128)(2,1)}, bf16[3,288,1536]{2,1,0:T(8,128)(2,1)}, u32[]{:S(2)}, u32[]{:S(2)}) collective-permute-start(bf16[3,288,1536]{2,1,0:T(8,128)(2,1)} %get-tuple-element.442), channel_id=1, source_target_pairs={{0,16},{8,24},{16,0},{24,8},{1,17},{9,25},{17,1},{25,9},{2,18},{10... | collective-permute-start | bytes 7962632 | tf_op jit(solution)/shard_map/ppermute | solution.py:813
  433.7 125.9 %collective-permute-start.2 = (bf16[3,288,1536]{2,1,0:T(8,128)(2,1)}, bf16[3,288,1536]{2,1,0:T(8,128)(2,1)}, u32[]{:S(2)}, u32[]{:S(2)}) collective-permute-start(bf16[3,288,1536]{2,1,0:T(8,128)(2,1)} %get-tuple-element.441), channel_id=1, source_target_pairs={{0,24},{8,16},{16,8},{24,0},{1,25},{9,17},{17,9},{25,1},{2,26},{10... | collective-permute-start | bytes 7962632 | tf_op jit(solution)/shard_map/ppermute | solution.py:813
  460.2 3.9 copy-start.11
Sparse Core Ops, SparseCore 0:
  315.8 32.4 reduce-scatter.15
  350.7 29.0 reduce-scatter.17
  382.0 49.0 all-gather.1
  433.2 49.3 reduce-scatter.9
  486.0 86.5 reduce-scatter.11
  575.9 28.6 reduce-scatter.13

commit v4 on v3

--- a/solution.py
+++ b/solution.py
@@ -737,6 +737,459 @@
         ),
         name="front",
     )(n1, cot, qkv_weight, bias_rows, out_weight, mlp_rows, cosine, sine, mask)
+
+
+def unturn(rows, cosine, sine, half):
+    return rows * cosine + pltpu.roll(rows * sine, half, 1)
+
+
+def back_kernel(chips, scale,
+                n2g_ref, state_ref, cot_ref, tokens_ref, gains_ref, attn_ref, q_ref, kv_ref, mask_ref,
+                cos_ref, sin_ref, wq_ref, wo_ref, n1_ref, terms_ref,
+                tok_grad_ref, wq_grad_ref, wo_grad_ref, gain_ref, mlp_ref,
+                wo, stbuf, n1x, at_stage, at_all, dq_stage, gq_in, kv_part, km_in, k_sum, k_own, kr_in,
+                cols, part, left_in, right_in, wgrad, wm_in, w_send_buf, w_in, o_terms, o_send_buf, o_in,
+                m_own, m_in, gain_own, gain_in, gain_mid, gain_mid_in, state_grad,
+                lsem, s_send, s_recv, a_send, a_recv, q_send, q_recv, km_send, km_recv, kr_send, kr_recv,
+                r_send, r_recv, wm_send, wm_recv, w_send, w_recv, o_send, o_recv, m_send, m_recv,
+                ml_sem, g_send, g_recv, h_send, h_recv):
+    p = Place(chips)
+    grps = 4
+    shard, width = n2g_ref.shape
+    slots = 2 * chips
+    heads_per = H // KVH
+    half = HD // 2
+    low, wide = jnp.bfloat16, jnp.float32
+    block = terms_ref.shape[1] // grps
+    mhalf = block // 2
+    last = chips - 1
+
+    loads = [
+        pltpu.make_async_copy(wo_ref, wo, lsem.at[0]),
+        pltpu.make_async_copy(n1_ref.at[:, p.core], n1x.at[:, :, pl.ds(0, width)], lsem.at[1]),
+    ]
+    for copy in loads:
+        copy.start()
+
+    def seq_peer(i):
+        return (p.seq + i) % slots
+
+    barrier = pltpu.get_barrier_semaphore()
+    for i in range(1, slots):
+        pl.semaphore_signal(barrier, inc=1, device_id=(p.grp, seq_peer(i)), device_id_type=MESH)
+    for b in range(1, grps):
+        pl.semaphore_signal(barrier, inc=1, device_id=(p.peer(b), p.seq), device_id_type=MESH)
+    pl.semaphore_wait(barrier, slots - 1 + grps - 1)
+
+    def m_rows(b, i):
+        return terms_ref.at[:, pl.ds(b * block + i * mhalf, mhalf)]
+
+    def m_copy(slot, src, peer):
+        return remote(src, m_in.at[slot], m_send.at[slot], m_recv.at[slot], p.peer(peer), p.seq)
+
+    m_first = [
+        m_copy(1, m_rows(3, 0), 1), m_copy(3, m_rows(3, 1), 2),
+        m_copy(0, m_rows(1, 0), 1), m_copy(2, m_rows(2, 1), 2),
+    ]
+    for copy in m_first:
+        copy.start()
+    m_second = [m_copy(4, m_own.at[0], 1), m_copy(5, m_own.at[1], 2)]
+    m_loads = [
+        pltpu.make_async_copy(m_rows(1, 1), m_own.at[0], ml_sem.at[0]),
+        pltpu.make_async_copy(m_rows(2, 0), m_own.at[1], ml_sem.at[1]),
+        pltpu.make_async_copy(m_rows(0, 0), m_own.at[2], ml_sem.at[2]),
+        pltpu.make_async_copy(m_rows(0, 1), m_own.at[3], ml_sem.at[3]),
+    ]
+    for copy in m_loads:
+        copy.start()
+
+    state = state_ref[...]
+    gain_two = gains_ref[1]
+    n2g = n2g_ref[...]
+    scale_two = lax.rsqrt(jnp.mean(state * state, axis=-1, keepdims=True) + EPS)
+    normed = state * scale_two
+    gain_own[1] = jnp.sum(n2g * normed, axis=0, keepdims=True)
+    lifted = n2g * gain_two
+    state_grad[...] = cot_ref[...].astype(wide) + scale_two * (
+        lifted - normed * jnp.mean(lifted * normed, axis=-1, keepdims=True)
+    )
+    state_low = state_grad[...].astype(low)
+    stbuf[p.chip, p.core] = state_low
+    line = RailGather(p, lambda chip, core: stbuf.at[chip, core], s_send, s_recv)
+    line.start()
+
+    attn = attn_ref[...]
+    unit = wo.shape[0] // (grps * slots)
+    at_rows = attn.astype(low).T
+    at_stage[...] = at_rows.reshape(grps, slots, unit, shard)
+
+    def at_copy(i, to):
+        return remote(
+            at_stage.at[:, to], at_all.at[:, :, pl.ds(pl.multiple_of(p.seq * shard, shard), shard)],
+            a_send.at[i], a_recv.at[p.seq], p.grp, to,
+        )
+
+    def at_arrival(slot):
+        return remote(
+            at_stage.at[:, slot], at_all.at[:, :, pl.ds(pl.multiple_of(slot * shard, shard), shard)],
+            a_send.at[0], a_recv.at[slot], p.grp, p.mate,
+        )
+
+    for i in range(1, slots):
+        at_copy(i, seq_peer(i)).start()
+    at_all[:, :, pl.ds(pl.multiple_of(p.seq * shard, shard), shard)] = at_stage[:, p.seq]
+
+    loads[0].wait()
+    attn_grad = lax.dot_general(state_low, wo[...], CONTRACT_LAST, preferred_element_type=wide).astype(low)
+    line.forward(1)
+    mask = mask_ref[...]
+    keys_total = mask.shape[1]
+    own_cos, own_sin = cos_ref[p.chip, p.core], sin_ref[p.chip, p.core]
+
+    def km_copy(head):
+        return remote(
+            kv_part.at[head, 1 - p.core], km_in.at[head], km_send.at[head], km_recv.at[head], p.grp, p.mate
+        )
+
+    def kr_copy(head):
+        return remote(
+            k_sum.at[head], kr_in.at[p.chip], kr_send.at[head], kr_recv.at[p.chip], p.grp, 2 * head + p.core
+        )
+
+    def kr_arrival(chip):
+        return remote(k_sum.at[chip], kr_in.at[chip], kr_send.at[chip], kr_recv.at[chip], p.grp, p.mate)
+
+    def q_copy(chip):
+        return remote(
+            dq_stage.at[chip], gq_in.at[p.chip], q_send.at[chip], q_recv.at[p.chip], p.grp, 2 * chip + p.core
+        )
+
+    def q_arrival(chip):
+        return remote(dq_stage.at[chip], gq_in.at[chip], q_send.at[chip], q_recv.at[chip], p.grp, p.mate)
+
+    def key_sum(head):
+        km_copy(head).wait_recv()
+        total = kv_part[head, p.core].astype(wide) + km_in[head].astype(wide)
+
+        @pl.when(p.chip == head)
+        def _():
+            k_own[...] = total
+
+        @pl.when(p.chip != head)
+        def _():
+            k_sum[head] = total.astype(low)
+            kr_copy(head).start()
+
+    for kv in range(KVH):
+        heads = [kv * heads_per + i for i in range(heads_per)]
+        queries = jnp.concatenate([q_ref[h % chips, h // chips] for h in heads], axis=0)
+        grads = jnp.concatenate([attn_grad[:, h * HD : (h + 1) * HD] for h in heads], axis=0)
+        mixed = jnp.concatenate([attn[:, h * HD : (h + 1) * HD] for h in heads], axis=0)
+        delta = jnp.sum(grads.astype(wide) * mixed, axis=-1, keepdims=True)
+        keys = kv_ref[kv].reshape(keys_total, HD)
+        values = kv_ref[KVH + kv].reshape(keys_total, HD)
+        scores = lax.dot_general(queries, keys, CONTRACT_LAST, preferred_element_type=wide) * scale
+        scores = (scores.reshape(heads_per, shard, keys_total) + mask[None]).reshape(heads_per * shard, keys_total)
+        weights = jnp.exp(scores - jnp.max(scores, axis=-1, keepdims=True))
+        probs = weights * (1.0 / jnp.sum(weights, axis=-1, keepdims=True))
+        prob_grad = lax.dot_general(grads, values, CONTRACT_LAST, preferred_element_type=wide)
+        score_grad = (probs * (prob_grad - delta)).astype(low)
+        key_grad = lax.dot_general(score_grad, queries, CONTRACT_FIRST, preferred_element_type=wide) * scale
+        value_grad = lax.dot_general(probs.astype(low), grads, CONTRACT_FIRST, preferred_element_type=wide)
+        kv_part[kv] = key_grad.astype(low).reshape(2, chips, shard, HD)
+        kv_part[KVH + kv] = value_grad.astype(low).reshape(2, chips, shard, HD)
+        km_copy(kv).start()
+        km_copy(KVH + kv).start()
+        query_grad = jnp.dot(score_grad, keys, preferred_element_type=wide) * scale
+        for i, h in enumerate(heads):
+            turned = unturn(query_grad[i * shard : (i + 1) * shard], own_cos, own_sin, half).astype(low)
+            dq_stage[h % chips, h // chips] = turned
+
+            @pl.when(p.chip == h % chips)
+            def _(turned=turned, h=h):
+                gq_in[h % chips, h // chips] = turned
+
+        line.forward(2 + kv)
+    for chip in range(chips):
+        pl.when(chip != p.chip)(lambda chip=chip: q_copy(chip).start())
+    for head in (0, 2, 1, 3):
+        key_sum(head)
+    loads[1].wait()
+    lane = lax.broadcasted_iota(jnp.int32, (chips, shard, HD), 2)
+    n1x[:, :, width:] = jnp.where(lane == 0, 1.0, 0.0).astype(low)
+    for chip in range(chips):
+        line.wait_mate(chip)
+    for i in range(1, slots):
+        at_arrival(seq_peer(i)).wait_recv()
+    o_terms[...] = jnp.dot(
+        at_all[...].reshape(grps * unit, slots * shard), stbuf[...].reshape(slots * shard, width),
+        preferred_element_type=wide,
+    ).reshape(grps, unit, width)
+    o_send_buf[...] = o_terms[...].astype(low)
+
+    def o_copy(b):
+        return remote(
+            o_send_buf.at[p.peer(b)], o_in.at[b], o_send.at[b], o_recv.at[b], p.peer(b), p.seq
+        )
+
+    for b in range(1, grps):
+        o_copy(b).start()
+
+    def m_add(dst, src):
+        for j in range(3):
+            @pl.loop(0, mhalf // 16)
+            def _(t, j=j):
+                rows = pl.ds(pl.multiple_of(t * 16, 16), 16)
+                m_own[dst, j, rows] = (
+                    m_own[dst, j, rows].astype(wide) + m_in[src, j, rows].astype(wide)
+                ).astype(low)
+
+    for chip in range(chips):
+        pl.when(chip != p.chip)(lambda chip=chip: q_arrival(chip).wait_recv())
+        pl.when(chip != p.chip)(lambda chip=chip: kr_arrival(chip).wait_recv())
+    is_value = jnp.where(p.chip >= chips // 2, 1.0, 0.0)
+
+    @pl.loop(0, chips)
+    def _(chip):
+        key_total = k_own[chip]
+        for other in range(chips):
+            key_total = key_total + jnp.where(other == p.chip, 0.0, kr_in[other, chip].astype(wide))
+        turned = unturn(key_total, cos_ref[chip, p.core], sin_ref[chip, p.core], half)
+        last_head = (key_total * is_value + turned * (1.0 - is_value)).astype(low)
+        for b in range(grps):
+            place = p.peer(b)
+            query_head = gq_in[chip, jnp.minimum(place, grps - 2)]
+            cols[chip, :, b * HD : (b + 1) * HD] = jnp.where(place == grps - 1, last_head, query_head)
+        part[chip] = jnp.dot(
+            cols[chip], wq_ref[...], preferred_element_type=wide
+        ).astype(low)
+
+    def to_right(chip):
+        return remote(part.at[chip], left_in.at[chip], r_send.at[0, chip], r_recv.at[0, chip], p.grp, p.seq + 2)
+
+    def to_left(chip):
+        return remote(part.at[chip], right_in.at[chip], r_send.at[1, chip], r_recv.at[1, chip], p.grp, p.seq - 2)
+
+    def rail_step(order):
+        far = last - order
+
+        @pl.when(far > p.chip)
+        def _():
+            @pl.when(p.chip > 0)
+            def _():
+                to_right(far).wait_recv()
+                part[far] = (part[far].astype(wide) + left_in[far].astype(wide)).astype(low)
+
+            to_right(far).start()
+
+        @pl.when(order < p.chip)
+        def _():
+            @pl.when(p.chip < last)
+            def _():
+                to_left(order).wait_recv()
+                part[order] = (part[order].astype(wide) + right_in[order].astype(wide)).astype(low)
+
+            to_left(order).start()
+
+    rail_step(0)
+    wgrad[...] = lax.dot_general(
+        cols[...].reshape(chips * shard, grps * HD), n1x[...].reshape(chips * shard, width + HD),
+        CONTRACT_FIRST, preferred_element_type=wide,
+    ).reshape(grps, 2, half, width + HD)
+    wm = remote(wgrad.at[:, 1 - p.core], wm_in, wm_send, wm_recv, p.grp, p.mate)
+    wm.start()
+    rail_step(1)
+    wm.wait_recv()
+    w_send_buf[...] = (wgrad[:, p.core] + wm_in[...]).astype(low)
+
+    def w_copy(b):
+        return remote(w_send_buf.at[b], w_in.at[b], w_send.at[b], w_recv.at[b], p.peer(b), p.seq)
+
+    for b in range(1, grps):
+        w_copy(b).start()
+    rail_step(2)
+    m_loads[0].wait()
+    m_first[1].wait_recv()
+    m_add(0, 3)
+    m_second[0].start()
+    m_loads[1].wait()
+    m_first[0].wait_recv()
+    m_add(1, 1)
+    m_second[1].start()
+    rail_step(3)
+
+    tokens = tokens_ref[...].astype(wide)
+    tok_grad_ref[...] = part[p.chip].astype(wide)
+
+    @pl.when(p.chip > 0)
+    def _():
+        to_right(p.chip).wait_recv()
+        tok_grad_ref[...] += left_in[p.chip].astype(wide)
+
+    @pl.when(p.chip < last)
+    def _():
+        to_left(p.chip).wait_recv()
+        tok_grad_ref[...] += right_in[p.chip].astype(wide)
+
+    n1g = tok_grad_ref[...]
+    scale_one = lax.rsqrt(jnp.mean(tokens * tokens, axis=-1, keepdims=True) + EPS)
+    normed = tokens * scale_one
+    gain_own[0] = jnp.sum(n1g * normed, axis=0, keepdims=True)
+    lifted = n1g * gains_ref[0]
+    tok_grad_ref[...] = state_grad[...] + scale_one * (
+        lifted - normed * jnp.mean(lifted * normed, axis=-1, keepdims=True)
+    )
+
+    def g_copy(i):
+        return remote(gain_own, gain_in.at[i], g_send.at[i], g_recv.at[i], p.grp, seq_peer(i))
+
+    for i in range(1, slots):
+        g_copy(i).start()
+    total = gain_own[...]
+    for i in range(1, slots):
+        g_copy(i).wait_recv()
+        total = total + gain_in[i]
+    gain_mid[...] = total
+
+    def h_copy(b):
+        return remote(gain_mid, gain_mid_in.at[b], h_send.at[b], h_recv.at[b], p.peer(b), p.seq)
+
+    for b in range(1, grps):
+        h_copy(b).start()
+
+    wo_grad = o_terms[p.grp]
+    wq_grad = wgrad[0, p.core] + wm_in[0]
+    for b in range(1, grps):
+        o_copy(b).wait_recv()
+        wo_grad = wo_grad + o_in[b].astype(wide)
+        w_copy(b).wait_recv()
+        wq_grad = wq_grad + w_in[b].astype(wide)
+    wo_grad_ref[...] = wo_grad
+    wq_grad_ref[...] = wq_grad
+    total = gain_mid[...]
+    for b in range(1, grps):
+        h_copy(b).wait_recv()
+        total = total + gain_mid_in[b]
+    gain_ref[...] = total
+
+    m_loads[2].wait()
+    m_loads[3].wait()
+
+    def m_total(own, direct, second, i):
+        for j in range(3):
+            @pl.loop(0, mhalf // 16)
+            def _(t, j=j):
+                rows = pl.ds(pl.multiple_of(t * 16, 16), 16)
+                mlp_ref[j, pl.ds(pl.multiple_of(i * mhalf + t * 16, 16), 16)] = (
+                    m_own[own, j, rows].astype(wide) + m_in[direct, j, rows].astype(wide)
+                ) + m_in[second, j, rows].astype(wide)
+
+    m_first[2].wait_recv()
+    m_second[1].wait_recv()
+    m_total(2, 0, 5, 0)
+    m_first[3].wait_recv()
+    m_second[0].wait_recv()
+    m_total(3, 2, 4, 1)
+
+    for copy in m_first + m_second:
+        copy.wait_send()
+    line.drain()
+    wm.wait_send()
+    for i in range(1, slots):
+        at_copy(i, seq_peer(i)).wait_send()
+        g_copy(i).wait_send()
+    for b in range(1, grps):
+        o_copy(b).wait_send()
+        w_copy(b).wait_send()
+        h_copy(b).wait_send()
+    for chip in range(chips):
+        km_copy(chip).wait_send()
+
+        @pl.when(chip != p.chip)
+        def _(chip=chip):
+            q_copy(chip).wait_send()
+            kr_copy(chip).wait_send()
+
+        pl.when(chip > p.chip)(lambda chip=chip: to_right(chip).wait_send())
+        pl.when(chip < p.chip)(lambda chip=chip: to_left(chip).wait_send())
+
+
+def back_call(n2g, state, cotangent, tokens, gains, attn, q_heads, kv_heads, mask, cosine, sine,
+              qkv_all, out_full, n1_all, terms):
+    chips = cosine.shape[0]
+    grps = 4
+    slots = 2 * chips
+    shard, width = tokens.shape
+    att, block = out_full.shape[0], terms.shape[1] // grps
+    unit, half = att // (grps * slots), HD // 2
+    vm, dma = pltpu.VMEM, pltpu.SemaphoreType.DMA
+    anyspace = pl.BlockSpec(memory_space=pl.ANY)
+    vspec = pl.BlockSpec(memory_space=pltpu.VMEM)
+    low, wide = jnp.bfloat16, jnp.float32
+    struct = jax.ShapeDtypeStruct
+    return pl.pallas_call(
+        functools.partial(back_kernel, chips, 1.0 / math.sqrt(HD)),
+        out_shape=(
+            struct((shard, width), wide),
+            struct((half, width + HD), wide),
+            struct((unit, width), wide),
+            struct((2, 1, width), wide),
+            struct((3, block, width), wide),
+        ),
+        in_specs=[vspec] * 12 + [anyspace] * 3,
+        out_specs=(vspec,) * 5,
+        scratch_shapes=[
+            vm((att, width), low),
+            vm((chips, 2, shard, width), low),
+            vm((chips, shard, width + HD), low),
+            vm((grps, slots, unit, shard), low),
+            vm((grps, unit, slots * shard), low),
+            vm((chips, 3, shard, HD), low),
+            vm((chips, 3, shard, HD), low),
+            vm((chips, 2, chips, shard, HD), low),
+            vm((chips, chips, shard, HD), low),
+            vm((chips, chips, shard, HD), low),
+            vm((chips, shard, HD), wide),
+            vm((chips, chips, shard, HD), low),
+            vm((chips, shard, grps * HD), low),
+            vm((chips, shard, width), low),
+            vm((chips, shard, width), low),
+            vm((chips, shard, width), low),
+            vm((grps, 2, half, width + HD), wide),
+            vm((grps, half, width + HD), wide),
+            vm((grps, half, width + HD), low),
+            vm((grps, half, width + HD), low),
+            vm((grps, unit, width), wide),
+            vm((grps, unit, width), low),
+            vm((grps, unit, width), low),
+            vm((4, 3, block // 2, width), low),
+            vm((6, 3, block // 2, width), low),
+            vm((2, 1, width), wide),
+            vm((slots, 2, 1, width), wide),
+            vm((2, 1, width), wide),
+            vm((grps, 2, 1, width), wide),
+            vm((shard, width), wide),
+            dma((2,)),
+            dma((3, chips)), dma((chips, 2)),
+            dma((slots,)), dma((slots,)),
+            dma((chips,)), dma((chips,)),
+            dma((chips,)), dma((chips,)),
+            dma((chips,)), dma((chips,)),
+            dma((2, chips)), dma((2, chips)),
+            dma, dma,
+            dma((grps,)), dma((grps,)),
+            dma((grps,)), dma((grps,)),
+            dma((6,)), dma((6,)),
+            dma((4,)),
+            dma((slots,)), dma((slots,)),
+            dma((grps,)), dma((grps,)),
+        ],
+        compiler_params=pltpu.CompilerParams(
+            collective_id=3, has_side_effects=True, vmem_limit_bytes=62 * 2**20
+        ),
+        name="back",
+    )(n2g, state, cotangent, tokens, gains, attn, q_heads, kv_heads, mask, cosine, sine,
+      qkv_all, out_full, n1_all, terms)
 
 
 def columns_to_owners(rows, row_unit):
@@ -891,7 +1344,6 @@
         normed_one_all = n1_all.reshape(group_tok, -1)
         cotangent_all = cot_all.reshape(group_tok, -1)
         out_full = out_all.reshape(att_width, -1)
-        qkv_rows = lax.all_gather(qkv_weight, "grp", axis=0, tiled=True)
         query_rot = q_heads.transpose(2, 1, 0, 3).reshape(tok_rows, H, HD)
         kv_rows = kv_heads.reshape(2, KVH, 2, chips, tok_rows, HD).transpose(0, 3, 2, 4, 1, 5)
         keys_all, values_all = kv_rows.reshape(2, group_tok, kv_width)
@@ -1005,9 +1457,29 @@
         grad_part, out_part, mlp_terms = mlp_call(
             normed_two, cotangent_all.reshape(seq_count, tok_rows, -1), mlp_blocks
         )
-        mlp_grad = sum_blocks(mlp_terms, grp_count)[:, : mlp_weight.shape[0]].transpose(1, 0, 2)
-    else:
-        grad_part, out_part, mlp_grad = plain_mlp(normed_two, cotangent_all, mlp_weight)
+        output = (state + out_part).astype(jnp.bfloat16)
+        gains = jnp.stack([gain_one, gain_two])[:, None, :]
+        token_grad, qkv_terms, out_grad, gain_sums, mlp_sums = back_call(
+            grad_part, state, cotangent, tokens, gains, attn_wide, q_heads, kv_heads, mask,
+            by_shard(all_cosine), by_shard(all_sine), qkv_all.reshape(-1, qkv_all.shape[-1]),
+            out_full, n1_all, mlp_terms,
+        )
+        width = tokens.shape[1]
+        own = width // (grp_count * seq_count)
+        gain_parts = lax.dynamic_slice_in_dim(
+            gain_sums[:, 0], (grp_place * seq_count + seq_place) * own, own, 1
+        )
+        return (
+            output,
+            token_grad,
+            gain_parts[0],
+            qkv_terms[:, :width],
+            qkv_terms[:, width],
+            out_grad,
+            gain_parts[1],
+            mlp_sums[:, : mlp_weight.shape[0]].transpose(1, 0, 2),
+        )
+    grad_part, out_part, mlp_grad = plain_mlp(normed_two, cotangent_all, mlp_weight)
     output = (state + out_part).astype(jnp.bfloat16)
     unused_state, norm_two_back = jax.vjp(rms_scale, state, gain_two)
     state_norm_grad, gain_two_grad = norm_two_back(grad_part)

time: 622 us -> 425 us (0.68)
  blocking collectives: 168 us -> 0 us
  Pallas kernels: 256 us -> 395 us
  waiting for transfers between devices: 75.4 us -> 0 us
  other arithmetic: 32.7 us -> 11.5 us
  matrix products: 22.6 us -> 3.46 us
  local copies, waits for them, and re-layouts: 31.8 us -> 14 us
  between operations: 15.2 us -> 0.83 us
  starting transfers between devices: 14 us -> 0 us
    pallas_call x0 -> x1, Pallas kernels: none -> 139 us  [back_call(): pl.pallas_call(functools.partial(back_kernel, chips, 1.0 / math.sqrt(HD))...]
    unnamed x2 -> x0, blocking collectives: 134 us -> none
    unnamed x8 -> x0, waiting for transfers between devices: 61.9 us -> none
    all_to_all x1 -> x0, blocking collectives: 23.4 us -> none  [columns_to_owners(): return lax.all_to_all(split, 'seq', split_axis=0, concat_axis=0, tiled=True)]
    dot_general x9 -> x0, matrix products: 19.2 us -> none  [the longest x1 4.15 us: per_device(): lax.dot_general(qkv_grad_owned, normed_one_all, contract_first, preferred...]
    all_to_all x1 -> x0, waiting for transfers between devices: 13.5 us -> none  [columns_to_owners(): return lax.all_to_all(split, 'seq', split_axis=0, concat_axis=0, tiled=True)]
    all_to_all x1 -> x0, starting transfers between devices: 10.9 us -> none  [columns_to_owners(): return lax.all_to_all(split, 'seq', split_axis=0, concat_axis=0, tiled=True)]
    all_gather x1 -> x0, blocking collectives: 10.8 us -> none  [per_device(): qkv_rows = lax.all_gather(qkv_weight, 'grp', axis=0, tiled=True)]
  transfers between devices with their start and end apart: 10 -> 0, of which waited for: 3 -> 0; matrix products, arithmetic and copies ran while one was open for 6% -> 0% of each run, Pallas kernels for 0% -> 0%
where the time goes in v4:
time: 425 us
  Pallas kernels  395 us (93%)
  local copies, waits for them, and re-layouts  14 us (3%)
  other arithmetic  11.5 us (3%)
    pallas_call x1, Pallas kernels, back_call(): pl.pallas_call(functools.partial(back_kernel, chips, 1.0 / math.sqrt(HD))...  139 us
    pallas_call x1, Pallas kernels, front_call(): pl.pallas_call(functools.partial(front_kernel, chips, 1.0 / math.sqrt(HD)...  130 us
    pallas_call x1, Pallas kernels, mlp_call(): pl.pallas_call(functools.partial(mlp_kernel, chips, grps, row_tiles), out...  125 us

profile of v4, /device:TPU:9, one launch (start us, length us, event | category | flops | bytes accessed | tf_op | source)
XLA Modules:
  0.0 425.0 jit_solution(12523386342742426544)
XLA Ops:
  0.7 0.8 fusion.9
  1.5 0.2 select_reduce_fusion
  1.7 1.3 fusion.6
  3.0 1.4 compare_reduce_fusion
  4.4 0.1 eq.71
  4.5 0.1 reduce_min.12
  4.7 1.9 multiply_sine_fusion
  6.6 1.3 negate_select_fusion
  7.9 0.1 eq.79
  8.0 0.1 copy.21
  8.1 0.1 or.19
  8.2 0.1 copy.22
  8.4 0.7 iota_add_fusion.1
  9.1 1.0 and_select_fusion.mask_ref
  10.0 0.7 convert_element_type.38
  10.8 0.6 broadcast_in_dim.57.bias_ref
  11.4 1.7 pad.6.wm_ref.refs_0_
  13.1 0.2 fusion
  13.3 0.9 fusion.2.n1_ref
  14.2 130.3 %front.1 = (f32[128,1536]{1,0:T(8,128)}, f32[2,768,128]{2,1,0:T(8,128)}, bf16[4,3,128,128]{3,2,1,0:T(8,128)(2,1)}, bf16[4,2,4,128,128]{4,3,2,1,0:T(8,128)(2,1)},...) custom-call(bf16[128,1536]{1,0:T(8,128)(2,1)} %fusion.2.n1_ref, ...), custom_call_target="tpu_custom_call" | custom-call | tf_op jit(solution)/shard_map/front/pallas_call | solution.py:703
  144.5 3.5 multiply_reduce_fusion
  148.0 1.0 multiply_convert_fusion.n2_ref
  149.0 125.4 %mlp.1 = (f32[128,1536]{1,0:T(8,128)}, f32[128,1536]{1,0:T(8,128)}, bf16[3,1152,1536]{2,1,0:T(8,128)(2,1)}) custom-call(bf16[128,1536]{1,0:T(8,128)(2,1)} %multiply_convert_fusion.n2_ref, bf16[8,128,1536]{2,1,0:T(8,128)(2,1)} %bitcast.27, bf16[3,288,1536]{2,1,0:T(8,128)(2,1)} %pad.6.wm_ref.refs_0_, bf16[3,288,1536]{2,1,0:T(8,128)(2,1)} %get-tuple-element.29.refs_1_, ...), custom_call_target="tpu_custom_call" | custom-call | flops 32614907904 | bytes 31457280 | tf_op jit(solution)/shard_map/mlp/pallas_call | solution.py:348
  274.5 0.6 broadcast_in_dim.66.gains_ref
  275.1 139.5 %back.1 = (f32[128,1536]{1,0:T(8,128)}, f32[64,1664]{1,0:T(8,128)}, f32[48,1536]{1,0:T(8,128)}, f32[2,1,1536]{2,1,0:T(1,128)}, f32[3,288,1536]{2,1,0:T(8,128)}) custom-call(f32[128,1536]{1,0:T(8,128)} %get-tuple-element.33.n2g_ref, f32[128,1536]{1,0:T(8,128)} %copy-done, bf16[128,1536]{1,0:T(8,128)(2,1)} %cot_ref.3, bf16[128,1536]{1,0:T(8,128)(2,1)} %tokens_ref.1, ...), custom_call_target="tpu_custom_call" | custom-call | tf_op jit(solution)/shard_map/back/pallas_call | solution.py:1130
  414.6 5.3 %slice_bitcast_fusion = f32[280,3,1536]{2,0,1:T(8,128)} fusion(f32[3,288,1536]{2,1,0:T(8,128)} %get-tuple-element.43), kind=kLoop, calls=%fused_computation | loop fusion | bytes 10321920 | tf_op jit(solution)/shard_map/transpose | solution.py:1480
  419.9 0.8 slice.22
  420.7 1.3 fusion.4
  421.9 0.6 slice_reduce_fusion
  422.6 0.8 add_convert_fusion
  423.4 0.9 copy.25
  424.3 0.7 copy.26
  (35 shorter events, 0.4 us)
Async XLA Ops:
  0.6 10.7 %copy-start.3 = (bf16[280,3,1536]{2,0,1:T(8,128)(2,1)S(1)}, bf16[280,3,1536]{2,0,1:T(8,128)(2,1)}, u32[]{:S(2)}) copy-start(bf16[280,3,1536]{2,0,1:T(8,128)(2,1)} %param.17) | copy-start | bytes 7741444
  0.6 12.5 %copy-start.8 = (bf16[1536]{0:T(1024)(128)(2,1)S(1)}, bf16[1536]{0:T(1024)(128)(2,1)}, u32[]{:S(2)}) copy-start(bf16[1536]{0:T(1024)(128)(2,1)} %param.12) | copy-start | bytes 9220
  0.7 12.5 %copy-start.2 = (bf16[128,1536]{1,0:T(8,128)(2,1)S(1)}, bf16[128,1536]{1,0:T(8,128)(2,1)}, u32[]{:S(2)}) copy-start(bf16[128,1536]{1,0:T(8,128)(2,1)} %tokens_ref.1) | copy-start | bytes 1179652
  14.2 133.8 %copy-start.9 = (bf16[1536]{0:T(1024)(128)(2,1)S(1)}, bf16[1536]{0:T(1024)(128)(2,1)}, u32[]{:S(2)}) copy-start(bf16[1536]{0:T(1024)(128)(2,1)} %param.16) | copy-start | bytes 9220
  148.0 126.4 %copy-start = (f32[128,1536]{1,0:T(8,128)}, f32[128,1536]{1,0:T(8,128)S(1)}, u32[]{:S(2)}) copy-start(f32[128,1536]{1,0:T(8,128)S(1)} %get-tuple-element.53.state_ref) | copy-start | bytes 2359300
  414.5 5.4 %copy-start.6 = (f32[64,1664]{1,0:T(8,128)S(1)}, f32[64,1664]{1,0:T(8,128)}, u32[]{:S(2)}) copy-start(f32[64,1664]{1,0:T(8,128)} %get-tuple-element.41) | copy-start | bytes 1277956
  414.5 8.0 %copy-start.1 = (f32[128,1536]{1,0:T(8,128)S(1)}, f32[128,1536]{1,0:T(8,128)}, u32[]{:S(2)}) copy-start(f32[128,1536]{1,0:T(8,128)} %copy-done) | copy-start | bytes 2359300
  414.6 8.0 %copy-start.5 = (f32[128,1536]{1,0:T(8,128)S(1)}, f32[128,1536]{1,0:T(8,128)}, u32[]{:S(2)}) copy-start(f32[128,1536]{1,0:T(8,128)} %get-tuple-element.32) | copy-start | bytes 2359300
  414.6 8.8 %copy-start.4 = (f32[128,1536]{1,0:T(8,128)S(1)}, f32[128,1536]{1,0:T(8,128)}, u32[]{:S(2)}) copy-start(f32[128,1536]{1,0:T(8,128)} %get-tuple-element.65) | copy-start | bytes 2359300
  414.6 9.7 %copy-start.7 = (f32[48,1536]{1,0:T(8,128)S(1)}, f32[48,1536]{1,0:T(8,128)}, u32[]{:S(2)}) copy-start(f32[48,1536]{1,0:T(8,128)} %get-tuple-element.69) | copy-start | bytes 884740

commit v5 on v4

--- a/solution.py
+++ b/solution.py
@@ -78,300 +78,6 @@
     near = jnp.where(order % 2 == 1, place - offset, place + offset)
     rest = jnp.where(place < chips - 1 - place, order, chips - 1 - order)
     return jnp.where(order <= both, near, rest)
-
-
-def line_barrier(chips):
-    grp, seq = lax.axis_index("grp"), lax.axis_index("seq")
-    chip, core = seq // 2, seq % 2
-    mate = seq + 1 - 2 * core
-    barrier = pltpu.get_barrier_semaphore()
-
-    def greet(other):
-        pl.semaphore_signal(barrier, inc=1, device_id=(grp, other), device_id_type=MESH)
-
-    greet(mate)
-    pl.when(chip > 0)(lambda: greet(seq - 2))
-    pl.when(chip < chips - 1)(lambda: greet(seq + 2))
-    inner = jnp.where((chip > 0) & (chip < chips - 1), 1, 0)
-    pl.semaphore_wait(barrier, 2 + inner)
-
-
-class LineGather:
-    def __init__(self, buf, send_sem, recv_sem, chips):
-        self.buf, self.send_sem, self.recv_sem, self.chips = buf, send_sem, recv_sem, chips
-        self.grp, self.seq = lax.axis_index("grp"), lax.axis_index("seq")
-        self.chip, self.core = self.seq // 2, self.seq % 2
-        self.mate = self.seq + 1 - 2 * self.core
-
-    def copy(self, way, slot):
-        to = (self.seq + 2, self.seq - 2, self.mate)[way]
-        return remote(
-            self.buf.at[slot], self.buf.at[slot], self.send_sem.at[way, slot],
-            self.recv_sem.at[slot], self.grp, to,
-        )
-
-    def wait_recv(self, slot):
-        self.copy(2, slot).wait_recv()
-
-    def start(self):
-        pl.when(self.chip < self.chips - 1)(lambda: self.copy(0, self.seq).start())
-        pl.when(self.chip > 0)(lambda: self.copy(1, self.seq).start())
-        self.copy(2, self.seq).start()
-
-    def forward(self, step):
-        @pl.when(self.chip - step >= 0)
-        def _():
-            slot = self.seq - 2 * step
-            self.wait_recv(slot)
-            pl.when(self.chip < self.chips - 1)(lambda: self.copy(0, slot).start())
-            self.copy(2, slot).start()
-
-        @pl.when(self.chip + step < self.chips)
-        def _():
-            slot = self.seq + 2 * step
-            self.wait_recv(slot)
-            pl.when(self.chip > 0)(lambda: self.copy(1, slot).start())
-            self.copy(2, slot).start()
-
-    def wait_mate(self, chip):
-        self.wait_recv(2 * chip + 1 - self.core)
-
-    def drain(self):
-        for other in range(self.chips):
-            slot = 2 * other + self.core
-            self.copy(2, slot).wait_send()
-            pl.when((other <= self.chip) & (self.chip < self.chips - 1))(
-                lambda slot=slot: self.copy(0, slot).wait_send()
-            )
-            pl.when((other >= self.chip) & (self.chip > 0))(
-                lambda slot=slot: self.copy(1, slot).wait_send()
-            )
-
-
-class LineScatter:
-    def __init__(self, part, mate_in, left_in, right_in, send_sem, recv_sem, chips):
-        self.part, self.mate_in, self.left_in, self.right_in = part, mate_in, left_in, right_in
-        self.send_sem, self.recv_sem, self.chips = send_sem, recv_sem, chips
-        self.grp, self.seq = lax.axis_index("grp"), lax.axis_index("seq")
-        self.chip, self.core = self.seq // 2, self.seq % 2
-        self.mate = self.seq + 1 - 2 * self.core
-
-    def to_mate(self, r, chip):
-        return remote(
-            self.part.at[r, 2 * chip + 1 - self.core], self.mate_in.at[r, chip],
-            self.send_sem.at[0, r, chip], self.recv_sem.at[0, r, chip], self.grp, self.mate,
-        )
-
-    def to_right(self, r, chip):
-        return remote(
-            self.part.at[r, 2 * chip + self.core], self.left_in.at[r, chip],
-            self.send_sem.at[1, r, chip], self.recv_sem.at[1, r, chip], self.grp, self.seq + 2,
-        )
-
-    def to_left(self, r, chip):
-        return remote(
-            self.part.at[r, 2 * chip + self.core], self.right_in.at[r, chip],
-            self.send_sem.at[2, r, chip], self.recv_sem.at[2, r, chip], self.grp, self.seq - 2,
-        )
-
-    def step(self, r, order):
-        last = self.chips - 1
-        far = last - order
-
-        @pl.when(far > self.chip)
-        def _():
-            self.to_mate(r, far).wait_recv()
-            slot = 2 * far + self.core
-            total = self.part[r, slot].astype(jnp.float32) + self.mate_in[r, far].astype(jnp.float32)
-
-            @pl.when(self.chip > 0)
-            def _():
-                self.to_right(r, far).wait_recv()
-                self.part[r, slot] = (total + self.left_in[r, far].astype(jnp.float32)).astype(jnp.bfloat16)
-
-            @pl.when(self.chip == 0)
-            def _():
-                self.part[r, slot] = total.astype(jnp.bfloat16)
-
-            self.to_right(r, far).start()
-
-        @pl.when(order < self.chip)
-        def _():
-            self.to_mate(r, order).wait_recv()
-            slot = 2 * order + self.core
-            total = self.part[r, slot].astype(jnp.float32) + self.mate_in[r, order].astype(jnp.float32)
-
-            @pl.when(self.chip < last)
-            def _():
-                self.to_left(r, order).wait_recv()
-                self.part[r, slot] = (total + self.right_in[r, order].astype(jnp.float32)).astype(jnp.bfloat16)
-
-            @pl.when(self.chip == last)
-            def _():
-                self.part[r, slot] = total.astype(jnp.bfloat16)
-
-            self.to_left(r, order).start()
-
-    def finish(self, r, out_ref):
-        self.to_mate(r, self.chip).wait_recv()
-        out_ref[...] = self.part[r, self.seq].astype(jnp.float32) + self.mate_in[r, self.chip].astype(jnp.float32)
-
-        @pl.when(self.chip > 0)
-        def _():
-            self.to_right(r, self.chip).wait_recv()
-            out_ref[...] += self.left_in[r, self.chip].astype(jnp.float32)
-
-        @pl.when(self.chip < self.chips - 1)
-        def _():
-            self.to_left(r, self.chip).wait_recv()
-            out_ref[...] += self.right_in[r, self.chip].astype(jnp.float32)
-
-    def drain(self, r):
-        for other in range(self.chips):
-            self.to_mate(r, other).wait_send()
-            pl.when(other > self.chip)(lambda other=other: self.to_right(r, other).wait_send())
-            pl.when(other < self.chip)(lambda other=other: self.to_left(r, other).wait_send())
-
-
-def mlp_kernel(chips, grps, row_tiles, n2_ref, cot_ref, *refs):
-    w_refs, refs = refs[:grps], refs[grps:]
-    (
-        n2g_ref, outp_ref, grads_ref, tok, w, acts, part, mate_in, left_in, right_in, stage,
-        lsem, gsend, grecv, ssend, srecv, wsem, osem,
-    ) = refs
-    seq = lax.axis_index("seq")
-    chip, core = seq // 2, seq % 2
-    shard, width = n2_ref.shape
-    units = w.shape[1]
-    block = units // grps
-    tile = units // row_tiles
-    own = pltpu.make_async_copy(n2_ref, tok.at[0, seq], lsem.at[0])
-    own.start()
-    cot_copy = pltpu.make_async_copy(cot_ref, tok.at[1], lsem.at[1])
-    cot_copy.start()
-
-    def w_copy(j, b):
-        return pltpu.make_async_copy(w_refs[b].at[j], w.at[j, pl.ds(b * block, block)], wsem.at[j, b])
-
-    for j in range(3):
-        for b in range(grps):
-            w_copy(j, b).start()
-    line_barrier(chips)
-    gather = LineGather(tok.at[0], gsend, grecv, chips)
-    scatter = LineScatter(part, mate_in, left_in, right_in, ssend, srecv, chips)
-    own.wait()
-    gather.start()
-
-    @pl.loop(0, chips)
-    def _(order):
-        @pl.when(order == 0)
-        def _():
-            cot_copy.wait()
-            for j in range(3):
-                for b in range(grps):
-                    w_copy(j, b).wait()
-
-        pl.when(order > 0)(lambda: gather.forward(order))
-        at = nearest_chip(chip, order, chips)
-        gather.wait_mate(at)
-        x = tok[0, pl.ds(2 * at, 2)].reshape(2 * shard, width)
-        y = tok[1, pl.ds(2 * at, 2)].reshape(2 * shard, width)
-        gate = lax.dot_general(x, w[0], CONTRACT_LAST, preferred_element_type=jnp.float32)
-        up = lax.dot_general(x, w[1], CONTRACT_LAST, preferred_element_type=jnp.float32)
-        unit_grad = lax.dot_general(y, w[2], CONTRACT_LAST, preferred_element_type=jnp.float32)
-        sig = 1.0 / (1.0 + jnp.exp(-gate))
-        silu = gate * sig
-        rows = pl.ds(at * (2 * shard), 2 * shard)
-        gate_grad = (unit_grad * up * sig * (1.0 + gate * (1.0 - sig))).astype(jnp.bfloat16)
-        up_grad = (unit_grad * silu).astype(jnp.bfloat16)
-        acts[0, rows] = gate_grad
-        acts[1, rows] = up_grad
-        acts[2, rows] = (silu * up).astype(jnp.bfloat16)
-        back = jnp.dot(gate_grad, w[0], preferred_element_type=jnp.float32) + jnp.dot(
-            up_grad, w[1], preferred_element_type=jnp.float32
-        )
-        part[0, pl.ds(2 * at, 2)] = back.astype(jnp.bfloat16).reshape(2, shard, width)
-        scatter.to_mate(0, at).start()
-
-    def out_copy(t):
-        return pltpu.make_async_copy(
-            stage.at[t % 2],
-            grads_ref.at[t // row_tiles, pl.ds((t % row_tiles) * tile, tile)],
-            osem.at[t % 2],
-        )
-
-    @pl.loop(0, 3 * row_tiles)
-    def _(t):
-        @pl.when(t < 2 * chips)
-        def _():
-            scatter.step(t // chips, t % chips)
-
-        @pl.when(t < chips)
-        def _():
-            h = acts[2, pl.ds(t * (2 * shard), 2 * shard)]
-            part[1, pl.ds(2 * t, 2)] = (
-                jnp.dot(h, w[2], preferred_element_type=jnp.float32)
-                .astype(jnp.bfloat16).reshape(2, shard, width)
-            )
-            scatter.to_mate(1, t).start()
-
-        @pl.when(t >= 2)
-        def _():
-            out_copy(t - 2).wait()
-
-        kind = t // row_tiles
-        lhs = acts[kind, :, pl.ds(pl.multiple_of((t % row_tiles) * tile, 128), tile)]
-        rhs = tok[kind // 2].reshape(2 * chips * shard, width)
-        stage[t % 2] = lax.dot_general(
-            lhs, rhs, CONTRACT_FIRST, preferred_element_type=jnp.float32
-        ).astype(jnp.bfloat16)
-        out_copy(t).start()
-
-    scatter.finish(0, n2g_ref)
-    scatter.finish(1, outp_ref)
-    out_copy(3 * row_tiles - 2).wait()
-    out_copy(3 * row_tiles - 1).wait()
-    gather.drain()
-    scatter.drain(0)
-    scatter.drain(1)
-
-
-def mlp_call(n2, cot_all, w_blocks, row_tiles=3):
-    grps, (_, block, width) = len(w_blocks), w_blocks[0].shape
-    slots, shard, _ = cot_all.shape
-    chips = slots // 2
-    units = grps * block
-    vm, anyspace = pltpu.VMEM, pl.BlockSpec(memory_space=pl.ANY)
-    vspec = pl.BlockSpec(memory_space=pltpu.VMEM)
-    dma = pltpu.SemaphoreType.DMA
-    flops = 2 * 9 * slots * shard * units * width
-    return pl.pallas_call(
-        functools.partial(mlp_kernel, chips, grps, row_tiles),
-        out_shape=(
-            jax.ShapeDtypeStruct((shard, width), jnp.float32),
-            jax.ShapeDtypeStruct((shard, width), jnp.float32),
-            jax.ShapeDtypeStruct((3, units, width), jnp.bfloat16),
-        ),
-        in_specs=[vspec, anyspace] + [anyspace] * grps,
-        out_specs=(vspec, vspec, anyspace),
-        scratch_shapes=[
-            vm((2, slots, shard, width), jnp.bfloat16),
-            vm((3, units, width), jnp.bfloat16),
-            vm((3, slots * shard, units), jnp.bfloat16),
-            vm((2, slots, shard, width), jnp.bfloat16),
-            vm((2, chips, shard, width), jnp.bfloat16),
-            vm((2, chips, shard, width), jnp.bfloat16),
-            vm((2, chips, shard, width), jnp.bfloat16),
-            vm((2, units // row_tiles, width), jnp.bfloat16),
-            dma((2,)), dma((3, slots)), dma((slots,)), dma((3, 2, chips)), dma((3, 2, chips)),
-            dma((3, grps)), dma((2,)),
-        ],
-        compiler_params=pltpu.CompilerParams(
-            collective_id=1, has_side_effects=True, vmem_limit_bytes=62 * 2**20
-        ),
-        cost_estimate=pl.CostEstimate(flops=flops, bytes_accessed=30 * 2**20, transcendentals=0),
-        name="mlp",
-    )(n2, cot_all, *w_blocks)
 
 
 class Place:
@@ -453,13 +159,93 @@
             )
 
 
+class LineScatter:
+    def __init__(self, place, part, mate_in, left_in, right_in, send_sem, recv_sem):
+        self.place, self.part = place, part
+        self.mate_in, self.left_in, self.right_in = mate_in, left_in, right_in
+        self.send_sem, self.recv_sem = send_sem, recv_sem
+
+    def copy(self, way, src, landing, r, chip, to):
+        return remote(
+            src, landing.at[r, chip], self.send_sem.at[way, r, chip], self.recv_sem.at[way, r, chip],
+            self.place.grp, to,
+        )
+
+    def to_mate(self, r, chip):
+        p = self.place
+        return self.copy(0, self.part.at[r, 2 * chip + 1 - p.core], self.mate_in, r, chip, p.mate)
+
+    def to_right(self, r, chip):
+        p = self.place
+        return self.copy(1, self.part.at[r, 2 * chip + p.core], self.left_in, r, chip, p.seq + 2)
+
+    def to_left(self, r, chip):
+        p = self.place
+        return self.copy(2, self.part.at[r, 2 * chip + p.core], self.right_in, r, chip, p.seq - 2)
+
+    def step(self, r, chip):
+        p = self.place
+        last = p.chips - 1
+        slot = 2 * chip + p.core
+
+        @pl.when(chip != p.chip)
+        def _():
+            self.to_mate(r, chip).wait_recv()
+            total = self.part[r, slot].astype(jnp.float32) + self.mate_in[r, chip].astype(jnp.float32)
+            self.part[r, slot] = total.astype(jnp.bfloat16)
+
+        @pl.when(chip > p.chip)
+        def _():
+            @pl.when(p.chip > 0)
+            def _():
+                self.to_right(r, chip).wait_recv()
+                self.part[r, slot] = (
+                    self.part[r, slot].astype(jnp.float32) + self.left_in[r, chip].astype(jnp.float32)
+                ).astype(jnp.bfloat16)
+
+            self.to_right(r, chip).start()
+
+        @pl.when(chip < p.chip)
+        def _():
+            @pl.when(p.chip < last)
+            def _():
+                self.to_left(r, chip).wait_recv()
+                self.part[r, slot] = (
+                    self.part[r, slot].astype(jnp.float32) + self.right_in[r, chip].astype(jnp.float32)
+                ).astype(jnp.bfloat16)
+
+            self.to_left(r, chip).start()
+
+    def finish(self, r, out_ref):
+        p = self.place
+        self.to_mate(r, p.chip).wait_recv()
+        out_ref[...] = self.part[r, p.seq].astype(jnp.float32) + self.mate_in[r, p.chip].astype(jnp.float32)
+
+        @pl.when(p.chip > 0)
+        def _():
+            self.to_right(r, p.chip).wait_recv()
+            out_ref[...] += self.left_in[r, p.chip].astype(jnp.float32)
+
+        @pl.when(p.chip < p.chips - 1)
+        def _():
+            self.to_left(r, p.chip).wait_recv()
+            out_ref[...] += self.right_in[r, p.chip].astype(jnp.float32)
+
+    def drain(self, r):
+        p = self.place
+        for other in range(p.chips):
+            self.to_mate(r, other).wait_send()
+            pl.when(other > p.chip)(lambda other=other: self.to_right(r, other).wait_send())
+            pl.when(other < p.chip)(lambda other=other: self.to_left(r, other).wait_send())
+
+
 def front_kernel(chips, scale,
-                 n1_ref, cot_ref, wq_ref, bias_ref, wo_ref, wm_ref, cos_ref, sin_ref, mask_ref,
-                 attn_ref, lse_ref, q_out_ref, kv_out_ref, n1_all_ref, cot_all_ref, wo_all_ref, wq_all_ref,
-                 wm1_ref, wm2_ref, wm3_ref,
-                 nbuf, wq, bias, stage, qbuf, kvbuf,
-                 lsem, n_send, n_recv, c_send, c_recv, o_send, o_recv, ox_send, ox_recv, om_send, om_recv,
-                 wq_send, wq_recv, b_send, b_recv, m_send, m_recv, q_send, q_recv, k_send, k_recv):
+                 tokens_ref, gains_ref, cot_ref, wq_ref, bias_ref, wo_ref, wm_ref, cos_ref, sin_ref, mask_ref,
+                 attn_ref, state_ref, q_out_ref, kv_out_ref, n1_all_ref, n2_all_ref, cot_all_ref, wo_all_ref,
+                 wq_all_ref, columns_ref, wm1_ref, wm2_ref, wm3_ref,
+                 nbuf, n2buf, wq, wo, bias, stage, qbuf, kvbuf, columns,
+                 lsem, n_send, n_recv, n2_send, n2_recv, c_send, c_recv, o_send, o_recv, ox_send, ox_recv,
+                 om_send, om_recv, wq_send, wq_recv, b_send, b_recv, m_send, m_recv, q_send, q_recv, k_send, k_recv):
     p = Place(chips)
     grps = 4
     half = wq_ref.shape[0]
@@ -469,19 +255,21 @@
     part = wm_ref.shape[1] // 2
 
     own = [
-        pltpu.make_async_copy(n1_ref, nbuf.at[p.chip, p.core], lsem.at[0]),
-        pltpu.make_async_copy(wq_ref, wq.at[0, rows], lsem.at[1]),
-        pltpu.make_async_copy(bias_ref, bias.at[0, p.core], lsem.at[2]),
-        pltpu.make_async_copy(wo_ref, wo_all_ref.at[p.grp, p.chip, p.core], lsem.at[3]),
-        pltpu.make_async_copy(cot_ref, cot_all_ref.at[p.chip, p.core], lsem.at[4]),
+        pltpu.make_async_copy(wq_ref, wq.at[0, rows], lsem.at[0]),
+        pltpu.make_async_copy(bias_ref, bias.at[0, p.core], lsem.at[1]),
+        pltpu.make_async_copy(wo_ref, wo.at[p.grp, p.chip, p.core], lsem.at[2]),
+        pltpu.make_async_copy(cot_ref, cot_all_ref.at[p.chip, p.core], lsem.at[3]),
     ]
     for copy in own:
         copy.start()
+    tokens = tokens_ref[...].astype(jnp.float32)
+    nbuf[p.chip, p.core] = rms_scale(tokens, gains_ref[0]).astype(jnp.bfloat16)
     p.barrier(grps)
 
     n1_line = RailGather(p, lambda chip, core: nbuf.at[chip, core], n_send, n_recv)
     cot_line = RailGather(p, lambda chip, core: cot_all_ref.at[chip, core], c_send, c_recv)
-    out_line = RailGather(p, lambda chip, core: wo_all_ref.at[p.grp, chip, core], o_send, o_recv)
+    n2_line = RailGather(p, lambda chip, core: n2buf.at[chip, core], n2_send, n2_recv)
+    out_line = RailGather(p, lambda chip, core: wo.at[p.grp, chip, core], o_send, o_recv)
 
     def wq_direct(b):
         return remote(wq_ref, wq.at[b, rows], wq_send.at[0, b], wq_recv.at[b, 0], p.peer(b), p.seq)
@@ -507,13 +295,20 @@
             p.peer(3 - b), p.seq,
         )
 
-    def out_cross(b):
-        view = lambda grp: wo_all_ref.at[grp, :, p.core]
-        return remote(view(p.grp), view(p.grp), ox_send.at[b], ox_recv.at[b], p.peer(b), p.seq)
-
-    def out_mate(b):
-        view = wo_all_ref.at[p.peer(b), :, p.core]
-        return remote(view, view, om_send.at[b], om_recv.at[b], p.grp, p.mate)
+    def out_view(grp, i, core):
+        return wo.at[grp, pl.ds(i * (chips // 2), chips // 2), core]
+
+    def out_direct(b, i):
+        view = out_view(p.grp, i, p.core)
+        return remote(view, view, ox_send.at[b, i], ox_recv.at[b, i], p.peer(b), p.seq)
+
+    def out_forward(b):
+        view = out_view(p.peer(b), b - 1, p.core)
+        return remote(view, view, ox_send.at[3, b - 1], ox_recv.at[3, b - 1], p.peer(3 - b), p.seq)
+
+    def out_mate(b, i, core):
+        view = out_view(p.peer(b), i, core)
+        return remote(view, view, om_send.at[b, i], om_recv.at[b, i], p.grp, p.mate)
 
     def q_copy(chip):
         return remote(
@@ -541,16 +336,15 @@
         view = kvbuf.at[head, core, chip]
         return remote(view, view, k_send.at[1, head, chip], k_recv.at[head, core, chip], p.grp, p.mate)
 
+    own[0].wait()
     own[1].wait()
-    own[2].wait()
     for b in range(1, grps):
         wq_direct(b).start()
         bias_direct(b).start()
     wq_mate(0).start()
     bias_mate(0).start()
-    own[0].wait()
     n1_line.start()
-    own[3].wait()
+    own[2].wait()
     out_line.start()
     for b in range(1, grps):
         wq_direct(b).wait_recv()
@@ -596,9 +390,11 @@
             pl.when(to_chip != p.chip)(lambda to_chip=to_chip: k_copy(at, to_chip).start())
         k_mate(p.chip, at, stage.at[at, 3]).start()
 
-    for b in range(1, grps):
-        out_cross(b).start()
-    own[4].wait()
+    for b in (1, 2):
+        out_direct(b, b - 1).start()
+    for b in (1, 2):
+        out_direct(b, 2 - b).start()
+    own[3].wait()
     cot_line.start()
 
     @pl.loop(0, chips)
@@ -614,9 +410,6 @@
         pl.when(chip != p.chip)(lambda chip=chip: q_arrival(chip).wait_recv())
         for head in range(chips):
             k_arrival(head, 1 - p.core, chip).wait_recv()
-    for b in (1, 2):
-        m_direct(b, b - 1).wait_recv()
-        m_forward(b).start()
     cot_line.forward(1)
 
     mask = mask_ref[...]
@@ -629,46 +422,72 @@
         values = kvbuf[KVH + kv].reshape(mask.shape[1], 2 * half)
         scores = lax.dot_general(queries, keys, CONTRACT_LAST, preferred_element_type=jnp.float32) * scale
         scores = scores.reshape(heads_per, shard, mask.shape[1]) + mask[None]
-        top = jnp.max(scores, axis=-1, keepdims=True)
-        weights = jnp.exp(scores - top)
-        total = jnp.sum(weights, axis=-1, keepdims=True)
-        probs = (weights / total).astype(jnp.bfloat16).reshape(heads_per * shard, mask.shape[1])
+        weights = jnp.exp(scores - jnp.max(scores, axis=-1, keepdims=True))
+        inverse = 1.0 / jnp.sum(weights, axis=-1, keepdims=True)
+        probs = (weights * inverse).astype(jnp.bfloat16).reshape(heads_per * shard, mask.shape[1])
         mixed = jnp.dot(probs, values, preferred_element_type=jnp.float32)
-        log_total = (top + jnp.log(total)).reshape(heads_per * shard, 1)
-        lse_ref[kv] = jnp.broadcast_to(log_total, (heads_per * shard, 2 * half))
         for i, h in enumerate(heads):
             attn_ref[:, h * 2 * half : (h + 1) * 2 * half] = mixed[i * shard : (i + 1) * shard]
+        if kv == 0:
+            for b in (1, 2):
+                out_direct(b, b - 1).wait_recv()
+                out_forward(b).start()
+                out_mate(b, b - 1, p.core).start()
         cot_line.forward(kv + 2)
 
-    for b in range(1, grps):
-        out_cross(b).wait_recv()
-        out_mate(b).start()
+    for b in (1, 2):
+        out_direct(b, 2 - b).wait_recv()
+        out_mate(b, 2 - b, p.core).start()
+    for b in (1, 2):
+        m_direct(b, b - 1).wait_recv()
+        m_forward(b).start()
     m_direct(1, 1).start()
     m_direct(2, 0).start()
+    attn_low = attn_ref[...].astype(jnp.bfloat16)
+    unit = wo.shape[3]
+    columns[...] = attn_low.T.reshape(columns.shape)
+    for i in (0, 1):
+        out_forward(i + 1).wait_recv()
+        out_mate(3, i, p.core).start()
+    for b in range(1, grps):
+        for i in (0, 1):
+            out_mate(b, i, 1 - p.core).wait_recv()
+    for chip in range(chips):
+        out_line.wait_mate(chip)
+    state = tokens_ref[...].astype(jnp.float32) + jnp.dot(
+        attn_low, wo[...].reshape(grps * chips * 2 * unit, tokens_ref.shape[1]),
+        preferred_element_type=jnp.float32,
+    )
+    state_ref[...] = state
+    n2buf[p.chip, p.core] = rms_scale(state, gains_ref[1]).astype(jnp.bfloat16)
+    n2_line.start()
     outs = [
-        pltpu.make_async_copy(nbuf, n1_all_ref, lsem.at[5]),
-        pltpu.make_async_copy(wq, wq_all_ref, lsem.at[6]),
-        pltpu.make_async_copy(qbuf, q_out_ref, lsem.at[7]),
-        pltpu.make_async_copy(kvbuf, kv_out_ref, lsem.at[8]),
+        pltpu.make_async_copy(nbuf, n1_all_ref, lsem.at[4]),
+        pltpu.make_async_copy(wq, wq_all_ref, lsem.at[5]),
+        pltpu.make_async_copy(qbuf, q_out_ref, lsem.at[6]),
+        pltpu.make_async_copy(kvbuf, kv_out_ref, lsem.at[7]),
+        pltpu.make_async_copy(wo, wo_all_ref, lsem.at[8]),
+        pltpu.make_async_copy(columns, columns_ref, lsem.at[9]),
     ]
     for chip in range(chips):
         n1_line.wait_mate(chip)
-        out_line.wait_mate(chip)
-        cot_line.wait_mate(chip)
     for copy in outs:
         copy.start()
+    for step in range(1, chips):
+        n2_line.forward(step)
+    for chip in range(chips):
+        cot_line.wait_mate(chip)
+        n2_line.wait_mate(chip)
+    last = pltpu.make_async_copy(n2buf, n2_all_ref, lsem.at[10])
+    last.start()
     for b in (1, 2):
         m_direct(b, 2 - b).wait_recv()
         m_forward(3 - b).wait_recv()
-    for b in range(1, grps):
-        om = remote(
-            wo_all_ref.at[p.peer(b), :, 1 - p.core], wo_all_ref.at[p.peer(b), :, 1 - p.core],
-            om_send.at[b], om_recv.at[b], p.grp, p.mate,
-        )
-        om.wait_recv()
     for copy in outs:
         copy.wait()
+    last.wait()
     n1_line.drain()
+    n2_line.drain()
     out_line.drain()
     cot_line.drain()
     for b in range(grps):
@@ -677,12 +496,14 @@
     for b in range(1, grps):
         wq_direct(b).wait_send()
         bias_direct(b).wait_send()
-        out_cross(b).wait_send()
-        out_mate(b).wait_send()
+        for i in (0, 1):
+            out_mate(b, i, p.core).wait_send()
     for b in (1, 2):
-        m_direct(b, 0).wait_send()
-        m_direct(b, 1).wait_send()
+        for i in (0, 1):
+            m_direct(b, i).wait_send()
+            out_direct(b, i).wait_send()
         m_forward(b).wait_send()
+        out_forward(b).wait_send()
     for chip in range(chips):
         pl.when(chip != p.chip)(lambda chip=chip: q_copy(chip).wait_send())
         for other in range(chips):
@@ -690,42 +511,50 @@
             k_mate(other, chip).wait_send()
 
 
-def front_call(n1, cot, qkv_weight, bias_rows, out_weight, mlp_rows, cosine, sine, mask):
+def front_call(tokens, gains, cot, qkv_weight, bias_rows, out_weight, mlp_rows, cosine, sine, mask):
     chips = cosine.shape[0]
     grps = 4
-    shard, width = n1.shape
+    shard, width = tokens.shape
     half = qkv_weight.shape[0]
     vm, dma = pltpu.VMEM, pltpu.SemaphoreType.DMA
     anyspace = pl.BlockSpec(memory_space=pl.ANY)
     vspec = pl.BlockSpec(memory_space=pltpu.VMEM)
     low, wide = jnp.bfloat16, jnp.float32
     struct = jax.ShapeDtypeStruct
+    wo_shape = (grps, chips, 2) + out_weight.shape
+    columns_shape = (grps, 2 * chips, out_weight.shape[0], shard)
     return pl.pallas_call(
         functools.partial(front_kernel, chips, 1.0 / math.sqrt(HD)),
         out_shape=(
             struct((shard, H * HD), wide),
-            struct((KVH, H // KVH * shard, HD), wide),
+            struct((shard, width), wide),
             struct((chips, 3, shard, HD), low),
             struct((chips, 2, chips, shard, HD), low),
             struct((chips, 2, shard, width), low),
             struct((chips, 2, shard, width), low),
-            struct((grps, chips, 2) + out_weight.shape, low),
+            struct((chips, 2, shard, width), low),
+            struct(wo_shape, low),
             struct((grps, 2 * half, width), low),
+            struct(columns_shape, low),
         ) + (struct(mlp_rows.shape, low),) * 3,
-        in_specs=[anyspace] * 6 + [vspec] * 3,
-        out_specs=(vspec,) * 2 + (anyspace,) * 9,
+        in_specs=[vspec] * 2 + [anyspace] * 5 + [vspec] * 3,
+        out_specs=(vspec,) * 2 + (anyspace,) * 11,
         scratch_shapes=[
             vm((chips, 2, shard, width), low),
+            vm((chips, 2, shard, width), low),
             vm((grps, 2 * half, width), low),
+            vm(wo_shape, low),
             vm((grps, 2) + bias_rows.shape, wide),
             vm((chips, grps, shard, HD), low),
             vm((chips, 3, shard, HD), low),
             vm((chips, 2, chips, shard, HD), low),
-            dma((9,)),
+            vm(columns_shape, low),
+            dma((11,)),
             dma((3, chips)), dma((chips, 2)),
             dma((3, chips)), dma((chips, 2)),
             dma((3, chips)), dma((chips, 2)),
-            dma((grps,)), dma((grps,)), dma((grps,)), dma((grps,)),
+            dma((3, chips)), dma((chips, 2)),
+            dma((grps, 2)), dma((grps, 2)), dma((grps, 2)), dma((grps, 2)),
             dma((2, grps)), dma((grps, 2)),
             dma((2, grps)), dma((grps, 2)),
             dma((grps, 2)), dma((grps, 2)),
@@ -733,10 +562,175 @@
             dma((2, chips, chips)), dma((chips, 2, chips)),
         ],
         compiler_params=pltpu.CompilerParams(
-            collective_id=2, has_side_effects=True, vmem_limit_bytes=56 * 2**20
+            collective_id=2, has_side_effects=True, vmem_limit_bytes=60 * 2**20
         ),
         name="front",
-    )(n1, cot, qkv_weight, bias_rows, out_weight, mlp_rows, cosine, sine, mask)
+    )(tokens, gains, cot, qkv_weight, bias_rows, out_weight, mlp_rows, cosine, sine, mask)
+
+
+def mlp_kernel(chips, grps, row_tiles, n2_ref, cot_ref, columns_ref, *refs):
+    w_refs, refs = refs[:grps], refs[grps:]
+    (
+        n2g_ref, outp_ref, grads_ref, owned_ref, tok, w, acts, part, mate_in, left_in, right_in, stage, owned,
+        lsem, ssend, srecv, wsem, osem, a_send, a_recv,
+    ) = refs
+    p = Place(chips)
+    slots = 2 * chips
+    shard, width = n2_ref.shape[1:]
+    units = w.shape[1]
+    block = units // grps
+    tile = units // row_tiles
+    loads = [
+        pltpu.make_async_copy(n2_ref, tok.at[0], lsem.at[0]),
+        pltpu.make_async_copy(cot_ref, tok.at[1], lsem.at[1]),
+        pltpu.make_async_copy(columns_ref.at[:, p.seq], owned.at[:, :, pl.ds(pl.multiple_of(p.seq * shard, shard), shard)], lsem.at[2]),
+    ]
+    for copy in loads:
+        copy.start()
+
+    def w_copy(j, b):
+        return pltpu.make_async_copy(w_refs[b].at[j], w.at[j, pl.ds(b * block, block)], wsem.at[j, b])
+
+    for j in range(3):
+        for b in range(grps):
+            w_copy(j, b).start()
+
+    def seq_peer(i):
+        return (p.seq + i) % slots
+
+    barrier = pltpu.get_barrier_semaphore()
+    for i in range(1, slots):
+        pl.semaphore_signal(barrier, inc=1, device_id=(p.grp, seq_peer(i)), device_id_type=MESH)
+    pl.semaphore_wait(barrier, slots - 1)
+    scatter = LineScatter(p, part, mate_in, left_in, right_in, ssend, srecv)
+
+    def a_copy(i, to, slot):
+        return remote(
+            columns_ref.at[:, to], owned.at[:, :, pl.ds(pl.multiple_of(slot * shard, shard), shard)],
+            a_send.at[i], a_recv.at[slot], p.grp, to,
+        )
+
+    for i in range(1, slots):
+        a_copy(i, seq_peer(i), p.seq).start()
+    for copy in loads:
+        copy.wait()
+    for j in range(3):
+        for b in range(grps):
+            w_copy(j, b).wait()
+
+    @pl.loop(0, chips + 1)
+    def _(order):
+        @pl.when(order < chips)
+        def _():
+            at = nearest_chip(p.chip, chips - 1 - order, chips)
+            x = tok[0, pl.ds(2 * at, 2)].reshape(2 * shard, width)
+            y = tok[1, pl.ds(2 * at, 2)].reshape(2 * shard, width)
+            gate = lax.dot_general(x, w[0], CONTRACT_LAST, preferred_element_type=jnp.float32)
+            up = lax.dot_general(x, w[1], CONTRACT_LAST, preferred_element_type=jnp.float32)
+            unit_grad = lax.dot_general(y, w[2], CONTRACT_LAST, preferred_element_type=jnp.float32)
+            sig = 1.0 / (1.0 + jnp.exp(-gate))
+            silu = gate * sig
+            rows = pl.ds(at * (2 * shard), 2 * shard)
+            gate_grad = (unit_grad * up * sig * (1.0 + gate * (1.0 - sig))).astype(jnp.bfloat16)
+            up_grad = (unit_grad * silu).astype(jnp.bfloat16)
+            acts[0, rows] = gate_grad
+            acts[1, rows] = up_grad
+            acts[2, rows] = (silu * up).astype(jnp.bfloat16)
+            back = jnp.dot(gate_grad, w[0], preferred_element_type=jnp.float32) + jnp.dot(
+                up_grad, w[1], preferred_element_type=jnp.float32
+            )
+            part[0, pl.ds(2 * at, 2)] = back.astype(jnp.bfloat16).reshape(2, shard, width)
+            scatter.to_mate(0, at).start()
+
+        pl.when(order > 0)(lambda: scatter.step(0, nearest_chip(p.chip, chips - order, chips)))
+
+    def out_copy(t):
+        return pltpu.make_async_copy(
+            stage.at[t % 2],
+            grads_ref.at[t // row_tiles, pl.ds((t % row_tiles) * tile, tile)],
+            osem.at[t % 2],
+        )
+
+    @pl.loop(0, 3 * row_tiles)
+    def _(t):
+        @pl.when(t < chips)
+        def _():
+            at = nearest_chip(p.chip, chips - 1 - t, chips)
+            h = acts[2, pl.ds(at * (2 * shard), 2 * shard)]
+            part[1, pl.ds(2 * at, 2)] = (
+                jnp.dot(h, w[2], preferred_element_type=jnp.float32)
+                .astype(jnp.bfloat16).reshape(2, shard, width)
+            )
+            scatter.to_mate(1, at).start()
+
+        @pl.when((t > 0) & (t <= chips))
+        def _():
+            scatter.step(1, nearest_chip(p.chip, chips - t, chips))
+
+        @pl.when(t >= 2)
+        def _():
+            out_copy(t - 2).wait()
+
+        kind = t // row_tiles
+        lhs = acts[kind, :, pl.ds(pl.multiple_of((t % row_tiles) * tile, 128), tile)]
+        rhs = tok[kind // 2].reshape(2 * chips * shard, width)
+        stage[t % 2] = lax.dot_general(
+            lhs, rhs, CONTRACT_FIRST, preferred_element_type=jnp.float32
+        ).astype(jnp.bfloat16)
+        out_copy(t).start()
+
+    scatter.finish(0, n2g_ref)
+    for i in range(1, slots):
+        a_copy(i, seq_peer(i), seq_peer(i)).wait_recv()
+    moved = pltpu.make_async_copy(owned, owned_ref, lsem.at[0])
+    moved.start()
+    scatter.finish(1, outp_ref)
+    out_copy(3 * row_tiles - 2).wait()
+    out_copy(3 * row_tiles - 1).wait()
+    moved.wait()
+    scatter.drain(0)
+    scatter.drain(1)
+    for i in range(1, slots):
+        a_copy(i, seq_peer(i), p.seq).wait_send()
+
+
+def mlp_call(n2_all, cot_all, columns, w_blocks, row_tiles=3):
+    grps, (_, block, width) = len(w_blocks), w_blocks[0].shape
+    slots, shard, _ = cot_all.shape
+    chips = slots // 2
+    units = grps * block
+    vm, anyspace = pltpu.VMEM, pl.BlockSpec(memory_space=pl.ANY)
+    vspec = pl.BlockSpec(memory_space=pltpu.VMEM)
+    dma = pltpu.SemaphoreType.DMA
+    owned_shape = columns.shape[:1] + columns.shape[2:3] + (slots * shard,)
+    return pl.pallas_call(
+        functools.partial(mlp_kernel, chips, grps, row_tiles),
+        out_shape=(
+            jax.ShapeDtypeStruct((shard, width), jnp.float32),
+            jax.ShapeDtypeStruct((shard, width), jnp.float32),
+            jax.ShapeDtypeStruct((3, units, width), jnp.bfloat16),
+            jax.ShapeDtypeStruct(owned_shape, jnp.bfloat16),
+        ),
+        in_specs=[anyspace] * (3 + grps),
+        out_specs=(vspec, vspec, anyspace, anyspace),
+        scratch_shapes=[
+            vm((2, slots, shard, width), jnp.bfloat16),
+            vm((3, units, width), jnp.bfloat16),
+            vm((3, slots * shard, units), jnp.bfloat16),
+            vm((2, slots, shard, width), jnp.bfloat16),
+            vm((2, chips, shard, width), jnp.bfloat16),
+            vm((2, chips, shard, width), jnp.bfloat16),
+            vm((2, chips, shard, width), jnp.bfloat16),
+            vm((2, units // row_tiles, width), jnp.bfloat16),
+            vm(owned_shape, jnp.bfloat16),
+            dma((3,)), dma((3, 2, chips)), dma((3, 2, chips)),
+            dma((3, grps)), dma((2,)), dma((slots,)), dma((slots,)),
+        ],
+        compiler_params=pltpu.CompilerParams(
+            collective_id=1, has_side_effects=True, vmem_limit_bytes=62 * 2**20
+        ),
+        name="mlp",
+    )(n2_all, cot_all, columns, *w_blocks)
 
 
 def unturn(rows, cosine, sine, half):
@@ -745,12 +739,12 @@
 
 def back_kernel(chips, scale,
                 n2g_ref, state_ref, cot_ref, tokens_ref, gains_ref, attn_ref, q_ref, kv_ref, mask_ref,
-                cos_ref, sin_ref, wq_ref, wo_ref, n1_ref, terms_ref,
+                cos_ref, sin_ref, wq_ref, wo_ref, n1_ref, terms_ref, owned_ref,
                 tok_grad_ref, wq_grad_ref, wo_grad_ref, gain_ref, mlp_ref,
-                wo, stbuf, n1x, at_stage, at_all, dq_stage, gq_in, kv_part, km_in, k_sum, k_own, kr_in,
+                wo, stbuf, n1x, at_all, dq_stage, gq_in, kv_part, km_in, k_sum, k_own, kr_in,
                 cols, part, left_in, right_in, wgrad, wm_in, w_send_buf, w_in, o_terms, o_send_buf, o_in,
                 m_own, m_in, gain_own, gain_in, gain_mid, gain_mid_in, state_grad,
-                lsem, s_send, s_recv, a_send, a_recv, q_send, q_recv, km_send, km_recv, kr_send, kr_recv,
+                lsem, s_send, s_recv, q_send, q_recv, km_send, km_recv, kr_send, kr_recv,
                 r_send, r_recv, wm_send, wm_recv, w_send, w_recv, o_send, o_recv, m_send, m_recv,
                 ml_sem, g_send, g_recv, h_send, h_recv):
     p = Place(chips)
@@ -767,6 +761,7 @@
     loads = [
         pltpu.make_async_copy(wo_ref, wo, lsem.at[0]),
         pltpu.make_async_copy(n1_ref.at[:, p.core], n1x.at[:, :, pl.ds(0, width)], lsem.at[1]),
+        pltpu.make_async_copy(owned_ref, at_all, lsem.at[2]),
     ]
     for copy in loads:
         copy.start()
@@ -820,25 +815,6 @@
 
     attn = attn_ref[...]
     unit = wo.shape[0] // (grps * slots)
-    at_rows = attn.astype(low).T
-    at_stage[...] = at_rows.reshape(grps, slots, unit, shard)
-
-    def at_copy(i, to):
-        return remote(
-            at_stage.at[:, to], at_all.at[:, :, pl.ds(pl.multiple_of(p.seq * shard, shard), shard)],
-            a_send.at[i], a_recv.at[p.seq], p.grp, to,
-        )
-
-    def at_arrival(slot):
-        return remote(
-            at_stage.at[:, slot], at_all.at[:, :, pl.ds(pl.multiple_of(slot * shard, shard), shard)],
-            a_send.at[0], a_recv.at[slot], p.grp, p.mate,
-        )
-
-    for i in range(1, slots):
-        at_copy(i, seq_peer(i)).start()
-    at_all[:, :, pl.ds(pl.multiple_of(p.seq * shard, shard), shard)] = at_stage[:, p.seq]
-
     loads[0].wait()
     attn_grad = lax.dot_general(state_low, wo[...], CONTRACT_LAST, preferred_element_type=wide).astype(low)
     line.forward(1)
@@ -919,8 +895,7 @@
     n1x[:, :, width:] = jnp.where(lane == 0, 1.0, 0.0).astype(low)
     for chip in range(chips):
         line.wait_mate(chip)
-    for i in range(1, slots):
-        at_arrival(seq_peer(i)).wait_recv()
+    loads[2].wait()
     o_terms[...] = jnp.dot(
         at_all[...].reshape(grps * unit, slots * shard), stbuf[...].reshape(slots * shard, width),
         preferred_element_type=wide,
@@ -1096,7 +1071,6 @@
     line.drain()
     wm.wait_send()
     for i in range(1, slots):
-        at_copy(i, seq_peer(i)).wait_send()
         g_copy(i).wait_send()
     for b in range(1, grps):
         o_copy(b).wait_send()
@@ -1115,7 +1089,7 @@
 
 
 def back_call(n2g, state, cotangent, tokens, gains, attn, q_heads, kv_heads, mask, cosine, sine,
-              qkv_all, out_full, n1_all, terms):
+              qkv_all, out_full, n1_all, terms, owned):
     chips = cosine.shape[0]
     grps = 4
     slots = 2 * chips
@@ -1136,13 +1110,12 @@
             struct((2, 1, width), wide),
             struct((3, block, width), wide),
         ),
-        in_specs=[vspec] * 12 + [anyspace] * 3,
+        in_specs=[vspec] * 12 + [anyspace] * 4,
         out_specs=(vspec,) * 5,
         scratch_shapes=[
             vm((att, width), low),
             vm((chips, 2, shard, width), low),
             vm((chips, shard, width + HD), low),
-            vm((grps, slots, unit, shard), low),
             vm((grps, unit, slots * shard), low),
             vm((chips, 3, shard, HD), low),
             vm((chips, 3, shard, HD), low),
@@ -1169,9 +1142,8 @@
             vm((2, 1, width), wide),
             vm((grps, 2, 1, width), wide),
             vm((shard, width), wide),
-            dma((2,)),
+            dma((3,)),
             dma((3, chips)), dma((chips, 2)),
-            dma((slots,)), dma((slots,)),
             dma((chips,)), dma((chips,)),
             dma((chips,)), dma((chips,)),
             dma((chips,)), dma((chips,)),
@@ -1189,7 +1161,7 @@
         ),
         name="back",
     )(n2g, state, cotangent, tokens, gains, attn, q_heads, kv_heads, mask, cosine, sine,
-      qkv_all, out_full, n1_all, terms)
+      qkv_all, out_full, n1_all, terms, owned)
 
 
 def columns_to_owners(rows, row_unit):
@@ -1260,23 +1232,6 @@
 def padded_rows(mlp_weight):
     rows = mlp_weight.transpose(1, 0, 2)
     return jnp.pad(rows, ((0, 0), (0, -rows.shape[1] % 32), (0, 0)))
-
-
-def from_peer(values, offset, grp_count):
-    return lax.ppermute(values, "grp", [(g, g ^ offset) for g in range(grp_count)])
-
-
-def exchange_blocks(rows, grp_count):
-    return [rows] + [from_peer(rows, offset, grp_count) for offset in range(1, grp_count)]
-
-
-def sum_blocks(terms, grp_count):
-    block = terms.shape[1] // grp_count
-    total = terms[:, :block].astype(jnp.float32)
-    for offset in range(1, grp_count):
-        piece = terms[:, offset * block : (offset + 1) * block]
-        total = total + from_peer(piece, offset, grp_count).astype(jnp.float32)
-    return total
 
 
 def per_device(
@@ -1334,135 +1289,22 @@
         bias_row = jnp.where(seq_place % 2 == 0, bias_pair, jnp.roll(bias_pair, HD // 2))
         bias_rows8 = jnp.broadcast_to(bias_row[None, :], (8, HD))
         own_rows = padded_rows(mlp_weight)
+        gains = jnp.stack([gain_one, gain_two])[:, None, :]
         (
-            attn_wide, lse, q_heads, kv_heads, n1_all, cot_all, out_all, qkv_all, *peer_rows
+            attn_wide, state, q_heads, kv_heads, n1_all, n2_all, cot_all, out_all, qkv_all, columns, *peer_rows
         ) = front_call(
-            normed_one, cotangent, qkv_weight, bias_rows8, out_weight, own_rows,
+            tokens, gains, cotangent, qkv_weight, bias_rows8, out_weight, own_rows,
             by_shard(all_cosine), by_shard(all_sine), mask,
         )
-        mlp_blocks = [own_rows, *peer_rows]
-        normed_one_all = n1_all.reshape(group_tok, -1)
-        cotangent_all = cot_all.reshape(group_tok, -1)
-        out_full = out_all.reshape(att_width, -1)
-        query_rot = q_heads.transpose(2, 1, 0, 3).reshape(tok_rows, H, HD)
-        kv_rows = kv_heads.reshape(2, KVH, 2, chips, tok_rows, HD).transpose(0, 3, 2, 4, 1, 5)
-        keys_all, values_all = kv_rows.reshape(2, group_tok, kv_width)
-    else:
-        normed_one_all = lax.all_gather(normed_one, "seq", axis=0, tiled=True)
-        qkv_rows = lax.all_gather(qkv_weight, "grp", axis=0, tiled=True)
-        bias_rows = lax.all_gather(qkv_bias, "grp", axis=0, tiled=True)
-        cotangent_all = lax.all_gather(cotangent, "seq", axis=0, tiled=True)
-        out_full = lax.all_gather(out_weight, AXES, axis=0, tiled=True)
-        projected = lax.dot_general(
-            normed_one_all, qkv_rows, contract_last, preferred_element_type=jnp.float32
-        )
-        projected = (projected + bias_rows.astype(jnp.float32)[None, :]).astype(jnp.bfloat16)
-        projected = owners_to_columns(projected, qkv_weight.shape[0]).astype(jnp.float32)
-        query_rot = rotate(
-            projected[:, :att_width].reshape(tok_rows, H, HD), cosine_table, sine_table
-        ).astype(jnp.bfloat16)
-        key_rot = rotate(
-            projected[:, att_width : att_width + kv_width].reshape(tok_rows, KVH, HD),
-            cosine_table,
-            sine_table,
-        ).astype(jnp.bfloat16)
-        value_low = projected[:, att_width + kv_width :].astype(jnp.bfloat16)
-        keys_all, values_all = (
-            lax.all_gather(key_rot.reshape(tok_rows, kv_width), "seq", axis=0, tiled=True),
-            lax.all_gather(value_low, "seq", axis=0, tiled=True),
-        )
-    queries = (
-        query_rot.reshape(tok_rows, KVH, heads_per, HD)
-        .transpose(1, 2, 0, 3)
-        .reshape(KVH, query_rows, HD)
-    )
-    key_block = min(512, group_tok)
-    block_count = group_tok // key_block
-    block_order = jnp.arange(block_count, dtype=jnp.int32)
-
-    def block_mask(block_index):
-        key_index = block_index * key_block + jnp.arange(key_block, dtype=jnp.int32)
-        key_shard = key_index // tok_rows
-        onehot = key_shard[:, None] == shard_order[None, :]
-        key_seg = jnp.sum(jnp.where(onehot, segments[None, :], 0), axis=1)
-        key_pos = jnp.sum(jnp.where(onehot, starts[None, :], 0), axis=1) + key_index % tok_rows
-        visible = (key_seg == 0) | (key_seg == own_seg)
-        return visible[None, :] & (key_pos[None, :] <= query_pos[:, None])
-
-    def block_keys(block_index):
-        key_part = lax.dynamic_slice_in_dim(
-            keys_all, block_index * key_block, key_block, 0
-        ).reshape(key_block, KVH, HD)
-        value_part = lax.dynamic_slice_in_dim(
-            values_all, block_index * key_block, key_block, 0
-        ).reshape(key_block, KVH, HD)
-        return (key_part, value_part)
-
-    def block_scores(key_part):
-        return (
-            jnp.einsum("krd,jkd->krj", queries, key_part, preferred_element_type=jnp.float32)
-            * score_scale
-        )
-
-    if use_kernels:
-        log_total = lse[:, :, 0]
-    else:
-        def stat_step(stats_now, block_index):
-            allowed = block_mask(block_index)
-
-            def stat_visit(current):
-                top_old, total_old = current
-                key_part, value_part = block_keys(block_index)
-                scores = jnp.where(allowed[None], block_scores(key_part), -1e30)
-                top_new = jnp.maximum(top_old, jnp.max(scores, axis=-1))
-                weights = jnp.where(allowed[None], jnp.exp(scores - top_new[..., None]), 0.0)
-                return (top_new, total_old * jnp.exp(top_old - top_new) + jnp.sum(weights, axis=-1))
-
-            return (lax.cond(jnp.any(allowed), stat_visit, lambda current: current, stats_now), None)
-
-        start_stats = (
-            jnp.full((KVH, query_rows), -1e30, jnp.float32),
-            jnp.zeros((KVH, query_rows), jnp.float32),
-        )
-        (top_all, total_all), unused = lax.scan(stat_step, start_stats, block_order)
-        log_total = top_all + jnp.log(total_all)
-
-        def mix_step(mixed_sum, block_index):
-            allowed = block_mask(block_index)
-
-            def mix_visit(current):
-                key_part, value_part = block_keys(block_index)
-                prob_low = jnp.where(
-                    allowed[None], jnp.exp(block_scores(key_part) - log_total[..., None]), 0.0
-                ).astype(jnp.bfloat16)
-                return current + jnp.einsum(
-                    "krj,jkd->krd", prob_low, value_part, preferred_element_type=jnp.float32
-                )
-
-            return (lax.cond(jnp.any(allowed), mix_visit, lambda current: current, mixed_sum), None)
-
-        mixed_sum, unused = lax.scan(
-            mix_step, jnp.zeros((KVH, query_rows, HD), jnp.float32), block_order
-        )
-        attn_wide = (
-            mixed_sum.reshape(KVH, heads_per, tok_rows, HD)
-            .transpose(2, 0, 1, 3)
-            .reshape(tok_rows, att_width)
-        )
-    attn_low = attn_wide.astype(jnp.bfloat16)
-    attn_proj = jnp.dot(attn_low, out_full, preferred_element_type=jnp.float32)
-    state = tokens_wide + attn_proj
-    normed_two = rms_scale(state, gain_two).astype(jnp.bfloat16)
-    if use_kernels:
-        grad_part, out_part, mlp_terms = mlp_call(
-            normed_two, cotangent_all.reshape(seq_count, tok_rows, -1), mlp_blocks
+        by_slot = lambda rows: rows.reshape((seq_count,) + rows.shape[2:])
+        grad_part, out_part, mlp_terms, owned = mlp_call(
+            by_slot(n2_all), by_slot(cot_all), columns, [own_rows, *peer_rows]
         )
         output = (state + out_part).astype(jnp.bfloat16)
-        gains = jnp.stack([gain_one, gain_two])[:, None, :]
         token_grad, qkv_terms, out_grad, gain_sums, mlp_sums = back_call(
             grad_part, state, cotangent, tokens, gains, attn_wide, q_heads, kv_heads, mask,
             by_shard(all_cosine), by_shard(all_sine), qkv_all.reshape(-1, qkv_all.shape[-1]),
-            out_full, n1_all, mlp_terms,
+            out_all.reshape(att_width, -1), n1_all, mlp_terms, owned,
         )
         width = tokens.shape[1]
         own = width // (grp_count * seq_count)
@@ -1479,6 +1321,108 @@
             gain_parts[1],
             mlp_sums[:, : mlp_weight.shape[0]].transpose(1, 0, 2),
         )
+    normed_one_all = lax.all_gather(normed_one, "seq", axis=0, tiled=True)
+    qkv_rows = lax.all_gather(qkv_weight, "grp", axis=0, tiled=True)
+    bias_rows = lax.all_gather(qkv_bias, "grp", axis=0, tiled=True)
+    cotangent_all = lax.all_gather(cotangent, "seq", axis=0, tiled=True)
+    out_full = lax.all_gather(out_weight, AXES, axis=0, tiled=True)
+    projected = lax.dot_general(
+        normed_one_all, qkv_rows, contract_last, preferred_element_type=jnp.float32
+    )
+    projected = (projected + bias_rows.astype(jnp.float32)[None, :]).astype(jnp.bfloat16)
+    projected = owners_to_columns(projected, qkv_weight.shape[0]).astype(jnp.float32)
+    query_rot = rotate(
+        projected[:, :att_width].reshape(tok_rows, H, HD), cosine_table, sine_table
+    ).astype(jnp.bfloat16)
+    key_rot = rotate(
+        projected[:, att_width : att_width + kv_width].reshape(tok_rows, KVH, HD),
+        cosine_table,
+        sine_table,
+    ).astype(jnp.bfloat16)
+    value_low = projected[:, att_width + kv_width :].astype(jnp.bfloat16)
+    keys_all, values_all = (
+        lax.all_gather(key_rot.reshape(tok_rows, kv_width), "seq", axis=0, tiled=True),
+        lax.all_gather(value_low, "seq", axis=0, tiled=True),
+    )
+    queries = (
+        query_rot.reshape(tok_rows, KVH, heads_per, HD)
+        .transpose(1, 2, 0, 3)
+        .reshape(KVH, query_rows, HD)
+    )
+    key_block = min(512, group_tok)
+    block_count = group_tok // key_block
+    block_order = jnp.arange(block_count, dtype=jnp.int32)
+
+    def block_mask(block_index):
+        key_index = block_index * key_block + jnp.arange(key_block, dtype=jnp.int32)
+        key_shard = key_index // tok_rows
+        onehot = key_shard[:, None] == shard_order[None, :]
+        key_seg = jnp.sum(jnp.where(onehot, segments[None, :], 0), axis=1)
+        key_pos = jnp.sum(jnp.where(onehot, starts[None, :], 0), axis=1) + key_index % tok_rows
+        visible = (key_seg == 0) | (key_seg == own_seg)
+        return visible[None, :] & (key_pos[None, :] <= query_pos[:, None])
+
+    def block_keys(block_index):
+        key_part = lax.dynamic_slice_in_dim(
+            keys_all, block_index * key_block, key_block, 0
+        ).reshape(key_block, KVH, HD)
+        value_part = lax.dynamic_slice_in_dim(
+            values_all, block_index * key_block, key_block, 0
+        ).reshape(key_block, KVH, HD)
+        return (key_part, value_part)
+
+    def block_scores(key_part):
+        return (
+            jnp.einsum("krd,jkd->krj", queries, key_part, preferred_element_type=jnp.float32)
+            * score_scale
+        )
+
+    def stat_step(stats_now, block_index):
+        allowed = block_mask(block_index)
+
+        def stat_visit(current):
+            top_old, total_old = current
+            key_part, value_part = block_keys(block_index)
+            scores = jnp.where(allowed[None], block_scores(key_part), -1e30)
+            top_new = jnp.maximum(top_old, jnp.max(scores, axis=-1))
+            weights = jnp.where(allowed[None], jnp.exp(scores - top_new[..., None]), 0.0)
+            return (top_new, total_old * jnp.exp(top_old - top_new) + jnp.sum(weights, axis=-1))
+
+        return (lax.cond(jnp.any(allowed), stat_visit, lambda current: current, stats_now), None)
+
+    start_stats = (
+        jnp.full((KVH, query_rows), -1e30, jnp.float32),
+        jnp.zeros((KVH, query_rows), jnp.float32),
+    )
+    (top_all, total_all), unused = lax.scan(stat_step, start_stats, block_order)
+    log_total = top_all + jnp.log(total_all)
+
+    def mix_step(mixed_sum, block_index):
+        allowed = block_mask(block_index)
+
+        def mix_visit(current):
+            key_part, value_part = block_keys(block_index)
+            prob_low = jnp.where(
+                allowed[None], jnp.exp(block_scores(key_part) - log_total[..., None]), 0.0
+            ).astype(jnp.bfloat16)
+            return current + jnp.einsum(
+                "krj,jkd->krd", prob_low, value_part, preferred_element_type=jnp.float32
+            )
+
+        return (lax.cond(jnp.any(allowed), mix_visit, lambda current: current, mixed_sum), None)
+
+    mixed_sum, unused = lax.scan(
+        mix_step, jnp.zeros((KVH, query_rows, HD), jnp.float32), block_order
+    )
+    attn_wide = (
+        mixed_sum.reshape(KVH, heads_per, tok_rows, HD)
+        .transpose(2, 0, 1, 3)
+        .reshape(tok_rows, att_width)
+    )
+    attn_low = attn_wide.astype(jnp.bfloat16)
+    attn_proj = jnp.dot(attn_low, out_full, preferred_element_type=jnp.float32)
+    state = tokens_wide + attn_proj
+    normed_two = rms_scale(state, gain_two).astype(jnp.bfloat16)
     grad_part, out_part, mlp_grad = plain_mlp(normed_two, cotangent_all, mlp_weight)
     output = (state + out_part).astype(jnp.bfloat16)
     unused_state, norm_two_back = jax.vjp(rms_scale, state, gain_two)

time: 425 us -> 386 us (0.908)
  Pallas kernels: 395 us -> 358 us
    pallas_call x1, Pallas kernels: 125 us -> 84.1 us  [mlp_call(): pl.pallas_call(functools.partial(mlp_kernel, chips, grps, row_tiles), out...]
    pallas_call x1, Pallas kernels: 130 us -> 141 us  [front_call(): pl.pallas_call(functools.partial(front_kernel, chips, 1.0 / math.sqrt(HD)...]
    pallas_call x1, Pallas kernels: 139 us -> 133 us  [back_call(): pl.pallas_call(functools.partial(back_kernel, chips, 1.0 / math.sqrt(HD))...]
where the time goes in v5:
time: 386 us; the launch traced here: 385 us
  Pallas kernels  358 us (93%)
  local copies, waits for them, and re-layouts  16.9 us (4%)
  other arithmetic  9.56 us (2%)
    pallas_call x1, Pallas kernels, front_call(): pl.pallas_call(functools.partial(front_kernel, chips, 1.0 / math.sqrt(HD)...  141 us
    pallas_call x1, Pallas kernels, back_call(): pl.pallas_call(functools.partial(back_kernel, chips, 1.0 / math.sqrt(HD))...  133 us
    pallas_call x1, Pallas kernels, mlp_call(): pl.pallas_call(functools.partial(mlp_kernel, chips, grps, row_tiles), out...  84.1 us

profile of v5, /device:TPU:9, one launch (start us, length us, event | category | flops | bytes accessed | tf_op | source)
XLA Modules:
  0.0 385.1 jit_solution(12076329916406136113)
XLA Ops:
  0.7 0.8 convert_element_type.19
  1.5 0.1 broadcast_select_fusion
  1.5 0.7 fusion.4
  2.2 0.2 select_reduce_fusion
  2.4 1.3 fusion.2
  3.8 1.4 compare_reduce_fusion
  5.1 0.1 eq.79
  5.2 0.1 eq.71
  5.3 0.1 copy.21
  5.4 0.1 or.19
  5.5 0.1 broadcast_bitcast_fusion
  5.6 0.7 iota_add_fusion.1
  6.2 0.1 reduce_min.12
  6.3 0.1 copy.22
  6.5 0.6 broadcast_in_dim.53.bias_ref
  7.2 0.7 stack.12
  7.9 0.7 stack.13
  8.6 0.6 reshape.186.gains_ref
  9.2 1.0 and_select_fusion.mask_ref
  10.2 1.9 multiply_sine_fusion
  12.0 1.3 negate_select_fusion
  13.3 1.7 pad.6.wm_ref.refs_0_
  15.1 140.8 %front.1 = (f32[128,1536]{1,0:T(8,128)}, f32[128,1536]{1,0:T(8,128)}, bf16[4,3,128,128]{3,2,1,0:T(8,128)(2,1)}, bf16[4,2,4,128,128]{4,3,2,1,0:T(8,128)(2,1)}, bf...) custom-call(bf16[128,1536]{1,0:T(8,128)(2,1)} %tokens_ref.3, ...), custom_call_target="tpu_custom_call" | custom-call | tf_op jit(solution)/shard_map/front/pallas_call | solution.py:526
  155.9 84.1 %mlp.1 = (f32[128,1536]{1,0:T(8,128)}, f32[128,1536]{1,0:T(8,128)}, bf16[3,1152,1536]{2,1,0:T(8,128)(2,1)}, bf16[4,48,1024]{2,1,0:T(8,128)(2,1)}) custom-call(bf16[8,128,1536]{2,1,0:T(8,128)(2,1)} %bitcast.22, bf16[8,128,1536]{2,1,0:T(8,128)(2,1)} %bitcast.23, bf16[4,8,48,128]{3,2,1,0:T(8,128)(2,1)} %get-tuple-element.33.columns_ref, ...), custom_call_target="tpu_custom_call" | custom-call | tf_op jit(solution)/shard_map/mlp/pallas_call | solution.py:706
  240.0 133.0 %back.1 = (f32[128,1536]{1,0:T(8,128)}, f32[64,1664]{1,0:T(8,128)}, f32[48,1536]{1,0:T(8,128)}, f32[2,1,1536]{2,1,0:T(1,128)}, f32[3,288,1536]{2,1,0:T(8,128)}) custom-call(f32[128,1536]{1,0:T(8,128)} %get-tuple-element.38.n2g_ref, f32[128,1536]{1,0:T(8,128)} %get-tuple-element.30.state_ref, bf16[128,1536]{1,0:T(8,128)(2,1)} %cot_ref.3, ...), custom_call_target="tpu_custom_call" | custom-call | tf_op jit(solution)/shard_map/back/pallas_call | solution.py:1104
  373.0 0.8 add_convert_fusion
  373.9 1.2 fusion
  375.1 1.4 slice_reduce_fusion
  376.5 1.8 slice.22
  378.2 5.2 %slice_bitcast_fusion = f32[280,3,1536]{2,0,1:T(8,128)} fusion(f32[3,288,1536]{2,1,0:T(8,128)} %get-tuple-element.51), kind=kLoop, calls=%fused_computation | loop fusion | bytes 10321920 | tf_op jit(solution)/shard_map/transpose | solution.py:1322
  383.5 0.9 copy.25
  384.4 0.7 copy.26
  (17 shorter events, 0.2 us)
Async XLA Ops:
  0.6 12.7 %copy-start.1 = (bf16[280,3,1536]{2,0,1:T(8,128)(2,1)S(1)}, bf16[280,3,1536]{2,0,1:T(8,128)(2,1)}, u32[]{:S(2)}) copy-start(bf16[280,3,1536]{2,0,1:T(8,128)(2,1)} %param.17) | copy-start | bytes 7741444
  240.0 133.1 %copy-start = (f32[128,1536]{1,0:T(8,128)S(1)}, f32[128,1536]{1,0:T(8,128)}, u32[]{:S(2)}) copy-start(f32[128,1536]{1,0:T(8,128)} %get-tuple-element.30.state_ref) | copy-start | bytes 2359300
  240.0 133.1 %copy-start.3 = (f32[128,1536]{1,0:T(8,128)S(1)}, f32[128,1536]{1,0:T(8,128)}, u32[]{:S(2)}) copy-start(f32[128,1536]{1,0:T(8,128)} %get-tuple-element.37) | copy-start | bytes 2359300
  378.2 5.2 %copy-start.2 = (f32[128,1536]{1,0:T(8,128)S(1)}, f32[128,1536]{1,0:T(8,128)}, u32[]{:S(2)}) copy-start(f32[128,1536]{1,0:T(8,128)} %get-tuple-element.71) | copy-start | bytes 2359300
  378.2 6.1 %copy-start.4 = (f32[48,1536]{1,0:T(8,128)S(1)}, f32[48,1536]{1,0:T(8,128)}, u32[]{:S(2)}) copy-start(f32[48,1536]{1,0:T(8,128)} %get-tuple-element.75) | copy-start | bytes 884740

commit v6 on v5

--- a/solution.py
+++ b/solution.py
@@ -240,10 +240,11 @@
 
 
 def front_kernel(chips, scale,
-                 tokens_ref, gains_ref, cot_ref, wq_ref, bias_ref, wo_ref, wm_ref, cos_ref, sin_ref, mask_ref,
-                 attn_ref, state_ref, q_out_ref, kv_out_ref, n1_all_ref, n2_all_ref, cot_all_ref, wo_all_ref,
-                 wq_all_ref, columns_ref, wm1_ref, wm2_ref, wm3_ref,
-                 nbuf, n2buf, wq, wo, bias, stage, qbuf, kvbuf, columns,
+                 tokens_ref, gain_one_ref, gain_two_ref, segment_ref, freq_ref, bias_ref,
+                 cot_ref, wq_ref, wo_ref, wm_ref,
+                 attn_ref, state_ref, cos_ref, sin_ref, mask_ref, q_out_ref, kv_out_ref, n1_all_ref, n2_all_ref,
+                 cot_all_ref, wo_all_ref, wq_all_ref, columns_ref, wm1_ref, wm2_ref, wm3_ref,
+                 nbuf, n2buf, wq, wo, bias_own, bias, stage, qbuf, kvbuf, columns,
                  lsem, n_send, n_recv, n2_send, n2_recv, c_send, c_recv, o_send, o_recv, ox_send, ox_recv,
                  om_send, om_recv, wq_send, wq_recv, b_send, b_recv, m_send, m_recv, q_send, q_recv, k_send, k_recv):
     p = Place(chips)
@@ -256,14 +257,19 @@
 
     own = [
         pltpu.make_async_copy(wq_ref, wq.at[0, rows], lsem.at[0]),
-        pltpu.make_async_copy(bias_ref, bias.at[0, p.core], lsem.at[1]),
         pltpu.make_async_copy(wo_ref, wo.at[p.grp, p.chip, p.core], lsem.at[2]),
         pltpu.make_async_copy(cot_ref, cot_all_ref.at[p.chip, p.core], lsem.at[3]),
     ]
     for copy in own:
         copy.start()
     tokens = tokens_ref[...].astype(jnp.float32)
-    nbuf[p.chip, p.core] = rms_scale(tokens, gains_ref[0]).astype(jnp.bfloat16)
+    nbuf[p.chip, p.core] = rms_scale(tokens, gain_one_ref[...].astype(jnp.float32)).astype(jnp.bfloat16)
+    shard = tokens.shape[0]
+    lane = lax.broadcasted_iota(jnp.int32, (1, 2 * half), 1)
+    bias_wide = bias_ref[...].astype(jnp.float32)
+    bias_pair = jnp.concatenate([bias_wide, bias_wide], axis=1)
+    bias_own[...] = jnp.broadcast_to(jnp.where(lane // half == p.core, bias_pair, 0.0), bias_own.shape)
+    bias[0, p.core] = bias_own[...]
     p.barrier(grps)
 
     n1_line = RailGather(p, lambda chip, core: nbuf.at[chip, core], n_send, n_recv)
@@ -278,21 +284,24 @@
         return remote(wq.at[b, rows], wq.at[b, rows], wq_send.at[1, b], wq_recv.at[b, 1], p.grp, p.mate)
 
     def bias_direct(b):
-        return remote(bias_ref, bias.at[b, p.core], b_send.at[0, b], b_recv.at[b, 0], p.peer(b), p.seq)
+        return remote(bias_own, bias.at[b, p.core], b_send.at[0, b], b_recv.at[b, 0], p.peer(b), p.seq)
 
     def bias_mate(b):
         return remote(bias.at[b, p.core], bias.at[b, p.core], b_send.at[1, b], b_recv.at[b, 1], p.grp, p.mate)
 
-    def m_half(ref, i):
-        return ref.at[:, pl.ds(i * part, part)]
-
-    def m_direct(b, i):
-        return remote(m_half(wm_ref, i), m_half(wm_refs[b], i), m_send.at[b, i], m_recv.at[b, i], p.peer(b), p.seq)
-
-    def m_forward(b):
+    def m_part(ref, i, j):
+        return ref.at[j, pl.ds(i * part, part)]
+
+    def m_direct(b, i, j):
         return remote(
-            m_half(wm_refs[b], b - 1), m_half(wm3_ref, b - 1), m_send.at[3, b - 1], m_recv.at[3, b - 1],
-            p.peer(3 - b), p.seq,
+            m_part(wm_ref, i, j), m_part(wm_refs[b], i, j), m_send.at[b, i, j], m_recv.at[b, i, j],
+            p.peer(b), p.seq,
+        )
+
+    def m_forward(b, j):
+        return remote(
+            m_part(wm_refs[b], b - 1, j), m_part(wm3_ref, b - 1, j), m_send.at[3, b - 1, j],
+            m_recv.at[3, b - 1, j], p.peer(3 - b), p.seq,
         )
 
     def out_view(grp, i, core):
@@ -336,23 +345,59 @@
         view = kvbuf.at[head, core, chip]
         return remote(view, view, k_send.at[1, head, chip], k_recv.at[head, core, chip], p.grp, p.mate)
 
+    def make_tables():
+        segs = [segment_ref[p.grp, t] for t in range(2 * chips)]
+        starts = []
+        for t in range(2 * chips):
+            first = jnp.int32(t)
+            for other in reversed(range(t)):
+                first = jnp.where(segs[other] == segs[t], jnp.int32(other), first)
+            starts.append(
+                jnp.where(segs[t] == 0, jnp.int32(t * shard), chips * shard + (t - first) * shard)
+            )
+
+        def own_of(values):
+            own = values[0]
+            for t in range(1, 2 * chips):
+                own = jnp.where(p.seq == t, values[t], own)
+            return own
+
+        own_seg, own_start = own_of(segs), own_of(starts)
+        row = lax.broadcasted_iota(jnp.int32, (shard, 2 * half), 0)
+        column = lax.broadcasted_iota(jnp.int32, (shard, 2 * half), 1)
+        freq = freq_ref[...]
+        sign = jnp.where(column < half, -1.0, 1.0)
+        for chip in range(chips):
+            start = jnp.where(p.core == 0, starts[2 * chip], starts[2 * chip + 1])
+            angle = (start + row).astype(jnp.float32) * freq
+            cos_ref[chip] = jnp.cos(angle)
+            sin_ref[chip] = jnp.sin(angle) * sign
+        for core in range(2):
+            for chip in range(chips):
+                t = 2 * chip + core
+                seen = jnp.where((segs[t] == 0) | (segs[t] == own_seg), jnp.int32(1), jnp.int32(0))
+                allowed = (starts[t] + column <= own_start + row) & (row * 0 + seen > 0)
+                block = core * chips + chip
+                mask_ref[:, block * shard : (block + 1) * shard] = jnp.where(allowed, 0.0, -1e30)
+
     own[0].wait()
-    own[1].wait()
     for b in range(1, grps):
         wq_direct(b).start()
         bias_direct(b).start()
     wq_mate(0).start()
     bias_mate(0).start()
     n1_line.start()
-    own[2].wait()
+    own[1].wait()
     out_line.start()
     for b in range(1, grps):
         wq_direct(b).wait_recv()
         wq_mate(b).start()
         bias_direct(b).wait_recv()
         bias_mate(b).start()
-    m_direct(1, 0).start()
-    m_direct(2, 1).start()
+    for j in (0, 1):
+        m_direct(1, 0, j).start()
+        m_direct(2, 1, j).start()
+    make_tables()
     for b in range(grps):
         wq_mate(b).wait_recv()
         bias_mate(b).wait_recv()
@@ -368,7 +413,7 @@
         x = nbuf[at, p.core]
         weights = wq[...].reshape(grps * 2 * half, x.shape[1])
         rows_all = lax.dot_general(x, weights, CONTRACT_LAST, preferred_element_type=jnp.float32)
-        cosine, sine = cos_ref[at, p.core], sin_ref[at, p.core]
+        cosine, sine = cos_ref[at], sin_ref[at]
         for b in range(grps):
             u = rows_all[:, 2 * half * b : 2 * half * (b + 1)] + (bias[b, 0, 0:1] + bias[b, 1, 0:1])
             turned = u * cosine + pltpu.roll(u, half, 1) * sine
@@ -394,7 +439,7 @@
         out_direct(b, b - 1).start()
     for b in (1, 2):
         out_direct(b, 2 - b).start()
-    own[3].wait()
+    own[2].wait()
     cot_line.start()
 
     @pl.loop(0, chips)
@@ -413,7 +458,6 @@
     cot_line.forward(1)
 
     mask = mask_ref[...]
-    shard = mask.shape[0]
     heads_per = H // KVH
     for kv in range(KVH):
         heads = [kv * heads_per + i for i in range(heads_per)]
@@ -433,16 +477,20 @@
                 out_direct(b, b - 1).wait_recv()
                 out_forward(b).start()
                 out_mate(b, b - 1, p.core).start()
+            for b in (1, 2):
+                for j in (0, 1):
+                    m_direct(b, b - 1, j).wait_recv()
+                    m_forward(b, j).start()
+            m_direct(1, 0, 2).start()
+            m_direct(2, 1, 2).start()
         cot_line.forward(kv + 2)
 
     for b in (1, 2):
         out_direct(b, 2 - b).wait_recv()
         out_mate(b, 2 - b, p.core).start()
-    for b in (1, 2):
-        m_direct(b, b - 1).wait_recv()
-        m_forward(b).start()
-    m_direct(1, 1).start()
-    m_direct(2, 0).start()
+    for j in range(3):
+        m_direct(1, 1, j).start()
+        m_direct(2, 0, j).start()
     attn_low = attn_ref[...].astype(jnp.bfloat16)
     unit = wo.shape[3]
     columns[...] = attn_low.T.reshape(columns.shape)
@@ -459,7 +507,7 @@
         preferred_element_type=jnp.float32,
     )
     state_ref[...] = state
-    n2buf[p.chip, p.core] = rms_scale(state, gains_ref[1]).astype(jnp.bfloat16)
+    n2buf[p.chip, p.core] = rms_scale(state, gain_two_ref[...].astype(jnp.float32)).astype(jnp.bfloat16)
     n2_line.start()
     outs = [
         pltpu.make_async_copy(nbuf, n1_all_ref, lsem.at[4]),
@@ -473,7 +521,11 @@
         n1_line.wait_mate(chip)
     for copy in outs:
         copy.start()
-    for step in range(1, chips):
+    n2_line.forward(1)
+    for b in (1, 2):
+        m_direct(b, b - 1, 2).wait_recv()
+        m_forward(b, 2).start()
+    for step in range(2, chips):
         n2_line.forward(step)
     for chip in range(chips):
         cot_line.wait_mate(chip)
@@ -481,8 +533,9 @@
     last = pltpu.make_async_copy(n2buf, n2_all_ref, lsem.at[10])
     last.start()
     for b in (1, 2):
-        m_direct(b, 2 - b).wait_recv()
-        m_forward(3 - b).wait_recv()
+        for j in range(3):
+            m_direct(b, 2 - b, j).wait_recv()
+            m_forward(3 - b, j).wait_recv()
     for copy in outs:
         copy.wait()
     last.wait()
@@ -500,9 +553,11 @@
             out_mate(b, i, p.core).wait_send()
     for b in (1, 2):
         for i in (0, 1):
-            m_direct(b, i).wait_send()
+            for j in range(3):
+                m_direct(b, i, j).wait_send()
             out_direct(b, i).wait_send()
-        m_forward(b).wait_send()
+        for j in range(3):
+            m_forward(b, j).wait_send()
         out_forward(b).wait_send()
     for chip in range(chips):
         pl.when(chip != p.chip)(lambda chip=chip: q_copy(chip).wait_send())
@@ -511,8 +566,8 @@
             k_mate(other, chip).wait_send()
 
 
-def front_call(tokens, gains, cot, qkv_weight, bias_rows, out_weight, mlp_rows, cosine, sine, mask):
-    chips = cosine.shape[0]
+def front_call(tokens, gain_one, gain_two, segments, freqs, bias, cot, qkv_weight, out_weight, mlp_rows):
+    chips = segments.shape[1] // 2
     grps = 4
     shard, width = tokens.shape
     half = qkv_weight.shape[0]
@@ -528,6 +583,9 @@
         out_shape=(
             struct((shard, H * HD), wide),
             struct((shard, width), wide),
+            struct((chips, shard, HD), wide),
+            struct((chips, shard, HD), wide),
+            struct((shard, 2 * chips * shard), wide),
             struct((chips, 3, shard, HD), low),
             struct((chips, 2, chips, shard, HD), low),
             struct((chips, 2, shard, width), low),
@@ -537,14 +595,18 @@
             struct((grps, 2 * half, width), low),
             struct(columns_shape, low),
         ) + (struct(mlp_rows.shape, low),) * 3,
-        in_specs=[vspec] * 2 + [anyspace] * 5 + [vspec] * 3,
-        out_specs=(vspec,) * 2 + (anyspace,) * 11,
+        in_specs=[vspec] * 3
+        + [pl.BlockSpec(memory_space=pltpu.SMEM)]
+        + [vspec] * 2
+        + [anyspace] * 4,
+        out_specs=(vspec,) * 5 + (anyspace,) * 11,
         scratch_shapes=[
             vm((chips, 2, shard, width), low),
             vm((chips, 2, shard, width), low),
             vm((grps, 2 * half, width), low),
             vm(wo_shape, low),
-            vm((grps, 2) + bias_rows.shape, wide),
+            vm((8, HD), wide),
+            vm((grps, 2, 8, HD), wide),
             vm((chips, grps, shard, HD), low),
             vm((chips, 3, shard, HD), low),
             vm((chips, 2, chips, shard, HD), low),
@@ -557,7 +619,7 @@
             dma((grps, 2)), dma((grps, 2)), dma((grps, 2)), dma((grps, 2)),
             dma((2, grps)), dma((grps, 2)),
             dma((2, grps)), dma((grps, 2)),
-            dma((grps, 2)), dma((grps, 2)),
+            dma((grps, 2, 3)), dma((grps, 2, 3)),
             dma((chips,)), dma((chips,)),
             dma((2, chips, chips)), dma((chips, 2, chips)),
         ],
@@ -565,7 +627,7 @@
             collective_id=2, has_side_effects=True, vmem_limit_bytes=60 * 2**20
         ),
         name="front",
-    )(tokens, gains, cot, qkv_weight, bias_rows, out_weight, mlp_rows, cosine, sine, mask)
+    )(tokens, gain_one, gain_two, segments, freqs, bias, cot, qkv_weight, out_weight, mlp_rows)
 
 
 def mlp_kernel(chips, grps, row_tiles, n2_ref, cot_ref, columns_ref, *refs):
@@ -738,8 +800,8 @@
 
 
 def back_kernel(chips, scale,
-                n2g_ref, state_ref, cot_ref, tokens_ref, gains_ref, attn_ref, q_ref, kv_ref, mask_ref,
-                cos_ref, sin_ref, wq_ref, wo_ref, n1_ref, terms_ref, owned_ref,
+                n2g_ref, state_ref, cot_ref, tokens_ref, gain_one_ref, gain_two_ref, attn_ref, q_ref, kv_ref,
+                mask_ref, cos_ref, sin_ref, wq_ref, wo_ref, n1_ref, terms_ref, owned_ref,
                 tok_grad_ref, wq_grad_ref, wo_grad_ref, gain_ref, mlp_ref,
                 wo, stbuf, n1x, at_all, dq_stage, gq_in, kv_part, km_in, k_sum, k_own, kr_in,
                 cols, part, left_in, right_in, wgrad, wm_in, w_send_buf, w_in, o_terms, o_send_buf, o_in,
@@ -799,7 +861,7 @@
         copy.start()
 
     state = state_ref[...]
-    gain_two = gains_ref[1]
+    gain_two = gain_two_ref[...].astype(wide)
     n2g = n2g_ref[...]
     scale_two = lax.rsqrt(jnp.mean(state * state, axis=-1, keepdims=True) + EPS)
     normed = state * scale_two
@@ -820,7 +882,7 @@
     line.forward(1)
     mask = mask_ref[...]
     keys_total = mask.shape[1]
-    own_cos, own_sin = cos_ref[p.chip, p.core], sin_ref[p.chip, p.core]
+    own_cos, own_sin = cos_ref[p.chip], sin_ref[p.chip]
 
     def km_copy(head):
         return remote(
@@ -929,7 +991,7 @@
         key_total = k_own[chip]
         for other in range(chips):
             key_total = key_total + jnp.where(other == p.chip, 0.0, kr_in[other, chip].astype(wide))
-        turned = unturn(key_total, cos_ref[chip, p.core], sin_ref[chip, p.core], half)
+        turned = unturn(key_total, cos_ref[chip], sin_ref[chip], half)
         last_head = (key_total * is_value + turned * (1.0 - is_value)).astype(low)
         for b in range(grps):
             place = p.peer(b)
@@ -1010,7 +1072,7 @@
     scale_one = lax.rsqrt(jnp.mean(tokens * tokens, axis=-1, keepdims=True) + EPS)
     normed = tokens * scale_one
     gain_own[0] = jnp.sum(n1g * normed, axis=0, keepdims=True)
-    lifted = n1g * gains_ref[0]
+    lifted = n1g * gain_one_ref[...].astype(wide)
     tok_grad_ref[...] = state_grad[...] + scale_one * (
         lifted - normed * jnp.mean(lifted * normed, axis=-1, keepdims=True)
     )
@@ -1088,7 +1150,7 @@
         pl.when(chip < p.chip)(lambda chip=chip: to_left(chip).wait_send())
 
 
-def back_call(n2g, state, cotangent, tokens, gains, attn, q_heads, kv_heads, mask, cosine, sine,
+def back_call(n2g, state, cotangent, tokens, gain_one, gain_two, attn, q_heads, kv_heads, mask, cosine, sine,
               qkv_all, out_full, n1_all, terms, owned):
     chips = cosine.shape[0]
     grps = 4
@@ -1110,7 +1172,7 @@
             struct((2, 1, width), wide),
             struct((3, block, width), wide),
         ),
-        in_specs=[vspec] * 12 + [anyspace] * 4,
+        in_specs=[vspec] * 13 + [anyspace] * 4,
         out_specs=(vspec,) * 5,
         scratch_shapes=[
             vm((att, width), low),
@@ -1160,7 +1222,7 @@
             collective_id=3, has_side_effects=True, vmem_limit_bytes=62 * 2**20
         ),
         name="back",
-    )(n2g, state, cotangent, tokens, gains, attn, q_heads, kv_heads, mask, cosine, sine,
+    )(n2g, state, cotangent, tokens, gain_one, gain_two, attn, q_heads, kv_heads, mask, cosine, sine,
       qkv_all, out_full, n1_all, terms, owned)
 
 
@@ -1258,6 +1320,44 @@
     contract_first = CONTRACT_FIRST
     seq_place = lax.axis_index("seq")
     grp_place = lax.axis_index("grp")
+    use_kernels = (seq_count, grp_count, H, KVH, HD) == (8, 4, 12, 2, 128)
+    if use_kernels:
+        freqs = THETA ** (-(jnp.arange(HD // 2, dtype=jnp.float32) * 2.0) / HD)
+        freqs = jnp.concatenate([freqs, freqs])[None, :]
+        gain_rows = (gain_attn[None, :], gain_mlp[None, :])
+        own_rows = padded_rows(mlp_weight)
+        (
+            attn_wide, state, cosine, sine, mask, q_heads, kv_heads, n1_all, n2_all, cot_all, out_all,
+            qkv_all, columns, *peer_rows
+        ) = front_call(
+            tokens, *gain_rows, shard_segment, freqs, qkv_bias[None, :], cotangent, qkv_weight, out_weight,
+            own_rows,
+        )
+        by_slot = lambda rows: rows.reshape((seq_count,) + rows.shape[2:])
+        grad_part, out_part, mlp_terms, owned = mlp_call(
+            by_slot(n2_all), by_slot(cot_all), columns, [own_rows, *peer_rows]
+        )
+        output = (state + out_part).astype(jnp.bfloat16)
+        token_grad, qkv_terms, out_grad, gain_sums, mlp_sums = back_call(
+            grad_part, state, cotangent, tokens, *gain_rows, attn_wide, q_heads, kv_heads, mask,
+            cosine, sine, qkv_all.reshape(-1, qkv_all.shape[-1]),
+            out_all.reshape(att_width, -1), n1_all, mlp_terms, owned,
+        )
+        width = tokens.shape[1]
+        own = width // (grp_count * seq_count)
+        gain_parts = lax.dynamic_slice_in_dim(
+            gain_sums[:, 0], (grp_place * seq_count + seq_place) * own, own, 1
+        )
+        return (
+            output,
+            token_grad,
+            gain_parts[0],
+            qkv_terms[:, :width],
+            qkv_terms[:, width],
+            out_grad,
+            gain_parts[1],
+            mlp_sums[:, : mlp_weight.shape[0]].transpose(1, 0, 2),
+        )
     segments = lax.dynamic_index_in_dim(shard_segment, grp_place, 0, keepdims=False)
     starts = shard_starts(segments, tok_rows, group_tok // 2)
     shard_order = jnp.arange(seq_count, dtype=jnp.int32)
@@ -1270,57 +1370,6 @@
     gain_one = gain_attn.astype(jnp.float32)
     gain_two = gain_mlp.astype(jnp.float32)
     normed_one = rms_scale(tokens_wide, gain_one).astype(jnp.bfloat16)
-    use_kernels = (seq_count, grp_count, H, KVH, HD) == (8, 4, 12, 2, 128)
-    if use_kernels:
-        chips = seq_count // 2
-        lanes = jnp.arange(HD)
-        all_pos = (starts[:, None] + jnp.arange(tok_rows, dtype=jnp.int32)[None, :]).reshape(-1)
-        all_cosine, all_sine = rotary_tables(all_pos, HD)
-        all_sine = jnp.where(lanes < HD // 2, -all_sine, all_sine)
-        by_shard = lambda table: table.reshape(chips, 2, tok_rows, HD)
-        key_pos = all_pos.reshape(chips, 2, tok_rows).swapaxes(0, 1).reshape(-1)
-        key_seg = jnp.repeat(segments.reshape(chips, 2).swapaxes(0, 1).reshape(-1), tok_rows)
-        visible = ((key_seg == 0) | (key_seg == own_seg))[None, :] & (
-            key_pos[None, :] <= positions[:, None]
-        )
-        mask = jnp.where(visible, 0.0, -1e30).astype(jnp.float32)
-        bias_half = qkv_bias.astype(jnp.float32)
-        bias_pair = jnp.concatenate([bias_half, jnp.zeros_like(bias_half)])
-        bias_row = jnp.where(seq_place % 2 == 0, bias_pair, jnp.roll(bias_pair, HD // 2))
-        bias_rows8 = jnp.broadcast_to(bias_row[None, :], (8, HD))
-        own_rows = padded_rows(mlp_weight)
-        gains = jnp.stack([gain_one, gain_two])[:, None, :]
-        (
-            attn_wide, state, q_heads, kv_heads, n1_all, n2_all, cot_all, out_all, qkv_all, columns, *peer_rows
-        ) = front_call(
-            tokens, gains, cotangent, qkv_weight, bias_rows8, out_weight, own_rows,
-            by_shard(all_cosine), by_shard(all_sine), mask,
-        )
-        by_slot = lambda rows: rows.reshape((seq_count,) + rows.shape[2:])
-        grad_part, out_part, mlp_terms, owned = mlp_call(
-            by_slot(n2_all), by_slot(cot_all), columns, [own_rows, *peer_rows]
-        )
-        output = (state + out_part).astype(jnp.bfloat16)
-        token_grad, qkv_terms, out_grad, gain_sums, mlp_sums = back_call(
-            grad_part, state, cotangent, tokens, gains, attn_wide, q_heads, kv_heads, mask,
-            by_shard(all_cosine), by_shard(all_sine), qkv_all.reshape(-1, qkv_all.shape[-1]),
-            out_all.reshape(att_width, -1), n1_all, mlp_terms, owned,
-        )
-        width = tokens.shape[1]
-        own = width // (grp_count * seq_count)
-        gain_parts = lax.dynamic_slice_in_dim(
-            gain_sums[:, 0], (grp_place * seq_count + seq_place) * own, own, 1
-        )
-        return (
-            output,
-            token_grad,
-            gain_parts[0],
-            qkv_terms[:, :width],
-            qkv_terms[:, width],
-            out_grad,
-            gain_parts[1],
-            mlp_sums[:, : mlp_weight.shape[0]].transpose(1, 0, 2),
-        )
     normed_one_all = lax.all_gather(normed_one, "seq", axis=0, tiled=True)
     qkv_rows = lax.all_gather(qkv_weight, "grp", axis=0, tiled=True)
     bias_rows = lax.all_gather(qkv_bias, "grp", axis=0, tiled=True)

time: 386 us -> 371 us (0.961)
  other arithmetic: 9.56 us -> 1.43 us
  Pallas kernels: 358 us -> 354 us
    pallas_call x1, Pallas kernels: 84.1 us -> 75.1 us  [mlp_call(): pl.pallas_call(functools.partial(mlp_kernel, chips, grps, row_tiles), out...]
    pallas_call x1, Pallas kernels: 141 us -> 148 us  [front_call(): pl.pallas_call(functools.partial(front_kernel, chips, 1.0 / math.sqrt(HD)...]
where the time goes in v6:
time: 371 us
  Pallas kernels  354 us (95%)
  local copies, waits for them, and re-layouts  14.3 us (4%)
    pallas_call x1, Pallas kernels, front_call(): pl.pallas_call(functools.partial(front_kernel, chips, 1.0 / math.sqrt(HD)...  148 us
    pallas_call x1, Pallas kernels, back_call(): pl.pallas_call(functools.partial(back_kernel, chips, 1.0 / math.sqrt(HD))...  132 us
    pallas_call x1, Pallas kernels, mlp_call(): pl.pallas_call(functools.partial(mlp_kernel, chips, grps, row_tiles), out...  75.1 us

profile of v6, /device:TPU:9, one launch (start us, length us, event | category | flops | bytes accessed | tf_op | source)
XLA Modules:
  0.0 370.9 jit_solution(7331635283785494747)
XLA Ops:
  0.6 0.0 copy-start.5
  0.6 0.0 copy-start.6
  0.7 3.5 pad.4.wm_ref.refs_0_
  4.1 0.0 copy-done.5
  4.2 0.6 broadcast_in_dim.12.gain_one_ref
  4.8 0.0 copy-done.6
  4.8 0.6 broadcast_in_dim.13.gain_two_ref
  5.4 0.6 maximum_bitcast_fusion.freq_ref
  6.0 147.8 %front.1 = (f32[128,1536]{1,0:T(8,128)}, f32[128,1536]{1,0:T(8,128)}, f32[4,128,128]{2,1,0:T(8,128)}, f32[4,128,128]{2,1,0:T(8,128)}, f32[128,1024]{1,0:T(8,128)...) custom-call(bf16[128,1536]{1,0:T(8,128)(2,1)} %tokens_ref.3, ...), custom_call_target="tpu_custom_call" | custom-call | tf_op jit(solution)/shard_map/front/pallas_call | solution.py:581
  153.7 75.1 %mlp.1 = (f32[128,1536]{1,0:T(8,128)}, f32[128,1536]{1,0:T(8,128)}, bf16[3,1152,1536]{2,1,0:T(8,128)(2,1)}, bf16[4,48,1024]{2,1,0:T(8,128)(2,1)}) custom-call(bf16[8,128,1536]{2,1,0:T(8,128)(2,1)} %bitcast.15, bf16[8,128,1536]{2,1,0:T(8,128)(2,1)} %bitcast.16, bf16[4,8,48,128]{3,2,1,0:T(8,128)(2,1)} %get-tuple-element.36.columns_ref, ...), custom_call_target="tpu_custom_call" | custom-call | tf_op jit(solution)/shard_map/mlp/pallas_call | solution.py:768
  228.8 131.7 %back.1 = (f32[128,1536]{1,0:T(8,128)}, f32[64,1664]{1,0:T(8,128)}, f32[48,1536]{1,0:T(8,128)}, f32[2,1,1536]{2,1,0:T(1,128)}, f32[3,288,1536]{2,1,0:T(8,128)}) custom-call(f32[128,1536]{1,0:T(8,128)} %get-tuple-element.41.n2g_ref, f32[128,1536]{1,0:T(8,128)} %get-tuple-element.33.state_ref, bf16[128,1536]{1,0:T(8,128)(2,1)} %cot_ref.3, ...), custom_call_target="tpu_custom_call" | custom-call | tf_op jit(solution)/shard_map/back/pallas_call | solution.py:1166
  360.5 0.0 copy-start.3
  360.5 0.0 copy-start
  360.5 0.0 copy-start.2
  360.5 5.3 %slice_bitcast_fusion = f32[280,3,1536]{2,0,1:T(8,128)} fusion(f32[3,288,1536]{2,1,0:T(8,128)} %get-tuple-element.57), kind=kLoop, calls=%fused_computation | loop fusion | bytes 10321920 | tf_op jit(solution)/shard_map/transpose | solution.py:1359
  365.8 0.0 copy-start.1
  365.8 0.0 copy-start.4
  365.8 0.0 copy-done.3
  365.8 0.8 slice.18
  366.6 1.3 dynamic-slice_bitcast_fusion
  367.8 0.6 slice_reduce_fusion
  368.5 0.0 copy-done
  368.5 0.0 copy-done.2
  368.5 0.8 add_convert_fusion
  369.3 0.0 copy-done.1
  369.3 0.9 copy.19
  370.2 0.0 copy-done.4
  370.2 0.7 copy.20
  (1 shorter events, 0.0 us)
Async XLA Ops:
  0.6 3.5 copy-start.5
  0.6 4.1 %copy-start.6 = (bf16[1536]{0:T(1024)(128)(2,1)S(1)}, bf16[1536]{0:T(1024)(128)(2,1)}, u32[]{:S(2)}) copy-start(bf16[1536]{0:T(1024)(128)(2,1)} %param.16) | copy-start | bytes 9220
  360.5 5.3 %copy-start.3 = (f32[64,1664]{1,0:T(8,128)S(1)}, f32[64,1664]{1,0:T(8,128)}, u32[]{:S(2)}) copy-start(f32[64,1664]{1,0:T(8,128)} %get-tuple-element.55) | copy-start | bytes 1277956
  360.5 8.0 %copy-start = (f32[128,1536]{1,0:T(8,128)S(1)}, f32[128,1536]{1,0:T(8,128)}, u32[]{:S(2)}) copy-start(f32[128,1536]{1,0:T(8,128)} %get-tuple-element.33.state_ref) | copy-start | bytes 2359300
  360.5 8.0 %copy-start.2 = (f32[128,1536]{1,0:T(8,128)S(1)}, f32[128,1536]{1,0:T(8,128)}, u32[]{:S(2)}) copy-start(f32[128,1536]{1,0:T(8,128)} %get-tuple-element.40) | copy-start | bytes 2359300
  365.8 3.5 copy-start.1
  365.8 4.4 %copy-start.4 = (f32[48,1536]{1,0:T(8,128)S(1)}, f32[48,1536]{1,0:T(8,128)}, u32[]{:S(2)}) copy-start(f32[48,1536]{1,0:T(8,128)} %get-tuple-element.73) | copy-start | bytes 884740

commit v7 on v6

--- a/solution.py
+++ b/solution.py
@@ -304,20 +304,17 @@
             m_recv.at[3, b - 1, j], p.peer(3 - b), p.seq,
         )
 
-    def out_view(grp, i, core):
-        return wo.at[grp, pl.ds(i * (chips // 2), chips // 2), core]
-
-    def out_direct(b, i):
-        view = out_view(p.grp, i, p.core)
-        return remote(view, view, ox_send.at[b, i], ox_recv.at[b, i], p.peer(b), p.seq)
-
-    def out_forward(b):
-        view = out_view(p.peer(b), b - 1, p.core)
-        return remote(view, view, ox_send.at[3, b - 1], ox_recv.at[3, b - 1], p.peer(3 - b), p.seq)
-
-    def out_mate(b, i, core):
-        view = out_view(p.peer(b), i, core)
-        return remote(view, view, om_send.at[b, i], om_recv.at[b, i], p.grp, p.mate)
+    def out_cross(b, chip):
+        view = wo.at[p.grp, chip, p.core]
+        return remote(view, view, ox_send.at[b, chip], ox_recv.at[b, chip], p.peer(b), p.seq)
+
+    def out_arrival(b, chip):
+        view = wo.at[p.peer(b), chip, p.core]
+        return remote(view, view, ox_send.at[b, chip], ox_recv.at[b, chip], p.grp, p.mate)
+
+    def out_mate(b, core):
+        view = wo.at[p.peer(b), :, core]
+        return remote(view, view, om_send.at[b], om_recv.at[b], p.grp, p.mate)
 
     def q_copy(chip):
         return remote(
@@ -394,7 +391,9 @@
         wq_mate(b).start()
         bias_direct(b).wait_recv()
         bias_mate(b).start()
-    for j in (0, 1):
+    for b in range(1, grps):
+        out_cross(b, p.chip).start()
+    for j in range(3):
         m_direct(1, 0, j).start()
         m_direct(2, 1, j).start()
     make_tables()
@@ -408,6 +407,9 @@
         def _():
             n1_line.forward(order)
             out_line.forward(order)
+            for b in range(1, grps):
+                pl.when(p.chip - order >= 0)(lambda b=b: out_cross(b, p.chip - order).start())
+                pl.when(p.chip + order < chips)(lambda b=b: out_cross(b, p.chip + order).start())
 
         at = nearest_chip(p.chip, order, chips)
         x = nbuf[at, p.core]
@@ -435,10 +437,6 @@
             pl.when(to_chip != p.chip)(lambda to_chip=to_chip: k_copy(at, to_chip).start())
         k_mate(p.chip, at, stage.at[at, 3]).start()
 
-    for b in (1, 2):
-        out_direct(b, b - 1).start()
-    for b in (1, 2):
-        out_direct(b, 2 - b).start()
     own[2].wait()
     cot_line.start()
 
@@ -456,6 +454,13 @@
         for head in range(chips):
             k_arrival(head, 1 - p.core, chip).wait_recv()
     cot_line.forward(1)
+    for j in (0, 1):
+        for b in (1, 2):
+            m_direct(b, b - 1, j).wait_recv()
+            m_forward(b, j).start()
+    for j in range(3):
+        m_direct(1, 1, j).start()
+        m_direct(2, 0, j).start()
 
     mask = mask_ref[...]
     heads_per = H // KVH
@@ -472,34 +477,20 @@
         mixed = jnp.dot(probs, values, preferred_element_type=jnp.float32)
         for i, h in enumerate(heads):
             attn_ref[:, h * 2 * half : (h + 1) * 2 * half] = mixed[i * shard : (i + 1) * shard]
-        if kv == 0:
-            for b in (1, 2):
-                out_direct(b, b - 1).wait_recv()
-                out_forward(b).start()
-                out_mate(b, b - 1, p.core).start()
-            for b in (1, 2):
-                for j in (0, 1):
-                    m_direct(b, b - 1, j).wait_recv()
-                    m_forward(b, j).start()
-            m_direct(1, 0, 2).start()
-            m_direct(2, 1, 2).start()
         cot_line.forward(kv + 2)
 
+    for b in range(1, grps):
+        for chip in range(chips):
+            out_arrival(b, chip).wait_recv()
+        out_mate(b, p.core).start()
     for b in (1, 2):
-        out_direct(b, 2 - b).wait_recv()
-        out_mate(b, 2 - b, p.core).start()
-    for j in range(3):
-        m_direct(1, 1, j).start()
-        m_direct(2, 0, j).start()
+        m_direct(b, b - 1, 2).wait_recv()
+        m_forward(b, 2).start()
     attn_low = attn_ref[...].astype(jnp.bfloat16)
     unit = wo.shape[3]
     columns[...] = attn_low.T.reshape(columns.shape)
-    for i in (0, 1):
-        out_forward(i + 1).wait_recv()
-        out_mate(3, i, p.core).start()
     for b in range(1, grps):
-        for i in (0, 1):
-            out_mate(b, i, 1 - p.core).wait_recv()
+        out_mate(b, 1 - p.core).wait_recv()
     for chip in range(chips):
         out_line.wait_mate(chip)
     state = tokens_ref[...].astype(jnp.float32) + jnp.dot(
@@ -521,11 +512,7 @@
         n1_line.wait_mate(chip)
     for copy in outs:
         copy.start()
-    n2_line.forward(1)
-    for b in (1, 2):
-        m_direct(b, b - 1, 2).wait_recv()
-        m_forward(b, 2).start()
-    for step in range(2, chips):
+    for step in range(1, chips):
         n2_line.forward(step)
     for chip in range(chips):
         cot_line.wait_mate(chip)
@@ -549,16 +536,15 @@
     for b in range(1, grps):
         wq_direct(b).wait_send()
         bias_direct(b).wait_send()
-        for i in (0, 1):
-            out_mate(b, i, p.core).wait_send()
+        out_mate(b, p.core).wait_send()
+        for chip in range(chips):
+            out_cross(b, chip).wait_send()
     for b in (1, 2):
         for i in (0, 1):
             for j in range(3):
                 m_direct(b, i, j).wait_send()
-            out_direct(b, i).wait_send()
         for j in range(3):
             m_forward(b, j).wait_send()
-        out_forward(b).wait_send()
     for chip in range(chips):
         pl.when(chip != p.chip)(lambda chip=chip: q_copy(chip).wait_send())
         for other in range(chips):
@@ -616,7 +602,7 @@
             dma((3, chips)), dma((chips, 2)),
             dma((3, chips)), dma((chips, 2)),
             dma((3, chips)), dma((chips, 2)),
-            dma((grps, 2)), dma((grps, 2)), dma((grps, 2)), dma((grps, 2)),
+            dma((grps, chips)), dma((grps, chips)), dma((grps,)), dma((grps,)),
             dma((2, grps)), dma((grps, 2)),
             dma((2, grps)), dma((grps, 2)),
             dma((grps, 2, 3)), dma((grps, 2, 3)),
@@ -879,7 +865,6 @@
     unit = wo.shape[0] // (grps * slots)
     loads[0].wait()
     attn_grad = lax.dot_general(state_low, wo[...], CONTRACT_LAST, preferred_element_type=wide).astype(low)
-    line.forward(1)
     mask = mask_ref[...]
     keys_total = mask.shape[1]
     own_cos, own_sin = cos_ref[p.chip], sin_ref[p.chip]
@@ -947,11 +932,29 @@
             def _(turned=turned, h=h):
                 gq_in[h % chips, h // chips] = turned
 
-        line.forward(2 + kv)
+        line.forward(1 + kv)
     for chip in range(chips):
         pl.when(chip != p.chip)(lambda chip=chip: q_copy(chip).start())
     for head in (0, 2, 1, 3):
         key_sum(head)
+    def m_add(dst, src):
+        for j in range(3):
+            @pl.loop(0, mhalf // 16)
+            def _(t, j=j):
+                rows = pl.ds(pl.multiple_of(t * 16, 16), 16)
+                m_own[dst, j, rows] = (
+                    m_own[dst, j, rows].astype(wide) + m_in[src, j, rows].astype(wide)
+                ).astype(low)
+
+    m_loads[0].wait()
+    m_first[1].wait_recv()
+    m_add(0, 3)
+    m_second[0].start()
+    m_loads[1].wait()
+    m_first[0].wait_recv()
+    m_add(1, 1)
+    m_second[1].start()
+    line.forward(3)
     loads[1].wait()
     lane = lax.broadcasted_iota(jnp.int32, (chips, shard, HD), 2)
     n1x[:, :, width:] = jnp.where(lane == 0, 1.0, 0.0).astype(low)
@@ -972,22 +975,14 @@
     for b in range(1, grps):
         o_copy(b).start()
 
-    def m_add(dst, src):
-        for j in range(3):
-            @pl.loop(0, mhalf // 16)
-            def _(t, j=j):
-                rows = pl.ds(pl.multiple_of(t * 16, 16), 16)
-                m_own[dst, j, rows] = (
-                    m_own[dst, j, rows].astype(wide) + m_in[src, j, rows].astype(wide)
-                ).astype(low)
-
     for chip in range(chips):
         pl.when(chip != p.chip)(lambda chip=chip: q_arrival(chip).wait_recv())
         pl.when(chip != p.chip)(lambda chip=chip: kr_arrival(chip).wait_recv())
     is_value = jnp.where(p.chip >= chips // 2, 1.0, 0.0)
 
     @pl.loop(0, chips)
-    def _(chip):
+    def _(order):
+        chip = nearest_chip(p.chip, last - order, chips)
         key_total = k_own[chip]
         for other in range(chips):
             key_total = key_total + jnp.where(other == p.chip, 0.0, kr_in[other, chip].astype(wide))
@@ -1045,14 +1040,6 @@
     for b in range(1, grps):
         w_copy(b).start()
     rail_step(2)
-    m_loads[0].wait()
-    m_first[1].wait_recv()
-    m_add(0, 3)
-    m_second[0].start()
-    m_loads[1].wait()
-    m_first[0].wait_recv()
-    m_add(1, 1)
-    m_second[1].start()
     rail_step(3)
 
     tokens = tokens_ref[...].astype(wide)

time: 371 us -> 342 us (0.922)
  Pallas kernels: 354 us -> 323 us
    pallas_call x1, Pallas kernels: 148 us -> 131 us  [front_call(): pl.pallas_call(functools.partial(front_kernel, chips, 1.0 / math.sqrt(HD)...]
    pallas_call x1, Pallas kernels: 132 us -> 115 us  [back_call(): pl.pallas_call(functools.partial(back_kernel, chips, 1.0 / math.sqrt(HD))...]
where the time goes in v7:
time: 342 us; the launch traced here: 340 us
  Pallas kernels  323 us (94%)
  local copies, waits for them, and re-layouts  14.3 us (4%)
    pallas_call x1, Pallas kernels, front_call(): pl.pallas_call(functools.partial(front_kernel, chips, 1.0 / math.sqrt(HD)...  131 us
    pallas_call x1, Pallas kernels, back_call(): pl.pallas_call(functools.partial(back_kernel, chips, 1.0 / math.sqrt(HD))...  115 us
    pallas_call x1, Pallas kernels, mlp_call(): pl.pallas_call(functools.partial(mlp_kernel, chips, grps, row_tiles), out...  77.2 us

profile of v7, /device:TPU:9, one launch (start us, length us, event | category | flops | bytes accessed | tf_op | source)
XLA Modules:
  0.0 339.6 jit_solution(17975127105451502581)
XLA Ops:
  0.6 0.0 copy-start.5
  0.6 0.0 copy-start.6
  0.7 3.5 %pad.4.wm_ref.refs_0_ = bf16[3,288,1536]{2,1,0:T(8,128)(2,1)} pad(bf16[3,280,1536]{2,1,0:T(8,128)(2,1)} %bitcast.17, bf16[]{:T(256)} %constant.9.clone.1), padding=0_0x0_8x0_0 | pad | bytes 5234690 | tf_op jit(solution)/shard_map/jit(_pad)/pad | solution.py:1283
  4.1 0.0 copy-done.5
  4.2 0.6 broadcast_in_dim.12.gain_one_ref
  4.8 0.0 copy-done.6
  4.8 0.6 broadcast_in_dim.13.gain_two_ref
  5.4 0.6 maximum_bitcast_fusion.freq_ref
  6.0 130.6 %front.1 = (f32[128,1536]{1,0:T(8,128)}, f32[128,1536]{1,0:T(8,128)}, f32[4,128,128]{2,1,0:T(8,128)}, f32[4,128,128]{2,1,0:T(8,128)}, f32[128,1024]{1,0:T(8,128)...) custom-call(bf16[128,1536]{1,0:T(8,128)(2,1)} %tokens_ref.3, ...), custom_call_target="tpu_custom_call" | custom-call | tf_op jit(solution)/shard_map/front/pallas_call | solution.py:567
  136.6 77.2 %mlp.1 = (f32[128,1536]{1,0:T(8,128)}, f32[128,1536]{1,0:T(8,128)}, bf16[3,1152,1536]{2,1,0:T(8,128)(2,1)}, bf16[4,48,1024]{2,1,0:T(8,128)(2,1)}) custom-call(bf16[8,128,1536]{2,1,0:T(8,128)(2,1)} %bitcast.15, bf16[8,128,1536]{2,1,0:T(8,128)(2,1)} %bitcast.16, bf16[4,8,48,128]{3,2,1,0:T(8,128)(2,1)} %get-tuple-element.36.columns_ref, ...), custom_call_target="tpu_custom_call" | custom-call | tf_op jit(solution)/shard_map/mlp/pallas_call | solution.py:754
  213.8 115.3 %back.1 = (f32[128,1536]{1,0:T(8,128)}, f32[64,1664]{1,0:T(8,128)}, f32[48,1536]{1,0:T(8,128)}, f32[2,1,1536]{2,1,0:T(1,128)}, f32[3,288,1536]{2,1,0:T(8,128)}) custom-call(f32[128,1536]{1,0:T(8,128)} %get-tuple-element.41.n2g_ref, f32[128,1536]{1,0:T(8,128)} %get-tuple-element.33.state_ref, bf16[128,1536]{1,0:T(8,128)(2,1)} %cot_ref.3, ...), custom_call_target="tpu_custom_call" | custom-call | tf_op jit(solution)/shard_map/back/pallas_call | solution.py:1153
  329.1 0.0 copy-start.3
  329.1 0.0 copy-start
  329.2 0.0 copy-start.2
  329.2 5.3 %slice_bitcast_fusion = f32[280,3,1536]{2,0,1:T(8,128)} fusion(f32[3,288,1536]{2,1,0:T(8,128)} %get-tuple-element.57), kind=kLoop, calls=%fused_computation | loop fusion | bytes 10321920 | tf_op jit(solution)/shard_map/transpose | solution.py:1346
  334.5 0.0 copy-start.1
  334.5 0.0 copy-start.4
  334.5 0.0 copy-done.3
  334.5 0.8 slice.18
  335.2 1.3 dynamic-slice_bitcast_fusion
  336.5 0.6 slice_reduce_fusion
  337.1 0.0 copy-done
  337.1 0.0 copy-done.2
  337.1 0.8 add_convert_fusion
  338.0 0.0 copy-done.1
  338.0 0.9 copy.19
  338.8 0.0 copy-done.4
  338.8 0.7 copy.20
  (1 shorter events, 0.0 us)
Async XLA Ops:
  0.6 3.5 %copy-start.5 = (bf16[1536]{0:T(1024)(128)(2,1)S(1)}, bf16[1536]{0:T(1024)(128)(2,1)}, u32[]{:S(2)}) copy-start(bf16[1536]{0:T(1024)(128)(2,1)} %param.12) | copy-start | bytes 9220
  0.6 4.1 %copy-start.6 = (bf16[1536]{0:T(1024)(128)(2,1)S(1)}, bf16[1536]{0:T(1024)(128)(2,1)}, u32[]{:S(2)}) copy-start(bf16[1536]{0:T(1024)(128)(2,1)} %param.16) | copy-start | bytes 9220
  329.1 5.3 %copy-start.3 = (f32[64,1664]{1,0:T(8,128)S(1)}, f32[64,1664]{1,0:T(8,128)}, u32[]{:S(2)}) copy-start(f32[64,1664]{1,0:T(8,128)} %get-tuple-element.55) | copy-start | bytes 1277956
  329.1 8.0 %copy-start = (f32[128,1536]{1,0:T(8,128)S(1)}, f32[128,1536]{1,0:T(8,128)}, u32[]{:S(2)}) copy-start(f32[128,1536]{1,0:T(8,128)} %get-tuple-element.33.state_ref) | copy-start | bytes 2359300
  329.2 8.0 %copy-start.2 = (f32[128,1536]{1,0:T(8,128)S(1)}, f32[128,1536]{1,0:T(8,128)}, u32[]{:S(2)}) copy-start(f32[128,1536]{1,0:T(8,128)} %get-tuple-element.40) | copy-start | bytes 2359300
  334.5 3.5 %copy-start.1 = (f32[128,1536]{1,0:T(8,128)S(1)}, f32[128,1536]{1,0:T(8,128)}, u32[]{:S(2)}) copy-start(f32[128,1536]{1,0:T(8,128)} %get-tuple-element.69) | copy-start | bytes 2359300
  334.5 4.4 %copy-start.4 = (f32[48,1536]{1,0:T(8,128)S(1)}, f32[48,1536]{1,0:T(8,128)}, u32[]{:S(2)}) copy-start(f32[48,1536]{1,0:T(8,128)} %get-tuple-element.73) | copy-start | bytes 884740

commit v8 on v7

--- a/solution.py
+++ b/solution.py
@@ -437,8 +437,6 @@
             pl.when(to_chip != p.chip)(lambda to_chip=to_chip: k_copy(at, to_chip).start())
         k_mate(p.chip, at, stage.at[at, 3]).start()
 
-    own[2].wait()
-    cot_line.start()
 
     @pl.loop(0, chips)
     def _(order):
@@ -453,7 +451,8 @@
         pl.when(chip != p.chip)(lambda chip=chip: q_arrival(chip).wait_recv())
         for head in range(chips):
             k_arrival(head, 1 - p.core, chip).wait_recv()
-    cot_line.forward(1)
+    own[2].wait()
+    cot_line.start()
     for j in (0, 1):
         for b in (1, 2):
             m_direct(b, b - 1, j).wait_recv()
@@ -477,7 +476,7 @@
         mixed = jnp.dot(probs, values, preferred_element_type=jnp.float32)
         for i, h in enumerate(heads):
             attn_ref[:, h * 2 * half : (h + 1) * 2 * half] = mixed[i * shard : (i + 1) * shard]
-        cot_line.forward(kv + 2)
+        cot_line.forward(kv + 1)
 
     for b in range(1, grps):
         for chip in range(chips):
@@ -488,7 +487,8 @@
         m_forward(b, 2).start()
     attn_low = attn_ref[...].astype(jnp.bfloat16)
     unit = wo.shape[3]
-    columns[...] = attn_low.T.reshape(columns.shape)
+    for owner in range(grps):
+        columns[owner] = attn_low[:, owner * columns.shape[2] : (owner + 1) * columns.shape[2]]
     for b in range(1, grps):
         out_mate(b, 1 - p.core).wait_recv()
     for chip in range(chips):
@@ -500,6 +500,7 @@
     state_ref[...] = state
     n2buf[p.chip, p.core] = rms_scale(state, gain_two_ref[...].astype(jnp.float32)).astype(jnp.bfloat16)
     n2_line.start()
+    cot_line.forward(3)
     outs = [
         pltpu.make_async_copy(nbuf, n1_all_ref, lsem.at[4]),
         pltpu.make_async_copy(wq, wq_all_ref, lsem.at[5]),
@@ -563,7 +564,7 @@
     low, wide = jnp.bfloat16, jnp.float32
     struct = jax.ShapeDtypeStruct
     wo_shape = (grps, chips, 2) + out_weight.shape
-    columns_shape = (grps, 2 * chips, out_weight.shape[0], shard)
+    columns_shape = (grps, shard, H * HD // grps)
     return pl.pallas_call(
         functools.partial(front_kernel, chips, 1.0 / math.sqrt(HD)),
         out_shape=(
@@ -616,14 +617,17 @@
     )(tokens, gain_one, gain_two, segments, freqs, bias, cot, qkv_weight, out_weight, mlp_rows)
 
 
+FIRST_HOPS = ((1, 0, 1), (3, 0, 1), (2, 1, 2), (3, 1, 2))
+EARLY_HOPS = tuple((hop, kind) for kind in (2, 0) for hop in (1, 3, 0, 2))
+
+
 def mlp_kernel(chips, grps, row_tiles, n2_ref, cot_ref, columns_ref, *refs):
     w_refs, refs = refs[:grps], refs[grps:]
     (
-        n2g_ref, outp_ref, grads_ref, owned_ref, tok, w, acts, part, mate_in, left_in, right_in, stage, owned,
-        lsem, ssend, srecv, wsem, osem, a_send, a_recv,
+        n2g_ref, outp_ref, grads_ref, owned_ref, passing_ref, arrived_ref, tok, w, acts, part, mate_in, left_in, right_in, stage,
+        lsem, ssend, srecv, wsem, osem, a_send, a_recv, e_send, e_recv,
     ) = refs
     p = Place(chips)
-    slots = 2 * chips
     shard, width = n2_ref.shape[1:]
     units = w.shape[1]
     block = units // grps
@@ -631,7 +635,7 @@
     loads = [
         pltpu.make_async_copy(n2_ref, tok.at[0], lsem.at[0]),
         pltpu.make_async_copy(cot_ref, tok.at[1], lsem.at[1]),
-        pltpu.make_async_copy(columns_ref.at[:, p.seq], owned.at[:, :, pl.ds(pl.multiple_of(p.seq * shard, shard), shard)], lsem.at[2]),
+        pltpu.make_async_copy(columns_ref.at[p.grp], owned_ref.at[0], lsem.at[2]),
     ]
     for copy in loads:
         copy.start()
@@ -643,83 +647,53 @@
         for b in range(grps):
             w_copy(j, b).start()
 
-    def seq_peer(i):
-        return (p.seq + i) % slots
-
     barrier = pltpu.get_barrier_semaphore()
-    for i in range(1, slots):
-        pl.semaphore_signal(barrier, inc=1, device_id=(p.grp, seq_peer(i)), device_id_type=MESH)
-    pl.semaphore_wait(barrier, slots - 1)
+    inner = jnp.where((p.chip > 0) & (p.chip < chips - 1), 1, 0)
+
+    def greet(grp, seq):
+        pl.semaphore_signal(barrier, inc=1, device_id=(grp, seq), device_id_type=MESH)
+
+    greet(p.grp, p.mate)
+    pl.when(p.chip > 0)(lambda: greet(p.grp, p.seq - 2))
+    pl.when(p.chip < chips - 1)(lambda: greet(p.grp, p.seq + 2))
+    for b in range(1, grps):
+        greet(p.peer(b), p.seq)
+    pl.semaphore_wait(barrier, 2 + inner + grps - 1)
     scatter = LineScatter(p, part, mate_in, left_in, right_in, ssend, srecv)
 
-    def a_copy(i, to, slot):
+    def a_copy(b):
         return remote(
-            columns_ref.at[:, to], owned.at[:, :, pl.ds(pl.multiple_of(slot * shard, shard), shard)],
-            a_send.at[i], a_recv.at[slot], p.grp, to,
-        )
-
-    for i in range(1, slots):
-        a_copy(i, seq_peer(i), p.seq).start()
+            columns_ref.at[p.peer(b)], owned_ref.at[b], a_send.at[b], a_recv.at[b], p.peer(b), p.seq
+        )
+
+    for b in range(1, grps):
+        a_copy(b).start()
     for copy in loads:
         copy.wait()
     for j in range(3):
         for b in range(grps):
             w_copy(j, b).wait()
 
-    @pl.loop(0, chips + 1)
-    def _(order):
-        @pl.when(order < chips)
-        def _():
-            at = nearest_chip(p.chip, chips - 1 - order, chips)
-            x = tok[0, pl.ds(2 * at, 2)].reshape(2 * shard, width)
-            y = tok[1, pl.ds(2 * at, 2)].reshape(2 * shard, width)
-            gate = lax.dot_general(x, w[0], CONTRACT_LAST, preferred_element_type=jnp.float32)
-            up = lax.dot_general(x, w[1], CONTRACT_LAST, preferred_element_type=jnp.float32)
-            unit_grad = lax.dot_general(y, w[2], CONTRACT_LAST, preferred_element_type=jnp.float32)
-            sig = 1.0 / (1.0 + jnp.exp(-gate))
-            silu = gate * sig
-            rows = pl.ds(at * (2 * shard), 2 * shard)
-            gate_grad = (unit_grad * up * sig * (1.0 + gate * (1.0 - sig))).astype(jnp.bfloat16)
-            up_grad = (unit_grad * silu).astype(jnp.bfloat16)
-            acts[0, rows] = gate_grad
-            acts[1, rows] = up_grad
-            acts[2, rows] = (silu * up).astype(jnp.bfloat16)
-            back = jnp.dot(gate_grad, w[0], preferred_element_type=jnp.float32) + jnp.dot(
-                up_grad, w[1], preferred_element_type=jnp.float32
-            )
-            part[0, pl.ds(2 * at, 2)] = back.astype(jnp.bfloat16).reshape(2, shard, width)
-            scatter.to_mate(0, at).start()
-
-        pl.when(order > 0)(lambda: scatter.step(0, nearest_chip(p.chip, chips - order, chips)))
+    def kind_of(t):
+        return (t // row_tiles + 2) % 3
+
+    def early(slot, kind):
+        b, i, to = FIRST_HOPS[slot]
+        half = block // 2
+        rows = grads_ref.at[kind, pl.ds(b * block + i * half, half)]
+        land = arrived_ref.at[kind // 2, pl.ds(i * half, half)] if b < 3 else passing_ref.at[i, kind]
+        at = EARLY_HOPS.index((slot, kind))
+        return remote(rows, land, e_send.at[at], e_recv.at[at], p.peer(to), p.seq)
 
     def out_copy(t):
         return pltpu.make_async_copy(
             stage.at[t % 2],
-            grads_ref.at[t // row_tiles, pl.ds((t % row_tiles) * tile, tile)],
+            grads_ref.at[kind_of(t), pl.ds((t % row_tiles) * tile, tile)],
             osem.at[t % 2],
         )
 
-    @pl.loop(0, 3 * row_tiles)
-    def _(t):
-        @pl.when(t < chips)
-        def _():
-            at = nearest_chip(p.chip, chips - 1 - t, chips)
-            h = acts[2, pl.ds(at * (2 * shard), 2 * shard)]
-            part[1, pl.ds(2 * at, 2)] = (
-                jnp.dot(h, w[2], preferred_element_type=jnp.float32)
-                .astype(jnp.bfloat16).reshape(2, shard, width)
-            )
-            scatter.to_mate(1, at).start()
-
-        @pl.when((t > 0) & (t <= chips))
-        def _():
-            scatter.step(1, nearest_chip(p.chip, chips - t, chips))
-
-        @pl.when(t >= 2)
-        def _():
-            out_copy(t - 2).wait()
-
-        kind = t // row_tiles
+    def tile_grad(t):
+        kind = kind_of(t)
         lhs = acts[kind, :, pl.ds(pl.multiple_of((t % row_tiles) * tile, 128), tile)]
         rhs = tok[kind // 2].reshape(2 * chips * shard, width)
         stage[t % 2] = lax.dot_general(
@@ -727,19 +701,86 @@
         ).astype(jnp.bfloat16)
         out_copy(t).start()
 
+    def start_early(kind):
+        for hop in EARLY_HOPS:
+            if hop[1] == kind:
+                early(*hop).start()
+
+    def far_chip(order):
+        return nearest_chip(p.chip, chips - 1 - order, chips)
+
+    @pl.loop(0, chips + 1)
+    def _(order):
+        @pl.when(order < chips)
+        def _():
+            at = far_chip(order)
+            x = tok[0, pl.ds(2 * at, 2)].reshape(2 * shard, width)
+            gate = lax.dot_general(x, w[0], CONTRACT_LAST, preferred_element_type=jnp.float32)
+            up = lax.dot_general(x, w[1], CONTRACT_LAST, preferred_element_type=jnp.float32)
+            sig = 1.0 / (1.0 + jnp.exp(-gate))
+            silu = gate * sig
+            rows = pl.ds(at * (2 * shard), 2 * shard)
+            acts[0, rows] = (up * sig * (1.0 + gate * (1.0 - sig))).astype(jnp.bfloat16)
+            acts[1, rows] = silu.astype(jnp.bfloat16)
+            hidden = (silu * up).astype(jnp.bfloat16)
+            acts[2, rows] = hidden
+            part[1, pl.ds(2 * at, 2)] = (
+                jnp.dot(hidden, w[2], preferred_element_type=jnp.float32)
+                .astype(jnp.bfloat16).reshape(2, shard, width)
+            )
+            scatter.to_mate(1, at).start()
+
+        pl.when(order > 0)(lambda: scatter.step(1, far_chip(order - 1)))
+
+    @pl.loop(0, row_tiles)
+    def _(t):
+        pl.when(t >= 2)(lambda: out_copy(t - 2).wait())
+        tile_grad(t)
+
+    @pl.loop(0, chips + 1)
+    def _(order):
+        @pl.when(order < chips)
+        def _():
+            at = far_chip(order)
+            y = tok[1, pl.ds(2 * at, 2)].reshape(2 * shard, width)
+            unit_grad = lax.dot_general(y, w[2], CONTRACT_LAST, preferred_element_type=jnp.float32)
+            rows = pl.ds(at * (2 * shard), 2 * shard)
+            gate_grad = (unit_grad * acts[0, rows].astype(jnp.float32)).astype(jnp.bfloat16)
+            up_grad = (unit_grad * acts[1, rows].astype(jnp.float32)).astype(jnp.bfloat16)
+            acts[0, rows] = gate_grad
+            acts[1, rows] = up_grad
+            back = jnp.dot(gate_grad, w[0], preferred_element_type=jnp.float32) + jnp.dot(
+                up_grad, w[1], preferred_element_type=jnp.float32
+            )
+            part[0, pl.ds(2 * at, 2)] = back.astype(jnp.bfloat16).reshape(2, shard, width)
+            scatter.to_mate(0, at).start()
+
+        @pl.when(order == 1)
+        def _():
+            out_copy(row_tiles - 2).wait()
+            out_copy(row_tiles - 1).wait()
+            start_early(2)
+
+        pl.when(order > 0)(lambda: scatter.step(0, far_chip(order - 1)))
+
+    @pl.loop(row_tiles, 3 * row_tiles)
+    def _(t):
+        pl.when(t >= row_tiles + 2)(lambda: out_copy(t - 2).wait())
+        pl.when(t == 2 * row_tiles + 1)(lambda: start_early(0))
+        tile_grad(t)
+
     scatter.finish(0, n2g_ref)
-    for i in range(1, slots):
-        a_copy(i, seq_peer(i), seq_peer(i)).wait_recv()
-    moved = pltpu.make_async_copy(owned, owned_ref, lsem.at[0])
-    moved.start()
     scatter.finish(1, outp_ref)
     out_copy(3 * row_tiles - 2).wait()
     out_copy(3 * row_tiles - 1).wait()
-    moved.wait()
+    for hop in EARLY_HOPS:
+        early(*hop).wait_recv()
+        early(*hop).wait_send()
     scatter.drain(0)
     scatter.drain(1)
-    for i in range(1, slots):
-        a_copy(i, seq_peer(i), p.seq).wait_send()
+    for b in range(1, grps):
+        a_copy(b).wait_recv()
+        a_copy(b).wait_send()
 
 
 def mlp_call(n2_all, cot_all, columns, w_blocks, row_tiles=3):
@@ -750,17 +791,18 @@
     vm, anyspace = pltpu.VMEM, pl.BlockSpec(memory_space=pl.ANY)
     vspec = pl.BlockSpec(memory_space=pltpu.VMEM)
     dma = pltpu.SemaphoreType.DMA
-    owned_shape = columns.shape[:1] + columns.shape[2:3] + (slots * shard,)
     return pl.pallas_call(
         functools.partial(mlp_kernel, chips, grps, row_tiles),
         out_shape=(
             jax.ShapeDtypeStruct((shard, width), jnp.float32),
             jax.ShapeDtypeStruct((shard, width), jnp.float32),
             jax.ShapeDtypeStruct((3, units, width), jnp.bfloat16),
-            jax.ShapeDtypeStruct(owned_shape, jnp.bfloat16),
+            jax.ShapeDtypeStruct(columns.shape, jnp.bfloat16),
+            jax.ShapeDtypeStruct((2, 3, block // 2, width), jnp.bfloat16),
+            jax.ShapeDtypeStruct((2, block, width), jnp.bfloat16),
         ),
         in_specs=[anyspace] * (3 + grps),
-        out_specs=(vspec, vspec, anyspace, anyspace),
+        out_specs=(vspec, vspec) + (anyspace,) * 4,
         scratch_shapes=[
             vm((2, slots, shard, width), jnp.bfloat16),
             vm((3, units, width), jnp.bfloat16),
@@ -770,9 +812,9 @@
             vm((2, chips, shard, width), jnp.bfloat16),
             vm((2, chips, shard, width), jnp.bfloat16),
             vm((2, units // row_tiles, width), jnp.bfloat16),
-            vm(owned_shape, jnp.bfloat16),
             dma((3,)), dma((3, 2, chips)), dma((3, 2, chips)),
-            dma((3, grps)), dma((2,)), dma((slots,)), dma((slots,)),
+            dma((3, grps)), dma((2,)), dma((grps,)), dma((grps,)),
+            dma((len(EARLY_HOPS),)), dma((len(EARLY_HOPS),)),
         ],
         compiler_params=pltpu.CompilerParams(
             collective_id=1, has_side_effects=True, vmem_limit_bytes=62 * 2**20
@@ -787,13 +829,13 @@
 
 def back_kernel(chips, scale,
                 n2g_ref, state_ref, cot_ref, tokens_ref, gain_one_ref, gain_two_ref, attn_ref, q_ref, kv_ref,
-                mask_ref, cos_ref, sin_ref, wq_ref, wo_ref, n1_ref, terms_ref, owned_ref,
-                tok_grad_ref, wq_grad_ref, wo_grad_ref, gain_ref, mlp_ref,
+                mask_ref, cos_ref, sin_ref, wq_ref, wo_ref, n1_ref, terms_ref, owned_ref, passing_ref, early_ref,
+                tok_grad_ref, wq_grad_ref, wo_grad_ref, gain_ref, direct_ref, second_ref,
                 wo, stbuf, n1x, at_all, dq_stage, gq_in, kv_part, km_in, k_sum, k_own, kr_in,
-                cols, part, left_in, right_in, wgrad, wm_in, w_send_buf, w_in, o_terms, o_send_buf, o_in,
+                cols, part, left_in, right_in, wgrad, wm_in, w_send_buf, w_in, o_terms, ob_in, o_send_buf, o_in,
                 m_own, m_in, gain_own, gain_in, gain_mid, gain_mid_in, state_grad,
                 lsem, s_send, s_recv, q_send, q_recv, km_send, km_recv, kr_send, kr_recv,
-                r_send, r_recv, wm_send, wm_recv, w_send, w_recv, o_send, o_recv, m_send, m_recv,
+                r_send, r_recv, wm_send, wm_recv, w_send, w_recv, ob_send, ob_recv, o_send, o_recv, m_send, m_recv,
                 ml_sem, g_send, g_recv, h_send, h_recv):
     p = Place(chips)
     grps = 4
@@ -824,27 +866,55 @@
         pl.semaphore_signal(barrier, inc=1, device_id=(p.peer(b), p.seq), device_id_type=MESH)
     pl.semaphore_wait(barrier, slots - 1 + grps - 1)
 
-    def m_rows(b, i):
-        return terms_ref.at[:, pl.ds(b * block + i * mhalf, mhalf)]
-
-    def m_copy(slot, src, peer):
-        return remote(src, m_in.at[slot], m_send.at[slot], m_recv.at[slot], p.peer(peer), p.seq)
-
-    m_first = [
-        m_copy(1, m_rows(3, 0), 1), m_copy(3, m_rows(3, 1), 2),
-        m_copy(0, m_rows(1, 0), 1), m_copy(2, m_rows(2, 1), 2),
+    def m_rows(b, i, kind):
+        return terms_ref.at[kind, pl.ds(b * block + i * mhalf, mhalf)]
+
+    def m_first(hop, kind):
+        b, i, to = FIRST_HOPS[hop]
+        land = direct_ref.at[kind, pl.ds(i * mhalf, mhalf)] if b < 3 else m_in.at[i, kind]
+        return remote(
+            m_rows(b, i, kind), land, m_send.at[hop, kind], m_recv.at[hop, kind], p.peer(to), p.seq
+        )
+
+    def m_second(i, kind):
+        return remote(
+            m_own.at[i, kind], second_ref.at[kind, pl.ds(i * mhalf, mhalf)], m_send.at[4 + i, kind],
+            m_recv.at[4 + i, kind], p.peer(2 - i), p.seq,
+        )
+
+    late_hops = [(hop, kind) for kind in (1, 0, 2) for hop in (1, 3, 0, 2) if (hop, kind) not in EARLY_HOPS]
+    for hop in late_hops:
+        m_first(*hop).start()
+    m_loads = [
+        pltpu.make_async_copy(m_rows(2 - i, i, kind), m_own.at[i, kind], ml_sem.at[i, kind])
+        for i in (0, 1)
+        for kind in range(3)
     ]
-    for copy in m_first:
+    for hop, kind in EARLY_HOPS:
+        if FIRST_HOPS[hop][0] == 3:
+            i = FIRST_HOPS[hop][1]
+            m_loads.append(pltpu.make_async_copy(passing_ref.at[i, kind], m_in.at[i, kind], ml_sem.at[2 + i, kind]))
+    early_copies = [
+        pltpu.make_async_copy(early_ref.at[kind // 2], direct_ref.at[kind], ml_sem.at[4, kind]) for kind in (0, 2)
+    ]
+    for copy in early_copies:
         copy.start()
-    m_second = [m_copy(4, m_own.at[0], 1), m_copy(5, m_own.at[1], 2)]
-    m_loads = [
-        pltpu.make_async_copy(m_rows(1, 1), m_own.at[0], ml_sem.at[0]),
-        pltpu.make_async_copy(m_rows(2, 0), m_own.at[1], ml_sem.at[1]),
-        pltpu.make_async_copy(m_rows(0, 0), m_own.at[2], ml_sem.at[2]),
-        pltpu.make_async_copy(m_rows(0, 1), m_own.at[3], ml_sem.at[3]),
-    ]
     for copy in m_loads:
         copy.start()
+
+    def m_turn(kind):
+        for i in (0, 1):
+            if (1 + 2 * i, kind) in late_hops:
+                m_first(1 + 2 * i, kind).wait_recv()
+
+            @pl.loop(0, mhalf // 16)
+            def _(t, i=i):
+                rows = pl.ds(pl.multiple_of(t * 16, 16), 16)
+                m_own[i, kind, rows] = (
+                    m_own[i, kind, rows].astype(wide) + m_in[i, kind, rows].astype(wide)
+                ).astype(low)
+
+            m_second(i, kind).start()
 
     state = state_ref[...]
     gain_two = gain_two_ref[...].astype(wide)
@@ -857,9 +927,10 @@
         lifted - normed * jnp.mean(lifted * normed, axis=-1, keepdims=True)
     )
     state_low = state_grad[...].astype(low)
-    stbuf[p.chip, p.core] = state_low
-    line = RailGather(p, lambda chip, core: stbuf.at[chip, core], s_send, s_recv)
-    line.start()
+    stbuf[0] = state_low
+
+    def state_copy(b):
+        return remote(stbuf.at[0], stbuf.at[b], s_send.at[b], s_recv.at[b], p.peer(b), p.seq)
 
     attn = attn_ref[...]
     unit = wo.shape[0] // (grps * slots)
@@ -932,48 +1003,21 @@
             def _(turned=turned, h=h):
                 gq_in[h % chips, h // chips] = turned
 
-        line.forward(1 + kv)
+        if kv == 0:
+            for copy in m_loads:
+                copy.wait()
+            m_turn(2)
+            m_turn(0)
+            for b in range(1, grps):
+                state_copy(b).start()
     for chip in range(chips):
         pl.when(chip != p.chip)(lambda chip=chip: q_copy(chip).start())
     for head in (0, 2, 1, 3):
         key_sum(head)
-    def m_add(dst, src):
-        for j in range(3):
-            @pl.loop(0, mhalf // 16)
-            def _(t, j=j):
-                rows = pl.ds(pl.multiple_of(t * 16, 16), 16)
-                m_own[dst, j, rows] = (
-                    m_own[dst, j, rows].astype(wide) + m_in[src, j, rows].astype(wide)
-                ).astype(low)
-
-    m_loads[0].wait()
-    m_first[1].wait_recv()
-    m_add(0, 3)
-    m_second[0].start()
-    m_loads[1].wait()
-    m_first[0].wait_recv()
-    m_add(1, 1)
-    m_second[1].start()
-    line.forward(3)
+    m_turn(1)
     loads[1].wait()
     lane = lax.broadcasted_iota(jnp.int32, (chips, shard, HD), 2)
     n1x[:, :, width:] = jnp.where(lane == 0, 1.0, 0.0).astype(low)
-    for chip in range(chips):
-        line.wait_mate(chip)
-    loads[2].wait()
-    o_terms[...] = jnp.dot(
-        at_all[...].reshape(grps * unit, slots * shard), stbuf[...].reshape(slots * shard, width),
-        preferred_element_type=wide,
-    ).reshape(grps, unit, width)
-    o_send_buf[...] = o_terms[...].astype(low)
-
-    def o_copy(b):
-        return remote(
-            o_send_buf.at[p.peer(b)], o_in.at[b], o_send.at[b], o_recv.at[b], p.peer(b), p.seq
-        )
-
-    for b in range(1, grps):
-        o_copy(b).start()
 
     for chip in range(chips):
         pl.when(chip != p.chip)(lambda chip=chip: q_arrival(chip).wait_recv())
@@ -1040,6 +1084,28 @@
     for b in range(1, grps):
         w_copy(b).start()
     rail_step(2)
+    loads[2].wait()
+    for b in range(1, grps):
+        state_copy(b).wait_recv()
+    o_terms[...] = lax.dot_general(
+        at_all[...].reshape(grps * shard, slots * unit), stbuf[...].reshape(grps * shard, width),
+        CONTRACT_FIRST, preferred_element_type=wide,
+    ).reshape(chips, 2, unit, width)
+    ob = remote(o_terms.at[:, 1 - p.core], ob_in, ob_send, ob_recv, p.grp, p.mate)
+    ob.start()
+    ob.wait_recv()
+    o_send_buf[...] = (o_terms[:, p.core] + ob_in[...]).astype(low)
+
+    def o_copy(chip):
+        return remote(
+            o_send_buf.at[chip], o_in.at[p.chip], o_send.at[chip], o_recv.at[p.chip], p.grp, 2 * chip + p.core
+        )
+
+    def o_arrival(chip):
+        return remote(o_send_buf.at[chip], o_in.at[chip], o_send.at[chip], o_recv.at[chip], p.grp, p.mate)
+
+    for chip in range(chips):
+        pl.when(chip != p.chip)(lambda chip=chip: o_copy(chip).start())
     rail_step(3)
 
     tokens = tokens_ref[...].astype(wide)
@@ -1081,48 +1147,38 @@
     for b in range(1, grps):
         h_copy(b).start()
 
-    wo_grad = o_terms[p.grp]
     wq_grad = wgrad[0, p.core] + wm_in[0]
     for b in range(1, grps):
-        o_copy(b).wait_recv()
-        wo_grad = wo_grad + o_in[b].astype(wide)
         w_copy(b).wait_recv()
         wq_grad = wq_grad + w_in[b].astype(wide)
+    wq_grad_ref[...] = wq_grad
+    wo_grad = o_terms[p.chip, p.core] + ob_in[p.chip]
+    for chip in range(chips):
+        pl.when(chip != p.chip)(lambda chip=chip: o_arrival(chip).wait_recv())
+        wo_grad = wo_grad + jnp.where(chip == p.chip, 0.0, o_in[chip].astype(wide))
     wo_grad_ref[...] = wo_grad
-    wq_grad_ref[...] = wq_grad
     total = gain_mid[...]
     for b in range(1, grps):
         h_copy(b).wait_recv()
         total = total + gain_mid_in[b]
     gain_ref[...] = total
 
-    m_loads[2].wait()
-    m_loads[3].wait()
-
-    def m_total(own, direct, second, i):
-        for j in range(3):
-            @pl.loop(0, mhalf // 16)
-            def _(t, j=j):
-                rows = pl.ds(pl.multiple_of(t * 16, 16), 16)
-                mlp_ref[j, pl.ds(pl.multiple_of(i * mhalf + t * 16, 16), 16)] = (
-                    m_own[own, j, rows].astype(wide) + m_in[direct, j, rows].astype(wide)
-                ) + m_in[second, j, rows].astype(wide)
-
-    m_first[2].wait_recv()
-    m_second[1].wait_recv()
-    m_total(2, 0, 5, 0)
-    m_first[3].wait_recv()
-    m_second[0].wait_recv()
-    m_total(3, 2, 4, 1)
-
-    for copy in m_first + m_second:
-        copy.wait_send()
-    line.drain()
+    for hop, kind in late_hops:
+        if FIRST_HOPS[hop][0] < 3:
+            m_first(hop, kind).wait_recv()
+        m_first(hop, kind).wait_send()
+    for kind in (2, 0, 1):
+        for i in (0, 1):
+            m_second(i, kind).wait_recv()
+            m_second(i, kind).wait_send()
+    for copy in early_copies:
+        copy.wait()
+    ob.wait_send()
     wm.wait_send()
     for i in range(1, slots):
         g_copy(i).wait_send()
     for b in range(1, grps):
-        o_copy(b).wait_send()
+        state_copy(b).wait_send()
         w_copy(b).wait_send()
         h_copy(b).wait_send()
     for chip in range(chips):
@@ -1132,13 +1188,14 @@
         def _(chip=chip):
             q_copy(chip).wait_send()
             kr_copy(chip).wait_send()
+            o_copy(chip).wait_send()
 
         pl.when(chip > p.chip)(lambda chip=chip: to_right(chip).wait_send())
         pl.when(chip < p.chip)(lambda chip=chip: to_left(chip).wait_send())
 
 
 def back_call(n2g, state, cotangent, tokens, gain_one, gain_two, attn, q_heads, kv_heads, mask, cosine, sine,
-              qkv_all, out_full, n1_all, terms, owned):
+              qkv_all, out_full, n1_all, terms, owned, passing, early):
     chips = cosine.shape[0]
     grps = 4
     slots = 2 * chips
@@ -1157,15 +1214,16 @@
             struct((half, width + HD), wide),
             struct((unit, width), wide),
             struct((2, 1, width), wide),
-            struct((3, block, width), wide),
+            struct((3, block, width), low),
+            struct((3, block, width), low),
         ),
-        in_specs=[vspec] * 13 + [anyspace] * 4,
-        out_specs=(vspec,) * 5,
+        in_specs=[vspec] * 13 + [anyspace] * 6,
+        out_specs=(vspec,) * 4 + (anyspace,) * 2,
         scratch_shapes=[
             vm((att, width), low),
-            vm((chips, 2, shard, width), low),
+            vm((grps, shard, width), low),
             vm((chips, shard, width + HD), low),
-            vm((grps, unit, slots * shard), low),
+            vm((grps, shard, slots * unit), low),
             vm((chips, 3, shard, HD), low),
             vm((chips, 3, shard, HD), low),
             vm((chips, 2, chips, shard, HD), low),
@@ -1181,27 +1239,29 @@
             vm((grps, half, width + HD), wide),
             vm((grps, half, width + HD), low),
             vm((grps, half, width + HD), low),
-            vm((grps, unit, width), wide),
-            vm((grps, unit, width), low),
-            vm((grps, unit, width), low),
-            vm((4, 3, block // 2, width), low),
-            vm((6, 3, block // 2, width), low),
+            vm((chips, 2, unit, width), wide),
+            vm((chips, unit, width), wide),
+            vm((chips, unit, width), low),
+            vm((chips, unit, width), low),
+            vm((2, 3, block // 2, width), low),
+            vm((2, 3, block // 2, width), low),
             vm((2, 1, width), wide),
             vm((slots, 2, 1, width), wide),
             vm((2, 1, width), wide),
             vm((grps, 2, 1, width), wide),
             vm((shard, width), wide),
             dma((3,)),
-            dma((3, chips)), dma((chips, 2)),
+            dma((grps,)), dma((grps,)),
             dma((chips,)), dma((chips,)),
             dma((chips,)), dma((chips,)),
             dma((chips,)), dma((chips,)),
             dma((2, chips)), dma((2, chips)),
             dma, dma,
             dma((grps,)), dma((grps,)),
-            dma((grps,)), dma((grps,)),
-            dma((6,)), dma((6,)),
-            dma((4,)),
+            dma, dma,
+            dma((chips,)), dma((chips,)),
+            dma((6, 3)), dma((6, 3)),
+            dma((5, 3)),
             dma((slots,)), dma((slots,)),
             dma((grps,)), dma((grps,)),
         ],
@@ -1210,7 +1270,7 @@
         ),
         name="back",
     )(n2g, state, cotangent, tokens, gain_one, gain_two, attn, q_heads, kv_heads, mask, cosine, sine,
-      qkv_all, out_full, n1_all, terms, owned)
+      qkv_all, out_full, n1_all, terms, owned, passing, early)
 
 
 def columns_to_owners(rows, row_unit):
@@ -1321,14 +1381,18 @@
             own_rows,
         )
         by_slot = lambda rows: rows.reshape((seq_count,) + rows.shape[2:])
-        grad_part, out_part, mlp_terms, owned = mlp_call(
+        grad_part, out_part, mlp_terms, owned, passing, early = mlp_call(
             by_slot(n2_all), by_slot(cot_all), columns, [own_rows, *peer_rows]
         )
         output = (state + out_part).astype(jnp.bfloat16)
-        token_grad, qkv_terms, out_grad, gain_sums, mlp_sums = back_call(
+        token_grad, qkv_terms, out_grad, gain_sums, direct, second = back_call(
             grad_part, state, cotangent, tokens, *gain_rows, attn_wide, q_heads, kv_heads, mask,
             cosine, sine, qkv_all.reshape(-1, qkv_all.shape[-1]),
-            out_all.reshape(att_width, -1), n1_all, mlp_terms, owned,
+            out_all.reshape(att_width, -1), n1_all, mlp_terms, owned, passing, early,
+        )
+        units = mlp_weight.shape[0]
+        mlp_sums = sum(
+            rows[:, :units].astype(jnp.float32) for rows in (mlp_terms, direct, second)
         )
         width = tokens.shape[1]
         own = width // (grp_count * seq_count)
@@ -1343,7 +1407,7 @@
             qkv_terms[:, width],
             out_grad,
             gain_parts[1],
-            mlp_sums[:, : mlp_weight.shape[0]].transpose(1, 0, 2),
+            mlp_sums.transpose(1, 0, 2),
         )
     segments = lax.dynamic_index_in_dim(shard_segment, grp_place, 0, keepdims=False)
     starts = shard_starts(segments, tok_rows, group_tok // 2)

time: 342 us -> 330 us (0.965)
  Pallas kernels: 323 us -> 309 us
  other arithmetic: 1.43 us -> 8.17 us
  local copies, waits for them, and re-layouts: 14.3 us -> 8.96 us
    pallas_call x1, Pallas kernels: 115 us -> 95.6 us  [back_call(): pl.pallas_call(functools.partial(back_kernel, chips, 1.0 / math.sqrt(HD))...]
    pallas_call x1, Pallas kernels: 77.2 us -> 84.1 us  [mlp_call(): pl.pallas_call(functools.partial(mlp_kernel, chips, grps, row_tiles), out...]
    transpose x0 -> x1, other arithmetic: none -> 6.74 us  [per_device(): mlp_sums.transpose(1, 0, 2)]
    transpose x1 -> x0, local copies, waits for them, and re-layouts: 5.29 us -> none  [per_device(): mlp_sums[:, :mlp_weight.shape[0]].transpose(1, 0, 2)]
where the time goes in v8:
time: 330 us; the launch traced here: 327 us
  Pallas kernels  309 us (94%)
  local copies, waits for them, and re-layouts  8.96 us (3%)
  other arithmetic  8.17 us (2%)
    pallas_call x1, Pallas kernels, front_call(): pl.pallas_call(functools.partial(front_kernel, chips, 1.0 / math.sqrt(HD)...  129 us
    pallas_call x1, Pallas kernels, back_call(): pl.pallas_call(functools.partial(back_kernel, chips, 1.0 / math.sqrt(HD))...  95.6 us
    pallas_call x1, Pallas kernels, mlp_call(): pl.pallas_call(functools.partial(mlp_kernel, chips, grps, row_tiles), out...  84.1 us
    transpose x1, other arithmetic, per_device(): mlp_sums.transpose(1, 0, 2)  6.74 us

profile of v8, /device:TPU:9, one launch (start us, length us, event | category | flops | bytes accessed | tf_op | source)
XLA Modules:
  0.0 326.7 jit_solution(1831620887674633151)
XLA Ops:
  0.6 0.0 copy-start.5
  0.6 0.0 copy-start.6
  0.7 3.5 %pad.4.wm_ref.refs_0_ = bf16[3,288,1536]{2,1,0:T(8,128)(2,1)} pad(bf16[3,280,1536]{2,1,0:T(8,128)(2,1)} %bitcast.17, bf16[]{:T(256)} %constant.9.clone.1), padding=0_0x0_8x0_0 | pad | bytes 5234690 | tf_op jit(solution)/shard_map/jit(_pad)/pad | solution.py:1343
  4.1 0.0 copy-done.5
  4.2 0.6 broadcast_in_dim.12.gain_one_ref
  4.8 0.0 copy-done.6
  4.8 0.6 broadcast_in_dim.13.gain_two_ref
  5.4 0.6 maximum_bitcast_fusion.freq_ref
  6.0 129.3 %front.1 = (f32[128,1536]{1,0:T(8,128)}, f32[128,1536]{1,0:T(8,128)}, f32[4,128,128]{2,1,0:T(8,128)}, f32[4,128,128]{2,1,0:T(8,128)}, f32[128,1024]{1,0:T(8,128)...) custom-call(bf16[128,1536]{1,0:T(8,128)(2,1)} %tokens_ref.3, ...), custom_call_target="tpu_custom_call" | custom-call | tf_op jit(solution)/shard_map/front/pallas_call | solution.py:568
  135.2 84.1 %mlp.1 = (f32[128,1536]{1,0:T(8,128)}, f32[128,1536]{1,0:T(8,128)}, bf16[3,1152,1536]{2,1,0:T(8,128)(2,1)}, bf16[4,128,384]{2,1,0:T(8,128)(2,1)}, bf16[2,3,144,1...) custom-call(bf16[8,128,1536]{2,1,0:T(8,128)(2,1)} %bitcast.15, bf16[8,128,1536]{2,1,0:T(8,128)(2,1)} %bitcast.16, ...), custom_call_target="tpu_custom_call" | custom-call | tf_op jit(solution)/shard_map/mlp/pallas_call | solution.py:794
  219.3 95.6 %back.1 = (f32[128,1536]{1,0:T(8,128)}, f32[64,1664]{1,0:T(8,128)}, f32[48,1536]{1,0:T(8,128)}, f32[2,1,1536]{2,1,0:T(1,128)}, bf16[3,288,1536]{2,1,0:T(8,128)(2,1)}, /*index=5*/bf16[3,288,1536]{2,1,0:T(8,128)(2,1)}) custom-call(f32[128,1536]{1,0:T(8,128)} %get-tuple-element.44.n2g_ref, f32[128,1536]{1,0:T(8,128)} %get-tuple-element.36.state_ref, ...), custom_call_target="tpu_custom_call" | custom-call | tf_op jit(solution)/shard_map/back/pallas_call | solution.py:1210
  314.9 0.0 copy-start.3
  314.9 0.0 copy-start
  314.9 0.0 copy-start.2
  314.9 6.7 %add_bitcast_fusion = f32[280,3,1536]{2,0,1:T(8,128)} fusion(bf16[3,288,1536]{2,1,0:T(8,128)(2,1)} %get-tuple-element.63, bf16[3,288,1536]{2,1,0:T(8,128)(2,1)} %get-tuple-element.62, bf16[3,1152,1536]{2,1,0:T(8,128)(2,1)} %get-tuple-element.54.terms_ref), kind=kLoop, calls=%fused_computation | loop fusion | flops 6451200 | bytes 12902400 | tf_op jit(solution)/shard_map/transpose | solution.py:1410
  321.6 0.0 copy-start.1
  321.7 0.0 copy-start.4
  321.7 0.0 copy-done.3
  321.7 0.8 slice.24
  322.4 1.3 dynamic-slice_bitcast_fusion
  323.7 0.6 slice_reduce_fusion
  324.3 0.0 copy-done
  324.3 0.0 copy-done.2
  324.3 0.8 add_convert_fusion
  325.1 0.0 copy-done.1
  325.1 0.9 copy.19
  326.0 0.0 copy-done.4
  326.0 0.7 copy.20
  (1 shorter events, 0.0 us)
Async XLA Ops:
  0.6 3.5 %copy-start.5 = (bf16[1536]{0:T(1024)(128)(2,1)S(1)}, bf16[1536]{0:T(1024)(128)(2,1)}, u32[]{:S(2)}) copy-start(bf16[1536]{0:T(1024)(128)(2,1)} %param.12) | copy-start | bytes 9220
  0.6 4.1 %copy-start.6 = (bf16[1536]{0:T(1024)(128)(2,1)S(1)}, bf16[1536]{0:T(1024)(128)(2,1)}, u32[]{:S(2)}) copy-start(bf16[1536]{0:T(1024)(128)(2,1)} %param.16) | copy-start | bytes 9220
  314.9 6.8 %copy-start.3 = (f32[64,1664]{1,0:T(8,128)S(1)}, f32[64,1664]{1,0:T(8,128)}, u32[]{:S(2)}) copy-start(f32[64,1664]{1,0:T(8,128)} %get-tuple-element.60) | copy-start | bytes 1277956
  314.9 9.4 %copy-start = (f32[128,1536]{1,0:T(8,128)S(1)}, f32[128,1536]{1,0:T(8,128)}, u32[]{:S(2)}) copy-start(f32[128,1536]{1,0:T(8,128)} %get-tuple-element.36.state_ref) | copy-start | bytes 2359300
  314.9 9.4 %copy-start.2 = (f32[128,1536]{1,0:T(8,128)S(1)}, f32[128,1536]{1,0:T(8,128)}, u32[]{:S(2)}) copy-start(f32[128,1536]{1,0:T(8,128)} %get-tuple-element.43) | copy-start | bytes 2359300
  321.6 3.5 %copy-start.1 = (f32[128,1536]{1,0:T(8,128)S(1)}, f32[128,1536]{1,0:T(8,128)}, u32[]{:S(2)}) copy-start(f32[128,1536]{1,0:T(8,128)} %get-tuple-element.75) | copy-start | bytes 2359300
  321.7 4.4 %copy-start.4 = (f32[48,1536]{1,0:T(8,128)S(1)}, f32[48,1536]{1,0:T(8,128)}, u32[]{:S(2)}) copy-start(f32[48,1536]{1,0:T(8,128)} %get-tuple-element.79) | copy-start | bytes 884740

commit v9 on v8

--- a/solution.py
+++ b/solution.py
@@ -895,7 +895,9 @@
             i = FIRST_HOPS[hop][1]
             m_loads.append(pltpu.make_async_copy(passing_ref.at[i, kind], m_in.at[i, kind], ml_sem.at[2 + i, kind]))
     early_copies = [
-        pltpu.make_async_copy(early_ref.at[kind // 2], direct_ref.at[kind], ml_sem.at[4, kind]) for kind in (0, 2)
+        pltpu.make_async_copy(early_ref.at[kind // 2], direct_ref.at[kind], ml_sem.at[4, kind])
+        for kind in (0, 2)
+        if (0, kind) in EARLY_HOPS
     ]
     for copy in early_copies:
         copy.start()
@@ -953,13 +955,19 @@
     def kr_arrival(chip):
         return remote(k_sum.at[chip], kr_in.at[chip], kr_send.at[chip], kr_recv.at[chip], p.grp, p.mate)
 
-    def q_copy(chip):
+    q_parts = (pl.ds(0, 1), pl.ds(1, 2))
+
+    def q_copy(chip, i):
         return remote(
-            dq_stage.at[chip], gq_in.at[p.chip], q_send.at[chip], q_recv.at[p.chip], p.grp, 2 * chip + p.core
-        )
-
-    def q_arrival(chip):
-        return remote(dq_stage.at[chip], gq_in.at[chip], q_send.at[chip], q_recv.at[chip], p.grp, p.mate)
+            dq_stage.at[chip, q_parts[i]], gq_in.at[p.chip, q_parts[i]], q_send.at[chip, i],
+            q_recv.at[p.chip, i], p.grp, 2 * chip + p.core,
+        )
+
+    def q_arrival(chip, i):
+        return remote(
+            dq_stage.at[chip, q_parts[i]], gq_in.at[chip, q_parts[i]], q_send.at[chip, i],
+            q_recv.at[chip, i], p.grp, p.mate,
+        )
 
     def key_sum(head):
         km_copy(head).wait_recv()
@@ -1003,6 +1011,8 @@
             def _(turned=turned, h=h):
                 gq_in[h % chips, h // chips] = turned
 
+        for chip in range(chips):
+            pl.when(chip != p.chip)(lambda chip=chip: q_copy(chip, kv).start())
         if kv == 0:
             for copy in m_loads:
                 copy.wait()
@@ -1010,19 +1020,29 @@
             m_turn(0)
             for b in range(1, grps):
                 state_copy(b).start()
-    for chip in range(chips):
-        pl.when(chip != p.chip)(lambda chip=chip: q_copy(chip).start())
-    for head in (0, 2, 1, 3):
-        key_sum(head)
+            key_sum(0)
+            key_sum(KVH)
+    key_sum(1)
+    key_sum(KVH + 1)
     m_turn(1)
     loads[1].wait()
     lane = lax.broadcasted_iota(jnp.int32, (chips, shard, HD), 2)
     n1x[:, :, width:] = jnp.where(lane == 0, 1.0, 0.0).astype(low)
 
     for chip in range(chips):
-        pl.when(chip != p.chip)(lambda chip=chip: q_arrival(chip).wait_recv())
+        for i in (0, 1):
+            pl.when(chip != p.chip)(lambda chip=chip, i=i: q_arrival(chip, i).wait_recv())
         pl.when(chip != p.chip)(lambda chip=chip: kr_arrival(chip).wait_recv())
     is_value = jnp.where(p.chip >= chips // 2, 1.0, 0.0)
+
+    gain_one = gain_one_ref[...].astype(wide)
+    gain_own[0] = jnp.zeros_like(gain_own[0])
+
+    def to_right(chip):
+        return remote(part.at[chip], left_in.at[chip], r_send.at[0, chip], r_recv.at[0, chip], p.grp, p.seq + 2)
+
+    def to_left(chip):
+        return remote(part.at[chip], right_in.at[chip], r_send.at[1, chip], r_recv.at[1, chip], p.grp, p.seq - 2)
 
     @pl.loop(0, chips)
     def _(order):
@@ -1036,35 +1056,36 @@
             place = p.peer(b)
             query_head = gq_in[chip, jnp.minimum(place, grps - 2)]
             cols[chip, :, b * HD : (b + 1) * HD] = jnp.where(place == grps - 1, last_head, query_head)
-        part[chip] = jnp.dot(
-            cols[chip], wq_ref[...], preferred_element_type=wide
-        ).astype(low)
-
-    def to_right(chip):
-        return remote(part.at[chip], left_in.at[chip], r_send.at[0, chip], r_recv.at[0, chip], p.grp, p.seq + 2)
-
-    def to_left(chip):
-        return remote(part.at[chip], right_in.at[chip], r_send.at[1, chip], r_recv.at[1, chip], p.grp, p.seq - 2)
+        terms = jnp.dot(cols[chip], wq_ref[...], preferred_element_type=wide)
+        part[chip] = terms.astype(low)
+        gain_own[0] += jnp.sum(terms * n1x[chip, :, 0:width].astype(wide), axis=0, keepdims=True)
+        pl.when((p.chip == 0) & (chip > 0))(lambda: to_right(chip).start())
+        pl.when((p.chip == last) & (chip < last))(lambda: to_left(chip).start())
+
+    gain_own[0] = gain_own[0] / gain_one
+
+    def g_copy(i):
+        return remote(gain_own, gain_in.at[i], g_send.at[i], g_recv.at[i], p.grp, seq_peer(i))
+
+    def h_copy(b):
+        return remote(gain_mid, gain_mid_in.at[b], h_send.at[b], h_recv.at[b], p.peer(b), p.seq)
+
+    for i in range(1, slots):
+        g_copy(i).start()
 
     def rail_step(order):
         far = last - order
 
-        @pl.when(far > p.chip)
+        @pl.when((far > p.chip) & (p.chip > 0))
         def _():
-            @pl.when(p.chip > 0)
-            def _():
-                to_right(far).wait_recv()
-                part[far] = (part[far].astype(wide) + left_in[far].astype(wide)).astype(low)
-
+            to_right(far).wait_recv()
+            part[far] = (part[far].astype(wide) + left_in[far].astype(wide)).astype(low)
             to_right(far).start()
 
-        @pl.when(order < p.chip)
+        @pl.when((order < p.chip) & (p.chip < last))
         def _():
-            @pl.when(p.chip < last)
-            def _():
-                to_left(order).wait_recv()
-                part[order] = (part[order].astype(wide) + right_in[order].astype(wide)).astype(low)
-
+            to_left(order).wait_recv()
+            part[order] = (part[order].astype(wide) + right_in[order].astype(wide)).astype(low)
             to_left(order).start()
 
     rail_step(0)
@@ -1107,45 +1128,34 @@
     for chip in range(chips):
         pl.when(chip != p.chip)(lambda chip=chip: o_copy(chip).start())
     rail_step(3)
-
-    tokens = tokens_ref[...].astype(wide)
-    tok_grad_ref[...] = part[p.chip].astype(wide)
-
-    @pl.when(p.chip > 0)
-    def _():
-        to_right(p.chip).wait_recv()
-        tok_grad_ref[...] += left_in[p.chip].astype(wide)
-
-    @pl.when(p.chip < last)
-    def _():
-        to_left(p.chip).wait_recv()
-        tok_grad_ref[...] += right_in[p.chip].astype(wide)
-
-    n1g = tok_grad_ref[...]
-    scale_one = lax.rsqrt(jnp.mean(tokens * tokens, axis=-1, keepdims=True) + EPS)
-    normed = tokens * scale_one
-    gain_own[0] = jnp.sum(n1g * normed, axis=0, keepdims=True)
-    lifted = n1g * gain_one_ref[...].astype(wide)
-    tok_grad_ref[...] = state_grad[...] + scale_one * (
-        lifted - normed * jnp.mean(lifted * normed, axis=-1, keepdims=True)
-    )
-
-    def g_copy(i):
-        return remote(gain_own, gain_in.at[i], g_send.at[i], g_recv.at[i], p.grp, seq_peer(i))
-
-    for i in range(1, slots):
-        g_copy(i).start()
     total = gain_own[...]
     for i in range(1, slots):
         g_copy(i).wait_recv()
         total = total + gain_in[i]
     gain_mid[...] = total
-
-    def h_copy(b):
-        return remote(gain_mid, gain_mid_in.at[b], h_send.at[b], h_recv.at[b], p.peer(b), p.seq)
-
     for b in range(1, grps):
         h_copy(b).start()
+
+    tokens = tokens_ref[...].astype(wide)
+    tok_grad_ref[...] = part[p.chip].astype(wide)
+
+    @pl.when(p.chip > 0)
+    def _():
+        to_right(p.chip).wait_recv()
+        tok_grad_ref[...] += left_in[p.chip].astype(wide)
+
+    @pl.when(p.chip < last)
+    def _():
+        to_left(p.chip).wait_recv()
+        tok_grad_ref[...] += right_in[p.chip].astype(wide)
+
+    n1g = tok_grad_ref[...]
+    scale_one = lax.rsqrt(jnp.mean(tokens * tokens, axis=-1, keepdims=True) + EPS)
+    normed = tokens * scale_one
+    lifted = n1g * gain_one
+    tok_grad_ref[...] = state_grad[...] + scale_one * (
+        lifted - normed * jnp.mean(lifted * normed, axis=-1, keepdims=True)
+    )
 
     wq_grad = wgrad[0, p.core] + wm_in[0]
     for b in range(1, grps):
@@ -1186,7 +1196,8 @@
 
         @pl.when(chip != p.chip)
         def _(chip=chip):
-            q_copy(chip).wait_send()
+            q_copy(chip, 0).wait_send()
+            q_copy(chip, 1).wait_send()
             kr_copy(chip).wait_send()
             o_copy(chip).wait_send()
 
@@ -1252,7 +1263,7 @@
             vm((shard, width), wide),
             dma((3,)),
             dma((grps,)), dma((grps,)),
-            dma((chips,)), dma((chips,)),
+            dma((chips, 2)), dma((chips, 2)),
             dma((chips,)), dma((chips,)),
             dma((chips,)), dma((chips,)),
             dma((2, chips)), dma((2, chips)),

time: 330 us -> 323 us (0.979)
  Pallas kernels: 309 us -> 302 us
    pallas_call x1, Pallas kernels: 95.6 us -> 88.8 us  [back_call(): pl.pallas_call(functools.partial(back_kernel, chips, 1.0 / math.sqrt(HD))...]
where the time goes in v9:
time: 323 us; the launch traced here: 320 us
  Pallas kernels  302 us (93%)
  local copies, waits for them, and re-layouts  8.96 us (3%)
  other arithmetic  8.17 us (3%)
    pallas_call x1, Pallas kernels, front_call(): pl.pallas_call(functools.partial(front_kernel, chips, 1.0 / math.sqrt(HD)...  129 us
    pallas_call x1, Pallas kernels, back_call(): pl.pallas_call(functools.partial(back_kernel, chips, 1.0 / math.sqrt(HD))...  88.8 us
    pallas_call x1, Pallas kernels, mlp_call(): pl.pallas_call(functools.partial(mlp_kernel, chips, grps, row_tiles), out...  84.1 us
    transpose x1, other arithmetic, per_device(): mlp_sums.transpose(1, 0, 2)  6.74 us

profile of v9, /device:TPU:9, one launch (start us, length us, event | category | flops | bytes accessed | tf_op | source)
XLA Modules:
  0.0 320.0 jit_solution(7194860238949435491)
XLA Ops:
  0.6 0.0 copy-start.5
  0.6 0.0 copy-start.6
  0.7 3.5 %pad.4.wm_ref.refs_0_ = bf16[3,288,1536]{2,1,0:T(8,128)(2,1)} pad(bf16[3,280,1536]{2,1,0:T(8,128)(2,1)} %bitcast.17, bf16[]{:T(256)} %constant.9.clone.1), padding=0_0x0_8x0_0 | pad | bytes 5234690 | tf_op jit(solution)/shard_map/jit(_pad)/pad | solution.py:1354
  4.1 0.0 copy-done.5
  4.2 0.6 broadcast_in_dim.12.gain_one_ref
  4.8 0.0 copy-done.6
  4.8 0.6 broadcast_in_dim.13.gain_two_ref
  5.4 0.6 maximum_bitcast_fusion.freq_ref
  6.0 129.3 %front.1 = (f32[128,1536]{1,0:T(8,128)}, f32[128,1536]{1,0:T(8,128)}, f32[4,128,128]{2,1,0:T(8,128)}, f32[4,128,128]{2,1,0:T(8,128)}, f32[128,1024]{1,0:T(8,128)...) custom-call(bf16[128,1536]{1,0:T(8,128)(2,1)} %tokens_ref.3, ...), custom_call_target="tpu_custom_call" | custom-call | tf_op jit(solution)/shard_map/front/pallas_call | solution.py:568
  135.2 84.1 %mlp.1 = (f32[128,1536]{1,0:T(8,128)}, f32[128,1536]{1,0:T(8,128)}, bf16[3,1152,1536]{2,1,0:T(8,128)(2,1)}, bf16[4,128,384]{2,1,0:T(8,128)(2,1)}, bf16[2,3,144,1...) custom-call(bf16[8,128,1536]{2,1,0:T(8,128)(2,1)} %bitcast.15, bf16[8,128,1536]{2,1,0:T(8,128)(2,1)} %bitcast.16, ...), custom_call_target="tpu_custom_call" | custom-call | tf_op jit(solution)/shard_map/mlp/pallas_call | solution.py:794
  219.3 88.8 %back.1 = (f32[128,1536]{1,0:T(8,128)}, f32[64,1664]{1,0:T(8,128)}, f32[48,1536]{1,0:T(8,128)}, f32[2,1,1536]{2,1,0:T(1,128)}, bf16[3,288,1536]{2,1,0:T(8,128)(2,1)}, /*index=5*/bf16[3,288,1536]{2,1,0:T(8,128)(2,1)}) custom-call(f32[128,1536]{1,0:T(8,128)} %get-tuple-element.44.n2g_ref, f32[128,1536]{1,0:T(8,128)} %get-tuple-element.36.state_ref, ...), custom_call_target="tpu_custom_call" | custom-call | tf_op jit(solution)/shard_map/back/pallas_call | solution.py:1221
  308.1 0.0 copy-start.3
  308.1 0.0 copy-start
  308.1 0.0 copy-start.2
  308.2 6.7 %add_bitcast_fusion = f32[280,3,1536]{2,0,1:T(8,128)} fusion(bf16[3,288,1536]{2,1,0:T(8,128)(2,1)} %get-tuple-element.63, bf16[3,288,1536]{2,1,0:T(8,128)(2,1)} %get-tuple-element.62, bf16[3,1152,1536]{2,1,0:T(8,128)(2,1)} %get-tuple-element.54.terms_ref), kind=kLoop, calls=%fused_computation | loop fusion | flops 6451200 | bytes 12902400 | tf_op jit(solution)/shard_map/transpose | solution.py:1421
  314.9 0.0 copy-start.1
  314.9 0.0 copy-start.4
  314.9 0.0 copy-done.3
  314.9 0.8 slice.24
  315.7 1.3 dynamic-slice_bitcast_fusion
  316.9 0.6 slice_reduce_fusion
  317.6 0.0 copy-done
  317.6 0.0 copy-done.2
  317.6 0.8 add_convert_fusion
  318.4 0.0 copy-done.1
  318.4 0.9 copy.19
  319.3 0.0 copy-done.4
  319.3 0.7 copy.20
  (1 shorter events, 0.0 us)
Async XLA Ops:
  0.6 3.5 %copy-start.5 = (bf16[1536]{0:T(1024)(128)(2,1)S(1)}, bf16[1536]{0:T(1024)(128)(2,1)}, u32[]{:S(2)}) copy-start(bf16[1536]{0:T(1024)(128)(2,1)} %param.12) | copy-start | bytes 9220
  0.6 4.1 %copy-start.6 = (bf16[1536]{0:T(1024)(128)(2,1)S(1)}, bf16[1536]{0:T(1024)(128)(2,1)}, u32[]{:S(2)}) copy-start(bf16[1536]{0:T(1024)(128)(2,1)} %param.16) | copy-start | bytes 9220
  308.1 6.8 %copy-start.3 = (f32[64,1664]{1,0:T(8,128)S(1)}, f32[64,1664]{1,0:T(8,128)}, u32[]{:S(2)}) copy-start(f32[64,1664]{1,0:T(8,128)} %get-tuple-element.60) | copy-start | bytes 1277956
  308.1 9.4 %copy-start = (f32[128,1536]{1,0:T(8,128)S(1)}, f32[128,1536]{1,0:T(8,128)}, u32[]{:S(2)}) copy-start(f32[128,1536]{1,0:T(8,128)} %get-tuple-element.36.state_ref) | copy-start | bytes 2359300
  308.1 9.4 %copy-start.2 = (f32[128,1536]{1,0:T(8,128)S(1)}, f32[128,1536]{1,0:T(8,128)}, u32[]{:S(2)}) copy-start(f32[128,1536]{1,0:T(8,128)} %get-tuple-element.43) | copy-start | bytes 2359300
  314.9 3.5 %copy-start.1 = (f32[128,1536]{1,0:T(8,128)S(1)}, f32[128,1536]{1,0:T(8,128)}, u32[]{:S(2)}) copy-start(f32[128,1536]{1,0:T(8,128)} %get-tuple-element.75) | copy-start | bytes 2359300
  314.9 4.4 %copy-start.4 = (f32[48,1536]{1,0:T(8,128)S(1)}, f32[48,1536]{1,0:T(8,128)}, u32[]{:S(2)}) copy-start(f32[48,1536]{1,0:T(8,128)} %get-tuple-element.79) | copy-start | bytes 884740

commit v10 on v9

--- a/solution.py
+++ b/solution.py
@@ -737,36 +737,50 @@
         pl.when(t >= 2)(lambda: out_copy(t - 2).wait())
         tile_grad(t)
 
+    @pl.loop(0, chips)
+    def _(order):
+        at = far_chip(order)
+        y = tok[1, pl.ds(2 * at, 2)].reshape(2 * shard, width)
+        unit_grad = lax.dot_general(y, w[2], CONTRACT_LAST, preferred_element_type=jnp.float32)
+        rows = pl.ds(at * (2 * shard), 2 * shard)
+        acts[0, rows] = (unit_grad * acts[0, rows].astype(jnp.float32)).astype(jnp.bfloat16)
+        acts[1, rows] = (unit_grad * acts[1, rows].astype(jnp.float32)).astype(jnp.bfloat16)
+
+        @pl.when(order == 0)
+        def _():
+            out_copy(row_tiles - 2).wait()
+            out_copy(row_tiles - 1).wait()
+            start_early(2)
+
     @pl.loop(0, chips + 1)
     def _(order):
         @pl.when(order < chips)
         def _():
             at = far_chip(order)
-            y = tok[1, pl.ds(2 * at, 2)].reshape(2 * shard, width)
-            unit_grad = lax.dot_general(y, w[2], CONTRACT_LAST, preferred_element_type=jnp.float32)
             rows = pl.ds(at * (2 * shard), 2 * shard)
-            gate_grad = (unit_grad * acts[0, rows].astype(jnp.float32)).astype(jnp.bfloat16)
-            up_grad = (unit_grad * acts[1, rows].astype(jnp.float32)).astype(jnp.bfloat16)
-            acts[0, rows] = gate_grad
-            acts[1, rows] = up_grad
-            back = jnp.dot(gate_grad, w[0], preferred_element_type=jnp.float32) + jnp.dot(
-                up_grad, w[1], preferred_element_type=jnp.float32
+            back = jnp.dot(acts[0, rows], w[0], preferred_element_type=jnp.float32) + jnp.dot(
+                acts[1, rows], w[1], preferred_element_type=jnp.float32
             )
             part[0, pl.ds(2 * at, 2)] = back.astype(jnp.bfloat16).reshape(2, shard, width)
             scatter.to_mate(0, at).start()
 
-        @pl.when(order == 1)
+        @pl.when(order < row_tiles)
         def _():
-            out_copy(row_tiles - 2).wait()
-            out_copy(row_tiles - 1).wait()
-            start_early(2)
+            t = row_tiles + order
+            pl.when(order >= 2)(lambda: out_copy(t - 2).wait())
+            tile_grad(t)
+
+        @pl.when(order == row_tiles)
+        def _():
+            out_copy(2 * row_tiles - 2).wait()
+            out_copy(2 * row_tiles - 1).wait()
+            start_early(0)
 
         pl.when(order > 0)(lambda: scatter.step(0, far_chip(order - 1)))
 
-    @pl.loop(row_tiles, 3 * row_tiles)
+    @pl.loop(2 * row_tiles, 3 * row_tiles)
     def _(t):
-        pl.when(t >= row_tiles + 2)(lambda: out_copy(t - 2).wait())
-        pl.when(t == 2 * row_tiles + 1)(lambda: start_early(0))
+        pl.when(t >= 2 * row_tiles + 2)(lambda: out_copy(t - 2).wait())
         tile_grad(t)
 
     scatter.finish(0, n2g_ref)
@@ -833,7 +847,7 @@
                 tok_grad_ref, wq_grad_ref, wo_grad_ref, gain_ref, direct_ref, second_ref,
                 wo, stbuf, n1x, at_all, dq_stage, gq_in, kv_part, km_in, k_sum, k_own, kr_in,
                 cols, part, left_in, right_in, wgrad, wm_in, w_send_buf, w_in, o_terms, ob_in, o_send_buf, o_in,
-                m_own, m_in, gain_own, gain_in, gain_mid, gain_mid_in, state_grad,
+                m_own, m_in, early_rows, gain_own, gain_in, gain_mid, gain_mid_in, state_grad,
                 lsem, s_send, s_recv, q_send, q_recv, km_send, km_recv, kr_send, kr_recv,
                 r_send, r_recv, wm_send, wm_recv, w_send, w_recv, ob_send, ob_recv, o_send, o_recv, m_send, m_recv,
                 ml_sem, g_send, g_recv, h_send, h_recv):
@@ -894,13 +908,16 @@
         if FIRST_HOPS[hop][0] == 3:
             i = FIRST_HOPS[hop][1]
             m_loads.append(pltpu.make_async_copy(passing_ref.at[i, kind], m_in.at[i, kind], ml_sem.at[2 + i, kind]))
+    early_kinds = [kind for kind in (0, 2) if (0, kind) in EARLY_HOPS]
+    early_loads = [
+        pltpu.make_async_copy(early_ref.at[kind // 2], early_rows.at[kind // 2], ml_sem.at[4, kind])
+        for kind in early_kinds
+    ]
     early_copies = [
-        pltpu.make_async_copy(early_ref.at[kind // 2], direct_ref.at[kind], ml_sem.at[4, kind])
-        for kind in (0, 2)
-        if (0, kind) in EARLY_HOPS
+        pltpu.make_async_copy(early_rows.at[kind // 2], direct_ref.at[kind], ml_sem.at[4, kind])
+        for kind in early_kinds
     ]
-    for copy in early_copies:
-        copy.start()
+    m_loads += early_loads
     for copy in m_loads:
         copy.start()
 
@@ -1016,6 +1033,8 @@
         if kv == 0:
             for copy in m_loads:
                 copy.wait()
+            for copy in early_copies:
+                copy.start()
             m_turn(2)
             m_turn(0)
             for b in range(1, grps):
@@ -1256,6 +1275,7 @@
             vm((chips, unit, width), low),
             vm((2, 3, block // 2, width), low),
             vm((2, 3, block // 2, width), low),
+            vm((2, block, width), low),
             vm((2, 1, width), wide),
             vm((slots, 2, 1, width), wide),
             vm((2, 1, width), wide),

time: 323 us -> 317 us (0.981)
  Pallas kernels: 302 us -> 296 us
    pallas_call x1, Pallas kernels: 84.1 us -> 78.6 us  [mlp_call(): pl.pallas_call(functools.partial(mlp_kernel, chips, grps, row_tiles), out...]
where the time goes in v10:
time: 317 us; the launch traced here: 314 us
  Pallas kernels  296 us (93%)
  local copies, waits for them, and re-layouts  8.96 us (3%)
  other arithmetic  8.17 us (3%)
    pallas_call x1, Pallas kernels, front_call(): pl.pallas_call(functools.partial(front_kernel, chips, 1.0 / math.sqrt(HD)...  129 us
    pallas_call x1, Pallas kernels, back_call(): pl.pallas_call(functools.partial(back_kernel, chips, 1.0 / math.sqrt(HD))...  88 us
    pallas_call x1, Pallas kernels, mlp_call(): pl.pallas_call(functools.partial(mlp_kernel, chips, grps, row_tiles), out...  78.6 us
    transpose x1, other arithmetic, per_device(): mlp_sums.transpose(1, 0, 2)  6.74 us

profile of v10, /device:TPU:9, one launch (start us, length us, event | category | flops | bytes accessed | tf_op | source)
XLA Modules:
  0.0 313.7 jit_solution(11109992148199902687)
XLA Ops:
  0.6 0.0 copy-start.5
  0.6 0.0 copy-start.6
  0.7 3.5 %pad.4.wm_ref.refs_0_ = bf16[3,288,1536]{2,1,0:T(8,128)(2,1)} pad(bf16[3,280,1536]{2,1,0:T(8,128)(2,1)} %bitcast.17, bf16[]{:T(256)} %constant.9.clone.1), padding=0_0x0_8x0_0 | pad | bytes 5234690 | tf_op jit(solution)/shard_map/jit(_pad)/pad | solution.py:1374
  4.1 0.0 copy-done.5
  4.2 0.6 broadcast_in_dim.12.gain_one_ref
  4.8 0.0 copy-done.6
  4.8 0.6 broadcast_in_dim.13.gain_two_ref
  5.4 0.6 maximum_bitcast_fusion.freq_ref
  6.0 129.3 %front.1 = (f32[128,1536]{1,0:T(8,128)}, f32[128,1536]{1,0:T(8,128)}, f32[4,128,128]{2,1,0:T(8,128)}, f32[4,128,128]{2,1,0:T(8,128)}, f32[128,1024]{1,0:T(8,128)...) custom-call(bf16[128,1536]{1,0:T(8,128)(2,1)} %tokens_ref.3, ...), custom_call_target="tpu_custom_call" | custom-call | tf_op jit(solution)/shard_map/front/pallas_call | solution.py:568
  135.2 78.6 %mlp.1 = (f32[128,1536]{1,0:T(8,128)}, f32[128,1536]{1,0:T(8,128)}, bf16[3,1152,1536]{2,1,0:T(8,128)(2,1)}, bf16[4,128,384]{2,1,0:T(8,128)(2,1)}, bf16[2,3,144,1...) custom-call(bf16[8,128,1536]{2,1,0:T(8,128)(2,1)} %bitcast.15, bf16[8,128,1536]{2,1,0:T(8,128)(2,1)} %bitcast.16, ...), custom_call_target="tpu_custom_call" | custom-call | tf_op jit(solution)/shard_map/mlp/pallas_call | solution.py:808
  213.9 88.0 %back.1 = (f32[128,1536]{1,0:T(8,128)}, f32[64,1664]{1,0:T(8,128)}, f32[48,1536]{1,0:T(8,128)}, f32[2,1,1536]{2,1,0:T(1,128)}, bf16[3,288,1536]{2,1,0:T(8,128)(2,1)}, /*index=5*/bf16[3,288,1536]{2,1,0:T(8,128)(2,1)}) custom-call(f32[128,1536]{1,0:T(8,128)} %get-tuple-element.44.n2g_ref, f32[128,1536]{1,0:T(8,128)} %get-tuple-element.36.state_ref, ...), custom_call_target="tpu_custom_call" | custom-call | tf_op jit(solution)/shard_map/back/pallas_call | solution.py:1240
  301.8 0.0 copy-start.3
  301.9 0.0 copy-start
  301.9 0.0 copy-start.2
  301.9 6.7 %add_bitcast_fusion = f32[280,3,1536]{2,0,1:T(8,128)} fusion(bf16[3,288,1536]{2,1,0:T(8,128)(2,1)} %get-tuple-element.63, bf16[3,288,1536]{2,1,0:T(8,128)(2,1)} %get-tuple-element.62, bf16[3,1152,1536]{2,1,0:T(8,128)(2,1)} %get-tuple-element.54.terms_ref), kind=kLoop, calls=%fused_computation | loop fusion | flops 6451200 | bytes 12902400 | tf_op jit(solution)/shard_map/transpose | solution.py:1441
  308.6 0.0 copy-start.1
  308.6 0.0 copy-start.4
  308.6 0.0 copy-done.3
  308.6 0.8 slice.24
  309.4 1.3 dynamic-slice_bitcast_fusion
  310.7 0.6 slice_reduce_fusion
  311.3 0.0 copy-done
  311.3 0.0 copy-done.2
  311.3 0.8 add_convert_fusion
  312.1 0.0 copy-done.1
  312.1 0.9 copy.19
  313.0 0.0 copy-done.4
  313.0 0.7 copy.20
  (1 shorter events, 0.0 us)
Async XLA Ops:
  0.6 3.5 %copy-start.5 = (bf16[1536]{0:T(1024)(128)(2,1)S(1)}, bf16[1536]{0:T(1024)(128)(2,1)}, u32[]{:S(2)}) copy-start(bf16[1536]{0:T(1024)(128)(2,1)} %param.12) | copy-start | bytes 9220
  0.6 4.1 %copy-start.6 = (bf16[1536]{0:T(1024)(128)(2,1)S(1)}, bf16[1536]{0:T(1024)(128)(2,1)}, u32[]{:S(2)}) copy-start(bf16[1536]{0:T(1024)(128)(2,1)} %param.16) | copy-start | bytes 9220
  301.8 6.8 %copy-start.3 = (f32[64,1664]{1,0:T(8,128)S(1)}, f32[64,1664]{1,0:T(8,128)}, u32[]{:S(2)}) copy-start(f32[64,1664]{1,0:T(8,128)} %get-tuple-element.60) | copy-start | bytes 1277956
  301.9 9.4 %copy-start = (f32[128,1536]{1,0:T(8,128)S(1)}, f32[128,1536]{1,0:T(8,128)}, u32[]{:S(2)}) copy-start(f32[128,1536]{1,0:T(8,128)} %get-tuple-element.36.state_ref) | copy-start | bytes 2359300
  301.9 9.4 %copy-start.2 = (f32[128,1536]{1,0:T(8,128)S(1)}, f32[128,1536]{1,0:T(8,128)}, u32[]{:S(2)}) copy-start(f32[128,1536]{1,0:T(8,128)} %get-tuple-element.43) | copy-start | bytes 2359300
  308.6 3.5 %copy-start.1 = (f32[128,1536]{1,0:T(8,128)S(1)}, f32[128,1536]{1,0:T(8,128)}, u32[]{:S(2)}) copy-start(f32[128,1536]{1,0:T(8,128)} %get-tuple-element.75) | copy-start | bytes 2359300
  308.6 4.4 %copy-start.4 = (f32[48,1536]{1,0:T(8,128)S(1)}, f32[48,1536]{1,0:T(8,128)}, u32[]{:S(2)}) copy-start(f32[48,1536]{1,0:T(8,128)} %get-tuple-element.79) | copy-start | bytes 884740

commit v11 on v10

--- a/solution.py
+++ b/solution.py
@@ -637,8 +637,7 @@
         pltpu.make_async_copy(cot_ref, tok.at[1], lsem.at[1]),
         pltpu.make_async_copy(columns_ref.at[p.grp], owned_ref.at[0], lsem.at[2]),
     ]
-    for copy in loads:
-        copy.start()
+    loads[0].start()
 
     def w_copy(j, b):
         return pltpu.make_async_copy(w_refs[b].at[j], w.at[j, pl.ds(b * block, block)], wsem.at[j, b])
@@ -646,6 +645,8 @@
     for j in range(3):
         for b in range(grps):
             w_copy(j, b).start()
+    for copy in loads[1:]:
+        copy.start()
 
     barrier = pltpu.get_barrier_semaphore()
     inner = jnp.where((p.chip > 0) & (p.chip < chips - 1), 1, 0)
@@ -668,9 +669,8 @@
 
     for b in range(1, grps):
         a_copy(b).start()
-    for copy in loads:
-        copy.wait()
-    for j in range(3):
+    loads[0].wait()
+    for j in range(2):
         for b in range(grps):
             w_copy(j, b).wait()
 
@@ -708,6 +708,8 @@
 
     def far_chip(order):
         return nearest_chip(p.chip, chips - 1 - order, chips)
+
+    outer = (p.chip == 0) | (p.chip == chips - 1)
 
     @pl.loop(0, chips + 1)
     def _(order):
@@ -724,18 +726,28 @@
             acts[1, rows] = silu.astype(jnp.bfloat16)
             hidden = (silu * up).astype(jnp.bfloat16)
             acts[2, rows] = hidden
+
+            @pl.when(order == 0)
+            def _():
+                for b in range(grps):
+                    w_copy(2, b).wait()
+
             part[1, pl.ds(2 * at, 2)] = (
                 jnp.dot(hidden, w[2], preferred_element_type=jnp.float32)
                 .astype(jnp.bfloat16).reshape(2, shard, width)
             )
             scatter.to_mate(1, at).start()
 
-        pl.when(order > 0)(lambda: scatter.step(1, far_chip(order - 1)))
+        pl.when(outer & (order > 0))(lambda: scatter.step(1, far_chip(order - 1)))
+
+    for copy in loads[1:]:
+        copy.wait()
 
     @pl.loop(0, row_tiles)
     def _(t):
         pl.when(t >= 2)(lambda: out_copy(t - 2).wait())
         tile_grad(t)
+        pl.when(jnp.logical_not(outer))(lambda: scatter.step(1, far_chip(t)))
 
     @pl.loop(0, chips)
     def _(order):
@@ -776,11 +788,14 @@
             out_copy(2 * row_tiles - 1).wait()
             start_early(0)
 
-        pl.when(order > 0)(lambda: scatter.step(0, far_chip(order - 1)))
+        pl.when(outer & (order > 0))(lambda: scatter.step(0, far_chip(order - 1)))
+        pl.when(jnp.logical_not(outer) & (order >= 3))(lambda: scatter.step(0, far_chip(order - 3)))
 
     @pl.loop(2 * row_tiles, 3 * row_tiles)
     def _(t):
         pl.when(t >= 2 * row_tiles + 2)(lambda: out_copy(t - 2).wait())
+        late = t - 2 * row_tiles + chips + 1 - 3
+        pl.when(jnp.logical_not(outer) & (late < chips))(lambda: scatter.step(0, far_chip(late)))
         tile_grad(t)
 
     scatter.finish(0, n2g_ref)

time: 317 us -> 307 us (0.968)
  Pallas kernels: 296 us -> 286 us
    pallas_call x1, Pallas kernels: 78.6 us -> 70.9 us  [mlp_call(): pl.pallas_call(functools.partial(mlp_kernel, chips, grps, row_tiles), out...]
where the time goes in v11:
time: 307 us; the launch traced here: 304 us
  Pallas kernels  286 us (93%)
  local copies, waits for them, and re-layouts  8.96 us (3%)
  other arithmetic  8.17 us (3%)
    pallas_call x1, Pallas kernels, front_call(): pl.pallas_call(functools.partial(front_kernel, chips, 1.0 / math.sqrt(HD)...  129 us
    pallas_call x1, Pallas kernels, back_call(): pl.pallas_call(functools.partial(back_kernel, chips, 1.0 / math.sqrt(HD))...  86.2 us
    pallas_call x1, Pallas kernels, mlp_call(): pl.pallas_call(functools.partial(mlp_kernel, chips, grps, row_tiles), out...  70.9 us
    transpose x1, other arithmetic, per_device(): mlp_sums.transpose(1, 0, 2)  6.74 us

profile of v11, /device:TPU:9, one launch (start us, length us, event | category | flops | bytes accessed | tf_op | source)
XLA Modules:
  0.0 304.2 jit_solution(1077742711144311319)
XLA Ops:
  0.6 0.0 copy-start.5
  0.6 0.0 copy-start.6
  0.7 3.5 %pad.4.wm_ref.refs_0_ = bf16[3,288,1536]{2,1,0:T(8,128)(2,1)} pad(bf16[3,280,1536]{2,1,0:T(8,128)(2,1)} %bitcast.17, bf16[]{:T(256)} %constant.9.clone.1), padding=0_0x0_8x0_0 | pad | bytes 5234690 | tf_op jit(solution)/shard_map/jit(_pad)/pad | solution.py:1389
  4.1 0.0 copy-done.5
  4.2 0.6 broadcast_in_dim.12.gain_one_ref
  4.8 0.0 copy-done.6
  4.8 0.6 broadcast_in_dim.13.gain_two_ref
  5.4 0.6 maximum_bitcast_fusion.freq_ref
  6.0 129.3 %front.1 = (f32[128,1536]{1,0:T(8,128)}, f32[128,1536]{1,0:T(8,128)}, f32[4,128,128]{2,1,0:T(8,128)}, f32[4,128,128]{2,1,0:T(8,128)}, f32[128,1024]{1,0:T(8,128)...) custom-call(bf16[128,1536]{1,0:T(8,128)(2,1)} %tokens_ref.3, ...), custom_call_target="tpu_custom_call" | custom-call | tf_op jit(solution)/shard_map/front/pallas_call | solution.py:568
  135.2 70.9 %mlp.1 = (f32[128,1536]{1,0:T(8,128)}, f32[128,1536]{1,0:T(8,128)}, bf16[3,1152,1536]{2,1,0:T(8,128)(2,1)}, bf16[4,128,384]{2,1,0:T(8,128)(2,1)}, bf16[2,3,144,1...) custom-call(bf16[8,128,1536]{2,1,0:T(8,128)(2,1)} %bitcast.15, bf16[8,128,1536]{2,1,0:T(8,128)(2,1)} %bitcast.16, ...), custom_call_target="tpu_custom_call" | custom-call | tf_op jit(solution)/shard_map/mlp/pallas_call | solution.py:823
  206.1 86.2 %back.1 = (f32[128,1536]{1,0:T(8,128)}, f32[64,1664]{1,0:T(8,128)}, f32[48,1536]{1,0:T(8,128)}, f32[2,1,1536]{2,1,0:T(1,128)}, bf16[3,288,1536]{2,1,0:T(8,128)(2,1)}, /*index=5*/bf16[3,288,1536]{2,1,0:T(8,128)(2,1)}) custom-call(f32[128,1536]{1,0:T(8,128)} %get-tuple-element.44.n2g_ref, f32[128,1536]{1,0:T(8,128)} %get-tuple-element.36.state_ref, ...), custom_call_target="tpu_custom_call" | custom-call | tf_op jit(solution)/shard_map/back/pallas_call | solution.py:1255
  292.3 0.0 copy-start.3
  292.3 0.0 copy-start
  292.3 0.0 copy-start.2
  292.3 6.7 %add_bitcast_fusion = f32[280,3,1536]{2,0,1:T(8,128)} fusion(bf16[3,288,1536]{2,1,0:T(8,128)(2,1)} %get-tuple-element.63, bf16[3,288,1536]{2,1,0:T(8,128)(2,1)} %get-tuple-element.62, bf16[3,1152,1536]{2,1,0:T(8,128)(2,1)} %get-tuple-element.54.terms_ref), kind=kLoop, calls=%fused_computation | loop fusion | flops 6451200 | bytes 12902400 | tf_op jit(solution)/shard_map/transpose | solution.py:1456
  299.1 0.0 copy-start.1
  299.1 0.0 copy-start.4
  299.1 0.0 copy-done.3
  299.1 0.8 slice.24
  299.9 1.3 dynamic-slice_bitcast_fusion
  301.1 0.6 slice_reduce_fusion
  301.7 0.0 copy-done
  301.7 0.0 copy-done.2
  301.7 0.8 add_convert_fusion
  302.6 0.0 copy-done.1
  302.6 0.9 copy.19
  303.5 0.0 copy-done.4
  303.5 0.7 copy.20
  (1 shorter events, 0.0 us)
Async XLA Ops:
  0.6 3.5 %copy-start.5 = (bf16[1536]{0:T(1024)(128)(2,1)S(1)}, bf16[1536]{0:T(1024)(128)(2,1)}, u32[]{:S(2)}) copy-start(bf16[1536]{0:T(1024)(128)(2,1)} %param.12) | copy-start | bytes 9220
  0.6 4.1 %copy-start.6 = (bf16[1536]{0:T(1024)(128)(2,1)S(1)}, bf16[1536]{0:T(1024)(128)(2,1)}, u32[]{:S(2)}) copy-start(bf16[1536]{0:T(1024)(128)(2,1)} %param.16) | copy-start | bytes 9220
  292.3 6.8 %copy-start.3 = (f32[64,1664]{1,0:T(8,128)S(1)}, f32[64,1664]{1,0:T(8,128)}, u32[]{:S(2)}) copy-start(f32[64,1664]{1,0:T(8,128)} %get-tuple-element.60) | copy-start | bytes 1277956
  292.3 9.4 %copy-start = (f32[128,1536]{1,0:T(8,128)S(1)}, f32[128,1536]{1,0:T(8,128)}, u32[]{:S(2)}) copy-start(f32[128,1536]{1,0:T(8,128)} %get-tuple-element.36.state_ref) | copy-start | bytes 2359300
  292.3 9.4 %copy-start.2 = (f32[128,1536]{1,0:T(8,128)S(1)}, f32[128,1536]{1,0:T(8,128)}, u32[]{:S(2)}) copy-start(f32[128,1536]{1,0:T(8,128)} %get-tuple-element.43) | copy-start | bytes 2359300
  299.1 3.5 %copy-start.1 = (f32[128,1536]{1,0:T(8,128)S(1)}, f32[128,1536]{1,0:T(8,128)}, u32[]{:S(2)}) copy-start(f32[128,1536]{1,0:T(8,128)} %get-tuple-element.75) | copy-start | bytes 2359300
  299.1 4.4 %copy-start.4 = (f32[48,1536]{1,0:T(8,128)S(1)}, f32[48,1536]{1,0:T(8,128)}, u32[]{:S(2)}) copy-start(f32[48,1536]{1,0:T(8,128)} %get-tuple-element.79) | copy-start | bytes 884740

commit v12 on v11

--- a/solution.py
+++ b/solution.py
@@ -3,6 +3,7 @@
 
 import jax
 import jax.numpy as jnp
+import numpy as np
 from jax import lax
 from jax.experimental import pallas as pl
 from jax.experimental.pallas import tpu as pltpu
@@ -75,7 +76,8 @@
 def nearest_chip(place, order, chips):
     both = 2 * jnp.minimum(place, chips - 1 - place)
     offset = (order + 1) // 2
-    near = jnp.where(order % 2 == 1, place - offset, place + offset)
+    side = jnp.where((order % 2 == 1) == (place < chips - 1 - place), -1, 1)
+    near = place + side * offset
     rest = jnp.where(place < chips - 1 - place, order, chips - 1 - order)
     return jnp.where(order <= both, near, rest)
 
@@ -1107,20 +1109,29 @@
     for i in range(1, slots):
         g_copy(i).start()
 
+    def right_step(chip):
+        @pl.when((chip > p.chip) & (p.chip > 0))
+        def _():
+            to_right(chip).wait_recv()
+            part[chip] = (part[chip].astype(wide) + left_in[chip].astype(wide)).astype(low)
+            to_right(chip).start()
+
+    def left_step(chip):
+        @pl.when((chip < p.chip) & (p.chip < last))
+        def _():
+            to_left(chip).wait_recv()
+            part[chip] = (part[chip].astype(wide) + right_in[chip].astype(wide)).astype(low)
+            to_left(chip).start()
+
+    near_left = p.chip < chips // 2
+
     def rail_step(order):
-        far = last - order
-
-        @pl.when((far > p.chip) & (p.chip > 0))
-        def _():
-            to_right(far).wait_recv()
-            part[far] = (part[far].astype(wide) + left_in[far].astype(wide)).astype(low)
-            to_right(far).start()
-
-        @pl.when((order < p.chip) & (p.chip < last))
-        def _():
-            to_left(order).wait_recv()
-            part[order] = (part[order].astype(wide) + right_in[order].astype(wide)).astype(low)
-            to_left(order).start()
+        if order < chips:
+            pl.when(near_left)(lambda: right_step(last - order))
+            pl.when(jnp.logical_not(near_left))(lambda: left_step(order))
+        else:
+            pl.when(near_left)(lambda: left_step(order - chips))
+            pl.when(jnp.logical_not(near_left))(lambda: right_step(2 * chips - 1 - order))
 
     rail_step(0)
     wgrad[...] = lax.dot_general(
@@ -1138,7 +1149,8 @@
 
     for b in range(1, grps):
         w_copy(b).start()
-    rail_step(2)
+    for order in range(2, 2 * chips):
+        rail_step(order)
     loads[2].wait()
     for b in range(1, grps):
         state_copy(b).wait_recv()
@@ -1161,7 +1173,6 @@
 
     for chip in range(chips):
         pl.when(chip != p.chip)(lambda chip=chip: o_copy(chip).start())
-    rail_step(3)
     total = gain_own[...]
     for i in range(1, slots):
         g_copy(i).wait_recv()
@@ -1415,8 +1426,8 @@
     grp_place = lax.axis_index("grp")
     use_kernels = (seq_count, grp_count, H, KVH, HD) == (8, 4, 12, 2, 128)
     if use_kernels:
-        freqs = THETA ** (-(jnp.arange(HD // 2, dtype=jnp.float32) * 2.0) / HD)
-        freqs = jnp.concatenate([freqs, freqs])[None, :]
+        half_freqs = np.float32(THETA) ** (-(np.arange(HD // 2, dtype=np.float32) * np.float32(2.0)) / np.float32(HD))
+        freqs = np.concatenate([half_freqs, half_freqs])[None, :].astype(np.float32)
         gain_rows = (gain_attn[None, :], gain_mlp[None, :])
         own_rows = padded_rows(mlp_weight)
         (

time: 307 us -> 307 us (level)
  no operation moved by 1% of the time
where the time goes in v12:
time: 307 us; the launch traced here: 303 us
  Pallas kernels  286 us (93%)
  local copies, waits for them, and re-layouts  8.96 us (3%)
  other arithmetic  7.57 us (2%)
    pallas_call x1, Pallas kernels, front_call(): pl.pallas_call(functools.partial(front_kernel, chips, 1.0 / math.sqrt(HD)...  129 us
    pallas_call x1, Pallas kernels, back_call(): pl.pallas_call(functools.partial(back_kernel, chips, 1.0 / math.sqrt(HD))...  86.1 us
    pallas_call x1, Pallas kernels, mlp_call(): pl.pallas_call(functools.partial(mlp_kernel, chips, grps, row_tiles), out...  70.8 us
    transpose x1, other arithmetic, per_device(): mlp_sums.transpose(1, 0, 2)  6.74 us

profile of v12, /device:TPU:9, one launch (start us, length us, event | category | flops | bytes accessed | tf_op | source)
XLA Modules:
  0.0 303.5 jit_solution(15783430065869022035)
XLA Ops:
  0.6 0.0 copy-start.5
  0.6 0.0 copy-start.6
  0.7 3.5 %pad.4.wm_ref.refs_0_ = bf16[3,288,1536]{2,1,0:T(8,128)(2,1)} pad(bf16[3,280,1536]{2,1,0:T(8,128)(2,1)} %bitcast.15, bf16[]{:T(256)} %constant.6.clone.1), padding=0_0x0_8x0_0 | pad | bytes 5234690 | tf_op jit(solution)/shard_map/jit(_pad)/pad | solution.py:1400
  4.1 0.0 copy-done.5
  4.2 0.6 broadcast_in_dim.10.gain_two_ref
  4.8 0.0 copy-done.6
  4.8 0.6 broadcast_in_dim.9.gain_one_ref
  5.4 129.3 %front.1 = (f32[128,1536]{1,0:T(8,128)}, f32[128,1536]{1,0:T(8,128)}, f32[4,128,128]{2,1,0:T(8,128)}, f32[4,128,128]{2,1,0:T(8,128)}, f32[128,1024]{1,0:T(8,128)...) custom-call(bf16[128,1536]{1,0:T(8,128)(2,1)} %tokens_ref.3, ...), custom_call_target="tpu_custom_call" | custom-call | tf_op jit(solution)/shard_map/front/pallas_call | solution.py:570
  134.6 70.8 %mlp.1 = (f32[128,1536]{1,0:T(8,128)}, f32[128,1536]{1,0:T(8,128)}, bf16[3,1152,1536]{2,1,0:T(8,128)(2,1)}, bf16[4,128,384]{2,1,0:T(8,128)(2,1)}, bf16[2,3,144,1...) custom-call(bf16[8,128,1536]{2,1,0:T(8,128)(2,1)} %bitcast.13, bf16[8,128,1536]{2,1,0:T(8,128)(2,1)} %bitcast.14, ...), custom_call_target="tpu_custom_call" | custom-call | tf_op jit(solution)/shard_map/mlp/pallas_call | solution.py:825
  205.5 86.1 %back.1 = (f32[128,1536]{1,0:T(8,128)}, f32[64,1664]{1,0:T(8,128)}, f32[48,1536]{1,0:T(8,128)}, f32[2,1,1536]{2,1,0:T(1,128)}, bf16[3,288,1536]{2,1,0:T(8,128)(2,1)}, /*index=5*/bf16[3,288,1536]{2,1,0:T(8,128)(2,1)}) custom-call(f32[128,1536]{1,0:T(8,128)} %get-tuple-element.44.n2g_ref, f32[128,1536]{1,0:T(8,128)} %get-tuple-element.36.state_ref, ...), custom_call_target="tpu_custom_call" | custom-call | tf_op jit(solution)/shard_map/back/pallas_call | solution.py:1266
  291.6 0.0 copy-start.3
  291.6 0.0 copy-start
  291.6 0.0 copy-start.2
  291.6 6.7 %add_bitcast_fusion = f32[280,3,1536]{2,0,1:T(8,128)} fusion(bf16[3,288,1536]{2,1,0:T(8,128)(2,1)} %get-tuple-element.63, bf16[3,288,1536]{2,1,0:T(8,128)(2,1)} %get-tuple-element.62, bf16[3,1152,1536]{2,1,0:T(8,128)(2,1)} %get-tuple-element.54.terms_ref), kind=kLoop, calls=%fused_computation | loop fusion | flops 6451200 | bytes 12902400 | tf_op jit(solution)/shard_map/transpose | solution.py:1467
  298.4 0.0 copy-start.1
  298.4 0.0 copy-start.4
  298.4 0.0 copy-done.3
  298.4 0.8 slice.24
  299.2 1.3 dynamic-slice_bitcast_fusion
  300.4 0.6 slice_reduce_fusion
  301.0 0.0 copy-done
  301.0 0.0 copy-done.2
  301.0 0.8 add_convert_fusion
  301.9 0.0 copy-done.1
  301.9 0.9 copy.20
  302.8 0.0 copy-done.4
  302.8 0.7 copy.21
Async XLA Ops:
  0.6 3.5 %copy-start.5 = (bf16[1536]{0:T(1024)(128)(2,1)S(1)}, bf16[1536]{0:T(1024)(128)(2,1)}, u32[]{:S(2)}) copy-start(bf16[1536]{0:T(1024)(128)(2,1)} %param.17) | copy-start | bytes 9220
  0.6 4.1 %copy-start.6 = (bf16[1536]{0:T(1024)(128)(2,1)S(1)}, bf16[1536]{0:T(1024)(128)(2,1)}, u32[]{:S(2)}) copy-start(bf16[1536]{0:T(1024)(128)(2,1)} %param.13) | copy-start | bytes 9220
  291.6 6.8 %copy-start.3 = (f32[64,1664]{1,0:T(8,128)S(1)}, f32[64,1664]{1,0:T(8,128)}, u32[]{:S(2)}) copy-start(f32[64,1664]{1,0:T(8,128)} %get-tuple-element.60) | copy-start | bytes 1277956
  291.6 9.4 %copy-start = (f32[128,1536]{1,0:T(8,128)S(1)}, f32[128,1536]{1,0:T(8,128)}, u32[]{:S(2)}) copy-start(f32[128,1536]{1,0:T(8,128)} %get-tuple-element.36.state_ref) | copy-start | bytes 2359300
  291.6 9.4 %copy-start.2 = (f32[128,1536]{1,0:T(8,128)S(1)}, f32[128,1536]{1,0:T(8,128)}, u32[]{:S(2)}) copy-start(f32[128,1536]{1,0:T(8,128)} %get-tuple-element.43) | copy-start | bytes 2359300
  298.4 3.5 %copy-start.1 = (f32[128,1536]{1,0:T(8,128)S(1)}, f32[128,1536]{1,0:T(8,128)}, u32[]{:S(2)}) copy-start(f32[128,1536]{1,0:T(8,128)} %get-tuple-element.75) | copy-start | bytes 2359300
  298.4 4.4 %copy-start.4 = (f32[48,1536]{1,0:T(8,128)S(1)}, f32[48,1536]{1,0:T(8,128)}, u32[]{:S(2)}) copy-start(f32[48,1536]{1,0:T(8,128)} %get-tuple-element.79) | copy-start | bytes 884740

commit v13 on v12

--- a/solution.py
+++ b/solution.py
@@ -968,6 +968,8 @@
     def state_copy(b):
         return remote(stbuf.at[0], stbuf.at[b], s_send.at[b], s_recv.at[b], p.peer(b), p.seq)
 
+    for b in range(1, grps):
+        state_copy(b).start()
     attn = attn_ref[...]
     unit = wo.shape[0] // (grps * slots)
     loads[0].wait()
@@ -1054,8 +1056,6 @@
                 copy.start()
             m_turn(2)
             m_turn(0)
-            for b in range(1, grps):
-                state_copy(b).start()
             key_sum(0)
             key_sum(KVH)
     key_sum(1)

time: 307 us -> 307 us (level)
  no operation moved by 1% of the time
where the time goes in v13:
time: 307 us; the launch traced here: 303 us
  Pallas kernels  286 us (93%)
  local copies, waits for them, and re-layouts  8.96 us (3%)
  other arithmetic  7.57 us (2%)
    pallas_call x1, Pallas kernels, front_call(): pl.pallas_call(functools.partial(front_kernel, chips, 1.0 / math.sqrt(HD)...  129 us
    pallas_call x1, Pallas kernels, back_call(): pl.pallas_call(functools.partial(back_kernel, chips, 1.0 / math.sqrt(HD))...  86.1 us
    pallas_call x1, Pallas kernels, mlp_call(): pl.pallas_call(functools.partial(mlp_kernel, chips, grps, row_tiles), out...  70.8 us
    transpose x1, other arithmetic, per_device(): mlp_sums.transpose(1, 0, 2)  6.74 us

profile of v13, /device:TPU:9, one launch (start us, length us, event | category | flops | bytes accessed | tf_op | source)
XLA Modules:
  0.0 303.5 jit_solution(15642173715830547119)
XLA Ops:
  0.6 0.0 copy-start.5
  0.6 0.0 copy-start.6
  0.7 3.5 %pad.4.wm_ref.refs_0_ = bf16[3,288,1536]{2,1,0:T(8,128)(2,1)} pad(bf16[3,280,1536]{2,1,0:T(8,128)(2,1)} %bitcast.15, bf16[]{:T(256)} %constant.6.clone.1), padding=0_0x0_8x0_0 | pad | bytes 5234690 | tf_op jit(solution)/shard_map/jit(_pad)/pad | solution.py:1400
  4.1 0.0 copy-done.5
  4.2 0.6 broadcast_in_dim.10.gain_two_ref
  4.8 0.0 copy-done.6
  4.8 0.6 broadcast_in_dim.9.gain_one_ref
  5.4 129.3 %front.1 = (f32[128,1536]{1,0:T(8,128)}, f32[128,1536]{1,0:T(8,128)}, f32[4,128,128]{2,1,0:T(8,128)}, f32[4,128,128]{2,1,0:T(8,128)}, f32[128,1024]{1,0:T(8,128)...) custom-call(bf16[128,1536]{1,0:T(8,128)(2,1)} %tokens_ref.3, ...), custom_call_target="tpu_custom_call" | custom-call | tf_op jit(solution)/shard_map/front/pallas_call | solution.py:570
  134.6 70.8 %mlp.1 = (f32[128,1536]{1,0:T(8,128)}, f32[128,1536]{1,0:T(8,128)}, bf16[3,1152,1536]{2,1,0:T(8,128)(2,1)}, bf16[4,128,384]{2,1,0:T(8,128)(2,1)}, bf16[2,3,144,1...) custom-call(bf16[8,128,1536]{2,1,0:T(8,128)(2,1)} %bitcast.13, bf16[8,128,1536]{2,1,0:T(8,128)(2,1)} %bitcast.14, ...), custom_call_target="tpu_custom_call" | custom-call | tf_op jit(solution)/shard_map/mlp/pallas_call | solution.py:825
  205.5 86.1 %back.1 = (f32[128,1536]{1,0:T(8,128)}, f32[64,1664]{1,0:T(8,128)}, f32[48,1536]{1,0:T(8,128)}, f32[2,1,1536]{2,1,0:T(1,128)}, bf16[3,288,1536]{2,1,0:T(8,128)(2,1)}, /*index=5*/bf16[3,288,1536]{2,1,0:T(8,128)(2,1)}) custom-call(f32[128,1536]{1,0:T(8,128)} %get-tuple-element.44.n2g_ref, f32[128,1536]{1,0:T(8,128)} %get-tuple-element.36.state_ref, ...), custom_call_target="tpu_custom_call" | custom-call | tf_op jit(solution)/shard_map/back/pallas_call | solution.py:1266
  291.6 0.0 copy-start.3
  291.6 0.0 copy-start
  291.6 0.0 copy-start.2
  291.6 6.7 %add_bitcast_fusion = f32[280,3,1536]{2,0,1:T(8,128)} fusion(bf16[3,288,1536]{2,1,0:T(8,128)(2,1)} %get-tuple-element.63, bf16[3,288,1536]{2,1,0:T(8,128)(2,1)} %get-tuple-element.62, bf16[3,1152,1536]{2,1,0:T(8,128)(2,1)} %get-tuple-element.54.terms_ref), kind=kLoop, calls=%fused_computation | loop fusion | flops 6451200 | bytes 12902400 | tf_op jit(solution)/shard_map/transpose | solution.py:1467
  298.4 0.0 copy-start.1
  298.4 0.0 copy-start.4
  298.4 0.0 copy-done.3
  298.4 0.8 slice.24
  299.2 1.3 dynamic-slice_bitcast_fusion
  300.4 0.6 slice_reduce_fusion
  301.0 0.0 copy-done
  301.0 0.0 copy-done.2
  301.0 0.8 add_convert_fusion
  301.9 0.0 copy-done.1
  301.9 0.9 copy.20
  302.8 0.0 copy-done.4
  302.8 0.7 copy.21
Async XLA Ops:
  0.6 3.5 %copy-start.5 = (bf16[1536]{0:T(1024)(128)(2,1)S(1)}, bf16[1536]{0:T(1024)(128)(2,1)}, u32[]{:S(2)}) copy-start(bf16[1536]{0:T(1024)(128)(2,1)} %param.17) | copy-start | bytes 9220
  0.6 4.1 %copy-start.6 = (bf16[1536]{0:T(1024)(128)(2,1)S(1)}, bf16[1536]{0:T(1024)(128)(2,1)}, u32[]{:S(2)}) copy-start(bf16[1536]{0:T(1024)(128)(2,1)} %param.13) | copy-start | bytes 9220
  291.6 6.8 %copy-start.3 = (f32[64,1664]{1,0:T(8,128)S(1)}, f32[64,1664]{1,0:T(8,128)}, u32[]{:S(2)}) copy-start(f32[64,1664]{1,0:T(8,128)} %get-tuple-element.60) | copy-start | bytes 1277956
  291.6 9.4 %copy-start = (f32[128,1536]{1,0:T(8,128)S(1)}, f32[128,1536]{1,0:T(8,128)}, u32[]{:S(2)}) copy-start(f32[128,1536]{1,0:T(8,128)} %get-tuple-element.36.state_ref) | copy-start | bytes 2359300
  291.6 9.4 %copy-start.2 = (f32[128,1536]{1,0:T(8,128)S(1)}, f32[128,1536]{1,0:T(8,128)}, u32[]{:S(2)}) copy-start(f32[128,1536]{1,0:T(8,128)} %get-tuple-element.43) | copy-start | bytes 2359300
  298.4 3.5 %copy-start.1 = (f32[128,1536]{1,0:T(8,128)S(1)}, f32[128,1536]{1,0:T(8,128)}, u32[]{:S(2)}) copy-start(f32[128,1536]{1,0:T(8,128)} %get-tuple-element.75) | copy-start | bytes 2359300
  298.4 4.4 %copy-start.4 = (f32[48,1536]{1,0:T(8,128)S(1)}, f32[48,1536]{1,0:T(8,128)}, u32[]{:S(2)}) copy-start(f32[48,1536]{1,0:T(8,128)} %get-tuple-element.79) | copy-start | bytes 884740
